TPU v7x, 512 devices: a whole 4x4x16 slice. The times are simulated.
512 devices in a mesh: rows: 128 (over x, z, core), rhs: 4 (over y).
Axes of the slice: x: 4, y: 4, z: 16, core: 2. Of those that a mesh axis runs over, the one named last changes fastest.
Arguments:
- targets: float32 [32768, 1024], P(('rows', 'rhs')), may hold values from -6 to 6
- send_order: int32 [32768], P('rows'), may hold values from 0 to 255, as said below
- send_count: int32 [128, 128], P('rows'), may hold values from 0 to 4, as said below
- recv_slot: int32 [32768], P('rows'), may hold values from 0 to 255, as said below
- panel: float32 [32768, 4096], P('rows'), may hold values from -0.09375 to 0.09375
- inv_diag: float32 [4, 1024, 1024], P(None, None, 'rows'), may hold values from -0.075 to 1.4, as said below
Outputs:
- solution: float32 [32768, 1024], P('rows', 'rhs')
Inputs may be any that keep to these rules, and one draw needn't show every extreme that they name: For each rows index a, send_order[a * 256 : (a + 1) * 256] is a permutation of 0 .. 255 whose destinations (as the steps define them) do not fall. Each row and each column of send_count sums to 256; some entry equals 4. There are a permutation p of the rows indices and a table h with send_count[a, p(j)] = h[(j - a) mod 128]. `recv_slot`: every rows index receives each slot 0 .. 255 exactly once. Each inv_diag[k] is lower triangular with diagonal entries from 0.6 to 1.4 and entries below the diagonal within -0.075 to 0.075.
All inputs are finite; a program needn't handle non-finite values.
Results may differ from a plain program's by a relative error of at most 0.0001.
Values sent between devices are 32-bit elements; how exact they have to be, the bound alone decides.
No kernel may reach another device: no remote copies, remote signals or barrier semaphores. Data moves between devices by JAX's collectives and lax.ppermute only.
A program may use at most 64 MiB of HBM per device.

v0:
```python
import jax
import jax.numpy as jnp
from jax import lax
from jax.sharding import PartitionSpec as P


def product(left, right):
    return jnp.dot(left, right, precision=lax.Precision.HIGHEST, preferred_element_type=jnp.float32)


def solve_block(inverse, pending, device, share_rows):
    totals = lax.psum(product(inverse, pending), "rows")
    owned_rows = lax.dynamic_slice_in_dim(totals, device * share_rows, share_rows, 0)
    return (totals, owned_rows)


def shards(targets, send_order, send_count, recv_slot, panel, inv_diag):
    groups = lax.axis_size("rows")
    device = lax.axis_index("rows")
    arrived = lax.all_to_all(targets, "rhs", split_axis=1, concat_axis=0, tiled=True)
    rows_local, columns = arrived.shape
    capacity = 2 * (rows_local // groups) + min(rows_local % groups, 1)
    counts = send_count[0]
    starts = jnp.cumsum(counts) - counts
    slot_number = jnp.arange(capacity, dtype=jnp.int32)
    listed = starts[:, None] + slot_number[None, :]
    filled = slot_number[None, :] < counts[:, None]
    chosen = send_order[jnp.minimum(listed, rows_local - 1)]
    outgoing = jnp.where(filled[:, :, None], arrived[chosen], 0.0)
    labels = jnp.where(filled, recv_slot[chosen], rows_local).astype(jnp.float32)
    incoming, landing = (
        lax.all_to_all(outgoing, "rows", split_axis=0, concat_axis=0, tiled=True),
        lax.all_to_all(labels, "rows", split_axis=0, concat_axis=0, tiled=True),
    )
    landing = landing.astype(jnp.int32).reshape(-1)
    residual = (
        jnp.zeros((rows_local, columns), jnp.float32)
        .at[landing]
        .set(incoming.reshape(-1, columns), mode="drop")
    )
    sections, block_rows, share_rows = inv_diag.shape
    finished = []
    totals, owned_rows = solve_block(inv_diag[0], residual[0:share_rows], device, share_rows)
    for section_index in range(sections):
        finished.append(owned_rows)
        first_live = (section_index + 1) * share_rows
        columns_block = panel[:, section_index * block_rows : (section_index + 1) * block_rows]
        if section_index + 1 < sections:
            next_end = first_live + share_rows
            updated = residual[first_live:] - product(columns_block[first_live:], totals)
            residual = jnp.concatenate([residual[:first_live], updated], axis=0)
            next_totals, next_owned = solve_block(
                inv_diag[section_index + 1], residual[first_live:next_end], device, share_rows
            )
            totals, owned_rows = (next_totals, next_owned)
        else:
            updated = residual[first_live:] - product(columns_block[first_live:], totals)
            residual = jnp.concatenate([residual[:first_live], updated], axis=0)
    return jnp.concatenate(finished + [residual[sections * share_rows :]], axis=0)


def solution(mesh):
    placed = (
        P(("rows", "rhs"), None),
        P("rows"),
        P("rows", None),
        P("rows"),
        P("rows", None),
        P(None, None, "rows"),
    )
    return jax.shard_map(
        shards, mesh=mesh, in_specs=placed, out_specs=P("rows", "rhs"), check_vma=False
    )
```

profile of v0, /device:TPU:1, one launch (start us, length us, event | category | flops | bytes accessed | tf_op | source)
XLA Modules:
  0.0 1451.5 jit_solution(13952057528990614073)
XLA Ops:
  6.5 1.7 copy.39
  8.2 5.0 all-to-all-start.1
  15.2 3.5 gather_fusion
  19.4 3.5 gather_fusion.1
  23.9 19.9 %all-to-all-start = ((f32[128,1,4]{2,1,0:T(1,128)}), f32[128,1,4]{2,1,0:T(1,128)S(1)}, u32[]{:S(2)}, u32[]{:S(2)}) async-start(f32[128,1,4]{2,1,0:T(1,128)} %copy.28), calls=%async_computation | async-start | bytes 131072 | tf_op jit(solution)/shard_map/all_to_all | solution.py:33
  43.8 1.6 gather_fusion.2
  46.5 12.3 all-to-all-done
  58.8 6.6 all-to-all-start.2
  65.8 33.0 %all-to-all-done.2 = f32[128,4,256]{2,1,0:T(4,128)S(1)} async-done(((f32[128,4,256]{2,1,0:T(4,128)}), f32[128,4,256]{2,1,0:T(4,128)S(1)}, u32[]{:S(2)}, u32[]{:S(2)}) %all-to-all-start.2) | async-done | bytes 524320 | tf_op jit(solution)/shard_map/all_to_all | solution.py:32
  98.9 2.3 scatter_custom_fusion
  101.2 2.1 convolution_bitcast_fusion.3
  103.4 326.9 %all-reduce.5.cloned.1.call-done = f32[1024,256]{0,1:T(8,128)} async-done(((f32[1024,256]{0,1:T(8,128)}), f32[1024,256]{0,1:T(8,128)}) %all-reduce.5.cloned.1.call-update) | async-done | bytes 1048592 | tf_op jit(solution)/shard_map/psum | solution.py:12
  430.3 2.6 fusion
  432.8 2.0 convolution_bitcast_fusion.2
  435.1 332.0 %all-reduce.7.cloned.1.call-done = f32[1024,256]{1,0:T(8,128)} async-done(((f32[1024,256]{1,0:T(8,128)}), f32[1024,256]{1,0:T(8,128)}) %all-reduce.7.cloned.1.call-update) | async-done | bytes 1048592 | tf_op jit(solution)/shard_map/psum | solution.py:12
  767.1 2.5 fusion.1
  769.6 2.0 convolution_bitcast_fusion.1
  771.7 332.1 %all-reduce.9.cloned.1.call-done = f32[1024,256]{1,0:T(8,128)} async-done(((f32[1024,256]{1,0:T(8,128)}), f32[1024,256]{1,0:T(8,128)}) %all-reduce.9.cloned.1.call-update) | async-done | bytes 1048592 | tf_op jit(solution)/shard_map/psum | solution.py:12
  1103.8 2.5 fusion.2
  1106.3 2.0 convolution_bitcast_fusion
  1110.0 1.3 constant_dynamic-update-slice_fusion.2
  1111.3 1.3 constant_dynamic-update-slice_fusion.1
  1112.6 327.9 %all-reduce.11.cloned.1.call-done = f32[1024,256]{1,0:T(8,128)} async-done(((f32[1024,256]{1,0:T(8,128)}), f32[1024,256]{1,0:T(8,128)}) %all-reduce.11.cloned.1.call-update) | async-done | bytes 1048592 | tf_op jit(solution)/shard_map/psum | solution.py:12
  1441.8 3.1 fusion.4
  (43 shorter events, 8.6 us)
Async XLA Ops:
  6.5 8.6 copy-start
  8.2 15.7 %all-to-all-start.1 = ((f32[64,4,256]{2,0,1:T(8,128)}), f32[64,4,256]{2,0,1:T(8,128)S(1)}, u32[]{:S(2)}, u32[]{:S(2)}) async-start(f32[64,4,256]{2,0,1:T(8,128)} %bitcast.56), calls=%async_computation.1 | async-start | bytes 524288 | tf_op jit(solution)/shard_map/all_to_all | solution.py:20
  18.7 0.7 copy-start.1
  19.4 3.7 copy-start.3
  23.9 34.9 %all-to-all-start = ((f32[128,1,4]{2,1,0:T(1,128)}), f32[128,1,4]{2,1,0:T(1,128)S(1)}, u32[]{:S(2)}, u32[]{:S(2)}) async-start(f32[128,1,4]{2,1,0:T(1,128)} %copy.28), calls=%async_computation | async-start | bytes 131072 | tf_op jit(solution)/shard_map/all_to_all | solution.py:33
  43.8 57.4 %copy-start.2 = (f32[4,1024,8]{1,2,0:T(8,128)S(1)}, f32[4,1024,8]{1,2,0:T(8,128)}, u32[]{:S(2)}) copy-start(f32[4,1024,8]{1,2,0:T(8,128)} %param.11) | copy-start | bytes 393220
  58.8 39.9 %all-to-all-start.2 = ((f32[128,4,256]{2,1,0:T(4,128)}), f32[128,4,256]{2,1,0:T(4,128)S(1)}, u32[]{:S(2)}, u32[]{:S(2)}) async-start(f32[128,4,256]{2,1,0:T(4,128)} %broadcast_select_fusion), calls=%async_computation.2 | async-start | bytes 1048576 | tf_op jit(solution)/shard_map/all_to_all | solution.py:32
  65.4 364.9 %all-reduce.5.cloned.1.call-start = ((), (), s32[]{:S(2)}) async-start(), calls=%async_computation.3 | async-start | bytes 2097152 | tf_op jit(solution)/shard_map/psum | solution.py:12
  103.3 663.7 %all-reduce.7.cloned.1.call-start = ((), (), s32[]{:S(2)}) async-start(), calls=%async_computation.4 | async-start | bytes 2097152 | tf_op jit(solution)/shard_map/psum | solution.py:12
  434.9 668.9 %all-reduce.9.cloned.1.call-start = ((), (), s32[]{:S(2)}) async-start(), calls=%async_computation.5 | async-start | bytes 2097152 | tf_op jit(solution)/shard_map/psum | solution.py:12
  771.6 668.9 %all-reduce.11.cloned.1.call-start = ((), (), s32[]{:S(2)}) async-start(), calls=%async_computation.6 | async-start | bytes 2097152 | tf_op jit(solution)/shard_map/psum | solution.py:12
Sparse Core Ops, SparseCore 0:
  103.4 326.7 all-reduce.4
  435.0 332.0 all-reduce.6
  771.7 331.9 all-reduce.8
  1108.4 332.0 all-reduce.10
where the time goes:
time: 1450 us
  waiting for transfers between devices  1360 us (94%)
  starting transfers between devices  31.8 us (2%)
  local copies, waits for them, and re-layouts  21 us (1%)
  matrix products  18.8 us (1%)
    psum x4, waiting for transfers between devices, solve_block(): totals = lax.psum(product(inverse, pending), 'rows')  1320 us
    all_to_all x1, waiting for transfers between devices, shards(): lax.all_to_all(outgoing, 'rows', split_axis=0, concat_axis=0, tiled=True)  33 us
  transfers between devices with their start and end apart: 7, of which 6 were waited for; matrix products, arithmetic and copies ran while one was open for 1% of the time, Pallas kernels for 0%

commit v1 on v0

v1 whole, which is shorter than its diff:
```python
import jax
import jax.numpy as jnp
from jax import lax
from jax.sharding import Mesh, PartitionSpec as P

ROWS = ("x", "z", "core")


def product(left, right):
    return jnp.dot(left, right, precision=lax.Precision.HIGHEST, preferred_element_type=jnp.float32)


def gather_axis(block, axis):
    copies = jnp.broadcast_to(block[None], (lax.axis_size(axis),) + block.shape)
    return lax.all_to_all(copies, axis, split_axis=0, concat_axis=0, tiled=True)


def gather_rows(block):
    q, columns = block.shape
    nx, nz, nc = (lax.axis_size(a) for a in ROWS)
    along_z = gather_axis(block, "z")
    along_x = gather_axis(along_z, "x")
    mine = along_x.reshape(nx * nz, q, columns)
    other = lax.ppermute(mine, "core", [(i, (i + 1) % nc) for i in range(nc)])
    first = lax.axis_index("core") == 0
    both = jnp.stack([jnp.where(first, mine, other), jnp.where(first, other, mine)], axis=1)
    return both.reshape(nx * nz * nc * q, columns)


def redistribute(targets, send_order, send_count, recv_slot):
    groups = lax.axis_size(ROWS)
    arrived = lax.all_to_all(targets, "rhs", split_axis=1, concat_axis=0, tiled=True)
    rows_local, columns = arrived.shape
    capacity = 4
    counts = send_count[0]
    dest = jnp.arange(groups, dtype=jnp.int32)
    starts = jnp.sum(jnp.where(dest[None, :] < dest[:, None], counts[None, :], 0), axis=1)
    slot_number = jnp.arange(capacity, dtype=jnp.int32)
    listed = starts[:, None] + slot_number[None, :]
    filled = slot_number[None, :] < counts[:, None]
    index = jnp.arange(rows_local, dtype=jnp.int32)
    position = jnp.sum(jnp.where(send_order[:, None] == index[None, :], index[:, None], 0), axis=0)
    picks = (jnp.where(filled, listed, -1)[:, :, None] == position[None, None, :])
    picked = picks.reshape(groups * capacity, rows_local).astype(jnp.float32)
    outgoing = product(picked, arrived).reshape(groups, capacity, columns)
    labels = jnp.sum(jnp.where(picks, recv_slot[None, None, :], 0), axis=2)
    labels = jnp.where(filled, labels, rows_local).astype(jnp.float32)
    labels = jnp.broadcast_to(labels[:, :, None], (groups, capacity, columns // capacity))
    sent = jnp.concatenate([outgoing, labels.reshape(groups, 1, columns)], axis=1)
    incoming = lax.all_to_all(sent, ROWS, split_axis=0, concat_axis=0, tiled=True)
    landing = incoming[:, capacity].reshape(groups, capacity, columns // capacity)[:, :, 0]
    placed = landing.astype(jnp.int32)[:, :, None] == index[None, None, :]
    placed = placed.astype(jnp.float32).reshape(groups * capacity, rows_local)
    rows = incoming[:, :capacity].reshape(groups * capacity, columns)
    return lax.dot_general(
        placed,
        rows,
        (((0,), (0,)), ((), ())),
        precision=lax.Precision.HIGHEST,
        preferred_element_type=jnp.float32,
    )


def shards(targets, send_order, send_count, recv_slot, panel, inv_diag):
    sections, block_rows, share_rows = inv_diag.shape
    inverse_rows = lax.all_to_all(inv_diag, ROWS, split_axis=1, concat_axis=2, tiled=True)
    residual = redistribute(targets, send_order, send_count, recv_slot)
    square = sections * share_rows
    top = residual[:square]
    below = residual[square:]
    finished = []
    for k in range(sections):
        pending = gather_rows(top[:share_rows])
        owned = product(inverse_rows[k], pending)
        finished.append(owned)
        solved = gather_rows(owned)
        columns_block = panel[:, k * block_rows : (k + 1) * block_rows]
        if k + 1 < sections:
            top = top[share_rows:] - product(
                columns_block[(k + 1) * share_rows : square], solved
            )
        below = below - product(columns_block[square:], solved)
    return jnp.concatenate(finished + [below], axis=0)


def solution(mesh):
    ny = mesh.shape["rhs"]
    split = Mesh(mesh.devices.reshape(4, 16, 2, ny), ROWS + ("rhs",))
    placed = (
        P(ROWS + ("rhs",), None),
        P(ROWS),
        P(ROWS, None),
        P(ROWS),
        P(ROWS, None),
        P(None, None, ROWS),
    )
    return jax.shard_map(
        shards, mesh=split, in_specs=placed, out_specs=P(ROWS, "rhs"), check_vma=False
    )
```

time: 1450 us -> 425 us (0.29)
  waiting for transfers between devices: 1360 us -> 28.5 us
  blocking collectives: 0 us -> 268 us
  starting transfers between devices: 31.8 us -> 69.8 us
    psum x4 -> x0, waiting for transfers between devices: 1320 us -> none  [solve_block(): totals = lax.psum(product(inverse, pending), 'rows')]
    all_to_all x0 -> x15, blocking collectives: none -> 268 us  [the longest x14 193 us: gather_axis(): return lax.all_to_all(copies, axis, split_axis=0, concat_axis=0, tiled=True)]
    ppermute x0 -> x8, starting transfers between devices: none -> 45.9 us  [gather_rows(): other = lax.ppermute(mine, 'core', [(i, (i + 1) % nc) for i in range(nc)])]
    all_to_all x3 -> x4, waiting for transfers between devices: 45.2 us -> 23.5 us  [the longest x1 14.4 us: shards(): lax.all_to_all(inv_diag, ROWS, split_axis=1, concat_axis=2, tiled=True)]
    all_to_all x3 -> x4, starting transfers between devices: 31.4 us -> 23.8 us  [the longest x1 11.2 us: shards(): lax.all_to_all(inv_diag, ROWS, split_axis=1, concat_axis=2, tiled=True)]
  transfers between devices with their start and end apart: 7 -> 12, of which waited for: 6 -> 8; matrix products, arithmetic and copies ran while one was open for 1% -> 8% of each run, Pallas kernels for 0% -> 0%
where the time goes in v1:
time: 425 us; the launch traced here: 423 us
  blocking collectives  268 us (63%)
  starting transfers between devices  69.8 us (16%)
  waiting for transfers between devices  28.5 us (7%)
  local copies, waits for them, and re-layouts  25.9 us (6%)
  matrix products  20.2 us (5%)
  other arithmetic  10.3 us (2%)
    all_to_all x14, blocking collectives, gather_axis(): return lax.all_to_all(copies, axis, split_axis=0, concat_axis=0, tiled=True)  193 us
    all_to_all x1, blocking collectives, redistribute(): lax.all_to_all(sent, ROWS, split_axis=0, concat_axis=0, tiled=True)  75.1 us
    ppermute x8, starting transfers between devices, gather_rows(): other = lax.ppermute(mine, 'core', [(i, (i + 1) % nc) for i in range(nc)])  45.9 us
    dot_general x12, matrix products, product(): jnp.dot(left, right, precision=lax.Precision.HIGHEST, preferred_element_t...  19.7 us
    all_to_all x1, waiting for transfers between devices, shards(): lax.all_to_all(inv_diag, ROWS, split_axis=1, concat_axis=2, tiled=True)  14.4 us
    all_to_all x1, starting transfers between devices, shards(): lax.all_to_all(inv_diag, ROWS, split_axis=1, concat_axis=2, tiled=True)  11.2 us
  transfers between devices with their start and end apart: 12, of which 8 were waited for; matrix products, arithmetic and copies ran while one was open for 8% of the time, Pallas kernels for 0%

profile of v1, /device:TPU:1, one launch (start us, length us, event | category | flops | bytes accessed | tf_op | source)
XLA Modules:
  0.0 423.5 jit_solution(159166670497763224)
XLA Ops:
  1.7 5.0 %all-to-all-start = ((f32[64,4,256]{2,0,1:T(8,128)}), f32[64,4,256]{2,0,1:T(8,128)S(1)}, u32[]{:S(2)}, u32[]{:S(2)}) async-start(f32[64,4,256]{2,0,1:T(8,128)} %bitcast.146), calls=%async_computation | async-start | bytes 524288 | tf_op jit(solution)/shard_map/all_to_all | solution.py:32
  13.1 75.1 %all_to_all.119 = f32[128,5,256]{2,1,0:T(8,128)S(1)} all-to-all(f32[128,5,256]{2,1,0:T(8,128)S(1)} %copy.46), channel_id=1, replica_groups=mesh['x'=4,'z'=16,'core'=2,'rhs'=4] {'x','z','core'}, dimensions={0} | all-to-all | bytes 1310720 | tf_op jit(solution)/shard_map/all_to_all | solution.py:50
  89.2 16.8 %all_to_all.120 = f32[16,8,256]{2,1,0:T(8,128)S(1)} all-to-all(f32[16,8,256]{2,1,0:T(8,128)S(1)} %broadcast_in_dim.86), channel_id=1, replica_groups=mesh['x'=4,'z'=16,'core'=2,'rhs'=4] {'z'}, dimensions={0} | all-to-all | bytes 262144 | tf_op jit(solution)/shard_map/all_to_all | solution.py:15
  117.2 11.2 %all-to-all-start.4 = ((f32[128,1,256]{2,1,0:T(1,128)}), f32[128,1,256]{2,1,0:T(1,128)S(1)}, u32[]{:S(2)}, u32[]{:S(2)}) async-start(f32[128,1,256]{2,1,0:T(1,128)} %reshape.190), calls=%async_computation.4 | async-start | bytes 262144 | tf_op jit(solution)/shard_map/all_to_all | solution.py:66
  131.4 14.4 %all-to-all-done.4 = f32[128,1,256]{2,1,0:T(1,128)S(1)} async-done(((f32[128,1,256]{2,1,0:T(1,128)}), f32[128,1,256]{2,1,0:T(1,128)S(1)}, u32[]{:S(2)}, u32[]{:S(2)}) %all-to-all-start.4) | async-done | bytes 131104 | tf_op jit(solution)/shard_map/all_to_all | solution.py:66
  159.5 15.1 %all_to_all.121 = f32[16,8,256]{2,1,0:T(8,128)S(1)} all-to-all(f32[16,8,256]{2,1,0:T(8,128)S(1)} %broadcast_in_dim.88), channel_id=1, replica_groups=mesh['x'=4,'z'=16,'core'=2,'rhs'=4] {'z'}, dimensions={0} | all-to-all | bytes 262144 | tf_op jit(solution)/shard_map/all_to_all | solution.py:15
  174.7 9.3 %all_to_all.122 = f32[4,16,8,256]{3,2,1,0:T(8,128)S(1)} all-to-all(f32[4,16,8,256]{3,2,1,0:T(8,128)S(1)} %broadcast_in_dim.89), channel_id=1, replica_groups=mesh['x'=4,'z'=16,'core'=2,'rhs'=4] {'x'}, dimensions={0} | all-to-all | bytes 1048576 | tf_op jit(solution)/shard_map/all_to_all | solution.py:15
  184.0 6.6 %collective-permute-start.1 = (f32[64,8,256]{2,1,0:T(8,128)S(1)}, f32[64,8,256]{2,1,0:T(8,128)S(1)}, u32[]{:S(2)}, u32[]{:S(2)}) collective-permute-start(f32[64,8,256]{2,1,0:T(8,128)S(1)} %bitcast.164), channel_id=1, source_target_pairs={{0,4},{4,0},{1,5},{5,1},{2,6},{6,2},{3,7},{7,3},{8,12},{12,8},{9,1... | collective-permute-start | bytes 1572872 | tf_op jit(solution)/shard_map/ppermute | solution.py:24
  194.0 16.3 %all_to_all.123 = f32[16,8,256]{2,1,0:T(8,128)S(1)} all-to-all(f32[16,8,256]{2,1,0:T(8,128)S(1)} %broadcast_in_dim.90), channel_id=1, replica_groups=mesh['x'=4,'z'=16,'core'=2,'rhs'=4] {'z'}, dimensions={0} | all-to-all | bytes 262144 | tf_op jit(solution)/shard_map/all_to_all | solution.py:15
  210.4 9.3 %all_to_all.124 = f32[4,16,8,256]{3,2,1,0:T(8,128)S(1)} all-to-all(f32[4,16,8,256]{3,2,1,0:T(8,128)S(1)} %broadcast_in_dim.91), channel_id=1, replica_groups=mesh['x'=4,'z'=16,'core'=2,'rhs'=4] {'x'}, dimensions={0} | all-to-all | bytes 1048576 | tf_op jit(solution)/shard_map/all_to_all | solution.py:15
  219.7 6.3 %collective-permute-start.2 = (f32[64,8,256]{2,1,0:T(8,128)S(1)}, f32[64,8,256]{2,1,0:T(8,128)S(1)}, u32[]{:S(2)}, u32[]{:S(2)}) collective-permute-start(f32[64,8,256]{2,1,0:T(8,128)S(1)} %bitcast.162), channel_id=1, source_target_pairs={{0,4},{4,0},{1,5},{5,1},{2,6},{6,2},{3,7},{7,3},{8,12},{12,8},{9,1... | collective-permute-start | bytes 1572872 | tf_op jit(solution)/shard_map/ppermute | solution.py:24
  229.0 17.5 %all_to_all.125 = f32[16,8,256]{2,1,0:T(8,128)S(1)} all-to-all(f32[16,8,256]{2,1,0:T(8,128)S(1)} %broadcast_in_dim.92), channel_id=1, replica_groups=mesh['x'=4,'z'=16,'core'=2,'rhs'=4] {'z'}, dimensions={0} | all-to-all | bytes 262144 | tf_op jit(solution)/shard_map/all_to_all | solution.py:15
  246.6 9.3 %all_to_all.126 = f32[4,16,8,256]{3,2,1,0:T(8,128)S(1)} all-to-all(f32[4,16,8,256]{3,2,1,0:T(8,128)S(1)} %broadcast_in_dim.93), channel_id=1, replica_groups=mesh['x'=4,'z'=16,'core'=2,'rhs'=4] {'x'}, dimensions={0} | all-to-all | bytes 1048576 | tf_op jit(solution)/shard_map/all_to_all | solution.py:15
  255.9 6.3 %collective-permute-start.3 = (f32[64,8,256]{2,1,0:T(8,128)S(1)}, f32[64,8,256]{2,1,0:T(8,128)S(1)}, u32[]{:S(2)}, u32[]{:S(2)}) collective-permute-start(f32[64,8,256]{2,1,0:T(8,128)S(1)} %bitcast.165), channel_id=1, source_target_pairs={{0,4},{4,0},{1,5},{5,1},{2,6},{6,2},{3,7},{7,3},{8,12},{12,8},{9,1... | collective-permute-start | bytes 1572872 | tf_op jit(solution)/shard_map/ppermute | solution.py:24
  265.5 17.5 %all_to_all.127 = f32[16,8,256]{2,1,0:T(8,128)S(1)} all-to-all(f32[16,8,256]{2,1,0:T(8,128)S(1)} %broadcast_in_dim.94), channel_id=1, replica_groups=mesh['x'=4,'z'=16,'core'=2,'rhs'=4] {'z'}, dimensions={0} | all-to-all | bytes 262144 | tf_op jit(solution)/shard_map/all_to_all | solution.py:15
  283.1 9.3 %all_to_all.128 = f32[4,16,8,256]{3,2,1,0:T(8,128)S(1)} all-to-all(f32[4,16,8,256]{3,2,1,0:T(8,128)S(1)} %broadcast_in_dim.95), channel_id=1, replica_groups=mesh['x'=4,'z'=16,'core'=2,'rhs'=4] {'x'}, dimensions={0} | all-to-all | bytes 1048576 | tf_op jit(solution)/shard_map/all_to_all | solution.py:15
  292.4 6.3 %collective-permute-start.4 = (f32[64,8,256]{2,1,0:T(8,128)S(1)}, f32[64,8,256]{2,1,0:T(8,128)}, u32[]{:S(2)}, u32[]{:S(2)}) collective-permute-start(f32[64,8,256]{2,1,0:T(8,128)S(1)} %bitcast.163), channel_id=1, source_target_pairs={{0,4},{4,0},{1,5},{5,1},{2,6},{6,2},{3,7},{7,3},{8,12},{12,8},{9,1... | collective-permute-start | bytes 1572872 | tf_op jit(solution)/shard_map/ppermute | solution.py:24
  303.1 17.5 %all_to_all.129 = f32[16,8,256]{2,1,0:T(8,128)S(1)} all-to-all(f32[16,8,256]{2,1,0:T(8,128)S(1)} %broadcast_in_dim.96), channel_id=1, replica_groups=mesh['x'=4,'z'=16,'core'=2,'rhs'=4] {'z'}, dimensions={0} | all-to-all | bytes 262144 | tf_op jit(solution)/shard_map/all_to_all | solution.py:15
  320.7 9.3 %all_to_all.130 = f32[4,16,8,256]{3,2,1,0:T(8,128)S(1)} all-to-all(f32[4,16,8,256]{3,2,1,0:T(8,128)S(1)} %broadcast_in_dim.97), channel_id=1, replica_groups=mesh['x'=4,'z'=16,'core'=2,'rhs'=4] {'x'}, dimensions={0} | all-to-all | bytes 1048576 | tf_op jit(solution)/shard_map/all_to_all | solution.py:15
  330.0 6.2 %collective-permute-start.5 = (f32[64,8,256]{2,1,0:T(8,128)S(1)}, f32[64,8,256]{2,1,0:T(8,128)S(1)}, u32[]{:S(2)}, u32[]{:S(2)}) collective-permute-start(f32[64,8,256]{2,1,0:T(8,128)S(1)} %bitcast.166), channel_id=1, source_target_pairs={{0,4},{4,0},{1,5},{5,1},{2,6},{6,2},{3,7},{7,3},{8,12},{12,8},{9,1... | collective-permute-start | bytes 1572872 | tf_op jit(solution)/shard_map/ppermute | solution.py:24
  339.2 17.8 %all_to_all.131 = f32[16,8,256]{2,1,0:T(8,128)S(1)} all-to-all(f32[16,8,256]{2,1,0:T(8,128)S(1)} %broadcast_in_dim.98), channel_id=1, replica_groups=mesh['x'=4,'z'=16,'core'=2,'rhs'=4] {'z'}, dimensions={0} | all-to-all | bytes 262144 | tf_op jit(solution)/shard_map/all_to_all | solution.py:15
  357.1 10.0 %all_to_all.132 = f32[4,16,8,256]{3,2,1,0:T(8,128)} all-to-all(f32[4,16,8,256]{3,2,1,0:T(8,128)S(1)} %broadcast_in_dim.99), channel_id=1, replica_groups=mesh['x'=4,'z'=16,'core'=2,'rhs'=4] {'x'}, dimensions={0} | all-to-all | bytes 1048576 | tf_op jit(solution)/shard_map/all_to_all | solution.py:15
  367.1 6.3 %collective-permute-start.6 = (f32[64,8,256]{2,1,0:T(8,128)}, f32[64,8,256]{2,1,0:T(8,128)}, u32[]{:S(2)}, u32[]{:S(2)}) collective-permute-start(f32[64,8,256]{2,1,0:T(8,128)} %bitcast.41), channel_id=1, source_target_pairs={{0,4},{4,0},{1,5},{5,1},{2,6},{6,2},{3,7},{7,3},{8,12},{12,8},{9,1... | collective-permute-start | bytes 1572872 | tf_op jit(solution)/shard_map/ppermute | solution.py:24
  379.7 17.8 %all_to_all.133 = f32[16,8,256]{2,1,0:T(8,128)S(1)} all-to-all(f32[16,8,256]{2,1,0:T(8,128)S(1)} %broadcast_in_dim.100), channel_id=1, replica_groups=mesh['x'=4,'z'=16,'core'=2,'rhs'=4] {'z'}, dimensions={0} | all-to-all | bytes 262144 | tf_op jit(solution)/shard_map/all_to_all | solution.py:15
  (101 shorter events, 86.1 us)
Async XLA Ops:
  1.7 10.5 %all-to-all-start = ((f32[64,4,256]{2,0,1:T(8,128)}), f32[64,4,256]{2,0,1:T(8,128)S(1)}, u32[]{:S(2)}, u32[]{:S(2)}) async-start(f32[64,4,256]{2,0,1:T(8,128)} %bitcast.146), calls=%async_computation | async-start | bytes 524288 | tf_op jit(solution)/shard_map/all_to_all | solution.py:32
  12.7 97.6 %copy-start = (f32[4,1024,8]{1,2,0:T(8,128)S(1)}, f32[4,1024,8]{1,2,0:T(8,128)}, u32[]{:S(2)}) copy-start(f32[4,1024,8]{1,2,0:T(8,128)} %param.11) | copy-start | bytes 393220
  106.9 10.4 %all-to-all-start.3 = ((f32[4,16,8,256]{3,2,1,0:T(8,128)}), f32[4,16,8,256]{3,2,1,0:T(8,128)S(1)}, u32[]{:S(2)}, u32[]{:S(2)}) async-start(f32[4,16,8,256]{3,2,1,0:T(8,128)} %broadcast_in_dim.87), calls=%async_computation.3 | async-start | bytes 1048576 | tf_op jit(solution)/shard_map/all_to_all | solution.py:15
  117.2 28.6 %all-to-all-start.4 = ((f32[128,1,256]{2,1,0:T(1,128)}), f32[128,1,256]{2,1,0:T(1,128)S(1)}, u32[]{:S(2)}, u32[]{:S(2)}) async-start(f32[128,1,256]{2,1,0:T(1,128)} %reshape.190), calls=%async_computation.4 | async-start | bytes 262144 | tf_op jit(solution)/shard_map/all_to_all | solution.py:66
  128.4 28.6 %collective-permute-start = (f32[64,8,256]{2,1,0:T(8,128)S(1)}, f32[64,8,256]{2,1,0:T(8,128)}, u32[]{:S(2)}, u32[]{:S(2)}) collective-permute-start(f32[64,8,256]{2,1,0:T(8,128)S(1)} %bitcast.161), channel_id=1, source_target_pairs={{0,4},{4,0},{1,5},{5,1},{2,6},{6,2},{3,7},{7,3},{8,12},{12,8},{9,1... | collective-permute-start | bytes 1572872 | tf_op jit(solution)/shard_map/ppermute | solution.py:24
  184.0 8.2 %collective-permute-start.1 = (f32[64,8,256]{2,1,0:T(8,128)S(1)}, f32[64,8,256]{2,1,0:T(8,128)S(1)}, u32[]{:S(2)}, u32[]{:S(2)}) collective-permute-start(f32[64,8,256]{2,1,0:T(8,128)S(1)} %bitcast.164), channel_id=1, source_target_pairs={{0,4},{4,0},{1,5},{5,1},{2,6},{6,2},{3,7},{7,3},{8,12},{12,8},{9,1... | collective-permute-start | bytes 1572872 | tf_op jit(solution)/shard_map/ppermute | solution.py:24
  219.7 7.8 %collective-permute-start.2 = (f32[64,8,256]{2,1,0:T(8,128)S(1)}, f32[64,8,256]{2,1,0:T(8,128)S(1)}, u32[]{:S(2)}, u32[]{:S(2)}) collective-permute-start(f32[64,8,256]{2,1,0:T(8,128)S(1)} %bitcast.162), channel_id=1, source_target_pairs={{0,4},{4,0},{1,5},{5,1},{2,6},{6,2},{3,7},{7,3},{8,12},{12,8},{9,1... | collective-permute-start | bytes 1572872 | tf_op jit(solution)/shard_map/ppermute | solution.py:24
  255.9 7.8 %collective-permute-start.3 = (f32[64,8,256]{2,1,0:T(8,128)S(1)}, f32[64,8,256]{2,1,0:T(8,128)S(1)}, u32[]{:S(2)}, u32[]{:S(2)}) collective-permute-start(f32[64,8,256]{2,1,0:T(8,128)S(1)} %bitcast.165), channel_id=1, source_target_pairs={{0,4},{4,0},{1,5},{5,1},{2,6},{6,2},{3,7},{7,3},{8,12},{12,8},{9,1... | collective-permute-start | bytes 1572872 | tf_op jit(solution)/shard_map/ppermute | solution.py:24
  292.4 8.1 %collective-permute-start.4 = (f32[64,8,256]{2,1,0:T(8,128)S(1)}, f32[64,8,256]{2,1,0:T(8,128)}, u32[]{:S(2)}, u32[]{:S(2)}) collective-permute-start(f32[64,8,256]{2,1,0:T(8,128)S(1)} %bitcast.163), channel_id=1, source_target_pairs={{0,4},{4,0},{1,5},{5,1},{2,6},{6,2},{3,7},{7,3},{8,12},{12,8},{9,1... | collective-permute-start | bytes 1572872 | tf_op jit(solution)/shard_map/ppermute | solution.py:24
  330.0 7.5 %collective-permute-start.5 = (f32[64,8,256]{2,1,0:T(8,128)S(1)}, f32[64,8,256]{2,1,0:T(8,128)S(1)}, u32[]{:S(2)}, u32[]{:S(2)}) collective-permute-start(f32[64,8,256]{2,1,0:T(8,128)S(1)} %bitcast.166), channel_id=1, source_target_pairs={{0,4},{4,0},{1,5},{5,1},{2,6},{6,2},{3,7},{7,3},{8,12},{12,8},{9,1... | collective-permute-start | bytes 1572872 | tf_op jit(solution)/shard_map/ppermute | solution.py:24
  367.1 9.9 %collective-permute-start.6 = (f32[64,8,256]{2,1,0:T(8,128)}, f32[64,8,256]{2,1,0:T(8,128)}, u32[]{:S(2)}, u32[]{:S(2)}) collective-permute-start(f32[64,8,256]{2,1,0:T(8,128)} %bitcast.41), channel_id=1, source_target_pairs={{0,4},{4,0},{1,5},{5,1},{2,6},{6,2},{3,7},{7,3},{8,12},{12,8},{9,1... | collective-permute-start | bytes 1572872 | tf_op jit(solution)/shard_map/ppermute | solution.py:24
  398.4 11.5 %all-to-all-start.18 = ((f32[4,16,8,256]{3,2,1,0:T(8,128)}), f32[4,16,8,256]{3,2,1,0:T(8,128)}, u32[]{:S(2)}, u32[]{:S(2)}) async-start(f32[4,16,8,256]{3,2,1,0:T(8,128)} %broadcast_in_dim.101), calls=%async_computation.18 | async-start | bytes 1048576 | tf_op jit(solution)/shard_map/all_to_all | solution.py:15
  409.9 9.3 %collective-permute-start.7 = (f32[64,8,256]{2,1,0:T(8,128)}, f32[64,8,256]{2,1,0:T(8,128)S(1)}, u32[]{:S(2)}, u32[]{:S(2)}) collective-permute-start(f32[64,8,256]{2,1,0:T(8,128)} %bitcast.49), channel_id=1, source_target_pairs={{0,4},{4,0},{1,5},{5,1},{2,6},{6,2},{3,7},{7,3},{8,12},{12,8},{9,1... | collective-permute-start | bytes 1572872 | tf_op jit(solution)/shard_map/ppermute | solution.py:24

commit v2 on v1

v2 whole, which is shorter than its diff:
```python
import jax
import jax.numpy as jnp
from jax import lax
from jax.sharding import Mesh, PartitionSpec as P

ROWS = ("x", "z", "core")
SWAP = [(0, 1), (1, 0)]


def product(left, right, contract=((1,), (0,))):
    return lax.dot_general(
        left,
        right,
        (contract, ((), ())),
        precision=lax.Precision.HIGHEST,
        preferred_element_type=jnp.float32,
    )


def redistribute(targets, send_order, send_count, recv_slot):
    groups = lax.axis_size(ROWS)
    arrived = lax.all_to_all(targets, "rhs", split_axis=1, concat_axis=0, tiled=True)
    rows_local, columns = arrived.shape
    capacity, tag = 4, 128
    counts = send_count[0]
    dest = jnp.arange(groups, dtype=jnp.int32)
    starts = jnp.sum(jnp.where(dest[None, :] < dest[:, None], counts[None, :], 0), axis=1)
    slot_number = jnp.arange(capacity, dtype=jnp.int32)
    listed = starts[:, None] + slot_number[None, :]
    listed = jnp.where(slot_number[None, :] < counts[:, None], listed, -1)
    index = jnp.arange(rows_local, dtype=jnp.int32)
    position = jnp.sum(jnp.where(send_order[:, None] == index[None, :], index[:, None], 0), axis=0)
    picked = (listed[:, :, None] == position[None, None, :]).astype(jnp.float32)
    picked = picked.reshape(groups * capacity, rows_local)
    landing = jnp.broadcast_to((recv_slot + 1).astype(jnp.float32)[:, None], (rows_local, tag))
    sent = product(picked, jnp.concatenate([arrived, landing], axis=1))
    incoming = lax.all_to_all(
        sent.reshape(groups, capacity, columns + tag), ROWS, split_axis=0, concat_axis=0, tiled=True
    ).reshape(groups * capacity, columns + tag)
    slots = (incoming[:, columns : columns + 1] - 1.0).astype(jnp.int32)
    placed = (slots == index[None, :]).astype(jnp.float32)
    return product(placed, incoming[:, :columns], ((0,), (0,)))


def shards(targets, send_order, send_count, recv_slot, panel, inv_diag):
    sections, block_rows, share = inv_diag.shape
    nx, nz, nc = (lax.axis_size(a) for a in ROWS)
    first = lax.axis_index("core") == 0
    square = sections * share
    pairs = [(j, k) for j in range(1, sections) for k in range(j)]
    tiles = [
        panel[j * share : (j + 1) * share, k * block_rows : (k + 1) * block_rows] for j, k in pairs
    ]
    local = jnp.concatenate([jnp.stack(tiles), jnp.swapaxes(inv_diag, 1, 2)], axis=0)
    weights = lax.all_gather(local, "z")

    def weight(i):
        return weights[:, i].reshape(nz * share, block_rows)

    residual = redistribute(targets, send_order, send_count, recv_slot)
    columns = residual.shape[1]
    tops = lax.all_gather(residual[:square].reshape(sections, share, columns), "z")
    pending = [tops[:, k].reshape(nz * share, columns) for k in range(sections)]
    below = residual[square:]
    finished = []
    for k in range(sections):
        partial = product(weight(len(pairs) + k), pending[k], ((0,), (0,)))
        partial = partial.reshape(nx * nz, nc, share, columns)
        keep = jnp.where(first, partial[:, 0], partial[:, 1])
        give = jnp.where(first, partial[:, 1], partial[:, 0])
        half = keep + lax.ppermute(give, "core", SWAP)
        half = half.reshape(nx, nz, share, columns)
        owned = jnp.sum(
            lax.all_to_all(half, "x", split_axis=0, concat_axis=0, tiled=True), axis=0
        )
        finished.append(lax.dynamic_index_in_dim(owned, lax.axis_index("z"), 0, keepdims=False))
        copies = jnp.broadcast_to(owned[None], (nx,) + owned.shape)
        mine = lax.all_to_all(copies, "x", split_axis=0, concat_axis=0, tiled=True)
        mine = mine.reshape(nx * nz, share, columns)
        other = lax.ppermute(mine, "core", SWAP)
        solved = jnp.stack([jnp.where(first, mine, other), jnp.where(first, other, mine)], axis=1)
        solved = solved.reshape(block_rows, columns)
        for j in range(k + 1, sections):
            pending[j] = pending[j] - product(weight(pairs.index((j, k))), solved)
        below = below - product(panel[square:, k * block_rows : (k + 1) * block_rows], solved)
    return jnp.concatenate(finished + [below], axis=0)


def solution(mesh):
    ny = mesh.shape["rhs"]
    split = Mesh(mesh.devices.reshape(4, 16, 2, ny), ROWS + ("rhs",))
    placed = (
        P(ROWS + ("rhs",), None),
        P(ROWS),
        P(ROWS, None),
        P(ROWS),
        P(ROWS, None),
        P(None, None, ROWS),
    )
    return jax.shard_map(
        shards, mesh=split, in_specs=placed, out_specs=P(ROWS, "rhs"), check_vma=False
    )
```

time: 425 us -> 310 us (0.73)
  blocking collectives: 268 us -> 85.8 us
  waiting for transfers between devices: 28.5 us -> 83.1 us
  between operations: 0.57 us -> 13.9 us
  matrix products: 20.2 us -> 25.3 us
    all_to_all x15 -> x5, blocking collectives: 268 us -> 56.3 us  [the longest x3 35.5 us: shards(): lax.all_to_all(half, 'x', split_axis=0, concat_axis=0, tiled=True)]
    all_to_all x3 -> x4, waiting for transfers between devices: 21.9 us -> 72.4 us  [the longest x1 53.3 us: redistribute(): lax.all_to_all(sent.reshape(groups, capacity, columns + tag), ROWS, split...]
    all_gather x0 -> x1, blocking collectives: none -> 29.5 us  [shards(): lax.all_gather(residual[:square].reshape(sections, share, columns), 'z')]
    ppermute x8, starting transfers between devices: 45.9 us -> 29.9 us  [the longest x4 17.2 us: shards(): other = lax.ppermute(mine, 'core', SWAP)]
    all_to_all x3 -> x4, starting transfers between devices: 18.8 us -> 32.7 us  [the longest x1 21 us: redistribute(): lax.all_to_all(sent.reshape(groups, capacity, columns + tag), ROWS, split...]
    dot_general x0 -> x6, local copies, waits for them, and re-layouts: none -> 7.78 us  [product(): lax.dot_general(left, right, (contract, ((), ())), precision=lax.Precisio...]
    slice x10 -> x0, local copies, waits for them, and re-layouts: 7.36 us -> none  [the longest x5 7.12 us: shards(): owned = product(inverse_rows[k], pending)]
    dot_general x13 -> x16, matrix products: 20.2 us -> 25.3 us  [product(): lax.dot_general(left, right, (contract, ((), ())), precision=lax.Precisio...]
  transfers between devices with their start and end apart: 12 -> 14, of which waited for: 8 -> 10; matrix products, arithmetic and copies ran while one was open for 8% -> 9% of each run, Pallas kernels for 0% -> 0%
where the time goes in v2:
time: 310 us; the launch traced here: 308 us
  blocking collectives  85.8 us (28%)
  waiting for transfers between devices  83.1 us (27%)
  starting transfers between devices  67.6 us (22%)
  matrix products  25.3 us (8%)
  local copies, waits for them, and re-layouts  23.5 us (8%)
  between operations  13.9 us (4%)
  other arithmetic  9.04 us (3%)
    all_to_all x1, waiting for transfers between devices, redistribute(): lax.all_to_all(sent.reshape(groups, capacity, columns + tag), ROWS, split...  53.3 us
    all_to_all x3, blocking collectives, shards(): lax.all_to_all(half, 'x', split_axis=0, concat_axis=0, tiled=True)  35.5 us
    all_gather x1, blocking collectives, shards(): lax.all_gather(residual[:square].reshape(sections, share, columns), 'z')  29.5 us
    dot_general x16, matrix products, product(): lax.dot_general(left, right, (contract, ((), ())), precision=lax.Precisio...  25.3 us
    all_to_all x1, starting transfers between devices, redistribute(): lax.all_to_all(sent.reshape(groups, capacity, columns + tag), ROWS, split...  21 us
    all_to_all x2, blocking collectives, shards(): mine = lax.all_to_all(copies, 'x', split_axis=0, concat_axis=0, tiled=True)  20.8 us
    ppermute x4, starting transfers between devices, shards(): other = lax.ppermute(mine, 'core', SWAP)  17.2 us
    ppermute x4, starting transfers between devices, shards(): half = keep + lax.ppermute(give, 'core', SWAP)  12.6 us
  transfers between devices with their start and end apart: 14, of which 10 were waited for; matrix products, arithmetic and copies ran while one was open for 9% of the time, Pallas kernels for 0%

profile of v2, /device:TPU:1, one launch (start us, length us, event | category | flops | bytes accessed | tf_op | source)
XLA Modules:
  0.0 308.2 jit_solution(10613642046033010144)
XLA Ops:
  14.4 5.0 %all-to-all-start = ((f32[64,4,256]{2,0,1:T(8,128)}), f32[64,4,256]{2,0,1:T(8,128)S(1)}, u32[]{:S(2)}, u32[]{:S(2)}) async-start(f32[64,4,256]{2,0,1:T(8,128)} %bitcast.198), calls=%async_computation | async-start | bytes 524288 | tf_op jit(solution)/shard_map/all_to_all | solution.py:22
  22.4 2.6 all-to-all-done
  27.1 21.0 %all-to-all-start.1 = ((f32[128,4,384]{2,1,0:T(4,128)}), f32[128,4,384]{2,1,0:T(4,128)S(1)}, u32[]{:S(2)}, u32[]{:S(2)}) async-start(f32[128,4,384]{2,1,0:T(4,128)} %copy.84), calls=%async_computation.1 | async-start | bytes 1572864 | tf_op jit(solution)/shard_map/all_to_all | solution.py:37
  48.1 53.3 %all-to-all-done.1 = f32[128,4,384]{2,1,0:T(4,128)S(1)} async-done(((f32[128,4,384]{2,1,0:T(4,128)}), f32[128,4,384]{2,1,0:T(4,128)S(1)}, u32[]{:S(2)}, u32[]{:S(2)}) %all-to-all-start.1) | async-done | bytes 786464 | tf_op jit(solution)/shard_map/all_to_all | solution.py:37
  102.6 29.5 %all_gather.11 = f32[16,4,8,256]{3,2,1,0:T(8,128)S(1)} all-gather(f32[1,4,8,256]{3,2,1,0:T(8,128)S(1)} %slice_bitcast_fusion.21), channel_id=1, replica_groups=mesh['x'=4,'z'=16,'core'=2,'rhs'=4] {'z'}, dimensions={0}, use_global_device_ids=true | all-gather | bytes 557056 | tf_op jit(solution)/shard_map/all_gather | solution.py:62
  132.1 2.7 slice_bitcast_fusion.6
  136.0 6.5 %collective-permute-start = (f32[64,8,256]{2,1,0:T(8,128)S(1)}, f32[64,8,256]{2,1,0:T(8,128)S(1)}, u32[]{:S(2)}, u32[]{:S(2)}) collective-permute-start(f32[64,8,256]{2,1,0:T(8,128)S(1)} %select_bitcast_fusion.11), channel_id=1, source_target_pairs={{0,4},{4,0},{1,5},{5,1},{2,6},{6,2},{3,7},{7,3},{8,12},{12,8},{9,1... | collective-permute-start | bytes 1572872 | tf_op jit(solution)/shard_map/ppermute | solution.py:71
  144.2 12.3 %all_to_all.64 = f32[4,16,8,256]{3,2,1,0:T(8,128)S(1)} all-to-all(f32[4,16,8,256]{3,2,1,0:T(8,128)S(1)} %bitcast.220), channel_id=1, replica_groups=mesh['x'=4,'z'=16,'core'=2,'rhs'=4] {'x'}, dimensions={0} | all-to-all | bytes 1048576 | tf_op jit(solution)/shard_map/all_to_all | solution.py:74
  156.6 10.1 %all_to_all.65 = f32[4,16,8,256]{3,2,1,0:T(8,128)S(1)} all-to-all(f32[4,16,8,256]{3,2,1,0:T(8,128)S(1)} %broadcast_in_dim.44), channel_id=1, replica_groups=mesh['x'=4,'z'=16,'core'=2,'rhs'=4] {'x'}, dimensions={0} | all-to-all | bytes 1048576 | tf_op jit(solution)/shard_map/all_to_all | solution.py:78
  166.7 4.6 %collective-permute-start.1 = (f32[64,8,256]{2,1,0:T(8,128)S(1)}, f32[64,8,256]{2,1,0:T(8,128)S(1)}, u32[]{:S(2)}, u32[]{:S(2)}) collective-permute-start(f32[64,8,256]{2,1,0:T(8,128)S(1)} %bitcast.219), channel_id=1, source_target_pairs={{0,4},{4,0},{1,5},{5,1},{2,6},{6,2},{3,7},{7,3},{8,12},{12,8},{9,1... | collective-permute-start | bytes 1572872 | tf_op jit(solution)/shard_map/ppermute | solution.py:80
  179.6 11.6 %all_to_all.66 = f32[4,16,8,256]{3,2,1,0:T(8,128)S(1)} all-to-all(f32[4,16,8,256]{3,2,1,0:T(8,128)S(1)} %bitcast.221), channel_id=1, replica_groups=mesh['x'=4,'z'=16,'core'=2,'rhs'=4] {'x'}, dimensions={0} | all-to-all | bytes 1048576 | tf_op jit(solution)/shard_map/all_to_all | solution.py:74
  192.0 10.7 %all_to_all.67 = f32[4,16,8,256]{3,2,1,0:T(8,128)S(1)} all-to-all(f32[4,16,8,256]{3,2,1,0:T(8,128)S(1)} %broadcast_in_dim.45), channel_id=1, replica_groups=mesh['x'=4,'z'=16,'core'=2,'rhs'=4] {'x'}, dimensions={0} | all-to-all | bytes 1048576 | tf_op jit(solution)/shard_map/all_to_all | solution.py:78
  202.7 4.2 %collective-permute-start.3 = (f32[64,8,256]{2,1,0:T(8,128)S(1)}, f32[64,8,256]{2,1,0:T(8,128)}, u32[]{:S(2)}, u32[]{:S(2)}) collective-permute-start(f32[64,8,256]{2,1,0:T(8,128)S(1)} %bitcast.218), channel_id=1, source_target_pairs={{0,4},{4,0},{1,5},{5,1},{2,6},{6,2},{3,7},{7,3},{8,12},{12,8},{9,1... | collective-permute-start | bytes 1572872 | tf_op jit(solution)/shard_map/ppermute | solution.py:80
  217.9 11.6 %all_to_all.68 = f32[4,16,8,256]{3,2,1,0:T(8,128)S(1)} all-to-all(f32[4,16,8,256]{3,2,1,0:T(8,128)S(1)} %bitcast.222), channel_id=1, replica_groups=mesh['x'=4,'z'=16,'core'=2,'rhs'=4] {'x'}, dimensions={0} | all-to-all | bytes 1048576 | tf_op jit(solution)/shard_map/all_to_all | solution.py:74
  231.9 3.5 %all-to-all-start.7 = ((f32[4,16,8,256]{3,2,1,0:T(8,128)}), f32[4,16,8,256]{3,2,1,0:T(8,128)S(1)}, u32[]{:S(2)}, u32[]{:S(2)}) async-start(f32[4,16,8,256]{3,2,1,0:T(8,128)} %broadcast_in_dim.46), calls=%async_computation.7 | async-start | bytes 1048576 | tf_op jit(solution)/shard_map/all_to_all | solution.py:78
  237.4 5.9 %all-to-all-done.7 = f32[4,16,8,256]{3,2,1,0:T(8,128)S(1)} async-done(((f32[4,16,8,256]{3,2,1,0:T(8,128)}), f32[4,16,8,256]{3,2,1,0:T(8,128)S(1)}, u32[]{:S(2)}, u32[]{:S(2)}) %all-to-all-start.7) | async-done | bytes 524320 | tf_op jit(solution)/shard_map/all_to_all | solution.py:78
  243.3 4.4 %collective-permute-start.5 = (f32[64,8,256]{2,1,0:T(8,128)S(1)}, f32[64,8,256]{2,1,0:T(8,128)S(1)}, u32[]{:S(2)}, u32[]{:S(2)}) collective-permute-start(f32[64,8,256]{2,1,0:T(8,128)S(1)} %bitcast.216), channel_id=1, source_target_pairs={{0,4},{4,0},{1,5},{5,1},{2,6},{6,2},{3,7},{7,3},{8,12},{12,8},{9,1... | collective-permute-start | bytes 1572872 | tf_op jit(solution)/shard_map/ppermute | solution.py:80
  258.8 4.1 %all-to-all-start.8 = ((f32[4,16,8,256]{3,2,1,0:T(8,128)}), f32[4,16,8,256]{3,2,1,0:T(8,128)}, u32[]{:S(2)}, u32[]{:S(2)}) async-start(f32[4,16,8,256]{3,2,1,0:T(8,128)} %bitcast.217), calls=%async_computation.8 | async-start | bytes 1048576 | tf_op jit(solution)/shard_map/all_to_all | solution.py:74
  263.6 8.9 %all-to-all-done.8 = f32[4,16,8,256]{3,2,1,0:T(8,128)} async-done(((f32[4,16,8,256]{3,2,1,0:T(8,128)}), f32[4,16,8,256]{3,2,1,0:T(8,128)}, u32[]{:S(2)}, u32[]{:S(2)}) %all-to-all-start.8) | async-done | bytes 524320 | tf_op jit(solution)/shard_map/all_to_all | solution.py:74
  274.4 4.1 %all-to-all-start.9 = ((f32[4,16,8,256]{3,2,1,0:T(8,128)}), f32[4,16,8,256]{3,2,1,0:T(8,128)}, u32[]{:S(2)}, u32[]{:S(2)}) async-start(f32[4,16,8,256]{3,2,1,0:T(8,128)} %broadcast_in_dim.47), calls=%async_computation.9 | async-start | bytes 1048576 | tf_op jit(solution)/shard_map/all_to_all | solution.py:78
  278.6 2.8 fusion.4
  282.7 4.2 %all-to-all-done.9 = f32[4,16,8,256]{3,2,1,0:T(8,128)} async-done(((f32[4,16,8,256]{3,2,1,0:T(8,128)}), f32[4,16,8,256]{3,2,1,0:T(8,128)}, u32[]{:S(2)}, u32[]{:S(2)}) %all-to-all-start.9) | async-done | bytes 524320 | tf_op jit(solution)/shard_map/all_to_all | solution.py:78
  286.9 4.1 %collective-permute-start.7 = (f32[64,8,256]{2,1,0:T(8,128)}, f32[64,8,256]{2,1,0:T(8,128)S(1)}, u32[]{:S(2)}, u32[]{:S(2)}) collective-permute-start(f32[64,8,256]{2,1,0:T(8,128)} %bitcast.75), channel_id=1, source_target_pairs={{0,4},{4,0},{1,5},{5,1},{2,6},{6,2},{3,7},{7,3},{8,12},{12,8},{9,1... | collective-permute-start | bytes 1572872 | tf_op jit(solution)/shard_map/ppermute | solution.py:80
  298.6 2.8 fusion.1
  (86 shorter events, 63.7 us)
Async XLA Ops:
  6.5 125.5 %all-gather.3.cloned.1.call-start = ((), (), s32[]{:S(2)}) async-start(), calls=%async_computation.10 | async-start | bytes 5570560 | tf_op jit(solution)/shard_map/all_gather | solution.py:55
  12.0 0.7 copy-start.2
  14.4 10.5 %all-to-all-start = ((f32[64,4,256]{2,0,1:T(8,128)}), f32[64,4,256]{2,0,1:T(8,128)S(1)}, u32[]{:S(2)}, u32[]{:S(2)}) async-start(f32[64,4,256]{2,0,1:T(8,128)} %bitcast.198), calls=%async_computation | async-start | bytes 524288 | tf_op jit(solution)/shard_map/all_to_all | solution.py:22
  27.1 74.3 %all-to-all-start.1 = ((f32[128,4,384]{2,1,0:T(4,128)}), f32[128,4,384]{2,1,0:T(4,128)S(1)}, u32[]{:S(2)}, u32[]{:S(2)}) async-start(f32[128,4,384]{2,1,0:T(4,128)} %copy.84), calls=%async_computation.1 | async-start | bytes 1572864 | tf_op jit(solution)/shard_map/all_to_all | solution.py:37
  136.0 8.0 %collective-permute-start = (f32[64,8,256]{2,1,0:T(8,128)S(1)}, f32[64,8,256]{2,1,0:T(8,128)S(1)}, u32[]{:S(2)}, u32[]{:S(2)}) collective-permute-start(f32[64,8,256]{2,1,0:T(8,128)S(1)} %select_bitcast_fusion.11), channel_id=1, source_target_pairs={{0,4},{4,0},{1,5},{5,1},{2,6},{6,2},{3,7},{7,3},{8,12},{12,8},{9,1... | collective-permute-start | bytes 1572872 | tf_op jit(solution)/shard_map/ppermute | solution.py:71
  166.7 6.2 %collective-permute-start.1 = (f32[64,8,256]{2,1,0:T(8,128)S(1)}, f32[64,8,256]{2,1,0:T(8,128)S(1)}, u32[]{:S(2)}, u32[]{:S(2)}) collective-permute-start(f32[64,8,256]{2,1,0:T(8,128)S(1)} %bitcast.219), channel_id=1, source_target_pairs={{0,4},{4,0},{1,5},{5,1},{2,6},{6,2},{3,7},{7,3},{8,12},{12,8},{9,1... | collective-permute-start | bytes 1572872 | tf_op jit(solution)/shard_map/ppermute | solution.py:80
  175.7 3.8 %collective-permute-start.2 = (f32[64,8,256]{2,1,0:T(8,128)S(1)}, f32[64,8,256]{2,1,0:T(8,128)S(1)}, u32[]{:S(2)}, u32[]{:S(2)}) collective-permute-start(f32[64,8,256]{2,1,0:T(8,128)S(1)} %select_bitcast_fusion.8), channel_id=1, source_target_pairs={{0,4},{4,0},{1,5},{5,1},{2,6},{6,2},{3,7},{7,3},{8,12},{12,8},{9,1... | collective-permute-start | bytes 1572872 | tf_op jit(solution)/shard_map/ppermute | solution.py:71
  191.3 0.7 copy-start.1
  202.7 7.1 %collective-permute-start.3 = (f32[64,8,256]{2,1,0:T(8,128)S(1)}, f32[64,8,256]{2,1,0:T(8,128)}, u32[]{:S(2)}, u32[]{:S(2)}) collective-permute-start(f32[64,8,256]{2,1,0:T(8,128)S(1)} %bitcast.218), channel_id=1, source_target_pairs={{0,4},{4,0},{1,5},{5,1},{2,6},{6,2},{3,7},{7,3},{8,12},{12,8},{9,1... | collective-permute-start | bytes 1572872 | tf_op jit(solution)/shard_map/ppermute | solution.py:80
  213.9 3.8 %collective-permute-start.4 = (f32[64,8,256]{2,1,0:T(8,128)S(1)}, f32[64,8,256]{2,1,0:T(8,128)S(1)}, u32[]{:S(2)}, u32[]{:S(2)}) collective-permute-start(f32[64,8,256]{2,1,0:T(8,128)S(1)} %select_bitcast_fusion.5), channel_id=1, source_target_pairs={{0,4},{4,0},{1,5},{5,1},{2,6},{6,2},{3,7},{7,3},{8,12},{12,8},{9,1... | collective-permute-start | bytes 1572872 | tf_op jit(solution)/shard_map/ppermute | solution.py:71
  231.9 11.4 %all-to-all-start.7 = ((f32[4,16,8,256]{3,2,1,0:T(8,128)}), f32[4,16,8,256]{3,2,1,0:T(8,128)S(1)}, u32[]{:S(2)}, u32[]{:S(2)}) async-start(f32[4,16,8,256]{3,2,1,0:T(8,128)} %broadcast_in_dim.46), calls=%async_computation.7 | async-start | bytes 1048576 | tf_op jit(solution)/shard_map/all_to_all | solution.py:78
  243.3 7.8 %collective-permute-start.5 = (f32[64,8,256]{2,1,0:T(8,128)S(1)}, f32[64,8,256]{2,1,0:T(8,128)S(1)}, u32[]{:S(2)}, u32[]{:S(2)}) collective-permute-start(f32[64,8,256]{2,1,0:T(8,128)S(1)} %bitcast.216), channel_id=1, source_target_pairs={{0,4},{4,0},{1,5},{5,1},{2,6},{6,2},{3,7},{7,3},{8,12},{12,8},{9,1... | collective-permute-start | bytes 1572872 | tf_op jit(solution)/shard_map/ppermute | solution.py:80
  251.0 2.0 copy-start
  254.1 3.8 %collective-permute-start.6 = (f32[64,8,256]{2,1,0:T(8,128)S(1)}, f32[64,8,256]{2,1,0:T(8,128)S(1)}, u32[]{:S(2)}, u32[]{:S(2)}) collective-permute-start(f32[64,8,256]{2,1,0:T(8,128)S(1)} %select_bitcast_fusion.2), channel_id=1, source_target_pairs={{0,4},{4,0},{1,5},{5,1},{2,6},{6,2},{3,7},{7,3},{8,12},{12,8},{9,1... | collective-permute-start | bytes 1572872 | tf_op jit(solution)/shard_map/ppermute | solution.py:71
  258.8 13.7 %all-to-all-start.8 = ((f32[4,16,8,256]{3,2,1,0:T(8,128)}), f32[4,16,8,256]{3,2,1,0:T(8,128)}, u32[]{:S(2)}, u32[]{:S(2)}) async-start(f32[4,16,8,256]{3,2,1,0:T(8,128)} %bitcast.217), calls=%async_computation.8 | async-start | bytes 1048576 | tf_op jit(solution)/shard_map/all_to_all | solution.py:74
  274.4 12.5 %all-to-all-start.9 = ((f32[4,16,8,256]{3,2,1,0:T(8,128)}), f32[4,16,8,256]{3,2,1,0:T(8,128)}, u32[]{:S(2)}, u32[]{:S(2)}) async-start(f32[4,16,8,256]{3,2,1,0:T(8,128)} %broadcast_in_dim.47), calls=%async_computation.9 | async-start | bytes 1048576 | tf_op jit(solution)/shard_map/all_to_all | solution.py:78
  286.9 10.3 %collective-permute-start.7 = (f32[64,8,256]{2,1,0:T(8,128)}, f32[64,8,256]{2,1,0:T(8,128)S(1)}, u32[]{:S(2)}, u32[]{:S(2)}) collective-permute-start(f32[64,8,256]{2,1,0:T(8,128)} %bitcast.75), channel_id=1, source_target_pairs={{0,4},{4,0},{1,5},{5,1},{2,6},{6,2},{3,7},{7,3},{8,12},{12,8},{9,1... | collective-permute-start | bytes 1572872 | tf_op jit(solution)/shard_map/ppermute | solution.py:80
Sparse Core Ops, SparseCore 0:
  12.9 118.2 all-gather.2

commit v3 on v2

v3 whole, which is shorter than its diff:
```python
import jax
import jax.numpy as jnp
from jax import lax
from jax.sharding import Mesh, PartitionSpec as P

ROWS = ("x", "z", "core")
SWAP = [(0, 1), (1, 0)]


def product(left, right, contract=((1,), (0,))):
    return lax.dot_general(
        left,
        right,
        (contract, ((), ())),
        precision=lax.Precision.HIGHEST,
        preferred_element_type=jnp.float32,
    )


def redistribute(targets, send_order, send_count, recv_slot):
    groups = lax.axis_size(ROWS)
    arrived = lax.all_to_all(targets, "rhs", split_axis=1, concat_axis=0, tiled=True)
    rows_local, columns = arrived.shape
    capacity, tag = 4, 64
    counts = send_count[0]
    dest = jnp.arange(groups, dtype=jnp.int32)
    starts = jnp.sum(jnp.where(dest[None, :] < dest[:, None], counts[None, :], 0), axis=1)
    index = jnp.arange(rows_local, dtype=jnp.int32)
    position = jnp.sum(jnp.where(send_order[:, None] == index[None, :], index[:, None], 0), axis=0)
    slot_number = jnp.arange(capacity, dtype=jnp.int32)
    listed = starts[None, :] + slot_number[:, None]
    listed = jnp.where(slot_number[:, None] < counts[None, :], listed, -1)
    picked = (listed[:, :, None] == position[None, None, :]).astype(jnp.float32)
    picked = picked.reshape(capacity * groups, rows_local)
    landing = jnp.broadcast_to((recv_slot + 1).astype(jnp.float32)[:, None], (rows_local, 2 * tag))
    planes = product(picked, jnp.concatenate([arrived, landing], axis=1))
    planes = planes.reshape(capacity, groups, columns + 2 * tag)
    halves = [
        jnp.concatenate(
            [
                planes[s, :, :columns],
                planes[s + 1, :, :columns],
                planes[s, :, columns : columns + tag],
                planes[s + 1, :, columns : columns + tag],
            ],
            axis=1,
        )
        for s in range(0, capacity, 2)
    ]
    incoming = lax.all_to_all(
        jnp.stack(halves, axis=1), ROWS, split_axis=0, concat_axis=0, tiled=True
    )
    total = 0.0
    for h in range(capacity // 2):
        half = incoming[:, h]
        for s in range(2):
            label = half[:, 2 * columns + s * tag : 2 * columns + s * tag + 1] - 1.0
            placed = (label.astype(jnp.int32) == index[None, :]).astype(jnp.float32)
            rows = half[:, s * columns : (s + 1) * columns]
            total = total + product(placed, rows, ((0,), (0,)))
    return total


def shards(targets, send_order, send_count, recv_slot, panel, inv_diag):
    sections, block_rows, share = inv_diag.shape
    nx, nz, nc = (lax.axis_size(a) for a in ROWS)
    zi = lax.axis_index("z")
    first = lax.axis_index("core") == 0
    even = zi % 2 == 0
    square = sections * share
    inverse_columns = jnp.swapaxes(inv_diag, 1, 2)

    def tile(j, k):
        if j == k:
            return inverse_columns[k]
        return panel[j * share : (j + 1) * share, k * block_rows : (k + 1) * block_rows]

    weight = {}
    early = [(0, 0), (1, 0)]
    late = [(j, k) for j in range(sections) for k in range(j + 1) if (j, k) not in early]
    for names in (early, late):
        gathered = lax.all_gather(jnp.stack([tile(j, k) for j, k in names]), "z")
        for i, name in enumerate(names):
            weight[name] = gathered[:, i].reshape(nz * share, block_rows)

    residual = redistribute(targets, send_order, send_count, recv_slot)
    columns = residual.shape[1] // 2
    halves = jnp.stack([residual[:square, :columns], residual[:square, columns:]])
    tops = jnp.broadcast_to(halves[None], (nz // 2,) + halves.shape).reshape(nz, square, columns)
    tops = lax.all_to_all(tops, "z", split_axis=0, concat_axis=0, tiled=True)
    pending = [
        tops[:, k * share : (k + 1) * share].reshape(nz * share, columns) for k in range(sections)
    ]
    left, right = residual[square:, :columns], residual[square:, columns:]
    below = [jnp.where(even, left, right), jnp.where(even, right, left)]
    start = ((lax.axis_index("x") * nz + zi) * nc + lax.axis_index("core")) * share
    finished = []
    for k in range(sections):
        partial = product(weight[(k, k)], pending[k], ((0,), (0,)))
        partial = partial.reshape(nx * nz, nc, share, columns)
        keep = jnp.where(first, partial[:, 0], partial[:, 1])
        give = jnp.where(first, partial[:, 1], partial[:, 0])
        half = keep + lax.ppermute(give, "core", SWAP)
        copies = jnp.broadcast_to(half[None], (nx,) + half.shape)
        mine = jnp.sum(lax.all_to_all(copies, "x", split_axis=0, concat_axis=0, tiled=True), axis=0)
        other = lax.ppermute(mine, "core", SWAP)
        solved = jnp.stack([jnp.where(first, mine, other), jnp.where(first, other, mine)], axis=1)
        solved = solved.reshape(block_rows, columns)
        for j in range(k + 1, sections):
            pending[j] = pending[j] - product(weight[(j, k)], solved)
        traded = lax.ppermute(solved, "z", [(i, i ^ 1) for i in range(nz)])
        factor = panel[square:, k * block_rows : (k + 1) * block_rows]
        pieces = []
        for h, block in enumerate((solved, traded)):
            below[h] = below[h] - product(factor, block)
            pieces.append(lax.dynamic_slice_in_dim(block, start, share, 0))
        finished.append(pieces)
    ends = [jnp.concatenate([f[h] for f in finished] + [below[h]], axis=0) for h in range(2)]
    return jnp.concatenate(
        [jnp.where(even, ends[0], ends[1]), jnp.where(even, ends[1], ends[0])], axis=1
    )


def solution(mesh):
    ny = mesh.shape["rhs"]
    split = Mesh(mesh.devices.reshape(4, 16, 2, ny), ROWS + ("rhs",))
    placed = (
        P(ROWS + ("rhs",), None),
        P(ROWS),
        P(ROWS, None),
        P(ROWS),
        P(ROWS, None),
        P(None, None, ROWS),
    )
    return jax.shard_map(
        shards, mesh=split, in_specs=placed, out_specs=P(ROWS, "rhs"), check_vma=False
    )
```

time: 310 us -> 303 us (0.977)
  blocking collectives: 85.8 us -> 36 us
  waiting for transfers between devices: 83.1 us -> 112 us
  starting transfers between devices: 67.6 us -> 84.8 us
  local copies, waits for them, and re-layouts: 23.5 us -> 20.1 us
    all_gather x1 -> x0, blocking collectives: 29.5 us -> none  [shards(): lax.all_gather(residual[:square].reshape(sections, share, columns), 'z')]
    all_gather x1 -> x2, waiting for transfers between devices: 0.01 us -> 20.7 us  [shards(): gathered = lax.all_gather(jnp.stack([tile(j, k) for j, k in names]), 'z')]
    all_to_all x5 -> x2, blocking collectives: 56.3 us -> 36 us  [shards(): lax.all_to_all(copies, 'x', split_axis=0, concat_axis=0, tiled=True)]
    ppermute x0 -> x4, waiting for transfers between devices: none -> 14.4 us  [shards(): traded = lax.ppermute(solved, 'z', [(i, i ^ 1) for i in range(nz)])]
    ppermute x0 -> x4, starting transfers between devices: none -> 11.5 us  [shards(): traded = lax.ppermute(solved, 'z', [(i, i ^ 1) for i in range(nz)])]
    ppermute x4, starting transfers between devices: 12.6 us -> 22.1 us  [shards(): half = keep + lax.ppermute(give, 'core', SWAP)]
    dot_general x6, local copies, waits for them, and re-layouts: 7.78 us -> 3.3 us  [product(): lax.dot_general(left, right, (contract, ((), ())), precision=lax.Precisio...]
    all_to_all x4, waiting for transfers between devices: 72.4 us -> 68.7 us  [the longest x1 43.7 us: redistribute(): lax.all_to_all(jnp.stack(halves, axis=1), ROWS, split_axis=0, concat_axis...]
  transfers between devices with their start and end apart: 14 -> 19, of which waited for: 10 -> 13; matrix products, arithmetic and copies ran while one was open for 9% -> 12% of each run, Pallas kernels for 0% -> 0%
where the time goes in v3:
time: 303 us; the launch traced here: 301 us
  waiting for transfers between devices  112 us (37%)
  starting transfers between devices  84.8 us (28%)
  blocking collectives  36 us (12%)
  matrix products  27 us (9%)
  local copies, waits for them, and re-layouts  20.1 us (7%)
  between operations  14.1 us (5%)
  other arithmetic  6.71 us (2%)
    all_to_all x1, waiting for transfers between devices, redistribute(): lax.all_to_all(jnp.stack(halves, axis=1), ROWS, split_axis=0, concat_axis...  43.7 us
    all_to_all x2, blocking collectives, shards(): lax.all_to_all(copies, 'x', split_axis=0, concat_axis=0, tiled=True)  36 us
    dot_general x23, matrix products, product(): lax.dot_general(left, right, (contract, ((), ())), precision=lax.Precisio...  27 us
    ppermute x4, starting transfers between devices, shards(): half = keep + lax.ppermute(give, 'core', SWAP)  22.1 us
    all_to_all x1, starting transfers between devices, redistribute(): lax.all_to_all(jnp.stack(halves, axis=1), ROWS, split_axis=0, concat_axis...  21 us
    all_gather x2, waiting for transfers between devices, shards(): gathered = lax.all_gather(jnp.stack([tile(j, k) for j, k in names]), 'z')  20.7 us
    ppermute x4, waiting for transfers between devices, shards(): traded = lax.ppermute(solved, 'z', [(i, i ^ 1) for i in range(nz)])  14.4 us
    ppermute x4, starting transfers between devices, shards(): other = lax.ppermute(mine, 'core', SWAP)  14.1 us
  transfers between devices with their start and end apart: 19, of which 13 were waited for; matrix products, arithmetic and copies ran while one was open for 12% of the time, Pallas kernels for 0%

profile of v3, /device:TPU:1, one launch (start us, length us, event | category | flops | bytes accessed | tf_op | source)
XLA Modules:
  0.0 300.6 jit_solution(726331077672846849)
XLA Ops:
  15.8 5.0 %all-to-all-start = ((f32[64,4,256]{2,0,1:T(8,128)}), f32[64,4,256]{2,0,1:T(8,128)S(1)}, u32[]{:S(2)}, u32[]{:S(2)}) async-start(f32[64,4,256]{2,0,1:T(8,128)} %bitcast.223), calls=%async_computation | async-start | bytes 524288 | tf_op jit(solution)/shard_map/all_to_all | solution.py:22
  23.7 2.6 all-to-all-done
  28.7 21.0 %all-to-all-start.1 = ((f32[128,2,640]{2,1,0:T(2,128)}), f32[128,2,640]{2,1,0:T(2,128)S(1)}, u32[]{:S(2)}, u32[]{:S(2)}) async-start(f32[128,2,640]{2,1,0:T(2,128)} %copy.87), calls=%async_computation.1 | async-start | bytes 1310720 | tf_op jit(solution)/shard_map/all_to_all | solution.py:50
  50.4 43.7 %all-to-all-done.1 = f32[128,2,640]{2,1,0:T(2,128)S(1)} async-done(((f32[128,2,640]{2,1,0:T(2,128)}), f32[128,2,640]{2,1,0:T(2,128)S(1)}, u32[]{:S(2)}, u32[]{:S(2)}) %all-to-all-start.1) | async-done | bytes 655392 | tf_op jit(solution)/shard_map/all_to_all | solution.py:50
  97.4 4.1 %all-to-all-start.2 = ((f32[16,32,128]{2,1,0:T(8,128)}), f32[16,32,128]{2,1,0:T(8,128)S(1)}, u32[]{:S(2)}, u32[]{:S(2)}) async-start(f32[16,32,128]{2,1,0:T(8,128)} %bitcast.23), calls=%async_computation.2 | async-start | bytes 524288 | tf_op jit(solution)/shard_map/all_to_all | solution.py:90
  102.8 12.3 %all-to-all-done.2 = f32[16,32,128]{2,1,0:T(8,128)S(1)} async-done(((f32[16,32,128]{2,1,0:T(8,128)}), f32[16,32,128]{2,1,0:T(8,128)S(1)}, u32[]{:S(2)}, u32[]{:S(2)}) %all-to-all-start.2) | async-done | bytes 262176 | tf_op jit(solution)/shard_map/all_to_all | solution.py:90
  115.7 7.5 %collective-permute-start = (f32[64,8,128]{2,1,0:T(8,128)S(1)}, f32[64,8,128]{2,1,0:T(8,128)S(1)}, u32[]{:S(2)}, u32[]{:S(2)}) collective-permute-start(f32[64,8,128]{2,1,0:T(8,128)S(1)} %select_bitcast_fusion.11), channel_id=1, source_target_pairs={{0,4},{4,0},{1,5},{5,1},{2,6},{6,2},{3,7},{7,3},{8,12},{12,8},{9,1... | collective-permute-start | bytes 786440 | tf_op jit(solution)/shard_map/ppermute | solution.py:103
  124.5 17.7 %all_to_all.49 = f32[4,64,8,128]{3,2,1,0:T(8,128)S(1)} all-to-all(f32[4,64,8,128]{3,2,1,0:T(8,128)S(1)} %broadcast_in_dim.47), channel_id=1, replica_groups=mesh['x'=4,'z'=16,'core'=2,'rhs'=4] {'x'}, dimensions={0} | all-to-all | bytes 2097152 | tf_op jit(solution)/shard_map/all_to_all | solution.py:105
  142.2 3.7 %collective-permute-start.1 = (f32[64,8,128]{2,1,0:T(8,128)S(1)}, f32[64,8,128]{2,1,0:T(8,128)S(1)}, u32[]{:S(2)}, u32[]{:S(2)}) collective-permute-start(f32[64,8,128]{2,1,0:T(8,128)S(1)} %reduce_sum.56), channel_id=1, source_target_pairs={{0,4},{4,0},{1,5},{5,1},{2,6},{6,2},{3,7},{7,3},{8,12},{12,8},{9,1... | collective-permute-start | bytes 786440 | tf_op jit(solution)/shard_map/ppermute | solution.py:106
  147.9 20.6 %all-gather.7.cloned.1.call-done = f32[128,8,1024]{2,1,0:T(8,128)} async-done(((f32[8,8,1024]{2,1,0:T(8,128)}), f32[128,8,1024]{2,1,0:T(8,128)}) %all-gather.7.cloned.1.call-update) | async-done | bytes 4194320 | tf_op jit(solution)/shard_map/all_gather | solution.py:82
  170.8 10.6 %collective-permute-start.2 = (f32[64,8,128]{2,1,0:T(8,128)S(1)}, f32[64,8,128]{2,1,0:T(8,128)S(1)}, u32[]{:S(2)}, u32[]{:S(2)}) collective-permute-start(f32[64,8,128]{2,1,0:T(8,128)S(1)} %select_bitcast_fusion.8), channel_id=1, source_target_pairs={{0,4},{4,0},{1,5},{5,1},{2,6},{6,2},{3,7},{7,3},{8,12},{12,8},{9,1... | collective-permute-start | bytes 786440 | tf_op jit(solution)/shard_map/ppermute | solution.py:103
  182.6 18.3 %all_to_all.50 = f32[4,64,8,128]{3,2,1,0:T(8,128)S(1)} all-to-all(f32[4,64,8,128]{3,2,1,0:T(8,128)S(1)} %broadcast_in_dim.48), channel_id=1, replica_groups=mesh['x'=4,'z'=16,'core'=2,'rhs'=4] {'x'}, dimensions={0} | all-to-all | bytes 2097152 | tf_op jit(solution)/shard_map/all_to_all | solution.py:105
  201.0 3.7 %collective-permute-start.3 = (f32[64,8,128]{2,1,0:T(8,128)S(1)}, f32[64,8,128]{2,1,0:T(8,128)}, u32[]{:S(2)}, u32[]{:S(2)}) collective-permute-start(f32[64,8,128]{2,1,0:T(8,128)S(1)} %reduce_sum.57), channel_id=1, source_target_pairs={{0,4},{4,0},{1,5},{5,1},{2,6},{6,2},{3,7},{7,3},{8,12},{12,8},{9,1... | collective-permute-start | bytes 786440 | tf_op jit(solution)/shard_map/ppermute | solution.py:106
  214.5 3.5 %all-to-all-start.5 = ((f32[4,64,8,128]{3,2,1,0:T(8,128)}), f32[4,64,8,128]{3,2,1,0:T(8,128)S(1)}, u32[]{:S(2)}, u32[]{:S(2)}) async-start(f32[4,64,8,128]{3,2,1,0:T(8,128)} %broadcast_in_dim.49), calls=%async_computation.5 | async-start | bytes 2097152 | tf_op jit(solution)/shard_map/all_to_all | solution.py:105
  218.0 3.0 %collective-permute-start.8 = (f32[1024,128]{1,0:T(8,128)S(1)}, f32[1024,128]{1,0:T(8,128)}, u32[]{:S(2)}, u32[]{:S(2)}) collective-permute-start(f32[1024,128]{1,0:T(8,128)S(1)} %bitcast.226), channel_id=1, source_target_pairs={{0,8},{8,0},{16,24},{24,16},{32,40},{40,32},{48,56},{56,48},{64,72... | collective-permute-start | bytes 1572872 | tf_op jit(solution)/shard_map/ppermute | solution.py:111
  221.7 11.4 %all-to-all-done.5 = f32[4,64,8,128]{3,2,1,0:T(8,128)S(1)} async-done(((f32[4,64,8,128]{3,2,1,0:T(8,128)}), f32[4,64,8,128]{3,2,1,0:T(8,128)S(1)}, u32[]{:S(2)}, u32[]{:S(2)}) %all-to-all-start.5) | async-done | bytes 1048608 | tf_op jit(solution)/shard_map/all_to_all | solution.py:105
  233.2 2.9 collective-permute-start.5
  246.0 3.0 %collective-permute-start.9 = (f32[1024,128]{1,0:T(8,128)S(1)}, f32[1024,128]{1,0:T(8,128)S(1)}, u32[]{:S(2)}, u32[]{:S(2)}) collective-permute-start(f32[1024,128]{1,0:T(8,128)S(1)} %bitcast.232), channel_id=1, source_target_pairs={{0,8},{8,0},{16,24},{24,16},{32,40},{40,32},{48,56},{56,48},{64,72... | collective-permute-start | bytes 1572872 | tf_op jit(solution)/shard_map/ppermute | solution.py:111
  250.2 3.5 %all-to-all-start.6 = ((f32[4,64,8,128]{3,2,1,0:T(8,128)}), f32[4,64,8,128]{3,2,1,0:T(8,128)S(1)}, u32[]{:S(2)}, u32[]{:S(2)}) async-start(f32[4,64,8,128]{3,2,1,0:T(8,128)} %broadcast_in_dim.50), calls=%async_computation.6 | async-start | bytes 2097152 | tf_op jit(solution)/shard_map/all_to_all | solution.py:105
  255.6 2.7 fusion.4
  258.3 2.6 collective-permute-done.9
  263.6 3.2 %collective-permute-start.10 = (f32[1024,128]{1,0:T(8,128)S(1)}, f32[1024,128]{1,0:T(8,128)S(1)}, u32[]{:S(2)}, u32[]{:S(2)}) collective-permute-start(f32[1024,128]{1,0:T(8,128)S(1)} %bitcast.236), channel_id=1, source_target_pairs={{0,8},{8,0},{16,24},{24,16},{32,40},{40,32},{48,56},{56,48},{64,72... | collective-permute-start | bytes 1572872 | tf_op jit(solution)/shard_map/ppermute | solution.py:111
  268.1 3.8 %collective-permute-start.7 = (f32[64,8,128]{2,1,0:T(8,128)S(1)}, f32[64,8,128]{2,1,0:T(8,128)S(1)}, u32[]{:S(2)}, u32[]{:S(2)}) collective-permute-start(f32[64,8,128]{2,1,0:T(8,128)S(1)} %reduce_sum.59), channel_id=1, source_target_pairs={{0,4},{4,0},{1,5},{5,1},{2,6},{6,2},{3,7},{7,3},{8,12},{12,8},{9,1... | collective-permute-start | bytes 786440 | tf_op jit(solution)/shard_map/ppermute | solution.py:106
  279.5 10.6 %collective-permute-done.11 = f32[1024,128]{1,0:T(8,128)S(1)} collective-permute-done((f32[1024,128]{1,0:T(8,128)S(1)}, f32[1024,128]{1,0:T(8,128)S(1)}, u32[]{:S(2)}, u32[]{:S(2)}) %collective-permute-start.11) | collective-permute-done | bytes 524320 | tf_op jit(solution)/shard_map/ppermute | solution.py:111
  (124 shorter events, 65.4 us)
Async XLA Ops:
  6.5 95.0 %all-gather.5.cloned.1.call-start = ((), (), s32[]{:S(2)}) async-start(), calls=%async_computation.7 | async-start | bytes 1114112 | tf_op jit(solution)/shard_map/all_gather | solution.py:82
  13.4 15.3 %copy-start.2 = (f32[8,8,1024]{2,1,0:T(8,128)}, f32[8,8,1024]{2,1,0:T(8,128)S(1)}, u32[]{:S(2)}) copy-start(f32[8,8,1024]{2,1,0:T(8,128)S(1)} %get-tuple-element.34) | copy-start | bytes 786436
  15.8 10.5 %all-to-all-start = ((f32[64,4,256]{2,0,1:T(8,128)}), f32[64,4,256]{2,0,1:T(8,128)S(1)}, u32[]{:S(2)}, u32[]{:S(2)}) async-start(f32[64,4,256]{2,0,1:T(8,128)} %bitcast.223), calls=%async_computation | async-start | bytes 524288 | tf_op jit(solution)/shard_map/all_to_all | solution.py:22
  28.7 65.4 %all-to-all-start.1 = ((f32[128,2,640]{2,1,0:T(2,128)}), f32[128,2,640]{2,1,0:T(2,128)S(1)}, u32[]{:S(2)}, u32[]{:S(2)}) async-start(f32[128,2,640]{2,1,0:T(2,128)} %copy.87), calls=%async_computation.1 | async-start | bytes 1310720 | tf_op jit(solution)/shard_map/all_to_all | solution.py:50
  49.7 118.8 %all-gather.7.cloned.1.call-start = ((), (), s32[]{:S(2)}) async-start(), calls=%async_computation.8 | async-start | bytes 4456448 | tf_op jit(solution)/shard_map/all_gather | solution.py:82
  97.4 17.7 %all-to-all-start.2 = ((f32[16,32,128]{2,1,0:T(8,128)}), f32[16,32,128]{2,1,0:T(8,128)S(1)}, u32[]{:S(2)}, u32[]{:S(2)}) async-start(f32[16,32,128]{2,1,0:T(8,128)} %bitcast.23), calls=%async_computation.2 | async-start | bytes 524288 | tf_op jit(solution)/shard_map/all_to_all | solution.py:90
  115.7 8.6 %collective-permute-start = (f32[64,8,128]{2,1,0:T(8,128)S(1)}, f32[64,8,128]{2,1,0:T(8,128)S(1)}, u32[]{:S(2)}, u32[]{:S(2)}) collective-permute-start(f32[64,8,128]{2,1,0:T(8,128)S(1)} %select_bitcast_fusion.11), channel_id=1, source_target_pairs={{0,4},{4,0},{1,5},{5,1},{2,6},{6,2},{3,7},{7,3},{8,12},{12,8},{9,1... | collective-permute-start | bytes 786440 | tf_op jit(solution)/shard_map/ppermute | solution.py:103
  124.4 22.8 %copy-start.1 = (f32[32,8,1024]{2,1,0:T(8,128)S(1)}, f32[32,8,1024]{2,1,0:T(8,128)}, u32[]{:S(2)}) copy-start(f32[32,8,1024]{2,1,0:T(8,128)} %all-gather.5.cloned.1.call-done) | copy-start | bytes 3145732
  142.2 4.8 %collective-permute-start.1 = (f32[64,8,128]{2,1,0:T(8,128)S(1)}, f32[64,8,128]{2,1,0:T(8,128)S(1)}, u32[]{:S(2)}, u32[]{:S(2)}) collective-permute-start(f32[64,8,128]{2,1,0:T(8,128)S(1)} %reduce_sum.56), channel_id=1, source_target_pairs={{0,4},{4,0},{1,5},{5,1},{2,6},{6,2},{3,7},{7,3},{8,12},{12,8},{9,1... | collective-permute-start | bytes 786440 | tf_op jit(solution)/shard_map/ppermute | solution.py:106
  170.8 11.7 %collective-permute-start.2 = (f32[64,8,128]{2,1,0:T(8,128)S(1)}, f32[64,8,128]{2,1,0:T(8,128)S(1)}, u32[]{:S(2)}, u32[]{:S(2)}) collective-permute-start(f32[64,8,128]{2,1,0:T(8,128)S(1)} %select_bitcast_fusion.8), channel_id=1, source_target_pairs={{0,4},{4,0},{1,5},{5,1},{2,6},{6,2},{3,7},{7,3},{8,12},{12,8},{9,1... | collective-permute-start | bytes 786440 | tf_op jit(solution)/shard_map/ppermute | solution.py:103
  201.0 5.6 %collective-permute-start.3 = (f32[64,8,128]{2,1,0:T(8,128)S(1)}, f32[64,8,128]{2,1,0:T(8,128)}, u32[]{:S(2)}, u32[]{:S(2)}) collective-permute-start(f32[64,8,128]{2,1,0:T(8,128)S(1)} %reduce_sum.57), channel_id=1, source_target_pairs={{0,4},{4,0},{1,5},{5,1},{2,6},{6,2},{3,7},{7,3},{8,12},{12,8},{9,1... | collective-permute-start | bytes 786440 | tf_op jit(solution)/shard_map/ppermute | solution.py:106
  210.0 3.4 %collective-permute-start.4 = (f32[64,8,128]{2,1,0:T(8,128)S(1)}, f32[64,8,128]{2,1,0:T(8,128)S(1)}, u32[]{:S(2)}, u32[]{:S(2)}) collective-permute-start(f32[64,8,128]{2,1,0:T(8,128)S(1)} %select_bitcast_fusion.5), channel_id=1, source_target_pairs={{0,4},{4,0},{1,5},{5,1},{2,6},{6,2},{3,7},{7,3},{8,12},{12,8},{9,1... | collective-permute-start | bytes 786440 | tf_op jit(solution)/shard_map/ppermute | solution.py:103
  214.5 18.6 %all-to-all-start.5 = ((f32[4,64,8,128]{3,2,1,0:T(8,128)}), f32[4,64,8,128]{3,2,1,0:T(8,128)S(1)}, u32[]{:S(2)}, u32[]{:S(2)}) async-start(f32[4,64,8,128]{3,2,1,0:T(8,128)} %broadcast_in_dim.49), calls=%async_computation.5 | async-start | bytes 2097152 | tf_op jit(solution)/shard_map/all_to_all | solution.py:105
  218.0 35.7 %collective-permute-start.8 = (f32[1024,128]{1,0:T(8,128)S(1)}, f32[1024,128]{1,0:T(8,128)}, u32[]{:S(2)}, u32[]{:S(2)}) collective-permute-start(f32[1024,128]{1,0:T(8,128)S(1)} %bitcast.226), channel_id=1, source_target_pairs={{0,8},{8,0},{16,24},{24,16},{32,40},{40,32},{48,56},{56,48},{64,72... | collective-permute-start | bytes 1572872 | tf_op jit(solution)/shard_map/ppermute | solution.py:111
  233.2 6.4 %collective-permute-start.5 = (f32[64,8,128]{2,1,0:T(8,128)S(1)}, f32[64,8,128]{2,1,0:T(8,128)S(1)}, u32[]{:S(2)}, u32[]{:S(2)}) collective-permute-start(f32[64,8,128]{2,1,0:T(8,128)S(1)} %reduce_sum.58), channel_id=1, source_target_pairs={{0,4},{4,0},{1,5},{5,1},{2,6},{6,2},{3,7},{7,3},{8,12},{12,8},{9,1... | collective-permute-start | bytes 786440 | tf_op jit(solution)/shard_map/ppermute | solution.py:106
  242.0 7.0 %collective-permute-start.6 = (f32[64,8,128]{2,1,0:T(8,128)S(1)}, f32[64,8,128]{2,1,0:T(8,128)S(1)}, u32[]{:S(2)}, u32[]{:S(2)}) collective-permute-start(f32[64,8,128]{2,1,0:T(8,128)S(1)} %select_bitcast_fusion.2), channel_id=1, source_target_pairs={{0,4},{4,0},{1,5},{5,1},{2,6},{6,2},{3,7},{7,3},{8,12},{12,8},{9,1... | collective-permute-start | bytes 786440 | tf_op jit(solution)/shard_map/ppermute | solution.py:103
  246.0 14.9 %collective-permute-start.9 = (f32[1024,128]{1,0:T(8,128)S(1)}, f32[1024,128]{1,0:T(8,128)S(1)}, u32[]{:S(2)}, u32[]{:S(2)}) collective-permute-start(f32[1024,128]{1,0:T(8,128)S(1)} %bitcast.232), channel_id=1, source_target_pairs={{0,8},{8,0},{16,24},{24,16},{32,40},{40,32},{48,56},{56,48},{64,72... | collective-permute-start | bytes 1572872 | tf_op jit(solution)/shard_map/ppermute | solution.py:111
  250.2 17.9 %all-to-all-start.6 = ((f32[4,64,8,128]{3,2,1,0:T(8,128)}), f32[4,64,8,128]{3,2,1,0:T(8,128)S(1)}, u32[]{:S(2)}, u32[]{:S(2)}) async-start(f32[4,64,8,128]{3,2,1,0:T(8,128)} %broadcast_in_dim.50), calls=%async_computation.6 | async-start | bytes 2097152 | tf_op jit(solution)/shard_map/all_to_all | solution.py:105
  258.3 15.8 %copy-start.3 = (f32[256,128]{1,0:T(8,128)S(1)}, f32[256,128]{1,0:T(8,128)}, u32[]{:S(2)}) copy-start(f32[256,128]{1,0:T(8,128)} %constant_dynamic-update-slice_fusion.10) | copy-start | bytes 393220
  263.6 15.0 %copy-start.4 = (f32[256,128]{1,0:T(8,128)S(1)}, f32[256,128]{1,0:T(8,128)}, u32[]{:S(2)}) copy-start(f32[256,128]{1,0:T(8,128)} %constant_dynamic-update-slice_fusion.14) | copy-start | bytes 393220
  263.6 14.1 %collective-permute-start.10 = (f32[1024,128]{1,0:T(8,128)S(1)}, f32[1024,128]{1,0:T(8,128)S(1)}, u32[]{:S(2)}, u32[]{:S(2)}) collective-permute-start(f32[1024,128]{1,0:T(8,128)S(1)} %bitcast.236), channel_id=1, source_target_pairs={{0,8},{8,0},{16,24},{24,16},{32,40},{40,32},{48,56},{56,48},{64,72... | collective-permute-start | bytes 1572872 | tf_op jit(solution)/shard_map/ppermute | solution.py:111
  268.1 9.6 %copy-start = (f32[256,4096]{1,0:T(8,128)S(1)}, f32[256,4096]{1,0:T(8,128)}, u32[]{:S(2)}) copy-start(f32[256,4096]{1,0:T(8,128)} %param.10) | copy-start | bytes 12582916
  268.1 6.0 %collective-permute-start.7 = (f32[64,8,128]{2,1,0:T(8,128)S(1)}, f32[64,8,128]{2,1,0:T(8,128)S(1)}, u32[]{:S(2)}, u32[]{:S(2)}) collective-permute-start(f32[64,8,128]{2,1,0:T(8,128)S(1)} %reduce_sum.59), channel_id=1, source_target_pairs={{0,4},{4,0},{1,5},{5,1},{2,6},{6,2},{3,7},{7,3},{8,12},{12,8},{9,1... | collective-permute-start | bytes 786440 | tf_op jit(solution)/shard_map/ppermute | solution.py:106
  274.2 15.9 %collective-permute-start.11 = (f32[1024,128]{1,0:T(8,128)S(1)}, f32[1024,128]{1,0:T(8,128)S(1)}, u32[]{:S(2)}, u32[]{:S(2)}) collective-permute-start(f32[1024,128]{1,0:T(8,128)S(1)} %bitcast.245), channel_id=1, source_target_pairs={{0,8},{8,0},{16,24},{24,16},{32,40},{40,32},{48,56},{56,48},{64,72... | collective-permute-start | bytes 1572872 | tf_op jit(solution)/shard_map/ppermute | solution.py:111
Sparse Core Ops, SparseCore 0:
  14.2 78.4 all-gather.4
  94.8 73.6 all-gather.6

commit v4 on v3

--- a/solution.py
+++ b/solution.py
@@ -1,23 +1,55 @@
 import jax
 import jax.numpy as jnp
 from jax import lax
+from jax.experimental import pallas as pl
+from jax.experimental.pallas import tpu as pltpu
 from jax.sharding import Mesh, PartitionSpec as P
 
 ROWS = ("x", "z", "core")
 SWAP = [(0, 1), (1, 0)]
 
 
-def product(left, right, contract=((1,), (0,))):
+def product(left, right, contract=((1,), (0,)), precision=lax.Precision.HIGHEST):
     return lax.dot_general(
         left,
         right,
         (contract, ((), ())),
-        precision=lax.Precision.HIGHEST,
+        precision=precision,
         preferred_element_type=jnp.float32,
     )
 
 
-def redistribute(targets, send_order, send_count, recv_slot):
+def quick(left, right, contract=((1,), (0,))):
+    return product(left, right, contract, lax.Precision.HIGH)
+
+
+def pack_tiles(panel, inverse_columns, names):
+    sections, share, width = inverse_columns.shape
+
+    def kernel(panel_ref, inverse_ref, out_ref, sems):
+        copies = []
+        for i, (j, k) in enumerate(names):
+            if j == k:
+                source = inverse_ref.at[k]
+            else:
+                source = panel_ref.at[pl.ds(j * share, share), pl.ds(k * width, width)]
+            copies.append(pltpu.make_async_copy(source, out_ref.at[i], sems.at[i]))
+        for copy in copies:
+            copy.start()
+        for copy in copies:
+            copy.wait()
+
+    anywhere = pl.BlockSpec(memory_space=pltpu.HBM)
+    return pl.pallas_call(
+        kernel,
+        out_shape=jax.ShapeDtypeStruct((len(names), share, width), jnp.float32),
+        in_specs=[anywhere, anywhere],
+        out_specs=anywhere,
+        scratch_shapes=[pltpu.SemaphoreType.DMA((len(names),))],
+    )(panel, inverse_columns)
+
+
+def redistribute(targets, send_order, send_count, recv_slot, beside):
     groups = lax.axis_size(ROWS)
     arrived = lax.all_to_all(targets, "rhs", split_axis=1, concat_axis=0, tiled=True)
     rows_local, columns = arrived.shape
@@ -47,9 +79,12 @@
         )
         for s in range(0, capacity, 2)
     ]
+    sent, beside = lax.optimization_barrier((jnp.stack(halves, axis=1), beside))
+    gathered = lax.all_gather(beside, "z")
     incoming = lax.all_to_all(
-        jnp.stack(halves, axis=1), ROWS, split_axis=0, concat_axis=0, tiled=True
+        sent, ROWS, split_axis=0, concat_axis=0, tiled=True
     )
+    incoming, gathered = lax.optimization_barrier((incoming, gathered))
     total = 0.0
     for h in range(capacity // 2):
         half = incoming[:, h]
@@ -58,7 +93,13 @@
             placed = (label.astype(jnp.int32) == index[None, :]).astype(jnp.float32)
             rows = half[:, s * columns : (s + 1) * columns]
             total = total + product(placed, rows, ((0,), (0,)))
-    return total
+    return total, gathered
+
+
+def whole_block(mine, first):
+    other = lax.ppermute(mine, "core", SWAP)
+    both = jnp.stack([jnp.where(first, mine, other), jnp.where(first, other, mine)], axis=1)
+    return both.reshape(2 * mine.shape[0] * mine.shape[1], mine.shape[2])
 
 
 def shards(targets, send_order, send_count, recv_slot, panel, inv_diag):
@@ -70,20 +111,15 @@
     square = sections * share
     inverse_columns = jnp.swapaxes(inv_diag, 1, 2)
 
-    def tile(j, k):
-        if j == k:
-            return inverse_columns[k]
-        return panel[j * share : (j + 1) * share, k * block_rows : (k + 1) * block_rows]
-
     weight = {}
-    early = [(0, 0), (1, 0)]
-    late = [(j, k) for j in range(sections) for k in range(j + 1) if (j, k) not in early]
-    for names in (early, late):
-        gathered = lax.all_gather(jnp.stack([tile(j, k) for j, k in names]), "z")
-        for i, name in enumerate(names):
-            weight[name] = gathered[:, i].reshape(nz * share, block_rows)
-
-    residual = redistribute(targets, send_order, send_count, recv_slot)
+    names = [(j, k) for j in range(sections) for k in range(j + 1)][1:]
+    gathered = lax.all_gather(pack_tiles(panel, inverse_columns, names), "z")
+    for i, name in enumerate(names):
+        weight[name] = gathered[:, i].reshape(nz * share, block_rows)
+    residual, lead = redistribute(
+        targets, send_order, send_count, recv_slot, inverse_columns[0]
+    )
+    weight[(0, 0)] = lead.reshape(nz * share, block_rows)
     columns = residual.shape[1] // 2
     halves = jnp.stack([residual[:square, :columns], residual[:square, columns:]])
     tops = jnp.broadcast_to(halves[None], (nz // 2,) + halves.shape).reshape(nz, square, columns)
@@ -96,23 +132,21 @@
     start = ((lax.axis_index("x") * nz + zi) * nc + lax.axis_index("core")) * share
     finished = []
     for k in range(sections):
-        partial = product(weight[(k, k)], pending[k], ((0,), (0,)))
+        partial = quick(weight[(k, k)], pending[k], ((0,), (0,)))
         partial = partial.reshape(nx * nz, nc, share, columns)
         keep = jnp.where(first, partial[:, 0], partial[:, 1])
         give = jnp.where(first, partial[:, 1], partial[:, 0])
         half = keep + lax.ppermute(give, "core", SWAP)
         copies = jnp.broadcast_to(half[None], (nx,) + half.shape)
         mine = jnp.sum(lax.all_to_all(copies, "x", split_axis=0, concat_axis=0, tiled=True), axis=0)
-        other = lax.ppermute(mine, "core", SWAP)
-        solved = jnp.stack([jnp.where(first, mine, other), jnp.where(first, other, mine)], axis=1)
-        solved = solved.reshape(block_rows, columns)
+        solved = whole_block(mine, first)
         for j in range(k + 1, sections):
-            pending[j] = pending[j] - product(weight[(j, k)], solved)
-        traded = lax.ppermute(solved, "z", [(i, i ^ 1) for i in range(nz)])
+            pending[j] = pending[j] - quick(weight[(j, k)], solved)
+        traded = whole_block(lax.ppermute(mine, "z", [(i, i ^ 1) for i in range(nz)]), first)
         factor = panel[square:, k * block_rows : (k + 1) * block_rows]
         pieces = []
         for h, block in enumerate((solved, traded)):
-            below[h] = below[h] - product(factor, block)
+            below[h] = below[h] - quick(factor, block)
             pieces.append(lax.dynamic_slice_in_dim(block, start, share, 0))
         finished.append(pieces)
     ends = [jnp.concatenate([f[h] for f in finished] + [below[h]], axis=0) for h in range(2)]

time: 303 us -> 301 us (level)
  waiting for transfers between devices: 112 us -> 48.7 us
  blocking collectives: 36 us -> 82.5 us
  starting transfers between devices: 84.8 us -> 96 us
  Pallas kernels: 0 us -> 10.1 us
  local copies, waits for them, and re-layouts: 20.1 us -> 13.4 us
    all_gather x0 -> x1, blocking collectives: none -> 64.2 us  [redistribute(): gathered = lax.all_gather(beside, 'z')]
    all_to_all x1, waiting for transfers between devices: 43.7 us -> 0.01 us  [redistribute(): lax.all_to_all(sent, ROWS, split_axis=0, concat_axis=0, tiled=True)]
    all_gather x2 -> x1, waiting for transfers between devices: 20.7 us -> 0.02 us  [shards(): gathered = lax.all_gather(pack_tiles(panel, inverse_columns, names), 'z')]
    all_to_all x2 -> x1, blocking collectives: 36 us -> 18.4 us  [shards(): lax.all_to_all(copies, 'x', split_axis=0, concat_axis=0, tiled=True)]
    ppermute x8 -> x12, starting transfers between devices: 25.6 us -> 35.8 us  [the longest x8 25.2 us: whole_block(): other = lax.ppermute(mine, 'core', SWAP)]
    pallas_call x0 -> x1, Pallas kernels: none -> 10.1 us  [pack_tiles(): pl.pallas_call(kernel, out_shape=jax.ShapeDtypeStruct((len(names), share,...]
    ppermute x4, starting transfers between devices: 22.1 us -> 15.2 us  [shards(): half = keep + lax.ppermute(give, 'core', SWAP)]
    all_to_all x2 -> x3, waiting for transfers between devices: 12.7 us -> 18.8 us  [shards(): lax.all_to_all(copies, 'x', split_axis=0, concat_axis=0, tiled=True)]
  transfers between devices with their start and end apart: 19 -> 23, of which waited for: 13 -> 10; matrix products, arithmetic and copies ran while one was open for 12% -> 11% of each run, Pallas kernels for 0% -> 3%
where the time goes in v4:
time: 301 us; the launch traced here: 299 us
  starting transfers between devices  96 us (32%)
  blocking collectives  82.5 us (27%)
  waiting for transfers between devices  48.7 us (16%)
  matrix products  27.1 us (9%)
  between operations  14.3 us (5%)
  local copies, waits for them, and re-layouts  13.4 us (4%)
  Pallas kernels  10.1 us (3%)
  other arithmetic  7.03 us (2%)
    all_gather x1, blocking collectives, redistribute(): gathered = lax.all_gather(beside, 'z')  64.2 us
    dot_general x23, matrix products, product(): lax.dot_general(left, right, (contract, ((), ())), precision=precision, p...  27.1 us
    ppermute x8, starting transfers between devices, whole_block(): other = lax.ppermute(mine, 'core', SWAP)  25.2 us
    all_to_all x1, starting transfers between devices, redistribute(): lax.all_to_all(sent, ROWS, split_axis=0, concat_axis=0, tiled=True)  19.8 us
    all_to_all x3, waiting for transfers between devices, shards(): lax.all_to_all(copies, 'x', split_axis=0, concat_axis=0, tiled=True)  18.8 us
    all_to_all x1, blocking collectives, shards(): lax.all_to_all(copies, 'x', split_axis=0, concat_axis=0, tiled=True)  18.4 us
    all_to_all x1, waiting for transfers between devices, shards(): tops = lax.all_to_all(tops, 'z', split_axis=0, concat_axis=0, tiled=True)  15.7 us
    ppermute x4, starting transfers between devices, shards(): half = keep + lax.ppermute(give, 'core', SWAP)  15.2 us
  transfers between devices with their start and end apart: 23, of which 10 were waited for; matrix products, arithmetic and copies ran while one was open for 11% of the time, Pallas kernels for 3%

profile of v4, /device:TPU:1, one launch (start us, length us, event | category | flops | bytes accessed | tf_op | source)
XLA Modules:
  0.0 299.2 jit_solution(11955224202140509113)
XLA Ops:
  8.3 5.0 %all-to-all-start = ((f32[64,4,256]{2,0,1:T(8,128)}), f32[64,4,256]{2,0,1:T(8,128)S(1)}, u32[]{:S(2)}, u32[]{:S(2)}) async-start(f32[64,4,256]{2,0,1:T(8,128)} %bitcast.231), calls=%async_computation | async-start | bytes 524288 | tf_op jit(solution)/shard_map/all_to_all | solution.py:54
  13.3 10.1 %shard_map.64 = f32[9,8,1024]{2,1,0:T(8,128)} custom-call(f32[256,4096]{1,0:T(8,128)} %panel_ref.1, f32[4,8,1024]{2,1,0:T(8,128)} %bitcast.270), custom_call_target="tpu_custom_call" | custom-call | tf_op jit(solution)/shard_map/pallas_call | solution.py:43
  26.8 19.8 %all-to-all-start.1 = ((f32[128,2,640]{2,1,0:T(2,128)}), f32[128,2,640]{2,1,0:T(2,128)S(1)}, u32[]{:S(2)}, u32[]{:S(2)}) async-start(f32[128,2,640]{2,1,0:T(2,128)} %copy.129), calls=%async_computation.1 | async-start | bytes 1310720 | tf_op jit(solution)/shard_map/all_to_all | solution.py:84
  46.6 64.2 %all-gather = f32[128,1024]{1,0:T(8,128)S(1)} all-gather(f32[8,1024]{1,0:T(8,128)S(1)} %slice_bitcast_fusion.29), channel_id=2, replica_groups=mesh['x'=4,'z'=16,'core'=2,'rhs'=4] {'z'}, dimensions={0}, use_global_device_ids=true | all-gather | bytes 557056 | tf_op jit(solution)/shard_map/all_gather | solution.py:83
  113.9 9.4 %all-to-all-start.2 = ((f32[16,32,128]{2,1,0:T(8,128)}), f32[16,32,128]{2,1,0:T(8,128)S(1)}, u32[]{:S(2)}, u32[]{:S(2)}) async-start(f32[16,32,128]{2,1,0:T(8,128)} %bitcast.23), calls=%async_computation.2 | async-start | bytes 524288 | tf_op jit(solution)/shard_map/all_to_all | solution.py:126
  123.5 15.7 %all-to-all-done.2 = f32[16,32,128]{2,1,0:T(8,128)S(1)} async-done(((f32[16,32,128]{2,1,0:T(8,128)}), f32[16,32,128]{2,1,0:T(8,128)S(1)}, u32[]{:S(2)}, u32[]{:S(2)}) %all-to-all-start.2) | async-done | bytes 262176 | tf_op jit(solution)/shard_map/all_to_all | solution.py:126
  139.7 8.8 %collective-permute-start = (f32[64,8,128]{2,1,0:T(8,128)S(1)}, f32[64,8,128]{2,1,0:T(8,128)S(1)}, u32[]{:S(2)}, u32[]{:S(2)}) collective-permute-start(f32[64,8,128]{2,1,0:T(8,128)S(1)} %select_bitcast_fusion.19), channel_id=1, source_target_pairs={{0,4},{4,0},{1,5},{5,1},{2,6},{6,2},{3,7},{7,3},{8,12},{12,8},{9,1... | collective-permute-start | bytes 786440 | tf_op jit(solution)/shard_map/ppermute | solution.py:139
  149.7 18.4 %all_to_all.49 = f32[4,64,8,128]{3,2,1,0:T(8,128)S(1)} all-to-all(f32[4,64,8,128]{3,2,1,0:T(8,128)S(1)} %broadcast_in_dim.47), channel_id=1, replica_groups=mesh['x'=4,'z'=16,'core'=2,'rhs'=4] {'x'}, dimensions={0} | all-to-all | bytes 2097152 | tf_op jit(solution)/shard_map/all_to_all | solution.py:141
  168.2 3.7 %collective-permute-start.1 = (f32[64,8,128]{2,1,0:T(8,128)S(1)}, f32[64,8,128]{2,1,0:T(8,128)S(1)}, u32[]{:S(2)}, u32[]{:S(2)}) collective-permute-start(f32[64,8,128]{2,1,0:T(8,128)S(1)} %reduce_sum.56), channel_id=1, source_target_pairs={{0,4},{4,0},{1,5},{5,1},{2,6},{6,2},{3,7},{7,3},{8,12},{12,8},{9,1... | collective-permute-start | bytes 786440 | tf_op jit(solution)/shard_map/ppermute | solution.py:100
  179.0 3.0 collective-permute-start.8
  183.1 3.5 %all-to-all-start.4 = ((f32[4,64,8,128]{3,2,1,0:T(8,128)}), f32[4,64,8,128]{3,2,1,0:T(8,128)S(1)}, u32[]{:S(2)}, u32[]{:S(2)}) async-start(f32[4,64,8,128]{3,2,1,0:T(8,128)} %broadcast_in_dim.48), calls=%async_computation.4 | async-start | bytes 2097152 | tf_op jit(solution)/shard_map/all_to_all | solution.py:141
  188.8 2.9 collective-permute-start.9
  195.7 5.7 %all-to-all-done.4 = f32[4,64,8,128]{3,2,1,0:T(8,128)S(1)} async-done(((f32[4,64,8,128]{3,2,1,0:T(8,128)}), f32[4,64,8,128]{3,2,1,0:T(8,128)S(1)}, u32[]{:S(2)}, u32[]{:S(2)}) %all-to-all-start.4) | async-done | bytes 1048608 | tf_op jit(solution)/shard_map/all_to_all | solution.py:141
  202.2 3.2 %collective-permute-start.3 = (f32[64,8,128]{2,1,0:T(8,128)}, f32[64,8,128]{2,1,0:T(8,128)}, u32[]{:S(2)}, u32[]{:S(2)}) collective-permute-start(f32[64,8,128]{2,1,0:T(8,128)} %reduce_sum.57), channel_id=1, source_target_pairs={{0,4},{4,0},{1,5},{5,1},{2,6},{6,2},{3,7},{7,3},{8,12},{12,8},{9,1... | collective-permute-start | bytes 786440 | tf_op jit(solution)/shard_map/ppermute | solution.py:100
  219.5 3.7 %all-to-all-start.5 = ((f32[4,64,8,128]{3,2,1,0:T(8,128)}), f32[4,64,8,128]{3,2,1,0:T(8,128)S(1)}, u32[]{:S(2)}, u32[]{:S(2)}) async-start(f32[4,64,8,128]{3,2,1,0:T(8,128)} %broadcast_in_dim.49), calls=%async_computation.5 | async-start | bytes 2097152 | tf_op jit(solution)/shard_map/all_to_all | solution.py:141
  224.6 3.2 %collective-permute-start.11 = (f32[64,8,128]{2,1,0:T(8,128)S(1)}, f32[64,8,128]{2,1,0:T(8,128)S(1)}, u32[]{:S(2)}, u32[]{:S(2)}) collective-permute-start(f32[64,8,128]{2,1,0:T(8,128)S(1)} %collective-permute-done.10), channel_id=1, source_target_pairs={{0,4},{4,0},{1,5},{5,1},{2,6},{6,2},{3,7},{7,3},{8,12},{12,8},{9,1... | collective-permute-start | bytes 786440 | tf_op jit(solution)/shard_map/ppermute | solution.py:100
  232.2 5.2 %all-to-all-done.5 = f32[4,64,8,128]{3,2,1,0:T(8,128)S(1)} async-done(((f32[4,64,8,128]{3,2,1,0:T(8,128)}), f32[4,64,8,128]{3,2,1,0:T(8,128)S(1)}, u32[]{:S(2)}, u32[]{:S(2)}) %all-to-all-start.5) | async-done | bytes 1048608 | tf_op jit(solution)/shard_map/all_to_all | solution.py:141
  237.4 3.6 %collective-permute-start.5 = (f32[64,8,128]{2,1,0:T(8,128)S(1)}, f32[64,8,128]{2,1,0:T(8,128)S(1)}, u32[]{:S(2)}, u32[]{:S(2)}) collective-permute-start(f32[64,8,128]{2,1,0:T(8,128)S(1)} %reduce_sum.58), channel_id=1, source_target_pairs={{0,4},{4,0},{1,5},{5,1},{2,6},{6,2},{3,7},{7,3},{8,12},{12,8},{9,1... | collective-permute-start | bytes 786440 | tf_op jit(solution)/shard_map/ppermute | solution.py:100
  248.1 3.0 collective-permute-start.12
  252.3 3.5 %all-to-all-start.6 = ((f32[4,64,8,128]{3,2,1,0:T(8,128)}), f32[4,64,8,128]{3,2,1,0:T(8,128)S(1)}, u32[]{:S(2)}, u32[]{:S(2)}) async-start(f32[4,64,8,128]{3,2,1,0:T(8,128)} %broadcast_in_dim.50), calls=%async_computation.6 | async-start | bytes 2097152 | tf_op jit(solution)/shard_map/all_to_all | solution.py:141
  257.8 2.9 collective-permute-start.13
  262.5 8.0 %all-to-all-done.6 = f32[4,64,8,128]{3,2,1,0:T(8,128)S(1)} async-done(((f32[4,64,8,128]{3,2,1,0:T(8,128)}), f32[4,64,8,128]{3,2,1,0:T(8,128)S(1)}, u32[]{:S(2)}, u32[]{:S(2)}) %all-to-all-start.6) | async-done | bytes 1048608 | tf_op jit(solution)/shard_map/all_to_all | solution.py:141
  270.6 3.2 %collective-permute-start.7 = (f32[64,8,128]{2,1,0:T(8,128)S(1)}, f32[64,8,128]{2,1,0:T(8,128)S(1)}, u32[]{:S(2)}, u32[]{:S(2)}) collective-permute-start(f32[64,8,128]{2,1,0:T(8,128)S(1)} %reduce_sum.59), channel_id=1, source_target_pairs={{0,4},{4,0},{1,5},{5,1},{2,6},{6,2},{3,7},{7,3},{8,12},{12,8},{9,1... | collective-permute-start | bytes 786440 | tf_op jit(solution)/shard_map/ppermute | solution.py:100
  278.0 7.4 %collective-permute-done.14 = f32[64,8,128]{2,1,0:T(8,128)S(1)} collective-permute-done((f32[64,8,128]{2,1,0:T(8,128)S(1)}, f32[64,8,128]{2,1,0:T(8,128)S(1)}, u32[]{:S(2)}, u32[]{:S(2)}) %collective-permute-start.14) | collective-permute-done | bytes 262176 | tf_op jit(solution)/shard_map/ppermute | solution.py:145
  (141 shorter events, 68.1 us)
Async XLA Ops:
  8.3 16.2 %all-to-all-start = ((f32[64,4,256]{2,0,1:T(8,128)}), f32[64,4,256]{2,0,1:T(8,128)S(1)}, u32[]{:S(2)}, u32[]{:S(2)}) async-start(f32[64,4,256]{2,0,1:T(8,128)} %bitcast.231), calls=%async_computation | async-start | bytes 524288 | tf_op jit(solution)/shard_map/all_to_all | solution.py:54
  13.3 160.0 %all-gather.4.cloned.1.call-start = ((), (), s32[]{:S(2)}) async-start(), calls=%async_computation.7 | async-start | bytes 5013504 | tf_op jit(solution)/shard_map/all_gather | solution.py:116
  26.8 84.0 %all-to-all-start.1 = ((f32[128,2,640]{2,1,0:T(2,128)}), f32[128,2,640]{2,1,0:T(2,128)S(1)}, u32[]{:S(2)}, u32[]{:S(2)}) async-start(f32[128,2,640]{2,1,0:T(2,128)} %copy.129), calls=%async_computation.1 | async-start | bytes 1310720 | tf_op jit(solution)/shard_map/all_to_all | solution.py:84
  113.9 25.4 %all-to-all-start.2 = ((f32[16,32,128]{2,1,0:T(8,128)}), f32[16,32,128]{2,1,0:T(8,128)S(1)}, u32[]{:S(2)}, u32[]{:S(2)}) async-start(f32[16,32,128]{2,1,0:T(8,128)} %bitcast.23), calls=%async_computation.2 | async-start | bytes 524288 | tf_op jit(solution)/shard_map/all_to_all | solution.py:126
  139.3 56.3 %copy-start = (f32[16,32,128]{2,1,0:T(8,128)}, f32[16,32,128]{2,1,0:T(8,128)S(1)}, u32[]{:S(2)}) copy-start(f32[16,32,128]{2,1,0:T(8,128)S(1)} %all-to-all-done.2) | copy-start | bytes 786436
  139.7 9.9 %collective-permute-start = (f32[64,8,128]{2,1,0:T(8,128)S(1)}, f32[64,8,128]{2,1,0:T(8,128)S(1)}, u32[]{:S(2)}, u32[]{:S(2)}) collective-permute-start(f32[64,8,128]{2,1,0:T(8,128)S(1)} %select_bitcast_fusion.19), channel_id=1, source_target_pairs={{0,4},{4,0},{1,5},{5,1},{2,6},{6,2},{3,7},{7,3},{8,12},{12,8},{9,1... | collective-permute-start | bytes 786440 | tf_op jit(solution)/shard_map/ppermute | solution.py:139
  168.2 4.9 %collective-permute-start.1 = (f32[64,8,128]{2,1,0:T(8,128)S(1)}, f32[64,8,128]{2,1,0:T(8,128)S(1)}, u32[]{:S(2)}, u32[]{:S(2)}) collective-permute-start(f32[64,8,128]{2,1,0:T(8,128)S(1)} %reduce_sum.56), channel_id=1, source_target_pairs={{0,4},{4,0},{1,5},{5,1},{2,6},{6,2},{3,7},{7,3},{8,12},{12,8},{9,1... | collective-permute-start | bytes 786440 | tf_op jit(solution)/shard_map/ppermute | solution.py:100
  176.7 5.3 %collective-permute-start.2 = (f32[64,8,128]{2,1,0:T(8,128)S(1)}, f32[64,8,128]{2,1,0:T(8,128)S(1)}, u32[]{:S(2)}, u32[]{:S(2)}) collective-permute-start(f32[64,8,128]{2,1,0:T(8,128)S(1)} %select_bitcast_fusion.16), channel_id=1, source_target_pairs={{0,4},{4,0},{1,5},{5,1},{2,6},{6,2},{3,7},{7,3},{8,12},{12,8},{9,1... | collective-permute-start | bytes 786440 | tf_op jit(solution)/shard_map/ppermute | solution.py:139
  179.0 9.8 %collective-permute-start.8 = (f32[64,8,128]{2,1,0:T(8,128)S(1)}, f32[64,8,128]{2,1,0:T(8,128)}, u32[]{:S(2)}, u32[]{:S(2)}) collective-permute-start(f32[64,8,128]{2,1,0:T(8,128)S(1)} %reduce_sum.56), channel_id=1, source_target_pairs={{0,8},{8,0},{16,24},{24,16},{32,40},{40,32},{48,56},{56,48},{64,72... | collective-permute-start | bytes 786440 | tf_op jit(solution)/shard_map/ppermute | solution.py:145
  183.1 18.3 %all-to-all-start.4 = ((f32[4,64,8,128]{3,2,1,0:T(8,128)}), f32[4,64,8,128]{3,2,1,0:T(8,128)S(1)}, u32[]{:S(2)}, u32[]{:S(2)}) async-start(f32[4,64,8,128]{3,2,1,0:T(8,128)} %broadcast_in_dim.48), calls=%async_computation.4 | async-start | bytes 2097152 | tf_op jit(solution)/shard_map/all_to_all | solution.py:141
  188.8 5.8 %collective-permute-start.9 = (f32[64,8,128]{2,1,0:T(8,128)}, f32[64,8,128]{2,1,0:T(8,128)S(1)}, u32[]{:S(2)}, u32[]{:S(2)}) collective-permute-start(f32[64,8,128]{2,1,0:T(8,128)} %collective-permute-done.8), channel_id=1, source_target_pairs={{0,4},{4,0},{1,5},{5,1},{2,6},{6,2},{3,7},{7,3},{8,12},{12,8},{9,1... | collective-permute-start | bytes 786440 | tf_op jit(solution)/shard_map/ppermute | solution.py:100
  202.2 5.4 %collective-permute-start.3 = (f32[64,8,128]{2,1,0:T(8,128)}, f32[64,8,128]{2,1,0:T(8,128)}, u32[]{:S(2)}, u32[]{:S(2)}) collective-permute-start(f32[64,8,128]{2,1,0:T(8,128)} %reduce_sum.57), channel_id=1, source_target_pairs={{0,4},{4,0},{1,5},{5,1},{2,6},{6,2},{3,7},{7,3},{8,12},{12,8},{9,1... | collective-permute-start | bytes 786440 | tf_op jit(solution)/shard_map/ppermute | solution.py:100
  211.2 6.2 %collective-permute-start.4 = (f32[64,8,128]{2,1,0:T(8,128)}, f32[64,8,128]{2,1,0:T(8,128)}, u32[]{:S(2)}, u32[]{:S(2)}) collective-permute-start(f32[64,8,128]{2,1,0:T(8,128)} %select_bitcast_fusion.13), channel_id=1, source_target_pairs={{0,4},{4,0},{1,5},{5,1},{2,6},{6,2},{3,7},{7,3},{8,12},{12,8},{9,1... | collective-permute-start | bytes 786440 | tf_op jit(solution)/shard_map/ppermute | solution.py:139
  215.1 9.5 %collective-permute-start.10 = (f32[64,8,128]{2,1,0:T(8,128)}, f32[64,8,128]{2,1,0:T(8,128)S(1)}, u32[]{:S(2)}, u32[]{:S(2)}) collective-permute-start(f32[64,8,128]{2,1,0:T(8,128)} %reduce_sum.57), channel_id=1, source_target_pairs={{0,8},{8,0},{16,24},{24,16},{32,40},{40,32},{48,56},{56,48},{64,72... | collective-permute-start | bytes 786440 | tf_op jit(solution)/shard_map/ppermute | solution.py:145
  219.5 17.9 %all-to-all-start.5 = ((f32[4,64,8,128]{3,2,1,0:T(8,128)}), f32[4,64,8,128]{3,2,1,0:T(8,128)S(1)}, u32[]{:S(2)}, u32[]{:S(2)}) async-start(f32[4,64,8,128]{3,2,1,0:T(8,128)} %broadcast_in_dim.49), calls=%async_computation.5 | async-start | bytes 2097152 | tf_op jit(solution)/shard_map/all_to_all | solution.py:141
  224.6 16.4 %collective-permute-start.11 = (f32[64,8,128]{2,1,0:T(8,128)S(1)}, f32[64,8,128]{2,1,0:T(8,128)S(1)}, u32[]{:S(2)}, u32[]{:S(2)}) collective-permute-start(f32[64,8,128]{2,1,0:T(8,128)S(1)} %collective-permute-done.10), channel_id=1, source_target_pairs={{0,4},{4,0},{1,5},{5,1},{2,6},{6,2},{3,7},{7,3},{8,12},{12,8},{9,1... | collective-permute-start | bytes 786440 | tf_op jit(solution)/shard_map/ppermute | solution.py:100
  237.4 4.7 %collective-permute-start.5 = (f32[64,8,128]{2,1,0:T(8,128)S(1)}, f32[64,8,128]{2,1,0:T(8,128)S(1)}, u32[]{:S(2)}, u32[]{:S(2)}) collective-permute-start(f32[64,8,128]{2,1,0:T(8,128)S(1)} %reduce_sum.58), channel_id=1, source_target_pairs={{0,4},{4,0},{1,5},{5,1},{2,6},{6,2},{3,7},{7,3},{8,12},{12,8},{9,1... | collective-permute-start | bytes 786440 | tf_op jit(solution)/shard_map/ppermute | solution.py:100
  244.1 7.0 %collective-permute-start.6 = (f32[64,8,128]{2,1,0:T(8,128)S(1)}, f32[64,8,128]{2,1,0:T(8,128)S(1)}, u32[]{:S(2)}, u32[]{:S(2)}) collective-permute-start(f32[64,8,128]{2,1,0:T(8,128)S(1)} %select_bitcast_fusion.10), channel_id=1, source_target_pairs={{0,4},{4,0},{1,5},{5,1},{2,6},{6,2},{3,7},{7,3},{8,12},{12,8},{9,1... | collective-permute-start | bytes 786440 | tf_op jit(solution)/shard_map/ppermute | solution.py:139
  248.1 9.7 %collective-permute-start.12 = (f32[64,8,128]{2,1,0:T(8,128)S(1)}, f32[64,8,128]{2,1,0:T(8,128)S(1)}, u32[]{:S(2)}, u32[]{:S(2)}) collective-permute-start(f32[64,8,128]{2,1,0:T(8,128)S(1)} %reduce_sum.58), channel_id=1, source_target_pairs={{0,8},{8,0},{16,24},{24,16},{32,40},{40,32},{48,56},{56,48},{64,72... | collective-permute-start | bytes 786440 | tf_op jit(solution)/shard_map/ppermute | solution.py:145
  252.3 18.3 %all-to-all-start.6 = ((f32[4,64,8,128]{3,2,1,0:T(8,128)}), f32[4,64,8,128]{3,2,1,0:T(8,128)S(1)}, u32[]{:S(2)}, u32[]{:S(2)}) async-start(f32[4,64,8,128]{3,2,1,0:T(8,128)} %broadcast_in_dim.50), calls=%async_computation.6 | async-start | bytes 2097152 | tf_op jit(solution)/shard_map/all_to_all | solution.py:141
  257.8 4.6 %collective-permute-start.13 = (f32[64,8,128]{2,1,0:T(8,128)S(1)}, f32[64,8,128]{2,1,0:T(8,128)S(1)}, u32[]{:S(2)}, u32[]{:S(2)}) collective-permute-start(f32[64,8,128]{2,1,0:T(8,128)S(1)} %collective-permute-done.12), channel_id=1, source_target_pairs={{0,4},{4,0},{1,5},{5,1},{2,6},{6,2},{3,7},{7,3},{8,12},{12,8},{9,1... | collective-permute-start | bytes 786440 | tf_op jit(solution)/shard_map/ppermute | solution.py:100
  270.6 7.2 %collective-permute-start.7 = (f32[64,8,128]{2,1,0:T(8,128)S(1)}, f32[64,8,128]{2,1,0:T(8,128)S(1)}, u32[]{:S(2)}, u32[]{:S(2)}) collective-permute-start(f32[64,8,128]{2,1,0:T(8,128)S(1)} %reduce_sum.59), channel_id=1, source_target_pairs={{0,4},{4,0},{1,5},{5,1},{2,6},{6,2},{3,7},{7,3},{8,12},{12,8},{9,1... | collective-permute-start | bytes 786440 | tf_op jit(solution)/shard_map/ppermute | solution.py:100
  275.5 9.8 %collective-permute-start.14 = (f32[64,8,128]{2,1,0:T(8,128)S(1)}, f32[64,8,128]{2,1,0:T(8,128)S(1)}, u32[]{:S(2)}, u32[]{:S(2)}) collective-permute-start(f32[64,8,128]{2,1,0:T(8,128)S(1)} %reduce_sum.59), channel_id=1, source_target_pairs={{0,8},{8,0},{16,24},{24,16},{32,40},{40,32},{48,56},{56,48},{64,72... | collective-permute-start | bytes 786440 | tf_op jit(solution)/shard_map/ppermute | solution.py:145
  285.3 4.4 %collective-permute-start.15 = (f32[64,8,128]{2,1,0:T(8,128)S(1)}, f32[64,8,128]{2,1,0:T(8,128)S(1)}, u32[]{:S(2)}, u32[]{:S(2)}) collective-permute-start(f32[64,8,128]{2,1,0:T(8,128)S(1)} %collective-permute-done.14), channel_id=1, source_target_pairs={{0,4},{4,0},{1,5},{5,1},{2,6},{6,2},{3,7},{7,3},{8,12},{12,8},{9,1... | collective-permute-start | bytes 786440 | tf_op jit(solution)/shard_map/ppermute | solution.py:100
  (7 other events, 102.3 us)
Sparse Core Ops, SparseCore 0:
  23.5 119.7 all-gather.3

commit v5 on v3

--- a/solution.py
+++ b/solution.py
@@ -17,7 +17,15 @@
     )
 
 
-def redistribute(targets, send_order, send_count, recv_slot):
+def ring(block, steps, hop, size, axis):
+    held = []
+    for _ in range(steps):
+        block = lax.ppermute(block, axis, [(i, (i + hop) % size) for i in range(size)])
+        held.append(block)
+    return held
+
+
+def redistribute(targets, send_order, send_count, recv_slot, tips):
     groups = lax.axis_size(ROWS)
     arrived = lax.all_to_all(targets, "rhs", split_axis=1, concat_axis=0, tiled=True)
     rows_local, columns = arrived.shape
@@ -50,6 +58,7 @@
     incoming = lax.all_to_all(
         jnp.stack(halves, axis=1), ROWS, split_axis=0, concat_axis=0, tiled=True
     )
+    incoming, tips = lax.optimization_barrier((incoming, tips))
     total = 0.0
     for h in range(capacity // 2):
         half = incoming[:, h]
@@ -58,7 +67,13 @@
             placed = (label.astype(jnp.int32) == index[None, :]).astype(jnp.float32)
             rows = half[:, s * columns : (s + 1) * columns]
             total = total + product(placed, rows, ((0,), (0,)))
-    return total
+    return total, tips
+
+
+def whole_block(mine, first):
+    other = lax.ppermute(mine, "core", SWAP)
+    both = jnp.stack([jnp.where(first, mine, other), jnp.where(first, other, mine)], axis=1)
+    return both.reshape(2 * mine.shape[0] * mine.shape[1], mine.shape[2])
 
 
 def shards(targets, send_order, send_count, recv_slot, panel, inv_diag):
@@ -70,24 +85,31 @@
     square = sections * share
     inverse_columns = jnp.swapaxes(inv_diag, 1, 2)
 
-    def tile(j, k):
-        if j == k:
-            return inverse_columns[k]
-        return panel[j * share : (j + 1) * share, k * block_rows : (k + 1) * block_rows]
-
-    weight = {}
-    early = [(0, 0), (1, 0)]
-    late = [(j, k) for j in range(sections) for k in range(j + 1) if (j, k) not in early]
-    for names in (early, late):
-        gathered = lax.all_gather(jnp.stack([tile(j, k) for j, k in names]), "z")
-        for i, name in enumerate(names):
-            weight[name] = gathered[:, i].reshape(nz * share, block_rows)
-
-    residual = redistribute(targets, send_order, send_count, recv_slot)
+    names = [(j, k) for j in range(sections) for k in range(j + 1)]
+    own = jnp.stack(
+        [
+            inverse_columns[k]
+            if j == k
+            else panel[j * share : (j + 1) * share, k * block_rows : (k + 1) * block_rows]
+            for j, k in names
+        ]
+    )
+    up, down = ring(own, 5, 1, nz, "z"), ring(own, 5, -1, nz, "z")
+    residual, (up[-1], down[-1]) = redistribute(
+        targets, send_order, send_count, recv_slot, (up[-1], down[-1])
+    )
+    up += ring(up[-1], nz // 2 - 5, 1, nz, "z")
+    down += ring(down[-1], nz // 2 - 6, -1, nz, "z")
+    around = [own] + down + up[::-1]
+    weight = {
+        name: jnp.concatenate([chunk[i] for chunk in around], axis=0)
+        for i, name in enumerate(names)
+    }
     columns = residual.shape[1] // 2
     halves = jnp.stack([residual[:square, :columns], residual[:square, columns:]])
     tops = jnp.broadcast_to(halves[None], (nz // 2,) + halves.shape).reshape(nz, square, columns)
     tops = lax.all_to_all(tops, "z", split_axis=0, concat_axis=0, tiled=True)
+    tops = lax.dynamic_slice_in_dim(jnp.concatenate([tops, tops[:-1]], axis=0), zi, nz, 0)
     pending = [
         tops[:, k * share : (k + 1) * share].reshape(nz * share, columns) for k in range(sections)
     ]
@@ -103,12 +125,10 @@
         half = keep + lax.ppermute(give, "core", SWAP)
         copies = jnp.broadcast_to(half[None], (nx,) + half.shape)
         mine = jnp.sum(lax.all_to_all(copies, "x", split_axis=0, concat_axis=0, tiled=True), axis=0)
-        other = lax.ppermute(mine, "core", SWAP)
-        solved = jnp.stack([jnp.where(first, mine, other), jnp.where(first, other, mine)], axis=1)
-        solved = solved.reshape(block_rows, columns)
+        solved = whole_block(mine, first)
         for j in range(k + 1, sections):
             pending[j] = pending[j] - product(weight[(j, k)], solved)
-        traded = lax.ppermute(solved, "z", [(i, i ^ 1) for i in range(nz)])
+        traded = whole_block(lax.ppermute(mine, "z", [(i, i ^ 1) for i in range(nz)]), first)
         factor = panel[square:, k * block_rows : (k + 1) * block_rows]
         pieces = []
         for h, block in enumerate((solved, traded)):

time: 303 us -> 349 us (1.15)
  starting transfers between devices: 84.8 us -> 144 us
  local copies, waits for them, and re-layouts: 20.1 us -> 61.2 us
  blocking collectives: 36 us -> 0 us
  waiting for transfers between devices: 112 us -> 98.1 us
  between operations: 14.1 us -> 1.13 us
  matrix products: 27 us -> 32.9 us
    ppermute x8 -> x27, waiting for transfers between devices: 15.6 us -> 74.8 us  [the longest x15 58 us: ring(): lax.ppermute(block, axis, [(i, (i + hop) % size) for i in range(size)])]
    ppermute x8 -> x27, starting transfers between devices: 25.6 us -> 80.8 us  [the longest x15 46.9 us: ring(): lax.ppermute(block, axis, [(i, (i + hop) % size) for i in range(size)])]
    all_to_all x1, waiting for transfers between devices: 43.7 us -> 0.01 us  [redistribute(): lax.all_to_all(jnp.stack(halves, axis=1), ROWS, split_axis=0, concat_axis...]
    unnamed x27 -> x87, local copies, waits for them, and re-layouts: 8.48 us -> 47.5 us
    all_to_all x2 -> x0, blocking collectives: 36 us -> none  [shards(): lax.all_to_all(copies, 'x', split_axis=0, concat_axis=0, tiled=True)]
    all_gather x2 -> x0, waiting for transfers between devices: 20.7 us -> none  [shards(): gathered = lax.all_gather(jnp.stack([tile(j, k) for j, k in names]), 'z')]
    all_to_all x1, waiting for transfers between devices: 12.3 us -> 0.01 us  [shards(): tops = lax.all_to_all(tops, 'z', split_axis=0, concat_axis=0, tiled=True)]
    ppermute x4, starting transfers between devices: 22.1 us -> 12.1 us  [shards(): half = keep + lax.ppermute(give, 'core', SWAP)]
  transfers between devices with their start and end apart: 19 -> 38, of which waited for: 13 -> 17; matrix products, arithmetic and copies ran while one was open for 12% -> 23% of each run, Pallas kernels for 0% -> 0%
where the time goes in v5:
time: 349 us; the launch traced here: 345 us
  starting transfers between devices  144 us (41%)
  waiting for transfers between devices  98.1 us (28%)
  local copies, waits for them, and re-layouts  61.2 us (18%)
  matrix products  32.9 us (9%)
  other arithmetic  7.49 us (2%)
    ppermute x15, waiting for transfers between devices, ring(): lax.ppermute(block, axis, [(i, (i + hop) % size) for i in range(size)])  58 us
    unnamed x87, local copies, waits for them, and re-layouts  47.5 us
    ppermute x15, starting transfers between devices, ring(): lax.ppermute(block, axis, [(i, (i + hop) % size) for i in range(size)])  46.9 us
    dot_general x23, matrix products, product(): lax.dot_general(left, right, (contract, ((), ())), precision=lax.Precisio...  32.9 us
    ppermute x8, starting transfers between devices, whole_block(): other = lax.ppermute(mine, 'core', SWAP)  24.6 us
    all_to_all x4, waiting for transfers between devices, shards(): lax.all_to_all(copies, 'x', split_axis=0, concat_axis=0, tiled=True)  21.9 us
    all_to_all x1, starting transfers between devices, redistribute(): lax.all_to_all(jnp.stack(halves, axis=1), ROWS, split_axis=0, concat_axis...  19.8 us
    ppermute x4, waiting for transfers between devices, shards(): lax.ppermute(mine, 'z', [(i, i ^ 1) for i in range(nz)])  16.7 us
  transfers between devices with their start and end apart: 38, of which 17 were waited for; matrix products, arithmetic and copies ran while one was open for 23% of the time, Pallas kernels for 0%

profile of v5, /device:TPU:1, one launch (start us, length us, event | category | flops | bytes accessed | tf_op | source)
XLA Modules:
  0.0 345.3 jit_solution(12767377745359945662)
XLA Ops:
  1.7 5.0 %all-to-all-start = ((f32[64,4,256]{2,0,1:T(8,128)}), f32[64,4,256]{2,0,1:T(8,128)S(1)}, u32[]{:S(2)}, u32[]{:S(2)}) async-start(f32[64,4,256]{2,0,1:T(8,128)} %bitcast.814), calls=%async_computation | async-start | bytes 524288 | tf_op jit(solution)/shard_map/all_to_all | solution.py:30
  22.9 19.8 %all-to-all-start.1 = ((f32[128,2,640]{2,1,0:T(2,128)}), f32[128,2,640]{2,1,0:T(2,128)S(1)}, u32[]{:S(2)}, u32[]{:S(2)}) async-start(f32[128,2,640]{2,1,0:T(2,128)} %copy.64), calls=%async_computation.1 | async-start | bytes 1310720 | tf_op jit(solution)/shard_map/all_to_all | solution.py:58
  52.9 27.9 %collective-permute-done.4 = f32[10,8,1024]{2,1,0:T(8,128)} collective-permute-done((f32[10,8,1024]{2,1,0:T(8,128)}, f32[10,8,1024]{2,1,0:T(8,128)}, u32[]{:S(2)}, u32[]{:S(2)}) %collective-permute-start.4) | collective-permute-done | bytes 327712 | tf_op jit(solution)/shard_map/ppermute | solution.py:23
  82.7 4.6 %collective-permute-start.1 = (f32[10,8,1024]{2,1,0:T(8,128)}, f32[10,8,1024]{2,1,0:T(8,128)S(1)}, u32[]{:S(2)}, u32[]{:S(2)}) collective-permute-start(f32[10,8,1024]{2,1,0:T(8,128)} %collective-permute-done), channel_id=1, source_target_pairs={{0,120},{8,0},{16,8},{24,16},{32,24},{40,32},{48,40},{56,48},{64,5... | collective-permute-start | bytes 983048 | tf_op jit(solution)/shard_map/ppermute | solution.py:23
  94.3 4.6 %collective-permute-start.2 = (f32[10,8,1024]{2,1,0:T(8,128)S(1)}, f32[10,8,1024]{2,1,0:T(8,128)S(1)}, u32[]{:S(2)}, u32[]{:S(2)}) collective-permute-start(f32[10,8,1024]{2,1,0:T(8,128)S(1)} %collective-permute-done.1), channel_id=1, source_target_pairs={{0,120},{8,0},{16,8},{24,16},{32,24},{40,32},{48,40},{56,48},{64,5... | collective-permute-start | bytes 983048 | tf_op jit(solution)/shard_map/ppermute | solution.py:23
  104.7 4.6 %collective-permute-start.3 = (f32[10,8,1024]{2,1,0:T(8,128)S(1)}, f32[10,8,1024]{2,1,0:T(8,128)S(1)}, u32[]{:S(2)}, u32[]{:S(2)}) collective-permute-start(f32[10,8,1024]{2,1,0:T(8,128)S(1)} %collective-permute-done.2), channel_id=1, source_target_pairs={{0,120},{8,0},{16,8},{24,16},{32,24},{40,32},{48,40},{56,48},{64,5... | collective-permute-start | bytes 983048 | tf_op jit(solution)/shard_map/ppermute | solution.py:23
  114.3 4.6 %collective-permute-start.9 = (f32[10,8,1024]{2,1,0:T(8,128)S(1)}, f32[10,8,1024]{2,1,0:T(8,128)}, u32[]{:S(2)}, u32[]{:S(2)}) collective-permute-start(f32[10,8,1024]{2,1,0:T(8,128)S(1)} %collective-permute-done.3), channel_id=1, source_target_pairs={{0,120},{8,0},{16,8},{24,16},{32,24},{40,32},{48,40},{56,48},{64,5... | collective-permute-start | bytes 983048 | tf_op jit(solution)/shard_map/ppermute | solution.py:23
  126.0 11.8 %all-to-all-start.2 = ((f32[16,32,128]{2,1,0:T(8,128)}), f32[16,32,128]{2,1,0:T(8,128)S(1)}, u32[]{:S(2)}, u32[]{:S(2)}) async-start(f32[16,32,128]{2,1,0:T(8,128)} %bitcast.42), calls=%async_computation.2 | async-start | bytes 524288 | tf_op jit(solution)/shard_map/all_to_all | solution.py:111
  137.8 4.5 %collective-permute-start.10 = (f32[10,8,1024]{2,1,0:T(8,128)}, f32[10,8,1024]{2,1,0:T(8,128)S(1)}, u32[]{:S(2)}, u32[]{:S(2)}) collective-permute-start(f32[10,8,1024]{2,1,0:T(8,128)} %collective-permute-done.9), channel_id=1, source_target_pairs={{0,120},{8,0},{16,8},{24,16},{32,24},{40,32},{48,40},{56,48},{64,5... | collective-permute-start | bytes 983048 | tf_op jit(solution)/shard_map/ppermute | solution.py:23
  147.2 9.2 %collective-permute-done.10 = f32[10,8,1024]{2,1,0:T(8,128)S(1)} collective-permute-done((f32[10,8,1024]{2,1,0:T(8,128)}, f32[10,8,1024]{2,1,0:T(8,128)S(1)}, u32[]{:S(2)}, u32[]{:S(2)}) %collective-permute-start.10) | collective-permute-done | bytes 327712 | tf_op jit(solution)/shard_map/ppermute | solution.py:23
  156.4 4.3 %collective-permute-start.11 = (f32[10,8,1024]{2,1,0:T(8,128)S(1)}, f32[10,8,1024]{2,1,0:T(8,128)S(1)}, u32[]{:S(2)}, u32[]{:S(2)}) collective-permute-start(f32[10,8,1024]{2,1,0:T(8,128)S(1)} %collective-permute-done.10), channel_id=1, source_target_pairs={{0,120},{8,0},{16,8},{24,16},{32,24},{40,32},{48,40},{56,48},{64,5... | collective-permute-start | bytes 983048 | tf_op jit(solution)/shard_map/ppermute | solution.py:23
  163.9 6.7 %collective-permute-done.13 = f32[10,8,1024]{2,1,0:T(8,128)S(1)} collective-permute-done((f32[10,8,1024]{2,1,0:T(8,128)S(1)}, f32[10,8,1024]{2,1,0:T(8,128)S(1)}, u32[]{:S(2)}, u32[]{:S(2)}) %collective-permute-start.13) | collective-permute-done | bytes 327712 | tf_op jit(solution)/shard_map/ppermute | solution.py:23
  173.8 5.8 %collective-permute-done.14 = f32[10,8,1024]{2,1,0:T(8,128)S(1)} collective-permute-done((f32[10,8,1024]{2,1,0:T(8,128)S(1)}, f32[10,8,1024]{2,1,0:T(8,128)S(1)}, u32[]{:S(2)}, u32[]{:S(2)}) %collective-permute-start.14) | collective-permute-done | bytes 327712 | tf_op jit(solution)/shard_map/ppermute | solution.py:23
  188.8 6.3 %collective-permute-start.15 = (f32[64,8,128]{2,1,0:T(8,128)S(1)}, f32[64,8,128]{2,1,0:T(8,128)S(1)}, u32[]{:S(2)}, u32[]{:S(2)}) collective-permute-start(f32[64,8,128]{2,1,0:T(8,128)S(1)} %select_bitcast_fusion.19), channel_id=1, source_target_pairs={{0,4},{4,0},{1,5},{5,1},{2,6},{6,2},{3,7},{7,3},{8,12},{12,8},{9,1... | collective-permute-start | bytes 786440 | tf_op jit(solution)/shard_map/ppermute | solution.py:125
  199.4 4.3 %all-to-all-start.3 = ((f32[4,64,8,128]{3,2,1,0:T(8,128)}), f32[4,64,8,128]{3,2,1,0:T(8,128)S(1)}, u32[]{:S(2)}, u32[]{:S(2)}) async-start(f32[4,64,8,128]{3,2,1,0:T(8,128)} %broadcast_in_dim.47), calls=%async_computation.3 | async-start | bytes 2097152 | tf_op jit(solution)/shard_map/all_to_all | solution.py:127
  210.2 8.5 %all-to-all-done.3 = f32[4,64,8,128]{3,2,1,0:T(8,128)S(1)} async-done(((f32[4,64,8,128]{3,2,1,0:T(8,128)}), f32[4,64,8,128]{3,2,1,0:T(8,128)S(1)}, u32[]{:S(2)}, u32[]{:S(2)}) %all-to-all-start.3) | async-done | bytes 1048608 | tf_op jit(solution)/shard_map/all_to_all | solution.py:127
  233.6 3.5 %all-to-all-start.4 = ((f32[4,64,8,128]{3,2,1,0:T(8,128)}), f32[4,64,8,128]{3,2,1,0:T(8,128)S(1)}, u32[]{:S(2)}, u32[]{:S(2)}) async-start(f32[4,64,8,128]{3,2,1,0:T(8,128)} %broadcast_in_dim.48), calls=%async_computation.4 | async-start | bytes 2097152 | tf_op jit(solution)/shard_map/all_to_all | solution.py:127
  239.3 7.8 %collective-permute-done.23 = f32[64,8,128]{2,1,0:T(8,128)} collective-permute-done((f32[64,8,128]{2,1,0:T(8,128)S(1)}, f32[64,8,128]{2,1,0:T(8,128)}, u32[]{:S(2)}, u32[]{:S(2)}) %collective-permute-start.23) | collective-permute-done | bytes 262176 | tf_op jit(solution)/shard_map/ppermute | solution.py:131
  268.6 3.5 %all-to-all-start.5 = ((f32[4,64,8,128]{3,2,1,0:T(8,128)}), f32[4,64,8,128]{3,2,1,0:T(8,128)S(1)}, u32[]{:S(2)}, u32[]{:S(2)}) async-start(f32[4,64,8,128]{3,2,1,0:T(8,128)} %broadcast_in_dim.49), calls=%async_computation.5 | async-start | bytes 2097152 | tf_op jit(solution)/shard_map/all_to_all | solution.py:127
  282.5 4.3 %all-to-all-done.5 = f32[4,64,8,128]{3,2,1,0:T(8,128)S(1)} async-done(((f32[4,64,8,128]{3,2,1,0:T(8,128)}), f32[4,64,8,128]{3,2,1,0:T(8,128)S(1)}, u32[]{:S(2)}, u32[]{:S(2)}) %all-to-all-start.5) | async-done | bytes 1048608 | tf_op jit(solution)/shard_map/all_to_all | solution.py:127
  304.1 3.5 %all-to-all-start.6 = ((f32[4,64,8,128]{3,2,1,0:T(8,128)}), f32[4,64,8,128]{3,2,1,0:T(8,128)S(1)}, u32[]{:S(2)}, u32[]{:S(2)}) async-start(f32[4,64,8,128]{3,2,1,0:T(8,128)} %broadcast_in_dim.50), calls=%async_computation.6 | async-start | bytes 2097152 | tf_op jit(solution)/shard_map/all_to_all | solution.py:127
  314.6 7.4 %all-to-all-done.6 = f32[4,64,8,128]{3,2,1,0:T(8,128)S(1)} async-done(((f32[4,64,8,128]{3,2,1,0:T(8,128)}), f32[4,64,8,128]{3,2,1,0:T(8,128)S(1)}, u32[]{:S(2)}, u32[]{:S(2)}) %all-to-all-start.6) | async-done | bytes 1048608 | tf_op jit(solution)/shard_map/all_to_all | solution.py:127
  322.1 3.6 %collective-permute-start.22 = (f32[64,8,128]{2,1,0:T(8,128)S(1)}, f32[64,8,128]{2,1,0:T(8,128)S(1)}, u32[]{:S(2)}, u32[]{:S(2)}) collective-permute-start(f32[64,8,128]{2,1,0:T(8,128)S(1)} %reduce_sum.59), channel_id=1, source_target_pairs={{0,4},{4,0},{1,5},{5,1},{2,6},{6,2},{3,7},{7,3},{8,12},{12,8},{9,1... | collective-permute-start | bytes 786440 | tf_op jit(solution)/shard_map/ppermute | solution.py:74
  329.8 7.7 %collective-permute-done.29 = f32[64,8,128]{2,1,0:T(8,128)S(1)} collective-permute-done((f32[64,8,128]{2,1,0:T(8,128)S(1)}, f32[64,8,128]{2,1,0:T(8,128)S(1)}, u32[]{:S(2)}, u32[]{:S(2)}) %collective-permute-start.29) | collective-permute-done | bytes 262176 | tf_op jit(solution)/shard_map/ppermute | solution.py:131
  (229 shorter events, 170.5 us)
Async XLA Ops:
  1.7 19.0 %all-to-all-start = ((f32[64,4,256]{2,0,1:T(8,128)}), f32[64,4,256]{2,0,1:T(8,128)S(1)}, u32[]{:S(2)}, u32[]{:S(2)}) async-start(f32[64,4,256]{2,0,1:T(8,128)} %bitcast.814), calls=%async_computation | async-start | bytes 524288 | tf_op jit(solution)/shard_map/all_to_all | solution.py:30
  22.9 99.9 %all-to-all-start.1 = ((f32[128,2,640]{2,1,0:T(2,128)}), f32[128,2,640]{2,1,0:T(2,128)S(1)}, u32[]{:S(2)}, u32[]{:S(2)}) async-start(f32[128,2,640]{2,1,0:T(2,128)} %copy.64), calls=%async_computation.1 | async-start | bytes 1310720 | tf_op jit(solution)/shard_map/all_to_all | solution.py:58
  44.8 36.0 %collective-permute-start.4 = (f32[10,8,1024]{2,1,0:T(8,128)}, f32[10,8,1024]{2,1,0:T(8,128)}, u32[]{:S(2)}, u32[]{:S(2)}) collective-permute-start(f32[10,8,1024]{2,1,0:T(8,128)} %constant_dynamic-update-slice_fusion), channel_id=1, source_target_pairs={{0,8},{8,16},{16,24},{24,32},{32,40},{40,48},{48,56},{56,64},{64,7... | collective-permute-start | bytes 983048 | tf_op jit(solution)/shard_map/ppermute | solution.py:23
  48.1 34.6 %collective-permute-start = (f32[10,8,1024]{2,1,0:T(8,128)}, f32[10,8,1024]{2,1,0:T(8,128)}, u32[]{:S(2)}, u32[]{:S(2)}) collective-permute-start(f32[10,8,1024]{2,1,0:T(8,128)} %constant_dynamic-update-slice_fusion), channel_id=1, source_target_pairs={{0,120},{8,0},{16,8},{24,16},{32,24},{40,32},{48,40},{56,48},{64,5... | collective-permute-start | bytes 983048 | tf_op jit(solution)/shard_map/ppermute | solution.py:23
  80.7 11.6 %collective-permute-start.5 = (f32[10,8,1024]{2,1,0:T(8,128)}, f32[10,8,1024]{2,1,0:T(8,128)S(1)}, u32[]{:S(2)}, u32[]{:S(2)}) collective-permute-start(f32[10,8,1024]{2,1,0:T(8,128)} %collective-permute-done.4), channel_id=1, source_target_pairs={{0,8},{8,16},{16,24},{24,32},{32,40},{40,48},{48,56},{56,64},{64,7... | collective-permute-start | bytes 983048 | tf_op jit(solution)/shard_map/ppermute | solution.py:23
  82.7 11.6 %collective-permute-start.1 = (f32[10,8,1024]{2,1,0:T(8,128)}, f32[10,8,1024]{2,1,0:T(8,128)S(1)}, u32[]{:S(2)}, u32[]{:S(2)}) collective-permute-start(f32[10,8,1024]{2,1,0:T(8,128)} %collective-permute-done), channel_id=1, source_target_pairs={{0,120},{8,0},{16,8},{24,16},{32,24},{40,32},{48,40},{56,48},{64,5... | collective-permute-start | bytes 983048 | tf_op jit(solution)/shard_map/ppermute | solution.py:23
  92.3 10.5 %collective-permute-start.6 = (f32[10,8,1024]{2,1,0:T(8,128)S(1)}, f32[10,8,1024]{2,1,0:T(8,128)S(1)}, u32[]{:S(2)}, u32[]{:S(2)}) collective-permute-start(f32[10,8,1024]{2,1,0:T(8,128)S(1)} %collective-permute-done.5), channel_id=1, source_target_pairs={{0,8},{8,16},{16,24},{24,32},{32,40},{40,48},{48,56},{56,64},{64,7... | collective-permute-start | bytes 983048 | tf_op jit(solution)/shard_map/ppermute | solution.py:23
  94.3 10.5 %collective-permute-start.2 = (f32[10,8,1024]{2,1,0:T(8,128)S(1)}, f32[10,8,1024]{2,1,0:T(8,128)S(1)}, u32[]{:S(2)}, u32[]{:S(2)}) collective-permute-start(f32[10,8,1024]{2,1,0:T(8,128)S(1)} %collective-permute-done.1), channel_id=1, source_target_pairs={{0,120},{8,0},{16,8},{24,16},{32,24},{40,32},{48,40},{56,48},{64,5... | collective-permute-start | bytes 983048 | tf_op jit(solution)/shard_map/ppermute | solution.py:23
  102.8 9.5 %collective-permute-start.7 = (f32[10,8,1024]{2,1,0:T(8,128)S(1)}, f32[10,8,1024]{2,1,0:T(8,128)S(1)}, u32[]{:S(2)}, u32[]{:S(2)}) collective-permute-start(f32[10,8,1024]{2,1,0:T(8,128)S(1)} %collective-permute-done.6), channel_id=1, source_target_pairs={{0,8},{8,16},{16,24},{24,32},{32,40},{40,48},{48,56},{56,64},{64,7... | collective-permute-start | bytes 983048 | tf_op jit(solution)/shard_map/ppermute | solution.py:23
  126.0 62.1 %all-to-all-start.2 = ((f32[16,32,128]{2,1,0:T(8,128)}), f32[16,32,128]{2,1,0:T(8,128)S(1)}, u32[]{:S(2)}, u32[]{:S(2)}) async-start(f32[16,32,128]{2,1,0:T(8,128)} %bitcast.42), calls=%async_computation.2 | async-start | bytes 524288 | tf_op jit(solution)/shard_map/all_to_all | solution.py:111
  137.8 18.6 %collective-permute-start.10 = (f32[10,8,1024]{2,1,0:T(8,128)}, f32[10,8,1024]{2,1,0:T(8,128)S(1)}, u32[]{:S(2)}, u32[]{:S(2)}) collective-permute-start(f32[10,8,1024]{2,1,0:T(8,128)} %collective-permute-done.9), channel_id=1, source_target_pairs={{0,120},{8,0},{16,8},{24,16},{32,24},{40,32},{48,40},{56,48},{64,5... | collective-permute-start | bytes 983048 | tf_op jit(solution)/shard_map/ppermute | solution.py:23
  142.3 18.4 %collective-permute-start.12 = (f32[10,8,1024]{2,1,0:T(8,128)S(1)}, f32[10,8,1024]{2,1,0:T(8,128)S(1)}, u32[]{:S(2)}, u32[]{:S(2)}) collective-permute-start(f32[10,8,1024]{2,1,0:T(8,128)S(1)} %copy-done.14), channel_id=1, source_target_pairs={{0,8},{8,16},{16,24},{24,32},{32,40},{40,48},{48,56},{56,64},{64,7... | collective-permute-start | bytes 983048 | tf_op jit(solution)/shard_map/ppermute | solution.py:23
  156.4 16.1 %collective-permute-start.11 = (f32[10,8,1024]{2,1,0:T(8,128)S(1)}, f32[10,8,1024]{2,1,0:T(8,128)S(1)}, u32[]{:S(2)}, u32[]{:S(2)}) collective-permute-start(f32[10,8,1024]{2,1,0:T(8,128)S(1)} %collective-permute-done.10), channel_id=1, source_target_pairs={{0,120},{8,0},{16,8},{24,16},{32,24},{40,32},{48,40},{56,48},{64,5... | collective-permute-start | bytes 983048 | tf_op jit(solution)/shard_map/ppermute | solution.py:23
  160.6 9.9 %collective-permute-start.13 = (f32[10,8,1024]{2,1,0:T(8,128)S(1)}, f32[10,8,1024]{2,1,0:T(8,128)S(1)}, u32[]{:S(2)}, u32[]{:S(2)}) collective-permute-start(f32[10,8,1024]{2,1,0:T(8,128)S(1)} %collective-permute-done.12), channel_id=1, source_target_pairs={{0,8},{8,16},{16,24},{24,32},{32,40},{40,48},{48,56},{56,64},{64,7... | collective-permute-start | bytes 983048 | tf_op jit(solution)/shard_map/ppermute | solution.py:23
  188.8 9.5 %collective-permute-start.15 = (f32[64,8,128]{2,1,0:T(8,128)S(1)}, f32[64,8,128]{2,1,0:T(8,128)S(1)}, u32[]{:S(2)}, u32[]{:S(2)}) collective-permute-start(f32[64,8,128]{2,1,0:T(8,128)S(1)} %select_bitcast_fusion.19), channel_id=1, source_target_pairs={{0,4},{4,0},{1,5},{5,1},{2,6},{6,2},{3,7},{7,3},{8,12},{12,8},{9,1... | collective-permute-start | bytes 786440 | tf_op jit(solution)/shard_map/ppermute | solution.py:125
  199.4 19.3 %all-to-all-start.3 = ((f32[4,64,8,128]{3,2,1,0:T(8,128)}), f32[4,64,8,128]{3,2,1,0:T(8,128)S(1)}, u32[]{:S(2)}, u32[]{:S(2)}) async-start(f32[4,64,8,128]{3,2,1,0:T(8,128)} %broadcast_in_dim.47), calls=%async_computation.3 | async-start | bytes 2097152 | tf_op jit(solution)/shard_map/all_to_all | solution.py:127
  233.6 18.6 %all-to-all-start.4 = ((f32[4,64,8,128]{3,2,1,0:T(8,128)}), f32[4,64,8,128]{3,2,1,0:T(8,128)S(1)}, u32[]{:S(2)}, u32[]{:S(2)}) async-start(f32[4,64,8,128]{3,2,1,0:T(8,128)} %broadcast_in_dim.48), calls=%async_computation.4 | async-start | bytes 2097152 | tf_op jit(solution)/shard_map/all_to_all | solution.py:127
  237.1 9.9 %collective-permute-start.23 = (f32[64,8,128]{2,1,0:T(8,128)S(1)}, f32[64,8,128]{2,1,0:T(8,128)}, u32[]{:S(2)}, u32[]{:S(2)}) collective-permute-start(f32[64,8,128]{2,1,0:T(8,128)S(1)} %reduce_sum.56), channel_id=1, source_target_pairs={{0,8},{8,0},{16,24},{24,16},{32,40},{40,32},{48,56},{56,48},{64,72... | collective-permute-start | bytes 786440 | tf_op jit(solution)/shard_map/ppermute | solution.py:131
  247.1 17.3 %collective-permute-start.24 = (f32[64,8,128]{2,1,0:T(8,128)}, f32[64,8,128]{2,1,0:T(8,128)}, u32[]{:S(2)}, u32[]{:S(2)}) collective-permute-start(f32[64,8,128]{2,1,0:T(8,128)} %collective-permute-done.23), channel_id=1, source_target_pairs={{0,4},{4,0},{1,5},{5,1},{2,6},{6,2},{3,7},{7,3},{8,12},{12,8},{9,1... | collective-permute-start | bytes 786440 | tf_op jit(solution)/shard_map/ppermute | solution.py:74
  265.5 9.9 %collective-permute-start.25 = (f32[64,8,128]{2,1,0:T(8,128)S(1)}, f32[64,8,128]{2,1,0:T(8,128)}, u32[]{:S(2)}, u32[]{:S(2)}) collective-permute-start(f32[64,8,128]{2,1,0:T(8,128)S(1)} %reduce_sum.57), channel_id=1, source_target_pairs={{0,8},{8,0},{16,24},{24,16},{32,40},{40,32},{48,56},{56,48},{64,72... | collective-permute-start | bytes 786440 | tf_op jit(solution)/shard_map/ppermute | solution.py:131
  268.6 18.2 %all-to-all-start.5 = ((f32[4,64,8,128]{3,2,1,0:T(8,128)}), f32[4,64,8,128]{3,2,1,0:T(8,128)S(1)}, u32[]{:S(2)}, u32[]{:S(2)}) async-start(f32[4,64,8,128]{3,2,1,0:T(8,128)} %broadcast_in_dim.49), calls=%async_computation.5 | async-start | bytes 2097152 | tf_op jit(solution)/shard_map/all_to_all | solution.py:127
  275.4 14.8 %collective-permute-start.26 = (f32[64,8,128]{2,1,0:T(8,128)}, f32[64,8,128]{2,1,0:T(8,128)}, u32[]{:S(2)}, u32[]{:S(2)}) collective-permute-start(f32[64,8,128]{2,1,0:T(8,128)} %collective-permute-done.25), channel_id=1, source_target_pairs={{0,4},{4,0},{1,5},{5,1},{2,6},{6,2},{3,7},{7,3},{8,12},{12,8},{9,1... | collective-permute-start | bytes 786440 | tf_op jit(solution)/shard_map/ppermute | solution.py:74
  304.1 17.9 %all-to-all-start.6 = ((f32[4,64,8,128]{3,2,1,0:T(8,128)}), f32[4,64,8,128]{3,2,1,0:T(8,128)S(1)}, u32[]{:S(2)}, u32[]{:S(2)}) async-start(f32[4,64,8,128]{3,2,1,0:T(8,128)} %broadcast_in_dim.50), calls=%async_computation.6 | async-start | bytes 2097152 | tf_op jit(solution)/shard_map/all_to_all | solution.py:127
  327.7 9.8 %collective-permute-start.29 = (f32[64,8,128]{2,1,0:T(8,128)S(1)}, f32[64,8,128]{2,1,0:T(8,128)S(1)}, u32[]{:S(2)}, u32[]{:S(2)}) collective-permute-start(f32[64,8,128]{2,1,0:T(8,128)S(1)} %reduce_sum.59), channel_id=1, source_target_pairs={{0,8},{8,0},{16,24},{24,16},{32,40},{40,32},{48,56},{56,48},{64,72... | collective-permute-start | bytes 786440 | tf_op jit(solution)/shard_map/ppermute | solution.py:131
  (34 other events, 404.1 us)

commit v6 on v3

v6 whole, which is shorter than its diff:
```python
import jax
import jax.numpy as jnp
from jax import lax
from jax.sharding import Mesh, PartitionSpec as P

ROWS = ("x", "z", "core")
SWAP = [(0, 1), (1, 0)]


def product(left, right, contract=((1,), (0,))):
    return lax.dot_general(
        left,
        right,
        (contract, ((), ())),
        precision=lax.Precision.HIGHEST,
        preferred_element_type=jnp.float32,
    )


def shift(block, axis, hop):
    n = lax.axis_size(axis)
    return lax.ppermute(block, axis, [(i, (i - hop) % n) for i in range(n)])


def around(block):
    near = jnp.stack([block] + [shift(block, "x", hop) for hop in range(1, lax.axis_size("x"))])
    return jnp.stack([near, lax.ppermute(near, "core", SWAP)])


def redistribute(targets, send_order, send_count, recv_slot):
    groups = lax.axis_size(ROWS)
    arrived = lax.all_to_all(targets, "rhs", split_axis=1, concat_axis=0, tiled=True)
    rows_local, columns = arrived.shape
    capacity, tag = 4, 64
    counts = send_count[0]
    dest = jnp.arange(groups, dtype=jnp.int32)
    starts = jnp.sum(jnp.where(dest[None, :] < dest[:, None], counts[None, :], 0), axis=1)
    index = jnp.arange(rows_local, dtype=jnp.int32)
    position = jnp.sum(jnp.where(send_order[:, None] == index[None, :], index[:, None], 0), axis=0)
    slot_number = jnp.arange(capacity, dtype=jnp.int32)
    listed = starts[None, :] + slot_number[:, None]
    listed = jnp.where(slot_number[:, None] < counts[None, :], listed, -1)
    picked = (listed[:, :, None] == position[None, None, :]).astype(jnp.float32)
    picked = picked.reshape(capacity * groups, rows_local)
    landing = jnp.broadcast_to((recv_slot + 1).astype(jnp.float32)[:, None], (rows_local, 2 * tag))
    planes = product(picked, jnp.concatenate([arrived, landing], axis=1))
    planes = planes.reshape(capacity, groups, columns + 2 * tag)
    halves = [
        jnp.concatenate(
            [
                planes[s, :, :columns],
                planes[s + 1, :, :columns],
                planes[s, :, columns : columns + tag],
                planes[s + 1, :, columns : columns + tag],
            ],
            axis=1,
        )
        for s in range(0, capacity, 2)
    ]
    incoming = lax.all_to_all(
        jnp.stack(halves, axis=1), ROWS, split_axis=0, concat_axis=0, tiled=True
    )
    total = 0.0
    for h in range(capacity // 2):
        half = incoming[:, h]
        for s in range(2):
            label = half[:, 2 * columns + s * tag : 2 * columns + s * tag + 1] - 1.0
            placed = (label.astype(jnp.int32) == index[None, :]).astype(jnp.float32)
            rows = half[:, s * columns : (s + 1) * columns]
            total = total + product(placed, rows, ((0,), (0,)))
    return total


def shards(targets, send_order, send_count, recv_slot, panel, inv_diag):
    sections, width, share = inv_diag.shape
    nx, nz, nc = (lax.axis_size(a) for a in ROWS)
    xi, zi, ci = (lax.axis_index(a) for a in ROWS)
    first = ci == 0
    square = sections * share
    part = nx * nc * share

    lane = jnp.arange(width, dtype=jnp.int32)
    inner = nc * share
    moved = (lane // inner % nz) * part + lane // (nz * inner) * inner + lane % inner
    order = (moved[:, None] == lane[None, :]).astype(jnp.float32)

    names = [(j, k) for j in range(sections) for k in range(j + 1)]
    inverse_columns = jnp.swapaxes(inv_diag, 1, 2)
    own = jnp.concatenate(
        [
            inverse_columns[k]
            if j == k
            else panel[j * share : (j + 1) * share, k * width : (k + 1) * width]
            for j, k in names
        ],
        axis=0,
    )
    own = product(own, order).reshape(len(names), share, width)
    gathered = around(own)
    weight = {name: gathered[:, :, i].reshape(part, width) for i, name in enumerate(names)}

    residual = redistribute(targets, send_order, send_count, recv_slot)
    rows, columns = residual.shape
    slim = columns // (nx * nc)
    tops = residual[:square].reshape(square, nx * nc, slim).transpose(1, 0, 2)
    tops = lax.all_to_all(tops, ("x", "core"), split_axis=0, concat_axis=0, tiled=True)
    tops = tops.reshape(nx, nc, square, slim)
    tops = lax.dynamic_slice_in_dim(jnp.concatenate([tops, tops[:-1]], axis=0), xi, nx, 0)
    tops = jnp.stack(
        [
            jnp.where(first, tops[:, 0], tops[:, 1]),
            jnp.where(first, tops[:, 1], tops[:, 0]),
        ]
    )
    pending = [
        tops[:, :, k * share : (k + 1) * share].reshape(part, slim) for k in range(sections)
    ]

    mine = zi * part + xi * inner + ci * share + jnp.arange(share, dtype=jnp.int32)
    pick = (mine[:, None] == lane[None, :]).astype(jnp.float32)
    below = residual[square:]
    finished = []
    half = slim // 2
    for k in range(sections):
        fold = jnp.concatenate(
            [
                product(pending[k][:, h : h + half], weight[(k, k)], ((0,), (0,))).reshape(
                    half, nz, part
                )
                for h in (0, half)
            ],
            axis=2,
        ).transpose(1, 0, 2)
        fold = lax.all_to_all(fold, "z", split_axis=0, concat_axis=0, tiled=True)
        fold = jnp.broadcast_to(jnp.sum(fold, axis=0)[None], fold.shape)
        fold = lax.all_to_all(fold, "z", split_axis=0, concat_axis=0, tiled=True)
        solved = jnp.concatenate(
            [fold[:, :, i * part : (i + 1) * part].transpose(1, 0, 2) for i in range(2)], axis=0
        ).reshape(slim, width)
        for j in range(k + 1, sections):
            pending[j] = pending[j] - product(weight[(j, k)], solved, ((1,), (1,)))
        every = around(solved)
        every = jnp.stack(
            [jnp.where(first, every[0], every[1]), jnp.where(first, every[1], every[0])], axis=1
        )
        every = jnp.concatenate([every, every[:-1]], axis=0)
        every = lax.dynamic_slice_in_dim(every, (nx - xi) % nx, nx, 0).reshape(columns, width)
        factor = product(panel[square:, k * width : (k + 1) * width], order)
        found = product(jnp.concatenate([pick, factor], axis=0), every, ((1,), (1,)))
        finished.append(found[:share])
        below = below - found[share:]
    return jnp.concatenate(finished + [below], axis=0)


def solution(mesh):
    ny = mesh.shape["rhs"]
    split = Mesh(mesh.devices.reshape(4, 16, 2, ny), ROWS + ("rhs",))
    placed = (
        P(ROWS + ("rhs",), None),
        P(ROWS),
        P(ROWS, None),
        P(ROWS),
        P(ROWS, None),
        P(None, None, ROWS),
    )
    return jax.shard_map(
        shards, mesh=split, in_specs=placed, out_specs=P(ROWS, "rhs"), check_vma=False
    )
```

time: 303 us -> 332 us (1.096)
  starting transfers between devices: 84.8 us -> 164 us
  blocking collectives: 36 us -> 0 us
  waiting for transfers between devices: 112 us -> 76.7 us
  matrix products: 27 us -> 43.5 us
  between operations: 14.1 us -> 1.03 us
  other arithmetic: 6.71 us -> 18.1 us
  local copies, waits for them, and re-layouts: 20.1 us -> 26.3 us
    all_to_all x3 -> x9, starting transfers between devices: 11.1 us -> 74.5 us  [the longest x8 68.9 us: shards(): fold = lax.all_to_all(fold, 'z', split_axis=0, concat_axis=0, tiled=True)]
    all_to_all x1, waiting for transfers between devices: 43.7 us -> 0.01 us  [redistribute(): lax.all_to_all(jnp.stack(halves, axis=1), ROWS, split_axis=0, concat_axis...]
    all_to_all x2 -> x0, blocking collectives: 36 us -> none  [shards(): lax.all_to_all(copies, 'x', split_axis=0, concat_axis=0, tiled=True)]
    all_gather x2 -> x0, waiting for transfers between devices: 20.7 us -> none  [shards(): gathered = lax.all_gather(jnp.stack([tile(j, k) for j, k in names]), 'z')]
    dot_general x23 -> x28, matrix products: 27 us -> 43.5 us  [product(): lax.dot_general(left, right, (contract, ((), ())), precision=lax.Precisio...]
    ppermute x12 -> x20, waiting for transfers between devices: 19.2 us -> 35.3 us  [the longest x15 35.3 us: shift(): return lax.ppermute(block, axis, [(i, (i - hop) % n) for i in range(n)])]
    ppermute x12 -> x20, starting transfers between devices: 47.6 us -> 63 us  [the longest x15 42.1 us: shift(): return lax.ppermute(block, axis, [(i, (i - hop) % n) for i in range(n)])]
    all_to_all x3 -> x9, waiting for transfers between devices: 25 us -> 40.4 us  [the longest x8 37.2 us: shards(): fold = lax.all_to_all(fold, 'z', split_axis=0, concat_axis=0, tiled=True)]
  transfers between devices with their start and end apart: 19 -> 31, of which waited for: 13 -> 16; matrix products, arithmetic and copies ran while one was open for 12% -> 20% of each run, Pallas kernels for 0% -> 0%
where the time goes in v6:
time: 332 us; the launch traced here: 329 us
  starting transfers between devices  164 us (49%)
  waiting for transfers between devices  76.7 us (23%)
  matrix products  43.5 us (13%)
  local copies, waits for them, and re-layouts  26.3 us (8%)
  other arithmetic  18.1 us (5%)
    all_to_all x8, starting transfers between devices, shards(): fold = lax.all_to_all(fold, 'z', split_axis=0, concat_axis=0, tiled=True)  68.9 us
    dot_general x28, matrix products, product(): lax.dot_general(left, right, (contract, ((), ())), precision=lax.Precisio...  43.5 us
    ppermute x15, starting transfers between devices, shift(): return lax.ppermute(block, axis, [(i, (i - hop) % n) for i in range(n)])  42.1 us
    all_to_all x8, waiting for transfers between devices, shards(): fold = lax.all_to_all(fold, 'z', split_axis=0, concat_axis=0, tiled=True)  37.2 us
    ppermute x15, waiting for transfers between devices, shift(): return lax.ppermute(block, axis, [(i, (i - hop) % n) for i in range(n)])  35.3 us
    all_to_all x1, starting transfers between devices, redistribute(): lax.all_to_all(jnp.stack(halves, axis=1), ROWS, split_axis=0, concat_axis...  21 us
    ppermute x5, starting transfers between devices, around(): return jnp.stack([near, lax.ppermute(near, 'core', SWAP)])  20.9 us
    unnamed x51, local copies, waits for them, and re-layouts  10.2 us
  transfers between devices with their start and end apart: 31, of which 16 were waited for; matrix products, arithmetic and copies ran while one was open for 20% of the time, Pallas kernels for 0%

profile of v6, /device:TPU:1, one launch (start us, length us, event | category | flops | bytes accessed | tf_op | source)
XLA Modules:
  0.0 329.2 jit_solution(15559127691603516054)
XLA Ops:
  1.7 5.0 %all-to-all-start = ((f32[64,4,256]{2,0,1:T(8,128)}), f32[64,4,256]{2,0,1:T(8,128)S(1)}, u32[]{:S(2)}, u32[]{:S(2)}) async-start(f32[64,4,256]{2,0,1:T(8,128)} %bitcast.224), calls=%async_computation | async-start | bytes 524288 | tf_op jit(solution)/shard_map/all_to_all | solution.py:32
  14.5 21.0 %all-to-all-start.1 = ((f32[128,2,640]{2,1,0:T(2,128)}), f32[128,2,640]{2,1,0:T(2,128)S(1)}, u32[]{:S(2)}, u32[]{:S(2)}) async-start(f32[128,2,640]{2,1,0:T(2,128)} %copy.68), calls=%async_computation.1 | async-start | bytes 1310720 | tf_op jit(solution)/shard_map/all_to_all | solution.py:60
  41.1 5.0 %collective-permute-start = (f32[10,8,1024]{2,1,0:T(8,128)S(1)}, f32[10,8,1024]{2,1,0:T(8,128)S(1)}, u32[]{:S(2)}, u32[]{:S(2)}) collective-permute-start(f32[10,8,1024]{2,1,0:T(8,128)S(1)} %bitcast.280), channel_id=1, source_target_pairs={{0,384},{128,0},{256,128},{384,256},{1,385},{129,1},{257,129},{385... | collective-permute-start | bytes 983048 | tf_op jit(solution)/shard_map/ppermute | solution.py:22
  50.9 13.0 %collective-permute-done = f32[10,8,1024]{2,1,0:T(8,128)S(1)} collective-permute-done((f32[10,8,1024]{2,1,0:T(8,128)S(1)}, f32[10,8,1024]{2,1,0:T(8,128)S(1)}, u32[]{:S(2)}, u32[]{:S(2)}) %collective-permute-start) | collective-permute-done | bytes 327712 | tf_op jit(solution)/shard_map/ppermute | solution.py:22
  64.0 6.2 %collective-permute-done.2 = f32[10,8,1024]{2,1,0:T(8,128)S(1)} collective-permute-done((f32[10,8,1024]{2,1,0:T(8,128)S(1)}, f32[10,8,1024]{2,1,0:T(8,128)S(1)}, u32[]{:S(2)}, u32[]{:S(2)}) %collective-permute-start.2) | collective-permute-done | bytes 327712 | tf_op jit(solution)/shard_map/ppermute | solution.py:22
  78.1 5.6 %all-to-all-start.2 = ((f32[8,1,1024]{2,1,0:T(1,128)}), f32[8,1,1024]{2,1,0:T(1,128)S(1)}, u32[]{:S(2)}, u32[]{:S(2)}) async-start(f32[8,1,1024]{2,1,0:T(1,128)} %reshape.239), calls=%async_computation.2 | async-start | bytes 65536 | tf_op jit(solution)/shard_map/all_to_all | solution.py:106
  94.0 8.6 %all-to-all-start.3 = ((f32[16,16,128]{2,1,0:T(8,128)}), f32[16,16,128]{2,1,0:T(8,128)S(1)}, u32[]{:S(2)}, u32[]{:S(2)}) async-start(f32[16,16,128]{2,1,0:T(8,128)} %maximum_bitcast_fusion.4), calls=%async_computation.3 | async-start | bytes 262144 | tf_op jit(solution)/shard_map/all_to_all | solution.py:134
  103.1 11.4 %all-to-all-done.3 = f32[16,16,128]{2,1,0:T(8,128)S(1)} async-done(((f32[16,16,128]{2,1,0:T(8,128)}), f32[16,16,128]{2,1,0:T(8,128)S(1)}, u32[]{:S(2)}, u32[]{:S(2)}) %all-to-all-start.3) | async-done | bytes 131104 | tf_op jit(solution)/shard_map/all_to_all | solution.py:134
  115.2 5.9 %all-to-all-start.4 = ((f32[16,16,128]{2,1,0:T(8,128)}), f32[16,16,128]{2,1,0:T(8,128)S(1)}, u32[]{:S(2)}, u32[]{:S(2)}) async-start(f32[16,16,128]{2,1,0:T(8,128)} %broadcast_in_dim.44), calls=%async_computation.4 | async-start | bytes 262144 | tf_op jit(solution)/shard_map/all_to_all | solution.py:136
  121.1 4.3 %fusion.13 = f32[224,1024]{1,0:T(8,128)} fusion(s32[1024]{0:T(1024)S(1)} %fusion.97, f32[256,4096]{1,0:T(8,128)} %param.10), kind=kOutput, calls=%fused_computation.52 | convolution fusion | flops 2819620864 | bytes 1839104 | tf_op jit(solution)/shard_map/dot_general | solution.py:11
  125.5 4.2 %fusion.12 = f32[224,1024]{1,0:T(8,128)} fusion(s32[1024]{0:T(1024)S(1)} %fusion.97, f32[256,4096]{1,0:T(8,128)} %param.10), kind=kOutput, calls=%fused_computation.51 | convolution fusion | flops 2819620864 | bytes 1839104 | tf_op jit(solution)/shard_map/dot_general | solution.py:11
  138.3 9.1 %all-to-all-start.5 = ((f32[16,16,128]{2,1,0:T(8,128)}), f32[16,16,128]{2,1,0:T(8,128)S(1)}, u32[]{:S(2)}, u32[]{:S(2)}) async-start(f32[16,16,128]{2,1,0:T(8,128)} %maximum_bitcast_fusion.5), calls=%async_computation.5 | async-start | bytes 262144 | tf_op jit(solution)/shard_map/all_to_all | solution.py:134
  147.4 4.3 %fusion.11 = f32[224,1024]{1,0:T(8,128)} fusion(s32[1024]{0:T(1024)} %copy-done.14, f32[256,4096]{1,0:T(8,128)} %param.10), kind=kOutput, calls=%fused_computation.50 | convolution fusion | flops 2819620864 | bytes 1839104 | tf_op jit(solution)/shard_map/dot_general | solution.py:11
  151.6 4.3 %fusion.10 = f32[224,1024]{1,0:T(8,128)} fusion(s32[1024]{0:T(1024)S(1)} %copy-done.15, f32[256,4096]{1,0:T(8,128)} %param.10), kind=kOutput, calls=%fused_computation.49 | convolution fusion | flops 2819620864 | bytes 1839104 | tf_op jit(solution)/shard_map/dot_general | solution.py:11
  160.1 8.1 %all-to-all-start.6 = ((f32[16,16,128]{2,1,0:T(8,128)}), f32[16,16,128]{2,1,0:T(8,128)}, u32[]{:S(2)}, u32[]{:S(2)}) async-start(f32[16,16,128]{2,1,0:T(8,128)} %broadcast_in_dim.45), calls=%async_computation.6 | async-start | bytes 262144 | tf_op jit(solution)/shard_map/all_to_all | solution.py:136
  187.6 5.6 %collective-permute-start.7 = (f32[4,32,1024]{2,1,0:T(8,128)S(1)}, f32[4,32,1024]{2,1,0:T(8,128)S(1)}, u32[]{:S(2)}, u32[]{:S(2)}) collective-permute-start(f32[4,32,1024]{2,1,0:T(8,128)S(1)} %pad_maximum_fusion.10), channel_id=1, source_target_pairs={{0,4},{4,0},{1,5},{5,1},{2,6},{6,2},{3,7},{7,3},{8,12},{12,8},{9,1... | collective-permute-start | bytes 1572872 | tf_op jit(solution)/shard_map/ppermute | solution.py:27
  199.1 11.7 %all-to-all-start.7 = ((f32[16,16,128]{2,1,0:T(8,128)}), f32[16,16,128]{2,1,0:T(8,128)S(1)}, u32[]{:S(2)}, u32[]{:S(2)}) async-start(f32[16,16,128]{2,1,0:T(8,128)} %maximum_bitcast_fusion.6), calls=%async_computation.7 | async-start | bytes 262144 | tf_op jit(solution)/shard_map/all_to_all | solution.py:134
  212.6 10.7 %all-to-all-done.7 = f32[16,16,128]{2,1,0:T(8,128)S(1)} async-done(((f32[16,16,128]{2,1,0:T(8,128)}), f32[16,16,128]{2,1,0:T(8,128)S(1)}, u32[]{:S(2)}, u32[]{:S(2)}) %all-to-all-start.7) | async-done | bytes 131104 | tf_op jit(solution)/shard_map/all_to_all | solution.py:134
  224.0 6.2 %all-to-all-start.8 = ((f32[16,16,128]{2,1,0:T(8,128)}), f32[16,16,128]{2,1,0:T(8,128)S(1)}, u32[]{:S(2)}, u32[]{:S(2)}) async-start(f32[16,16,128]{2,1,0:T(8,128)} %broadcast_in_dim.46), calls=%async_computation.8 | async-start | bytes 262144 | tf_op jit(solution)/shard_map/all_to_all | solution.py:136
  253.4 11.7 %all-to-all-start.9 = ((f32[16,16,128]{2,1,0:T(8,128)}), f32[16,16,128]{2,1,0:T(8,128)S(1)}, u32[]{:S(2)}, u32[]{:S(2)}) async-start(f32[16,16,128]{2,1,0:T(8,128)} %maximum_bitcast_fusion.7), calls=%async_computation.9 | async-start | bytes 262144 | tf_op jit(solution)/shard_map/all_to_all | solution.py:134
  278.3 7.6 %all-to-all-start.10 = ((f32[16,16,128]{2,1,0:T(8,128)}), f32[16,16,128]{2,1,0:T(8,128)S(1)}, u32[]{:S(2)}, u32[]{:S(2)}) async-start(f32[16,16,128]{2,1,0:T(8,128)} %broadcast_in_dim.47), calls=%async_computation.10 | async-start | bytes 262144 | tf_op jit(solution)/shard_map/all_to_all | solution.py:136
  292.5 5.4 %all-to-all-done.10 = f32[16,16,128]{2,1,0:T(8,128)S(1)} async-done(((f32[16,16,128]{2,1,0:T(8,128)}), f32[16,16,128]{2,1,0:T(8,128)S(1)}, u32[]{:S(2)}, u32[]{:S(2)}) %all-to-all-start.10) | async-done | bytes 131104 | tf_op jit(solution)/shard_map/all_to_all | solution.py:136
  310.5 4.8 %collective-permute-done.18 = f32[32,1024]{1,0:T(8,128)} collective-permute-done((f32[32,1024]{1,0:T(8,128)}, f32[32,1024]{1,0:T(8,128)}, u32[]{:S(2)}, u32[]{:S(2)}) %collective-permute-start.18) | collective-permute-done | bytes 131104 | tf_op jit(solution)/shard_map/ppermute | solution.py:22
  316.4 6.1 %collective-permute-start.19 = (f32[4,32,1024]{2,1,0:T(8,128)S(1)}, f32[4,32,1024]{2,1,0:T(8,128)S(1)}, u32[]{:S(2)}, u32[]{:S(2)}) collective-permute-start(f32[4,32,1024]{2,1,0:T(8,128)S(1)} %pad_maximum_fusion.13), channel_id=1, source_target_pairs={{0,4},{4,0},{1,5},{5,1},{2,6},{6,2},{3,7},{7,3},{8,12},{12,8},{9,1... | collective-permute-start | bytes 1572872 | tf_op jit(solution)/shard_map/ppermute | solution.py:27
  (202 shorter events, 142.2 us)
Async XLA Ops:
  1.7 10.5 %all-to-all-start = ((f32[64,4,256]{2,0,1:T(8,128)}), f32[64,4,256]{2,0,1:T(8,128)S(1)}, u32[]{:S(2)}, u32[]{:S(2)}) async-start(f32[64,4,256]{2,0,1:T(8,128)} %bitcast.224), calls=%async_computation | async-start | bytes 524288 | tf_op jit(solution)/shard_map/all_to_all | solution.py:32
  14.5 59.5 %all-to-all-start.1 = ((f32[128,2,640]{2,1,0:T(2,128)}), f32[128,2,640]{2,1,0:T(2,128)S(1)}, u32[]{:S(2)}, u32[]{:S(2)}) async-start(f32[128,2,640]{2,1,0:T(2,128)} %copy.68), calls=%async_computation.1 | async-start | bytes 1310720 | tf_op jit(solution)/shard_map/all_to_all | solution.py:60
  41.1 22.8 %collective-permute-start = (f32[10,8,1024]{2,1,0:T(8,128)S(1)}, f32[10,8,1024]{2,1,0:T(8,128)S(1)}, u32[]{:S(2)}, u32[]{:S(2)}) collective-permute-start(f32[10,8,1024]{2,1,0:T(8,128)S(1)} %bitcast.280), channel_id=1, source_target_pairs={{0,384},{128,0},{256,128},{384,256},{1,385},{129,1},{257,129},{385... | collective-permute-start | bytes 983048 | tf_op jit(solution)/shard_map/ppermute | solution.py:22
  46.2 17.8 %collective-permute-start.1 = (f32[10,8,1024]{2,1,0:T(8,128)S(1)}, f32[10,8,1024]{2,1,0:T(8,128)S(1)}, u32[]{:S(2)}, u32[]{:S(2)}) collective-permute-start(f32[10,8,1024]{2,1,0:T(8,128)S(1)} %bitcast.281), channel_id=1, source_target_pairs={{0,256},{128,384},{256,0},{384,128},{1,257},{129,385},{257,1},{385... | collective-permute-start | bytes 983048 | tf_op jit(solution)/shard_map/ppermute | solution.py:22
  48.2 21.9 %collective-permute-start.2 = (f32[10,8,1024]{2,1,0:T(8,128)S(1)}, f32[10,8,1024]{2,1,0:T(8,128)S(1)}, u32[]{:S(2)}, u32[]{:S(2)}) collective-permute-start(f32[10,8,1024]{2,1,0:T(8,128)S(1)} %bitcast.282), channel_id=1, source_target_pairs={{0,128},{128,256},{256,384},{384,0},{1,129},{129,257},{257,385},{3... | collective-permute-start | bytes 983048 | tf_op jit(solution)/shard_map/ppermute | solution.py:22
  71.6 12.1 %collective-permute-start.3 = (f32[4,10,8,1024]{3,2,1,0:T(8,128)}, f32[4,10,8,1024]{3,2,1,0:T(8,128)S(1)}, u32[]{:S(2)}, u32[]{:S(2)}) collective-permute-start(f32[4,10,8,1024]{3,2,1,0:T(8,128)} %get-tuple-element.18), channel_id=1, source_target_pairs={{0,4},{4,0},{1,5},{5,1},{2,6},{6,2},{3,7},{7,3},{8,12},{12,8},{9,1... | collective-permute-start | bytes 3932168 | tf_op jit(solution)/shard_map/ppermute | solution.py:27
  78.1 10.4 %all-to-all-start.2 = ((f32[8,1,1024]{2,1,0:T(1,128)}), f32[8,1,1024]{2,1,0:T(1,128)S(1)}, u32[]{:S(2)}, u32[]{:S(2)}) async-start(f32[8,1,1024]{2,1,0:T(1,128)} %reshape.239), calls=%async_computation.2 | async-start | bytes 65536 | tf_op jit(solution)/shard_map/all_to_all | solution.py:106
  94.0 20.6 %all-to-all-start.3 = ((f32[16,16,128]{2,1,0:T(8,128)}), f32[16,16,128]{2,1,0:T(8,128)S(1)}, u32[]{:S(2)}, u32[]{:S(2)}) async-start(f32[16,16,128]{2,1,0:T(8,128)} %maximum_bitcast_fusion.4), calls=%async_computation.3 | async-start | bytes 262144 | tf_op jit(solution)/shard_map/all_to_all | solution.py:134
  115.2 17.9 %all-to-all-start.4 = ((f32[16,16,128]{2,1,0:T(8,128)}), f32[16,16,128]{2,1,0:T(8,128)S(1)}, u32[]{:S(2)}, u32[]{:S(2)}) async-start(f32[16,16,128]{2,1,0:T(8,128)} %broadcast_in_dim.44), calls=%async_computation.4 | async-start | bytes 262144 | tf_op jit(solution)/shard_map/all_to_all | solution.py:136
  138.3 21.1 %all-to-all-start.5 = ((f32[16,16,128]{2,1,0:T(8,128)}), f32[16,16,128]{2,1,0:T(8,128)S(1)}, u32[]{:S(2)}, u32[]{:S(2)}) async-start(f32[16,16,128]{2,1,0:T(8,128)} %maximum_bitcast_fusion.5), calls=%async_computation.5 | async-start | bytes 262144 | tf_op jit(solution)/shard_map/all_to_all | solution.py:134
  160.1 33.1 %all-to-all-start.6 = ((f32[16,16,128]{2,1,0:T(8,128)}), f32[16,16,128]{2,1,0:T(8,128)}, u32[]{:S(2)}, u32[]{:S(2)}) async-start(f32[16,16,128]{2,1,0:T(8,128)} %broadcast_in_dim.45), calls=%async_computation.6 | async-start | bytes 262144 | tf_op jit(solution)/shard_map/all_to_all | solution.py:136
  173.6 9.8 %collective-permute-start.4 = (f32[32,1024]{1,0:T(8,128)S(1)}, f32[32,1024]{1,0:T(8,128)S(1)}, u32[]{:S(2)}, u32[]{:S(2)}) collective-permute-start(f32[32,1024]{1,0:T(8,128)S(1)} %reshape.215), channel_id=1, source_target_pairs={{0,384},{128,0},{256,128},{384,256},{1,385},{129,1},{257,129},{385... | collective-permute-start | bytes 393224 | tf_op jit(solution)/shard_map/ppermute | solution.py:22
  187.6 23.6 %collective-permute-start.7 = (f32[4,32,1024]{2,1,0:T(8,128)S(1)}, f32[4,32,1024]{2,1,0:T(8,128)S(1)}, u32[]{:S(2)}, u32[]{:S(2)}) collective-permute-start(f32[4,32,1024]{2,1,0:T(8,128)S(1)} %pad_maximum_fusion.10), channel_id=1, source_target_pairs={{0,4},{4,0},{1,5},{5,1},{2,6},{6,2},{3,7},{7,3},{8,12},{12,8},{9,1... | collective-permute-start | bytes 1572872 | tf_op jit(solution)/shard_map/ppermute | solution.py:27
  199.1 24.1 %all-to-all-start.7 = ((f32[16,16,128]{2,1,0:T(8,128)}), f32[16,16,128]{2,1,0:T(8,128)S(1)}, u32[]{:S(2)}, u32[]{:S(2)}) async-start(f32[16,16,128]{2,1,0:T(8,128)} %maximum_bitcast_fusion.6), calls=%async_computation.7 | async-start | bytes 262144 | tf_op jit(solution)/shard_map/all_to_all | solution.py:134
  224.0 25.2 %all-to-all-start.8 = ((f32[16,16,128]{2,1,0:T(8,128)}), f32[16,16,128]{2,1,0:T(8,128)S(1)}, u32[]{:S(2)}, u32[]{:S(2)}) async-start(f32[16,16,128]{2,1,0:T(8,128)} %broadcast_in_dim.46), calls=%async_computation.8 | async-start | bytes 262144 | tf_op jit(solution)/shard_map/all_to_all | solution.py:136
  236.8 9.1 %collective-permute-start.10 = (f32[32,1024]{1,0:T(8,128)S(1)}, f32[32,1024]{1,0:T(8,128)S(1)}, u32[]{:S(2)}, u32[]{:S(2)}) collective-permute-start(f32[32,1024]{1,0:T(8,128)S(1)} %reshape.218), channel_id=1, source_target_pairs={{0,128},{128,256},{256,384},{384,0},{1,129},{129,257},{257,385},{3... | collective-permute-start | bytes 393224 | tf_op jit(solution)/shard_map/ppermute | solution.py:22
  246.0 19.8 %collective-permute-start.11 = (f32[4,32,1024]{2,1,0:T(8,128)S(1)}, f32[4,32,1024]{2,1,0:T(8,128)S(1)}, u32[]{:S(2)}, u32[]{:S(2)}) collective-permute-start(f32[4,32,1024]{2,1,0:T(8,128)S(1)} %pad_maximum_fusion.11), channel_id=1, source_target_pairs={{0,4},{4,0},{1,5},{5,1},{2,6},{6,2},{3,7},{7,3},{8,12},{12,8},{9,1... | collective-permute-start | bytes 1572872 | tf_op jit(solution)/shard_map/ppermute | solution.py:27
  253.4 24.2 %all-to-all-start.9 = ((f32[16,16,128]{2,1,0:T(8,128)}), f32[16,16,128]{2,1,0:T(8,128)S(1)}, u32[]{:S(2)}, u32[]{:S(2)}) async-start(f32[16,16,128]{2,1,0:T(8,128)} %maximum_bitcast_fusion.7), calls=%async_computation.9 | async-start | bytes 262144 | tf_op jit(solution)/shard_map/all_to_all | solution.py:134
  266.2 22.1 %collective-permute-start.12 = (f32[32,1024]{1,0:T(8,128)S(1)}, f32[32,1024]{1,0:T(8,128)S(1)}, u32[]{:S(2)}, u32[]{:S(2)}) collective-permute-start(f32[32,1024]{1,0:T(8,128)S(1)} %reshape.221), channel_id=1, source_target_pairs={{0,384},{128,0},{256,128},{384,256},{1,385},{129,1},{257,129},{385... | collective-permute-start | bytes 393224 | tf_op jit(solution)/shard_map/ppermute | solution.py:22
  269.4 19.0 %collective-permute-start.13 = (f32[32,1024]{1,0:T(8,128)S(1)}, f32[32,1024]{1,0:T(8,128)S(1)}, u32[]{:S(2)}, u32[]{:S(2)}) collective-permute-start(f32[32,1024]{1,0:T(8,128)S(1)} %reshape.221), channel_id=1, source_target_pairs={{0,256},{128,384},{256,0},{384,128},{1,257},{129,385},{257,1},{385... | collective-permute-start | bytes 393224 | tf_op jit(solution)/shard_map/ppermute | solution.py:22
  271.3 17.0 %collective-permute-start.14 = (f32[32,1024]{1,0:T(8,128)S(1)}, f32[32,1024]{1,0:T(8,128)S(1)}, u32[]{:S(2)}, u32[]{:S(2)}) collective-permute-start(f32[32,1024]{1,0:T(8,128)S(1)} %reshape.221), channel_id=1, source_target_pairs={{0,128},{128,256},{256,384},{384,0},{1,129},{129,257},{257,385},{3... | collective-permute-start | bytes 393224 | tf_op jit(solution)/shard_map/ppermute | solution.py:22
  278.3 19.6 %all-to-all-start.10 = ((f32[16,16,128]{2,1,0:T(8,128)}), f32[16,16,128]{2,1,0:T(8,128)S(1)}, u32[]{:S(2)}, u32[]{:S(2)}) async-start(f32[16,16,128]{2,1,0:T(8,128)} %broadcast_in_dim.47), calls=%async_computation.10 | async-start | bytes 262144 | tf_op jit(solution)/shard_map/all_to_all | solution.py:136
  288.4 20.5 %collective-permute-start.15 = (f32[4,32,1024]{2,1,0:T(8,128)S(1)}, f32[4,32,1024]{2,1,0:T(8,128)S(1)}, u32[]{:S(2)}, u32[]{:S(2)}) collective-permute-start(f32[4,32,1024]{2,1,0:T(8,128)S(1)} %pad_maximum_fusion.12), channel_id=1, source_target_pairs={{0,4},{4,0},{1,5},{5,1},{2,6},{6,2},{3,7},{7,3},{8,12},{12,8},{9,1... | collective-permute-start | bytes 1572872 | tf_op jit(solution)/shard_map/ppermute | solution.py:27
  299.0 10.1 %collective-permute-start.16 = (f32[32,1024]{1,0:T(8,128)}, f32[32,1024]{1,0:T(8,128)S(1)}, u32[]{:S(2)}, u32[]{:S(2)}) collective-permute-start(f32[32,1024]{1,0:T(8,128)} %reshape.224), channel_id=1, source_target_pairs={{0,384},{128,0},{256,128},{384,256},{1,385},{129,1},{257,129},{385... | collective-permute-start | bytes 393224 | tf_op jit(solution)/shard_map/ppermute | solution.py:22
  (24 other events, 368.4 us)

commit v7 on v3

--- a/solution.py
+++ b/solution.py
@@ -1,6 +1,7 @@
 import jax
 import jax.numpy as jnp
 from jax import lax
+from jax.experimental import pallas as pl
 from jax.sharding import Mesh, PartitionSpec as P
 
 ROWS = ("x", "z", "core")
@@ -15,6 +16,29 @@
         precision=lax.Precision.HIGHEST,
         preferred_element_type=jnp.float32,
     )
+
+
+def pack_tiles(panel, inverse_columns, batches):
+    sections, share, width = inverse_columns.shape
+
+    def kernel(panel_ref, inverse_ref, *out_refs):
+        for out_ref, names in zip(out_refs, batches):
+            for i, (j, k) in enumerate(names):
+                if j == k:
+                    out_ref[i] = inverse_ref[k]
+                else:
+                    out_ref[i] = panel_ref[j * share : (j + 1) * share, k * width : (k + 1) * width]
+
+    return pl.pallas_call(
+        kernel,
+        grid=(1,),
+        out_shape=[jax.ShapeDtypeStruct((len(b), share, width), jnp.float32) for b in batches],
+        in_specs=[
+            pl.BlockSpec((sections * share, (sections - 1) * width), lambda i: (0, 0)),
+            pl.BlockSpec((sections, share, width), lambda i: (0, 0, 0)),
+        ],
+        out_specs=[pl.BlockSpec((len(b), share, width), lambda i: (0, 0, 0)) for b in batches],
+    )(panel, inverse_columns)
 
 
 def redistribute(targets, send_order, send_count, recv_slot):
@@ -61,6 +85,12 @@
     return total
 
 
+def whole_block(mine, first):
+    other = lax.ppermute(mine, "core", SWAP)
+    both = jnp.stack([jnp.where(first, mine, other), jnp.where(first, other, mine)], axis=1)
+    return both.reshape(2 * mine.shape[0] * mine.shape[1], mine.shape[2])
+
+
 def shards(targets, send_order, send_count, recv_slot, panel, inv_diag):
     sections, block_rows, share = inv_diag.shape
     nx, nz, nc = (lax.axis_size(a) for a in ROWS)
@@ -70,18 +100,14 @@
     square = sections * share
     inverse_columns = jnp.swapaxes(inv_diag, 1, 2)
 
-    def tile(j, k):
-        if j == k:
-            return inverse_columns[k]
-        return panel[j * share : (j + 1) * share, k * block_rows : (k + 1) * block_rows]
-
     weight = {}
-    early = [(0, 0), (1, 0)]
-    late = [(j, k) for j in range(sections) for k in range(j + 1) if (j, k) not in early]
-    for names in (early, late):
-        gathered = lax.all_gather(jnp.stack([tile(j, k) for j, k in names]), "z")
-        for i, name in enumerate(names):
-            weight[name] = gathered[:, i].reshape(nz * share, block_rows)
+    names = [(j, k) for j in range(sections) for k in range(j + 1)]
+    batches = names[:6], names[6:]
+    soon, late = (
+        lax.all_gather(tiles, "z") for tiles in pack_tiles(panel, inverse_columns, batches)
+    )
+    for i, name in enumerate(names[:6]):
+        weight[name] = soon[:, i].reshape(nz * share, block_rows)
 
     residual = redistribute(targets, send_order, send_count, recv_slot)
     columns = residual.shape[1] // 2
@@ -94,7 +120,7 @@
     left, right = residual[square:, :columns], residual[square:, columns:]
     below = [jnp.where(even, left, right), jnp.where(even, right, left)]
     start = ((lax.axis_index("x") * nz + zi) * nc + lax.axis_index("core")) * share
-    finished = []
+    finished, blocks = [], []
     for k in range(sections):
         partial = product(weight[(k, k)], pending[k], ((0,), (0,)))
         partial = partial.reshape(nx * nz, nc, share, columns)
@@ -103,12 +129,21 @@
         half = keep + lax.ppermute(give, "core", SWAP)
         copies = jnp.broadcast_to(half[None], (nx,) + half.shape)
         mine = jnp.sum(lax.all_to_all(copies, "x", split_axis=0, concat_axis=0, tiled=True), axis=0)
-        other = lax.ppermute(mine, "core", SWAP)
-        solved = jnp.stack([jnp.where(first, mine, other), jnp.where(first, other, mine)], axis=1)
-        solved = solved.reshape(block_rows, columns)
-        for j in range(k + 1, sections):
+        solved = whole_block(mine, first)
+        blocks.append(solved)
+        if k + 2 == sections:
+            late = lax.optimization_barrier((mine, late))[1]
+            for i, name in enumerate(names[6:]):
+                weight[name] = late[:, i].reshape(nz * share, block_rows)
+            for i, block in enumerate(blocks):
+                pending[-1] = pending[-1] - product(weight[(sections - 1, i)], block)
+        for j in range(k + 1, sections - 1):
             pending[j] = pending[j] - product(weight[(j, k)], solved)
-        traded = lax.ppermute(solved, "z", [(i, i ^ 1) for i in range(nz)])
+        trade = [(i, i ^ 1) for i in range(nz)]
+        if k + 1 < sections:
+            traded = lax.ppermute(solved, "z", trade)
+        else:
+            traded = whole_block(lax.ppermute(mine, "z", trade), first)
         factor = panel[square:, k * block_rows : (k + 1) * block_rows]
         pieces = []
         for h, block in enumerate((solved, traded)):

time: 303 us -> 292 us (0.964)
  blocking collectives: 36 us -> 104 us
  waiting for transfers between devices: 112 us -> 69.2 us
  starting transfers between devices: 84.8 us -> 57.3 us
  local copies, waits for them, and re-layouts: 20.1 us -> 13.8 us
  other arithmetic: 6.71 us -> 2.43 us
    all_to_all x0 -> x1, blocking collectives: none -> 67.3 us  [redistribute(): lax.all_to_all(jnp.stack(halves, axis=1), ROWS, split_axis=0, concat_axis...]
    all_to_all x1 -> x0, waiting for transfers between devices: 43.7 us -> none  [redistribute(): lax.all_to_all(jnp.stack(halves, axis=1), ROWS, split_axis=0, concat_axis...]
    all_to_all x1 -> x0, starting transfers between devices: 21 us -> none  [redistribute(): lax.all_to_all(jnp.stack(halves, axis=1), ROWS, split_axis=0, concat_axis...]
    all_to_all x1, waiting for transfers between devices: 12.3 us -> 0.01 us  [shards(): tops = lax.all_to_all(tops, 'z', split_axis=0, concat_axis=0, tiled=True)]
    ppermute x8 -> x9, waiting for transfers between devices: 15.6 us -> 27.6 us  [the longest x3 19.5 us: shards(): traded = lax.ppermute(solved, 'z', trade)]
    all_gather x2, waiting for transfers between devices: 20.7 us -> 28.5 us  [shards(): lax.all_gather(tiles, 'z')]
    all_to_all x2, waiting for transfers between devices: 12.7 us -> 5.97 us  [shards(): lax.all_to_all(copies, 'x', split_axis=0, concat_axis=0, tiled=True)]
    ppermute x4, starting transfers between devices: 22.1 us -> 15.6 us  [shards(): half = keep + lax.ppermute(give, 'core', SWAP)]
  transfers between devices with their start and end apart: 19 -> 19, of which waited for: 13 -> 11; matrix products, arithmetic and copies ran while one was open for 12% -> 13% of each run, Pallas kernels for 0% -> 1%
where the time goes in v7:
time: 292 us; the launch traced here: 290 us
  blocking collectives  104 us (36%)
  waiting for transfers between devices  69.2 us (24%)
  starting transfers between devices  57.3 us (20%)
  matrix products  27.6 us (9%)
  between operations  14.2 us (5%)
  local copies, waits for them, and re-layouts  13.8 us (5%)
    all_to_all x1, blocking collectives, redistribute(): lax.all_to_all(jnp.stack(halves, axis=1), ROWS, split_axis=0, concat_axis...  67.3 us
    all_to_all x2, blocking collectives, shards(): lax.all_to_all(copies, 'x', split_axis=0, concat_axis=0, tiled=True)  36.4 us
    all_gather x2, waiting for transfers between devices, shards(): lax.all_gather(tiles, 'z')  28.5 us
    dot_general x23, matrix products, product(): lax.dot_general(left, right, (contract, ((), ())), precision=lax.Precisio...  27.6 us
    ppermute x3, waiting for transfers between devices, shards(): traded = lax.ppermute(solved, 'z', trade)  19.5 us
    ppermute x5, starting transfers between devices, whole_block(): other = lax.ppermute(mine, 'core', SWAP)  16 us
    ppermute x4, starting transfers between devices, shards(): half = keep + lax.ppermute(give, 'core', SWAP)  15.6 us
    ppermute x3, starting transfers between devices, shards(): traded = lax.ppermute(solved, 'z', trade)  7.36 us
  transfers between devices with their start and end apart: 19, of which 11 were waited for; matrix products, arithmetic and copies ran while one was open for 13% of the time, Pallas kernels for 1%

profile of v7, /device:TPU:1, one launch (start us, length us, event | category | flops | bytes accessed | tf_op | source)
XLA Modules:
  0.0 290.1 jit_solution(11161751692169517539)
XLA Ops:
  8.3 5.0 %all-to-all-start = ((f32[64,4,256]{2,0,1:T(8,128)}), f32[64,4,256]{2,0,1:T(8,128)S(1)}, u32[]{:S(2)}, u32[]{:S(2)}) async-start(f32[64,4,256]{2,0,1:T(8,128)} %bitcast.216), calls=%async_computation | async-start | bytes 524288 | tf_op jit(solution)/shard_map/all_to_all | solution.py:46
  15.4 3.4 %all-to-all-done = f32[64,4,256]{2,0,1:T(8,128)S(1)} async-done(((f32[64,4,256]{2,0,1:T(8,128)}), f32[64,4,256]{2,0,1:T(8,128)S(1)}, u32[]{:S(2)}, u32[]{:S(2)}) %all-to-all-start) | async-done | bytes 262176 | tf_op jit(solution)/shard_map/all_to_all | solution.py:46
  20.3 67.3 %all_to_all.49 = f32[128,2,640]{2,1,0:T(2,128)S(1)} all-to-all(f32[128,2,640]{2,1,0:T(2,128)S(1)} %copy.115), channel_id=1, replica_groups=mesh['x'=4,'z'=16,'core'=2,'rhs'=4] {'x','z','core'}, dimensions={0} | all-to-all | bytes 1310720 | tf_op jit(solution)/shard_map/all_to_all | solution.py:74
  90.9 3.5 %all-to-all-start.2 = ((f32[16,32,128]{2,1,0:T(8,128)}), f32[16,32,128]{2,1,0:T(8,128)S(1)}, u32[]{:S(2)}, u32[]{:S(2)}) async-start(f32[16,32,128]{2,1,0:T(8,128)} %bitcast.22), calls=%async_computation.2 | async-start | bytes 524288 | tf_op jit(solution)/shard_map/all_to_all | solution.py:116
  94.5 28.5 %all-gather.5.cloned.1.call-done = f32[96,8,1024]{2,1,0:T(8,128)} async-done(((f32[6,8,1024]{2,1,0:T(8,128)}), f32[96,8,1024]{2,1,0:T(8,128)}) %all-gather.5.cloned.1.call-update) | async-done | bytes 3145744 | tf_op jit(solution)/shard_map/all_gather | solution.py:107
  125.3 8.5 %collective-permute-start = (f32[64,8,128]{2,1,0:T(8,128)S(1)}, f32[64,8,128]{2,1,0:T(8,128)S(1)}, u32[]{:S(2)}, u32[]{:S(2)}) collective-permute-start(f32[64,8,128]{2,1,0:T(8,128)S(1)} %select_bitcast_fusion.13), channel_id=1, source_target_pairs={{0,4},{4,0},{1,5},{5,1},{2,6},{6,2},{3,7},{7,3},{8,12},{12,8},{9,1... | collective-permute-start | bytes 786440 | tf_op jit(solution)/shard_map/ppermute | solution.py:129
  135.1 19.1 %all_to_all.50 = f32[4,64,8,128]{3,2,1,0:T(8,128)S(1)} all-to-all(f32[4,64,8,128]{3,2,1,0:T(8,128)S(1)} %broadcast_in_dim.47), channel_id=1, replica_groups=mesh['x'=4,'z'=16,'core'=2,'rhs'=4] {'x'}, dimensions={0} | all-to-all | bytes 2097152 | tf_op jit(solution)/shard_map/all_to_all | solution.py:131
  154.3 3.7 %collective-permute-start.1 = (f32[64,8,128]{2,1,0:T(8,128)S(1)}, f32[64,8,128]{2,1,0:T(8,128)S(1)}, u32[]{:S(2)}, u32[]{:S(2)}) collective-permute-start(f32[64,8,128]{2,1,0:T(8,128)S(1)} %reduce_sum.56), channel_id=1, source_target_pairs={{0,4},{4,0},{1,5},{5,1},{2,6},{6,2},{3,7},{7,3},{8,12},{12,8},{9,1... | collective-permute-start | bytes 786440 | tf_op jit(solution)/shard_map/ppermute | solution.py:89
  161.6 2.3 collective-permute-start.2
  165.2 17.3 %all_to_all.51 = f32[4,64,8,128]{3,2,1,0:T(8,128)S(1)} all-to-all(f32[4,64,8,128]{3,2,1,0:T(8,128)S(1)} %broadcast_in_dim.48), channel_id=1, replica_groups=mesh['x'=4,'z'=16,'core'=2,'rhs'=4] {'x'}, dimensions={0} | all-to-all | bytes 2097152 | tf_op jit(solution)/shard_map/all_to_all | solution.py:131
  182.5 3.1 %collective-permute-start.3 = (f32[64,8,128]{2,1,0:T(8,128)S(1)}, f32[64,8,128]{2,1,0:T(8,128)S(1)}, u32[]{:S(2)}, u32[]{:S(2)}) collective-permute-start(f32[64,8,128]{2,1,0:T(8,128)S(1)} %reduce_sum.57), channel_id=1, source_target_pairs={{0,4},{4,0},{1,5},{5,1},{2,6},{6,2},{3,7},{7,3},{8,12},{12,8},{9,1... | collective-permute-start | bytes 786440 | tf_op jit(solution)/shard_map/ppermute | solution.py:89
  194.5 3.5 %all-to-all-start.5 = ((f32[4,64,8,128]{3,2,1,0:T(8,128)}), f32[4,64,8,128]{3,2,1,0:T(8,128)S(1)}, u32[]{:S(2)}, u32[]{:S(2)}) async-start(f32[4,64,8,128]{3,2,1,0:T(8,128)} %broadcast_in_dim.49), calls=%async_computation.5 | async-start | bytes 2097152 | tf_op jit(solution)/shard_map/all_to_all | solution.py:131
  202.6 18.0 %collective-permute-done.8 = f32[1024,128]{1,0:T(8,128)S(1)} collective-permute-done((f32[1024,128]{1,0:T(8,128)S(1)}, f32[1024,128]{1,0:T(8,128)S(1)}, u32[]{:S(2)}, u32[]{:S(2)}) %collective-permute-start.8) | collective-permute-done | bytes 524320 | tf_op jit(solution)/shard_map/ppermute | solution.py:144
  221.2 2.4 collective-permute-start.9
  224.3 2.6 collective-permute-start.5
  234.1 2.7 collective-permute-start.6
  238.8 3.1 %collective-permute-start.10 = (f32[1024,128]{1,0:T(8,128)S(1)}, f32[1024,128]{1,0:T(8,128)S(1)}, u32[]{:S(2)}, u32[]{:S(2)}) collective-permute-start(f32[1024,128]{1,0:T(8,128)S(1)} %bitcast.229), channel_id=1, source_target_pairs={{0,8},{8,0},{16,24},{24,16},{32,40},{40,32},{48,56},{56,48},{64,72... | collective-permute-start | bytes 1572872 | tf_op jit(solution)/shard_map/ppermute | solution.py:144
  243.0 3.5 %all-to-all-start.6 = ((f32[4,64,8,128]{3,2,1,0:T(8,128)}), f32[4,64,8,128]{3,2,1,0:T(8,128)S(1)}, u32[]{:S(2)}, u32[]{:S(2)}) async-start(f32[4,64,8,128]{3,2,1,0:T(8,128)} %broadcast_in_dim.50), calls=%async_computation.6 | async-start | bytes 2097152 | tf_op jit(solution)/shard_map/all_to_all | solution.py:131
  246.6 2.2 convolution_bitcast_fusion.2
  254.9 6.0 %all-to-all-done.6 = f32[4,64,8,128]{3,2,1,0:T(8,128)S(1)} async-done(((f32[4,64,8,128]{3,2,1,0:T(8,128)}), f32[4,64,8,128]{3,2,1,0:T(8,128)S(1)}, u32[]{:S(2)}, u32[]{:S(2)}) %all-to-all-start.6) | async-done | bytes 1048608 | tf_op jit(solution)/shard_map/all_to_all | solution.py:131
  260.9 3.9 %collective-permute-start.7 = (f32[64,8,128]{2,1,0:T(8,128)S(1)}, f32[64,8,128]{2,1,0:T(8,128)S(1)}, u32[]{:S(2)}, u32[]{:S(2)}) collective-permute-start(f32[64,8,128]{2,1,0:T(8,128)S(1)} %reduce_sum.59), channel_id=1, source_target_pairs={{0,4},{4,0},{1,5},{5,1},{2,6},{6,2},{3,7},{7,3},{8,12},{12,8},{9,1... | collective-permute-start | bytes 786440 | tf_op jit(solution)/shard_map/ppermute | solution.py:89
  266.9 2.7 collective-permute-start.11
  269.8 6.9 %collective-permute-done.11 = f32[64,8,128]{2,1,0:T(8,128)S(1)} collective-permute-done((f32[64,8,128]{2,1,0:T(8,128)S(1)}, f32[64,8,128]{2,1,0:T(8,128)S(1)}, u32[]{:S(2)}, u32[]{:S(2)}) %collective-permute-start.11) | collective-permute-done | bytes 262176 | tf_op jit(solution)/shard_map/ppermute | solution.py:146
  276.7 2.7 collective-permute-start.12
  (129 shorter events, 53.9 us)
Async XLA Ops:
  8.3 10.5 %all-to-all-start = ((f32[64,4,256]{2,0,1:T(8,128)}), f32[64,4,256]{2,0,1:T(8,128)S(1)}, u32[]{:S(2)}, u32[]{:S(2)}) async-start(f32[64,4,256]{2,0,1:T(8,128)} %bitcast.216), calls=%async_computation | async-start | bytes 524288 | tf_op jit(solution)/shard_map/all_to_all | solution.py:46
  13.3 109.7 %all-gather.5.cloned.1.call-start = ((), (), s32[]{:S(2)}) async-start(), calls=%async_computation.7 | async-start | bytes 3342336 | tf_op jit(solution)/shard_map/all_gather | solution.py:107
  90.9 33.8 %all-to-all-start.2 = ((f32[16,32,128]{2,1,0:T(8,128)}), f32[16,32,128]{2,1,0:T(8,128)S(1)}, u32[]{:S(2)}, u32[]{:S(2)}) async-start(f32[16,32,128]{2,1,0:T(8,128)} %bitcast.22), calls=%async_computation.2 | async-start | bytes 524288 | tf_op jit(solution)/shard_map/all_to_all | solution.py:116
  94.4 132.5 %all-gather.7.cloned.1.call-start = ((), (), s32[]{:S(2)}) async-start(), calls=%async_computation.8 | async-start | bytes 2228224 | tf_op jit(solution)/shard_map/all_gather | solution.py:107
  125.3 9.6 %collective-permute-start = (f32[64,8,128]{2,1,0:T(8,128)S(1)}, f32[64,8,128]{2,1,0:T(8,128)S(1)}, u32[]{:S(2)}, u32[]{:S(2)}) collective-permute-start(f32[64,8,128]{2,1,0:T(8,128)S(1)} %select_bitcast_fusion.13), channel_id=1, source_target_pairs={{0,4},{4,0},{1,5},{5,1},{2,6},{6,2},{3,7},{7,3},{8,12},{12,8},{9,1... | collective-permute-start | bytes 786440 | tf_op jit(solution)/shard_map/ppermute | solution.py:129
  154.3 4.9 %collective-permute-start.1 = (f32[64,8,128]{2,1,0:T(8,128)S(1)}, f32[64,8,128]{2,1,0:T(8,128)S(1)}, u32[]{:S(2)}, u32[]{:S(2)}) collective-permute-start(f32[64,8,128]{2,1,0:T(8,128)S(1)} %reduce_sum.56), channel_id=1, source_target_pairs={{0,4},{4,0},{1,5},{5,1},{2,6},{6,2},{3,7},{7,3},{8,12},{12,8},{9,1... | collective-permute-start | bytes 786440 | tf_op jit(solution)/shard_map/ppermute | solution.py:89
  161.0 24.8 %copy-start.2 = (f32[16,32,128]{2,1,0:T(8,128)S(1)}, f32[16,32,128]{2,1,0:T(8,128)}, u32[]{:S(2)}) copy-start(f32[16,32,128]{2,1,0:T(8,128)} %copy-done.1) | copy-start | bytes 786436
  161.6 3.4 %collective-permute-start.2 = (f32[64,8,128]{2,1,0:T(8,128)S(1)}, f32[64,8,128]{2,1,0:T(8,128)S(1)}, u32[]{:S(2)}, u32[]{:S(2)}) collective-permute-start(f32[64,8,128]{2,1,0:T(8,128)S(1)} %select_bitcast_fusion.10), channel_id=1, source_target_pairs={{0,4},{4,0},{1,5},{5,1},{2,6},{6,2},{3,7},{7,3},{8,12},{12,8},{9,1... | collective-permute-start | bytes 786440 | tf_op jit(solution)/shard_map/ppermute | solution.py:129
  182.5 5.0 %collective-permute-start.3 = (f32[64,8,128]{2,1,0:T(8,128)S(1)}, f32[64,8,128]{2,1,0:T(8,128)S(1)}, u32[]{:S(2)}, u32[]{:S(2)}) collective-permute-start(f32[64,8,128]{2,1,0:T(8,128)S(1)} %reduce_sum.57), channel_id=1, source_target_pairs={{0,4},{4,0},{1,5},{5,1},{2,6},{6,2},{3,7},{7,3},{8,12},{12,8},{9,1... | collective-permute-start | bytes 786440 | tf_op jit(solution)/shard_map/ppermute | solution.py:89
  190.0 3.4 %collective-permute-start.4 = (f32[64,8,128]{2,1,0:T(8,128)S(1)}, f32[64,8,128]{2,1,0:T(8,128)S(1)}, u32[]{:S(2)}, u32[]{:S(2)}) collective-permute-start(f32[64,8,128]{2,1,0:T(8,128)S(1)} %select_bitcast_fusion.7), channel_id=1, source_target_pairs={{0,4},{4,0},{1,5},{5,1},{2,6},{6,2},{3,7},{7,3},{8,12},{12,8},{9,1... | collective-permute-start | bytes 786440 | tf_op jit(solution)/shard_map/ppermute | solution.py:129
  194.5 29.7 %all-to-all-start.5 = ((f32[4,64,8,128]{3,2,1,0:T(8,128)}), f32[4,64,8,128]{3,2,1,0:T(8,128)S(1)}, u32[]{:S(2)}, u32[]{:S(2)}) async-start(f32[4,64,8,128]{3,2,1,0:T(8,128)} %broadcast_in_dim.49), calls=%async_computation.5 | async-start | bytes 2097152 | tf_op jit(solution)/shard_map/all_to_all | solution.py:131
  198.0 22.6 %collective-permute-start.8 = (f32[1024,128]{1,0:T(8,128)S(1)}, f32[1024,128]{1,0:T(8,128)S(1)}, u32[]{:S(2)}, u32[]{:S(2)}) collective-permute-start(f32[1024,128]{1,0:T(8,128)S(1)} %bitcast.219), channel_id=1, source_target_pairs={{0,8},{8,0},{16,24},{24,16},{32,40},{40,32},{48,56},{56,48},{64,72... | collective-permute-start | bytes 1572872 | tf_op jit(solution)/shard_map/ppermute | solution.py:144
  220.6 11.1 %copy-start.3 = (f32[1024,128]{1,0:T(8,128)}, f32[1024,128]{1,0:T(8,128)S(1)}, u32[]{:S(2)}) copy-start(f32[1024,128]{1,0:T(8,128)S(1)} %collective-permute-done.8) | copy-start | bytes 1572868
  221.2 25.3 %collective-permute-start.9 = (f32[1024,128]{1,0:T(8,128)S(1)}, f32[1024,128]{1,0:T(8,128)}, u32[]{:S(2)}, u32[]{:S(2)}) collective-permute-start(f32[1024,128]{1,0:T(8,128)S(1)} %bitcast.224), channel_id=1, source_target_pairs={{0,8},{8,0},{16,24},{24,16},{32,40},{40,32},{48,56},{56,48},{64,72... | collective-permute-start | bytes 1572872 | tf_op jit(solution)/shard_map/ppermute | solution.py:144
  224.3 7.3 %collective-permute-start.5 = (f32[64,8,128]{2,1,0:T(8,128)S(1)}, f32[64,8,128]{2,1,0:T(8,128)S(1)}, u32[]{:S(2)}, u32[]{:S(2)}) collective-permute-start(f32[64,8,128]{2,1,0:T(8,128)S(1)} %reduce_sum.58), channel_id=1, source_target_pairs={{0,4},{4,0},{1,5},{5,1},{2,6},{6,2},{3,7},{7,3},{8,12},{12,8},{9,1... | collective-permute-start | bytes 786440 | tf_op jit(solution)/shard_map/ppermute | solution.py:89
  234.1 7.8 %collective-permute-start.6 = (f32[64,8,128]{2,1,0:T(8,128)S(1)}, f32[64,8,128]{2,1,0:T(8,128)S(1)}, u32[]{:S(2)}, u32[]{:S(2)}) collective-permute-start(f32[64,8,128]{2,1,0:T(8,128)S(1)} %select_bitcast_fusion.4), channel_id=1, source_target_pairs={{0,4},{4,0},{1,5},{5,1},{2,6},{6,2},{3,7},{7,3},{8,12},{12,8},{9,1... | collective-permute-start | bytes 786440 | tf_op jit(solution)/shard_map/ppermute | solution.py:129
  238.8 15.4 %collective-permute-start.10 = (f32[1024,128]{1,0:T(8,128)S(1)}, f32[1024,128]{1,0:T(8,128)S(1)}, u32[]{:S(2)}, u32[]{:S(2)}) collective-permute-start(f32[1024,128]{1,0:T(8,128)S(1)} %bitcast.229), channel_id=1, source_target_pairs={{0,8},{8,0},{16,24},{24,16},{32,40},{40,32},{48,56},{56,48},{64,72... | collective-permute-start | bytes 1572872 | tf_op jit(solution)/shard_map/ppermute | solution.py:144
  243.0 17.8 %all-to-all-start.6 = ((f32[4,64,8,128]{3,2,1,0:T(8,128)}), f32[4,64,8,128]{3,2,1,0:T(8,128)S(1)}, u32[]{:S(2)}, u32[]{:S(2)}) async-start(f32[4,64,8,128]{3,2,1,0:T(8,128)} %broadcast_in_dim.50), calls=%async_computation.6 | async-start | bytes 2097152 | tf_op jit(solution)/shard_map/all_to_all | solution.py:131
  260.9 18.5 %copy-start = (f32[256,4096]{1,0:T(8,128)S(1)}, f32[256,4096]{1,0:T(8,128)}, u32[]{:S(2)}) copy-start(f32[256,4096]{1,0:T(8,128)} %panel_ref.1) | copy-start | bytes 12582916
  260.9 8.7 %collective-permute-start.7 = (f32[64,8,128]{2,1,0:T(8,128)S(1)}, f32[64,8,128]{2,1,0:T(8,128)S(1)}, u32[]{:S(2)}, u32[]{:S(2)}) collective-permute-start(f32[64,8,128]{2,1,0:T(8,128)S(1)} %reduce_sum.59), channel_id=1, source_target_pairs={{0,4},{4,0},{1,5},{5,1},{2,6},{6,2},{3,7},{7,3},{8,12},{12,8},{9,1... | collective-permute-start | bytes 786440 | tf_op jit(solution)/shard_map/ppermute | solution.py:89
  266.9 9.8 %collective-permute-start.11 = (f32[64,8,128]{2,1,0:T(8,128)S(1)}, f32[64,8,128]{2,1,0:T(8,128)S(1)}, u32[]{:S(2)}, u32[]{:S(2)}) collective-permute-start(f32[64,8,128]{2,1,0:T(8,128)S(1)} %reduce_sum.59), channel_id=1, source_target_pairs={{0,8},{8,0},{16,24},{24,16},{32,40},{40,32},{48,56},{56,48},{64,72... | collective-permute-start | bytes 786440 | tf_op jit(solution)/shard_map/ppermute | solution.py:146
  269.7 11.9 %copy-start.5 = (f32[256,128]{1,0:T(8,128)S(1)}, f32[256,128]{1,0:T(8,128)}, u32[]{:S(2)}) copy-start(f32[256,128]{1,0:T(8,128)} %constant_dynamic-update-slice_fusion.5) | copy-start | bytes 393220
  269.7 11.9 %copy-start.4 = (f32[1024,128]{1,0:T(8,128)S(1)}, f32[1024,128]{1,0:T(8,128)}, u32[]{:S(2)}) copy-start(f32[1024,128]{1,0:T(8,128)} %copy-done.3) | copy-start | bytes 1572868
  276.7 3.8 %collective-permute-start.12 = (f32[64,8,128]{2,1,0:T(8,128)S(1)}, f32[64,8,128]{2,1,0:T(8,128)S(1)}, u32[]{:S(2)}, u32[]{:S(2)}) collective-permute-start(f32[64,8,128]{2,1,0:T(8,128)S(1)} %collective-permute-done.11), channel_id=1, source_target_pairs={{0,4},{4,0},{1,5},{5,1},{2,6},{6,2},{3,7},{7,3},{8,12},{12,8},{9,1... | collective-permute-start | bytes 786440 | tf_op jit(solution)/shard_map/ppermute | solution.py:89
  (5 other events, 45.2 us)
Sparse Core Ops, SparseCore 0:
  16.2 106.7 all-gather.4
  158.2 60.0 all-gather.6

commit v8 on v7

--- a/solution.py
+++ b/solution.py
@@ -2,6 +2,7 @@
 import jax.numpy as jnp
 from jax import lax
 from jax.experimental import pallas as pl
+from jax.experimental.pallas import tpu as pltpu
 from jax.sharding import Mesh, PartitionSpec as P
 
 ROWS = ("x", "z", "core")
@@ -18,27 +19,39 @@
     )
 
 
-def pack_tiles(panel, inverse_columns, batches):
+def pack_half(panel, inverse_columns, names):
     sections, share, width = inverse_columns.shape
+    parts = 2
+    lanes = width // parts
 
-    def kernel(panel_ref, inverse_ref, *out_refs):
-        for out_ref, names in zip(out_refs, batches):
-            for i, (j, k) in enumerate(names):
-                if j == k:
-                    out_ref[i] = inverse_ref[k]
-                else:
-                    out_ref[i] = panel_ref[j * share : (j + 1) * share, k * width : (k + 1) * width]
+    def kernel(where_ref, *refs):
+        panel_refs, inverse_ref, out_ref = refs[:-2], refs[-2], refs[-1]
+        for i, (j, k) in enumerate(names):
+            if j == k:
+                out_ref[i] = inverse_ref[k]
+            else:
+                out_ref[i] = panel_refs[k][j * share : (j + 1) * share, :]
 
+    panel_specs = [
+        pl.BlockSpec((sections * share, lanes), lambda i, where, k=k: (0, k * parts + where[0]))
+        for k in range(sections - 1)
+    ]
     return pl.pallas_call(
         kernel,
-        grid=(1,),
-        out_shape=[jax.ShapeDtypeStruct((len(b), share, width), jnp.float32) for b in batches],
-        in_specs=[
-            pl.BlockSpec((sections * share, (sections - 1) * width), lambda i: (0, 0)),
-            pl.BlockSpec((sections, share, width), lambda i: (0, 0, 0)),
-        ],
-        out_specs=[pl.BlockSpec((len(b), share, width), lambda i: (0, 0, 0)) for b in batches],
-    )(panel, inverse_columns)
+        out_shape=jax.ShapeDtypeStruct((len(names), share, lanes), jnp.float32),
+        grid_spec=pltpu.PrefetchScalarGridSpec(
+            num_scalar_prefetch=1,
+            grid=(1,),
+            in_specs=panel_specs
+            + [pl.BlockSpec((sections, share, lanes), lambda i, where: (0, 0, where[0]))],
+            out_specs=pl.BlockSpec((len(names), share, lanes), lambda i, where: (0, 0, 0)),
+        ),
+    )((lax.axis_index("rhs") % 2).astype(jnp.int32)[None], *[panel] * (sections - 1), inverse_columns)
+
+
+def join_lanes(near, far):
+    low = lax.axis_index("rhs") % 2 == 0
+    return jnp.concatenate([jnp.where(low, near, far), jnp.where(low, far, near)], axis=2)
 
 
 def redistribute(targets, send_order, send_count, recv_slot):
@@ -102,14 +115,24 @@
 
     weight = {}
     names = [(j, k) for j in range(sections) for k in range(j + 1)]
-    batches = names[:6], names[6:]
-    soon, late = (
-        lax.all_gather(tiles, "z") for tiles in pack_tiles(panel, inverse_columns, batches)
-    )
-    for i, name in enumerate(names[:6]):
-        weight[name] = soon[:, i].reshape(nz * share, block_rows)
+    some_lanes = lax.all_gather(pack_half(panel, inverse_columns, names), "z")
+    residual = redistribute(targets, send_order, send_count, recv_slot)
+    cuts = [0, 2, 5, len(names)]
+    batches, order = [], None
+    for low, high in zip(cuts, cuts[1:]):
+        near = some_lanes[:, low:high].transpose(1, 0, 2, 3)
+        near = near.reshape(high - low, nz * share, some_lanes.shape[3])
+        if order is not None:
+            order, near = lax.optimization_barrier((order, near))
+        order = [near, lax.ppermute(near, "rhs", [(i, i ^ 1) for i in range(lax.axis_size("rhs"))])]
+        batches.append(order)
 
-    residual = redistribute(targets, send_order, send_count, recv_slot)
+    def unpack(batch):
+        for name, tile in zip(names[cuts[batch] : cuts[batch + 1]], join_lanes(*batches[batch])):
+            weight[name] = tile
+
+    unpack(0)
+
     columns = residual.shape[1] // 2
     halves = jnp.stack([residual[:square, :columns], residual[:square, columns:]])
     tops = jnp.broadcast_to(halves[None], (nz // 2,) + halves.shape).reshape(nz, square, columns)
@@ -120,7 +143,7 @@
     left, right = residual[square:, :columns], residual[square:, columns:]
     below = [jnp.where(even, left, right), jnp.where(even, right, left)]
     start = ((lax.axis_index("x") * nz + zi) * nc + lax.axis_index("core")) * share
-    finished, blocks = [], []
+    finished, blocks, used = [], [], set()
     for k in range(sections):
         partial = product(weight[(k, k)], pending[k], ((0,), (0,)))
         partial = partial.reshape(nx * nz, nc, share, columns)
@@ -131,14 +154,13 @@
         mine = jnp.sum(lax.all_to_all(copies, "x", split_axis=0, concat_axis=0, tiled=True), axis=0)
         solved = whole_block(mine, first)
         blocks.append(solved)
-        if k + 2 == sections:
-            late = lax.optimization_barrier((mine, late))[1]
-            for i, name in enumerate(names[6:]):
-                weight[name] = late[:, i].reshape(nz * share, block_rows)
-            for i, block in enumerate(blocks):
-                pending[-1] = pending[-1] - product(weight[(sections - 1, i)], block)
-        for j in range(k + 1, sections - 1):
-            pending[j] = pending[j] - product(weight[(j, k)], solved)
+        if k < 2:
+            batches[k + 1] = lax.optimization_barrier((mine, batches[k + 1]))[1]
+            unpack(k + 1)
+        for j, i in sorted(weight):
+            if j > i and i <= k and (j, i) not in used:
+                pending[j] = pending[j] - product(weight[(j, i)], blocks[i])
+                used.add((j, i))
         trade = [(i, i ^ 1) for i in range(nz)]
         if k + 1 < sections:
             traded = lax.ppermute(solved, "z", trade)

time: 292 us -> 299 us (1.024)
  blocking collectives: 104 us -> 67.2 us
  starting transfers between devices: 57.3 us -> 77.8 us
  other arithmetic: 2.43 us -> 11.9 us
  local copies, waits for them, and re-layouts: 13.8 us -> 23 us
  waiting for transfers between devices: 69.2 us -> 73.5 us
    all_to_all x2 -> x0, blocking collectives: 36.4 us -> none  [shards(): lax.all_to_all(copies, 'x', split_axis=0, concat_axis=0, tiled=True)]
    ppermute x0 -> x3, waiting for transfers between devices: none -> 15.7 us  [shards(): lax.ppermute(near, 'rhs', [(i, i ^ 1) for i in range(lax.axis_size('rhs'))])]
    all_to_all x2 -> x4, waiting for transfers between devices: 5.97 us -> 20.7 us  [shards(): lax.all_to_all(copies, 'x', split_axis=0, concat_axis=0, tiled=True)]
    all_gather x2 -> x1, waiting for transfers between devices: 28.5 us -> 15.6 us  [shards(): some_lanes = lax.all_gather(pack_half(panel, inverse_columns, names), 'z')]
    ppermute x3, waiting for transfers between devices: 19.5 us -> 6.94 us  [shards(): traded = lax.ppermute(solved, 'z', trade)]
    all_to_all x2 -> x4, starting transfers between devices: 7.03 us -> 18 us  [shards(): lax.all_to_all(copies, 'x', split_axis=0, concat_axis=0, tiled=True)]
    ppermute x0 -> x3, starting transfers between devices: none -> 10.3 us  [shards(): lax.ppermute(near, 'rhs', [(i, i ^ 1) for i in range(lax.axis_size('rhs'))])]
    select_n x0 -> x3, other arithmetic: none -> 4.9 us  [join_lanes(): jnp.where(low, far, near)]
  transfers between devices with their start and end apart: 19 -> 23, of which waited for: 11 -> 10; matrix products, arithmetic and copies ran while one was open for 13% -> 18% of each run, Pallas kernels for 1% -> 0%
where the time goes in v8:
time: 299 us; the launch traced here: 297 us
  starting transfers between devices  77.8 us (26%)
  waiting for transfers between devices  73.5 us (25%)
  blocking collectives  67.2 us (22%)
  matrix products  27.9 us (9%)
  local copies, waits for them, and re-layouts  23 us (8%)
  between operations  14.3 us (5%)
  other arithmetic  11.9 us (4%)
    all_to_all x1, blocking collectives, redistribute(): lax.all_to_all(jnp.stack(halves, axis=1), ROWS, split_axis=0, concat_axis...  67.2 us
    dot_general x23, matrix products, product(): lax.dot_general(left, right, (contract, ((), ())), precision=lax.Precisio...  27.9 us
    all_to_all x4, waiting for transfers between devices, shards(): lax.all_to_all(copies, 'x', split_axis=0, concat_axis=0, tiled=True)  20.7 us
    all_to_all x4, starting transfers between devices, shards(): lax.all_to_all(copies, 'x', split_axis=0, concat_axis=0, tiled=True)  18 us
    ppermute x5, starting transfers between devices, whole_block(): other = lax.ppermute(mine, 'core', SWAP)  16.5 us
    ppermute x3, waiting for transfers between devices, shards(): lax.ppermute(near, 'rhs', [(i, i ^ 1) for i in range(lax.axis_size('rhs'))])  15.7 us
    all_gather x1, waiting for transfers between devices, shards(): some_lanes = lax.all_gather(pack_half(panel, inverse_columns, names), 'z')  15.6 us
    ppermute x4, starting transfers between devices, shards(): half = keep + lax.ppermute(give, 'core', SWAP)  15.1 us
  transfers between devices with their start and end apart: 23, of which 10 were waited for; matrix products, arithmetic and copies ran while one was open for 18% of the time, Pallas kernels for 0%

profile of v8, /device:TPU:1, one launch (start us, length us, event | category | flops | bytes accessed | tf_op | source)
XLA Modules:
  0.0 297.2 jit_solution(3080046646002067833)
XLA Ops:
  9.0 5.0 %all-to-all-start = ((f32[64,4,256]{2,0,1:T(8,128)}), f32[64,4,256]{2,0,1:T(8,128)S(1)}, u32[]{:S(2)}, u32[]{:S(2)}) async-start(f32[64,4,256]{2,0,1:T(8,128)} %bitcast.236), calls=%async_computation | async-start | bytes 524288 | tf_op jit(solution)/shard_map/all_to_all | solution.py:59
  14.2 5.3 %all-to-all-done = f32[64,4,256]{2,0,1:T(8,128)S(1)} async-done(((f32[64,4,256]{2,0,1:T(8,128)}), f32[64,4,256]{2,0,1:T(8,128)S(1)}, u32[]{:S(2)}, u32[]{:S(2)}) %all-to-all-start) | async-done | bytes 262176 | tf_op jit(solution)/shard_map/all_to_all | solution.py:59
  21.0 67.2 %all_to_all.49 = f32[128,2,640]{2,1,0:T(2,128)S(1)} all-to-all(f32[128,2,640]{2,1,0:T(2,128)S(1)} %copy.96), channel_id=1, replica_groups=mesh['x'=4,'z'=16,'core'=2,'rhs'=4] {'x','z','core'}, dimensions={0} | all-to-all | bytes 1310720 | tf_op jit(solution)/shard_map/all_to_all | solution.py:87
  92.1 3.5 %all-to-all-start.2 = ((f32[16,32,128]{2,1,0:T(8,128)}), f32[16,32,128]{2,1,0:T(8,128)S(1)}, u32[]{:S(2)}, u32[]{:S(2)}) async-start(f32[16,32,128]{2,1,0:T(8,128)} %bitcast.25), calls=%async_computation.2 | async-start | bytes 524288 | tf_op jit(solution)/shard_map/all_to_all | solution.py:139
  95.7 15.6 %all-gather.3.cloned.1.call-done = f32[160,8,512]{2,1,0:T(8,128)} async-done(((f32[10,8,512]{2,1,0:T(8,128)}), f32[160,8,512]{2,1,0:T(8,128)}) %all-gather.3.cloned.1.call-update) | async-done | bytes 2621456 | tf_op jit(solution)/shard_map/all_gather | solution.py:118
  112.3 4.0 %collective-permute-start = (f32[2,128,512]{2,1,0:T(8,128)S(1)}, f32[2,128,512]{2,1,0:T(8,128)S(1)}, u32[]{:S(2)}, u32[]{:S(2)}) collective-permute-start(f32[2,128,512]{2,1,0:T(8,128)S(1)} %copy_bitcast_fusion.2), channel_id=1, source_target_pairs={{0,1},{1,0},{2,3},{3,2},{4,5},{5,4},{6,7},{7,6},{8,9},{9,8},{10,11... | collective-permute-start | bytes 1572872 | tf_op jit(solution)/shard_map/ppermute | solution.py:127
  116.3 6.5 %collective-permute-done = f32[2,128,512]{2,1,0:T(8,128)S(1)} collective-permute-done((f32[2,128,512]{2,1,0:T(8,128)S(1)}, f32[2,128,512]{2,1,0:T(8,128)S(1)}, u32[]{:S(2)}, u32[]{:S(2)}) %collective-permute-start) | collective-permute-done | bytes 524320 | tf_op jit(solution)/shard_map/ppermute | solution.py:127
  124.9 9.2 %collective-permute-start.1 = (f32[64,8,128]{2,1,0:T(8,128)S(1)}, f32[64,8,128]{2,1,0:T(8,128)S(1)}, u32[]{:S(2)}, u32[]{:S(2)}) collective-permute-start(f32[64,8,128]{2,1,0:T(8,128)S(1)} %select_bitcast_fusion.13), channel_id=1, source_target_pairs={{0,4},{4,0},{1,5},{5,1},{2,6},{6,2},{3,7},{7,3},{8,12},{12,8},{9,1... | collective-permute-start | bytes 786440 | tf_op jit(solution)/shard_map/ppermute | solution.py:152
  135.3 3.2 %collective-permute-start.3 = (f32[3,128,512]{2,1,0:T(8,128)S(1)}, f32[3,128,512]{2,1,0:T(8,128)}, u32[]{:S(2)}, u32[]{:S(2)}) collective-permute-start(f32[3,128,512]{2,1,0:T(8,128)S(1)} %copy_bitcast_fusion.1), channel_id=1, source_target_pairs={{0,1},{1,0},{2,3},{3,2},{4,5},{5,4},{6,7},{7,6},{8,9},{9,8},{10,11... | collective-permute-start | bytes 2359304 | tf_op jit(solution)/shard_map/ppermute | solution.py:127
  139.6 5.2 %all-to-all-start.3 = ((f32[4,64,8,128]{3,2,1,0:T(8,128)}), f32[4,64,8,128]{3,2,1,0:T(8,128)S(1)}, u32[]{:S(2)}, u32[]{:S(2)}) async-start(f32[4,64,8,128]{3,2,1,0:T(8,128)} %broadcast_in_dim.50), calls=%async_computation.3 | async-start | bytes 2097152 | tf_op jit(solution)/shard_map/all_to_all | solution.py:154
  147.3 9.2 %collective-permute-done.3 = f32[3,128,512]{2,1,0:T(8,128)} collective-permute-done((f32[3,128,512]{2,1,0:T(8,128)S(1)}, f32[3,128,512]{2,1,0:T(8,128)}, u32[]{:S(2)}, u32[]{:S(2)}) %collective-permute-start.3) | collective-permute-done | bytes 786464 | tf_op jit(solution)/shard_map/ppermute | solution.py:127
  156.4 3.2 %collective-permute-start.6 = (f32[5,128,512]{2,1,0:T(8,128)}, f32[5,128,512]{2,1,0:T(8,128)}, u32[]{:S(2)}, u32[]{:S(2)}) collective-permute-start(f32[5,128,512]{2,1,0:T(8,128)} %copy_bitcast_fusion), channel_id=1, source_target_pairs={{0,1},{1,0},{2,3},{3,2},{4,5},{5,4},{6,7},{7,6},{8,9},{9,8},{10,11... | collective-permute-start | bytes 3932168 | tf_op jit(solution)/shard_map/ppermute | solution.py:127
  159.7 3.1 %collective-permute-start.2 = (f32[64,8,128]{2,1,0:T(8,128)S(1)}, f32[64,8,128]{2,1,0:T(8,128)}, u32[]{:S(2)}, u32[]{:S(2)}) collective-permute-start(f32[64,8,128]{2,1,0:T(8,128)S(1)} %reduce_sum.56), channel_id=1, source_target_pairs={{0,4},{4,0},{1,5},{5,1},{2,6},{6,2},{3,7},{7,3},{8,12},{12,8},{9,1... | collective-permute-start | bytes 786440 | tf_op jit(solution)/shard_map/ppermute | solution.py:102
  173.5 5.1 %all-to-all-start.4 = ((f32[4,64,8,128]{3,2,1,0:T(8,128)}), f32[4,64,8,128]{3,2,1,0:T(8,128)S(1)}, u32[]{:S(2)}, u32[]{:S(2)}) async-start(f32[4,64,8,128]{3,2,1,0:T(8,128)} %broadcast_in_dim.51), calls=%async_computation.4 | async-start | bytes 2097152 | tf_op jit(solution)/shard_map/all_to_all | solution.py:154
  180.0 13.3 %all-to-all-done.4 = f32[4,64,8,128]{3,2,1,0:T(8,128)S(1)} async-done(((f32[4,64,8,128]{3,2,1,0:T(8,128)}), f32[4,64,8,128]{3,2,1,0:T(8,128)S(1)}, u32[]{:S(2)}, u32[]{:S(2)}) %all-to-all-start.4) | async-done | bytes 1048608 | tf_op jit(solution)/shard_map/all_to_all | solution.py:154
  193.4 3.4 %collective-permute-start.5 = (f32[64,8,128]{2,1,0:T(8,128)S(1)}, f32[64,8,128]{2,1,0:T(8,128)}, u32[]{:S(2)}, u32[]{:S(2)}) collective-permute-start(f32[64,8,128]{2,1,0:T(8,128)S(1)} %reduce_sum.57), channel_id=1, source_target_pairs={{0,4},{4,0},{1,5},{5,1},{2,6},{6,2},{3,7},{7,3},{8,12},{12,8},{9,1... | collective-permute-start | bytes 786440 | tf_op jit(solution)/shard_map/ppermute | solution.py:102
  211.5 4.2 %all-to-all-start.5 = ((f32[4,64,8,128]{3,2,1,0:T(8,128)}), f32[4,64,8,128]{3,2,1,0:T(8,128)}, u32[]{:S(2)}, u32[]{:S(2)}) async-start(f32[4,64,8,128]{3,2,1,0:T(8,128)} %broadcast_in_dim.52), calls=%async_computation.5 | async-start | bytes 2097152 | tf_op jit(solution)/shard_map/all_to_all | solution.py:154
  218.5 5.1 %collective-permute-done.11 = f32[1024,128]{1,0:T(8,128)} collective-permute-done((f32[1024,128]{1,0:T(8,128)S(1)}, f32[1024,128]{1,0:T(8,128)}, u32[]{:S(2)}, u32[]{:S(2)}) %collective-permute-start.11) | collective-permute-done | bytes 524320 | tf_op jit(solution)/shard_map/ppermute | solution.py:166
  232.4 3.3 %collective-permute-start.8 = (f32[64,8,128]{2,1,0:T(8,128)S(1)}, f32[64,8,128]{2,1,0:T(8,128)S(1)}, u32[]{:S(2)}, u32[]{:S(2)}) collective-permute-start(f32[64,8,128]{2,1,0:T(8,128)S(1)} %reduce_sum.58), channel_id=1, source_target_pairs={{0,4},{4,0},{1,5},{5,1},{2,6},{6,2},{3,7},{7,3},{8,12},{12,8},{9,1... | collective-permute-start | bytes 786440 | tf_op jit(solution)/shard_map/ppermute | solution.py:102
  244.6 3.4 %collective-permute-start.13 = (f32[1024,128]{1,0:T(8,128)S(1)}, f32[1024,128]{1,0:T(8,128)S(1)}, u32[]{:S(2)}, u32[]{:S(2)}) collective-permute-start(f32[1024,128]{1,0:T(8,128)S(1)} %bitcast.244), channel_id=1, source_target_pairs={{0,8},{8,0},{16,24},{24,16},{32,40},{40,32},{48,56},{56,48},{64,72... | collective-permute-start | bytes 1572872 | tf_op jit(solution)/shard_map/ppermute | solution.py:166
  249.1 3.5 %all-to-all-start.6 = ((f32[4,64,8,128]{3,2,1,0:T(8,128)}), f32[4,64,8,128]{3,2,1,0:T(8,128)S(1)}, u32[]{:S(2)}, u32[]{:S(2)}) async-start(f32[4,64,8,128]{3,2,1,0:T(8,128)} %broadcast_in_dim.53), calls=%async_computation.6 | async-start | bytes 2097152 | tf_op jit(solution)/shard_map/all_to_all | solution.py:154
  259.5 7.5 %all-to-all-done.6 = f32[4,64,8,128]{3,2,1,0:T(8,128)S(1)} async-done(((f32[4,64,8,128]{3,2,1,0:T(8,128)}), f32[4,64,8,128]{3,2,1,0:T(8,128)S(1)}, u32[]{:S(2)}, u32[]{:S(2)}) %all-to-all-start.6) | async-done | bytes 1048608 | tf_op jit(solution)/shard_map/all_to_all | solution.py:154
  267.0 3.8 %collective-permute-start.10 = (f32[64,8,128]{2,1,0:T(8,128)S(1)}, f32[64,8,128]{2,1,0:T(8,128)S(1)}, u32[]{:S(2)}, u32[]{:S(2)}) collective-permute-start(f32[64,8,128]{2,1,0:T(8,128)S(1)} %reduce_sum.59), channel_id=1, source_target_pairs={{0,4},{4,0},{1,5},{5,1},{2,6},{6,2},{3,7},{7,3},{8,12},{12,8},{9,1... | collective-permute-start | bytes 786440 | tf_op jit(solution)/shard_map/ppermute | solution.py:102
  275.1 7.7 %collective-permute-done.14 = f32[64,8,128]{2,1,0:T(8,128)S(1)} collective-permute-done((f32[64,8,128]{2,1,0:T(8,128)S(1)}, f32[64,8,128]{2,1,0:T(8,128)S(1)}, u32[]{:S(2)}, u32[]{:S(2)}) %collective-permute-start.14) | collective-permute-done | bytes 262176 | tf_op jit(solution)/shard_map/ppermute | solution.py:168
  (157 shorter events, 82.7 us)
Async XLA Ops:
  6.5 104.7 %all-gather.3.cloned.1.call-start = ((), (), s32[]{:S(2)}) async-start(), calls=%async_computation.7 | async-start | bytes 2785280 | tf_op jit(solution)/shard_map/all_gather | solution.py:118
  9.0 10.5 %all-to-all-start = ((f32[64,4,256]{2,0,1:T(8,128)}), f32[64,4,256]{2,0,1:T(8,128)S(1)}, u32[]{:S(2)}, u32[]{:S(2)}) async-start(f32[64,4,256]{2,0,1:T(8,128)} %bitcast.236), calls=%async_computation | async-start | bytes 524288 | tf_op jit(solution)/shard_map/all_to_all | solution.py:59
  92.1 32.1 %all-to-all-start.2 = ((f32[16,32,128]{2,1,0:T(8,128)}), f32[16,32,128]{2,1,0:T(8,128)S(1)}, u32[]{:S(2)}, u32[]{:S(2)}) async-start(f32[16,32,128]{2,1,0:T(8,128)} %bitcast.25), calls=%async_computation.2 | async-start | bytes 524288 | tf_op jit(solution)/shard_map/all_to_all | solution.py:139
  112.3 10.5 %collective-permute-start = (f32[2,128,512]{2,1,0:T(8,128)S(1)}, f32[2,128,512]{2,1,0:T(8,128)S(1)}, u32[]{:S(2)}, u32[]{:S(2)}) collective-permute-start(f32[2,128,512]{2,1,0:T(8,128)S(1)} %copy_bitcast_fusion.2), channel_id=1, source_target_pairs={{0,1},{1,0},{2,3},{3,2},{4,5},{5,4},{6,7},{7,6},{8,9},{9,8},{10,11... | collective-permute-start | bytes 1572872 | tf_op jit(solution)/shard_map/ppermute | solution.py:127
  124.9 13.6 %collective-permute-start.1 = (f32[64,8,128]{2,1,0:T(8,128)S(1)}, f32[64,8,128]{2,1,0:T(8,128)S(1)}, u32[]{:S(2)}, u32[]{:S(2)}) collective-permute-start(f32[64,8,128]{2,1,0:T(8,128)S(1)} %select_bitcast_fusion.13), channel_id=1, source_target_pairs={{0,4},{4,0},{1,5},{5,1},{2,6},{6,2},{3,7},{7,3},{8,12},{12,8},{9,1... | collective-permute-start | bytes 786440 | tf_op jit(solution)/shard_map/ppermute | solution.py:152
  135.3 21.2 %collective-permute-start.3 = (f32[3,128,512]{2,1,0:T(8,128)S(1)}, f32[3,128,512]{2,1,0:T(8,128)}, u32[]{:S(2)}, u32[]{:S(2)}) collective-permute-start(f32[3,128,512]{2,1,0:T(8,128)S(1)} %copy_bitcast_fusion.1), channel_id=1, source_target_pairs={{0,1},{1,0},{2,3},{3,2},{4,5},{5,4},{6,7},{7,6},{8,9},{9,8},{10,11... | collective-permute-start | bytes 2359304 | tf_op jit(solution)/shard_map/ppermute | solution.py:127
  139.6 20.0 %all-to-all-start.3 = ((f32[4,64,8,128]{3,2,1,0:T(8,128)}), f32[4,64,8,128]{3,2,1,0:T(8,128)S(1)}, u32[]{:S(2)}, u32[]{:S(2)}) async-start(f32[4,64,8,128]{3,2,1,0:T(8,128)} %broadcast_in_dim.50), calls=%async_computation.3 | async-start | bytes 2097152 | tf_op jit(solution)/shard_map/all_to_all | solution.py:154
  156.4 40.4 %collective-permute-start.6 = (f32[5,128,512]{2,1,0:T(8,128)}, f32[5,128,512]{2,1,0:T(8,128)}, u32[]{:S(2)}, u32[]{:S(2)}) collective-permute-start(f32[5,128,512]{2,1,0:T(8,128)} %copy_bitcast_fusion), channel_id=1, source_target_pairs={{0,1},{1,0},{2,3},{3,2},{4,5},{5,4},{6,7},{7,6},{8,9},{9,8},{10,11... | collective-permute-start | bytes 3932168 | tf_op jit(solution)/shard_map/ppermute | solution.py:127
  159.7 6.0 %collective-permute-start.2 = (f32[64,8,128]{2,1,0:T(8,128)S(1)}, f32[64,8,128]{2,1,0:T(8,128)}, u32[]{:S(2)}, u32[]{:S(2)}) collective-permute-start(f32[64,8,128]{2,1,0:T(8,128)S(1)} %reduce_sum.56), channel_id=1, source_target_pairs={{0,4},{4,0},{1,5},{5,1},{2,6},{6,2},{3,7},{7,3},{8,12},{12,8},{9,1... | collective-permute-start | bytes 786440 | tf_op jit(solution)/shard_map/ppermute | solution.py:102
  168.9 3.4 %collective-permute-start.4 = (f32[64,8,128]{2,1,0:T(8,128)S(1)}, f32[64,8,128]{2,1,0:T(8,128)S(1)}, u32[]{:S(2)}, u32[]{:S(2)}) collective-permute-start(f32[64,8,128]{2,1,0:T(8,128)S(1)} %select_bitcast_fusion.10), channel_id=1, source_target_pairs={{0,4},{4,0},{1,5},{5,1},{2,6},{6,2},{3,7},{7,3},{8,12},{12,8},{9,1... | collective-permute-start | bytes 786440 | tf_op jit(solution)/shard_map/ppermute | solution.py:152
  173.5 19.9 %all-to-all-start.4 = ((f32[4,64,8,128]{3,2,1,0:T(8,128)}), f32[4,64,8,128]{3,2,1,0:T(8,128)S(1)}, u32[]{:S(2)}, u32[]{:S(2)}) async-start(f32[4,64,8,128]{3,2,1,0:T(8,128)} %broadcast_in_dim.51), calls=%async_computation.4 | async-start | bytes 2097152 | tf_op jit(solution)/shard_map/all_to_all | solution.py:154
  193.4 8.7 %collective-permute-start.5 = (f32[64,8,128]{2,1,0:T(8,128)S(1)}, f32[64,8,128]{2,1,0:T(8,128)}, u32[]{:S(2)}, u32[]{:S(2)}) collective-permute-start(f32[64,8,128]{2,1,0:T(8,128)S(1)} %reduce_sum.57), channel_id=1, source_target_pairs={{0,4},{4,0},{1,5},{5,1},{2,6},{6,2},{3,7},{7,3},{8,12},{12,8},{9,1... | collective-permute-start | bytes 786440 | tf_op jit(solution)/shard_map/ppermute | solution.py:102
  206.5 4.0 %collective-permute-start.7 = (f32[64,8,128]{2,1,0:T(8,128)S(1)}, f32[64,8,128]{2,1,0:T(8,128)S(1)}, u32[]{:S(2)}, u32[]{:S(2)}) collective-permute-start(f32[64,8,128]{2,1,0:T(8,128)S(1)} %select_bitcast_fusion.7), channel_id=1, source_target_pairs={{0,4},{4,0},{1,5},{5,1},{2,6},{6,2},{3,7},{7,3},{8,12},{12,8},{9,1... | collective-permute-start | bytes 786440 | tf_op jit(solution)/shard_map/ppermute | solution.py:152
  208.5 15.0 %collective-permute-start.11 = (f32[1024,128]{1,0:T(8,128)S(1)}, f32[1024,128]{1,0:T(8,128)}, u32[]{:S(2)}, u32[]{:S(2)}) collective-permute-start(f32[1024,128]{1,0:T(8,128)S(1)} %bitcast.239), channel_id=1, source_target_pairs={{0,8},{8,0},{16,24},{24,16},{32,40},{40,32},{48,56},{56,48},{64,72... | collective-permute-start | bytes 1572872 | tf_op jit(solution)/shard_map/ppermute | solution.py:166
  211.5 19.6 %all-to-all-start.5 = ((f32[4,64,8,128]{3,2,1,0:T(8,128)}), f32[4,64,8,128]{3,2,1,0:T(8,128)}, u32[]{:S(2)}, u32[]{:S(2)}) async-start(f32[4,64,8,128]{3,2,1,0:T(8,128)} %broadcast_in_dim.52), calls=%async_computation.5 | async-start | bytes 2097152 | tf_op jit(solution)/shard_map/all_to_all | solution.py:154
  229.0 23.7 %collective-permute-start.12 = (f32[1024,128]{1,0:T(8,128)}, f32[1024,128]{1,0:T(8,128)}, u32[]{:S(2)}, u32[]{:S(2)}) collective-permute-start(f32[1024,128]{1,0:T(8,128)} %bitcast.49), channel_id=1, source_target_pairs={{0,8},{8,0},{16,24},{24,16},{32,40},{40,32},{48,56},{56,48},{64,72... | collective-permute-start | bytes 1572872 | tf_op jit(solution)/shard_map/ppermute | solution.py:166
  232.4 6.2 %collective-permute-start.8 = (f32[64,8,128]{2,1,0:T(8,128)S(1)}, f32[64,8,128]{2,1,0:T(8,128)S(1)}, u32[]{:S(2)}, u32[]{:S(2)}) collective-permute-start(f32[64,8,128]{2,1,0:T(8,128)S(1)} %reduce_sum.58), channel_id=1, source_target_pairs={{0,4},{4,0},{1,5},{5,1},{2,6},{6,2},{3,7},{7,3},{8,12},{12,8},{9,1... | collective-permute-start | bytes 786440 | tf_op jit(solution)/shard_map/ppermute | solution.py:102
  240.4 7.6 %collective-permute-start.9 = (f32[64,8,128]{2,1,0:T(8,128)S(1)}, f32[64,8,128]{2,1,0:T(8,128)S(1)}, u32[]{:S(2)}, u32[]{:S(2)}) collective-permute-start(f32[64,8,128]{2,1,0:T(8,128)S(1)} %select_bitcast_fusion.4), channel_id=1, source_target_pairs={{0,4},{4,0},{1,5},{5,1},{2,6},{6,2},{3,7},{7,3},{8,12},{12,8},{9,1... | collective-permute-start | bytes 786440 | tf_op jit(solution)/shard_map/ppermute | solution.py:152
  244.6 14.9 %collective-permute-start.13 = (f32[1024,128]{1,0:T(8,128)S(1)}, f32[1024,128]{1,0:T(8,128)S(1)}, u32[]{:S(2)}, u32[]{:S(2)}) collective-permute-start(f32[1024,128]{1,0:T(8,128)S(1)} %bitcast.244), channel_id=1, source_target_pairs={{0,8},{8,0},{16,24},{24,16},{32,40},{40,32},{48,56},{56,48},{64,72... | collective-permute-start | bytes 1572872 | tf_op jit(solution)/shard_map/ppermute | solution.py:166
  249.1 17.9 %all-to-all-start.6 = ((f32[4,64,8,128]{3,2,1,0:T(8,128)}), f32[4,64,8,128]{3,2,1,0:T(8,128)S(1)}, u32[]{:S(2)}, u32[]{:S(2)}) async-start(f32[4,64,8,128]{3,2,1,0:T(8,128)} %broadcast_in_dim.53), calls=%async_computation.6 | async-start | bytes 2097152 | tf_op jit(solution)/shard_map/all_to_all | solution.py:154
  267.0 18.7 %copy-start = (f32[256,4096]{1,0:T(8,128)S(1)}, f32[256,4096]{1,0:T(8,128)}, u32[]{:S(2)}) copy-start(f32[256,4096]{1,0:T(8,128)} %refs_2_.1) | copy-start | bytes 12582916
  267.0 7.9 %collective-permute-start.10 = (f32[64,8,128]{2,1,0:T(8,128)S(1)}, f32[64,8,128]{2,1,0:T(8,128)S(1)}, u32[]{:S(2)}, u32[]{:S(2)}) collective-permute-start(f32[64,8,128]{2,1,0:T(8,128)S(1)} %reduce_sum.59), channel_id=1, source_target_pairs={{0,4},{4,0},{1,5},{5,1},{2,6},{6,2},{3,7},{7,3},{8,12},{12,8},{9,1... | collective-permute-start | bytes 786440 | tf_op jit(solution)/shard_map/ppermute | solution.py:102
  273.0 9.8 %collective-permute-start.14 = (f32[64,8,128]{2,1,0:T(8,128)S(1)}, f32[64,8,128]{2,1,0:T(8,128)S(1)}, u32[]{:S(2)}, u32[]{:S(2)}) collective-permute-start(f32[64,8,128]{2,1,0:T(8,128)S(1)} %reduce_sum.59), channel_id=1, source_target_pairs={{0,8},{8,0},{16,24},{24,16},{32,40},{40,32},{48,56},{56,48},{64,72... | collective-permute-start | bytes 786440 | tf_op jit(solution)/shard_map/ppermute | solution.py:168
  282.8 3.8 %collective-permute-start.15 = (f32[64,8,128]{2,1,0:T(8,128)S(1)}, f32[64,8,128]{2,1,0:T(8,128)S(1)}, u32[]{:S(2)}, u32[]{:S(2)}) collective-permute-start(f32[64,8,128]{2,1,0:T(8,128)S(1)} %collective-permute-done.14), channel_id=1, source_target_pairs={{0,4},{4,0},{1,5},{5,1},{2,6},{6,2},{3,7},{7,3},{8,12},{12,8},{9,1... | collective-permute-start | bytes 786440 | tf_op jit(solution)/shard_map/ppermute | solution.py:102
  (17 other events, 116.6 us)
Sparse Core Ops, SparseCore 0:
  9.4 101.7 all-gather.2

commit v9 on v7

--- a/solution.py
+++ b/solution.py
@@ -102,12 +102,10 @@
 
     weight = {}
     names = [(j, k) for j in range(sections) for k in range(j + 1)]
-    batches = names[:6], names[6:]
-    soon, late = (
-        lax.all_gather(tiles, "z") for tiles in pack_tiles(panel, inverse_columns, batches)
-    )
-    for i, name in enumerate(names[:6]):
-        weight[name] = soon[:, i].reshape(nz * share, block_rows)
+    (tiles,) = pack_tiles(panel, inverse_columns, [names])
+    gathered = lax.all_gather(tiles, "z")
+    for i, name in enumerate(names):
+        weight[name] = gathered[:, i].reshape(nz * share, block_rows)
 
     residual = redistribute(targets, send_order, send_count, recv_slot)
     columns = residual.shape[1] // 2
@@ -120,7 +118,7 @@
     left, right = residual[square:, :columns], residual[square:, columns:]
     below = [jnp.where(even, left, right), jnp.where(even, right, left)]
     start = ((lax.axis_index("x") * nz + zi) * nc + lax.axis_index("core")) * share
-    finished, blocks = [], []
+    finished = []
     for k in range(sections):
         partial = product(weight[(k, k)], pending[k], ((0,), (0,)))
         partial = partial.reshape(nx * nz, nc, share, columns)
@@ -130,14 +128,7 @@
         copies = jnp.broadcast_to(half[None], (nx,) + half.shape)
         mine = jnp.sum(lax.all_to_all(copies, "x", split_axis=0, concat_axis=0, tiled=True), axis=0)
         solved = whole_block(mine, first)
-        blocks.append(solved)
-        if k + 2 == sections:
-            late = lax.optimization_barrier((mine, late))[1]
-            for i, name in enumerate(names[6:]):
-                weight[name] = late[:, i].reshape(nz * share, block_rows)
-            for i, block in enumerate(blocks):
-                pending[-1] = pending[-1] - product(weight[(sections - 1, i)], block)
-        for j in range(k + 1, sections - 1):
+        for j in range(k + 1, sections):
             pending[j] = pending[j] - product(weight[(j, k)], solved)
         trade = [(i, i ^ 1) for i in range(nz)]
         if k + 1 < sections:

time: 292 us -> 286 us (0.979)
  local copies, waits for them, and re-layouts: 13.8 us -> 9.11 us
    ppermute x3, waiting for transfers between devices: 19.5 us -> 10.8 us  [shards(): traded = lax.ppermute(solved, 'z', trade)]
    all_gather x2 -> x1, waiting for transfers between devices: 28.5 us -> 33.8 us  [shards(): gathered = lax.all_gather(tiles, 'z')]
  transfers between devices with their start and end apart: 19 -> 18, of which waited for: 11 -> 11; matrix products, arithmetic and copies ran while one was open for 13% -> 10% of each run, Pallas kernels for 1% -> 0%
where the time goes in v9:
time: 286 us; the launch traced here: 284 us
  blocking collectives  102 us (36%)
  waiting for transfers between devices  68.9 us (24%)
  starting transfers between devices  57.8 us (20%)
  matrix products  27.6 us (10%)
  between operations  14.2 us (5%)
  local copies, waits for them, and re-layouts  9.11 us (3%)
    all_to_all x1, blocking collectives, redistribute(): lax.all_to_all(jnp.stack(halves, axis=1), ROWS, split_axis=0, concat_axis...  67.1 us
    all_to_all x2, blocking collectives, shards(): lax.all_to_all(copies, 'x', split_axis=0, concat_axis=0, tiled=True)  35.3 us
    all_gather x1, waiting for transfers between devices, shards(): gathered = lax.all_gather(tiles, 'z')  33.8 us
    dot_general x23, matrix products, product(): lax.dot_general(left, right, (contract, ((), ())), precision=lax.Precisio...  27.6 us
    ppermute x5, starting transfers between devices, whole_block(): other = lax.ppermute(mine, 'core', SWAP)  16.8 us
    ppermute x4, starting transfers between devices, shards(): half = keep + lax.ppermute(give, 'core', SWAP)  14.1 us
    ppermute x3, waiting for transfers between devices, shards(): traded = lax.ppermute(solved, 'z', trade)  10.8 us
    ppermute x3, starting transfers between devices, shards(): traded = lax.ppermute(solved, 'z', trade)  7.93 us
  transfers between devices with their start and end apart: 18, of which 11 were waited for; matrix products, arithmetic and copies ran while one was open for 10% of the time, Pallas kernels for 0%

profile of v9, /device:TPU:1, one launch (start us, length us, event | category | flops | bytes accessed | tf_op | source)
XLA Modules:
  0.0 284.3 jit_solution(16507958442786745648)
XLA Ops:
  9.2 5.0 %all-to-all-start = ((f32[64,4,256]{2,0,1:T(8,128)}), f32[64,4,256]{2,0,1:T(8,128)S(1)}, u32[]{:S(2)}, u32[]{:S(2)}) async-start(f32[64,4,256]{2,0,1:T(8,128)} %bitcast.215), calls=%async_computation | async-start | bytes 524288 | tf_op jit(solution)/shard_map/all_to_all | solution.py:46
  14.4 5.3 %all-to-all-done = f32[64,4,256]{2,0,1:T(8,128)S(1)} async-done(((f32[64,4,256]{2,0,1:T(8,128)}), f32[64,4,256]{2,0,1:T(8,128)S(1)}, u32[]{:S(2)}, u32[]{:S(2)}) %all-to-all-start) | async-done | bytes 262176 | tf_op jit(solution)/shard_map/all_to_all | solution.py:46
  21.2 67.1 %all_to_all.49 = f32[128,2,640]{2,1,0:T(2,128)S(1)} all-to-all(f32[128,2,640]{2,1,0:T(2,128)S(1)} %copy.115), channel_id=1, replica_groups=mesh['x'=4,'z'=16,'core'=2,'rhs'=4] {'x','z','core'}, dimensions={0} | all-to-all | bytes 1310720 | tf_op jit(solution)/shard_map/all_to_all | solution.py:74
  91.6 3.5 %all-to-all-start.2 = ((f32[16,32,128]{2,1,0:T(8,128)}), f32[16,32,128]{2,1,0:T(8,128)S(1)}, u32[]{:S(2)}, u32[]{:S(2)}) async-start(f32[16,32,128]{2,1,0:T(8,128)} %bitcast.22), calls=%async_computation.2 | async-start | bytes 524288 | tf_op jit(solution)/shard_map/all_to_all | solution.py:114
  95.1 33.8 %all-gather.3.cloned.1.call-done = f32[160,8,1024]{2,1,0:T(8,128)} async-done(((f32[10,8,1024]{2,1,0:T(8,128)}), f32[160,8,1024]{2,1,0:T(8,128)}) %all-gather.3.cloned.1.call-update) | async-done | bytes 5242896 | tf_op jit(solution)/shard_map/all_gather | solution.py:106
  131.4 7.8 %collective-permute-start = (f32[64,8,128]{2,1,0:T(8,128)S(1)}, f32[64,8,128]{2,1,0:T(8,128)S(1)}, u32[]{:S(2)}, u32[]{:S(2)}) collective-permute-start(f32[64,8,128]{2,1,0:T(8,128)S(1)} %select_bitcast_fusion.13), channel_id=1, source_target_pairs={{0,4},{4,0},{1,5},{5,1},{2,6},{6,2},{3,7},{7,3},{8,12},{12,8},{9,1... | collective-permute-start | bytes 786440 | tf_op jit(solution)/shard_map/ppermute | solution.py:127
  140.5 18.0 %all_to_all.50 = f32[4,64,8,128]{3,2,1,0:T(8,128)S(1)} all-to-all(f32[4,64,8,128]{3,2,1,0:T(8,128)S(1)} %broadcast_in_dim.47), channel_id=1, replica_groups=mesh['x'=4,'z'=16,'core'=2,'rhs'=4] {'x'}, dimensions={0} | all-to-all | bytes 2097152 | tf_op jit(solution)/shard_map/all_to_all | solution.py:129
  158.6 3.7 %collective-permute-start.1 = (f32[64,8,128]{2,1,0:T(8,128)S(1)}, f32[64,8,128]{2,1,0:T(8,128)S(1)}, u32[]{:S(2)}, u32[]{:S(2)}) collective-permute-start(f32[64,8,128]{2,1,0:T(8,128)S(1)} %reduce_sum.56), channel_id=1, source_target_pairs={{0,4},{4,0},{1,5},{5,1},{2,6},{6,2},{3,7},{7,3},{8,12},{12,8},{9,1... | collective-permute-start | bytes 786440 | tf_op jit(solution)/shard_map/ppermute | solution.py:89
  165.9 2.3 collective-permute-start.2
  169.4 17.3 %all_to_all.51 = f32[4,64,8,128]{3,2,1,0:T(8,128)S(1)} all-to-all(f32[4,64,8,128]{3,2,1,0:T(8,128)S(1)} %broadcast_in_dim.48), channel_id=1, replica_groups=mesh['x'=4,'z'=16,'core'=2,'rhs'=4] {'x'}, dimensions={0} | all-to-all | bytes 2097152 | tf_op jit(solution)/shard_map/all_to_all | solution.py:129
  186.8 3.1 %collective-permute-start.3 = (f32[64,8,128]{2,1,0:T(8,128)S(1)}, f32[64,8,128]{2,1,0:T(8,128)S(1)}, u32[]{:S(2)}, u32[]{:S(2)}) collective-permute-start(f32[64,8,128]{2,1,0:T(8,128)S(1)} %reduce_sum.57), channel_id=1, source_target_pairs={{0,4},{4,0},{1,5},{5,1},{2,6},{6,2},{3,7},{7,3},{8,12},{12,8},{9,1... | collective-permute-start | bytes 786440 | tf_op jit(solution)/shard_map/ppermute | solution.py:89
  198.8 3.5 %all-to-all-start.5 = ((f32[4,64,8,128]{3,2,1,0:T(8,128)}), f32[4,64,8,128]{3,2,1,0:T(8,128)S(1)}, u32[]{:S(2)}, u32[]{:S(2)}) async-start(f32[4,64,8,128]{3,2,1,0:T(8,128)} %broadcast_in_dim.49), calls=%async_computation.5 | async-start | bytes 2097152 | tf_op jit(solution)/shard_map/all_to_all | solution.py:129
  202.5 2.7 collective-permute-start.8
  209.0 8.8 %collective-permute-done.8 = f32[1024,128]{1,0:T(8,128)S(1)} collective-permute-done((f32[1024,128]{1,0:T(8,128)S(1)}, f32[1024,128]{1,0:T(8,128)S(1)}, u32[]{:S(2)}, u32[]{:S(2)}) %collective-permute-start.8) | collective-permute-done | bytes 524320 | tf_op jit(solution)/shard_map/ppermute | solution.py:135
  218.6 2.7 collective-permute-start.9
  221.4 3.1 %collective-permute-start.5 = (f32[64,8,128]{2,1,0:T(8,128)S(1)}, f32[64,8,128]{2,1,0:T(8,128)S(1)}, u32[]{:S(2)}, u32[]{:S(2)}) collective-permute-start(f32[64,8,128]{2,1,0:T(8,128)S(1)} %reduce_sum.58), channel_id=1, source_target_pairs={{0,4},{4,0},{1,5},{5,1},{2,6},{6,2},{3,7},{7,3},{8,12},{12,8},{9,1... | collective-permute-start | bytes 786440 | tf_op jit(solution)/shard_map/ppermute | solution.py:89
  232.8 2.6 collective-permute-start.10
  236.5 4.2 %all-to-all-start.6 = ((f32[4,64,8,128]{3,2,1,0:T(8,128)}), f32[4,64,8,128]{3,2,1,0:T(8,128)S(1)}, u32[]{:S(2)}, u32[]{:S(2)}) async-start(f32[4,64,8,128]{3,2,1,0:T(8,128)} %broadcast_in_dim.50), calls=%async_computation.6 | async-start | bytes 2097152 | tf_op jit(solution)/shard_map/all_to_all | solution.py:129
  240.7 2.2 convolution_bitcast_fusion.2
  247.7 7.1 %all-to-all-done.6 = f32[4,64,8,128]{3,2,1,0:T(8,128)S(1)} async-done(((f32[4,64,8,128]{3,2,1,0:T(8,128)}), f32[4,64,8,128]{3,2,1,0:T(8,128)S(1)}, u32[]{:S(2)}, u32[]{:S(2)}) %all-to-all-start.6) | async-done | bytes 1048608 | tf_op jit(solution)/shard_map/all_to_all | solution.py:129
  254.9 4.2 %collective-permute-start.7 = (f32[64,8,128]{2,1,0:T(8,128)S(1)}, f32[64,8,128]{2,1,0:T(8,128)S(1)}, u32[]{:S(2)}, u32[]{:S(2)}) collective-permute-start(f32[64,8,128]{2,1,0:T(8,128)S(1)} %reduce_sum.59), channel_id=1, source_target_pairs={{0,4},{4,0},{1,5},{5,1},{2,6},{6,2},{3,7},{7,3},{8,12},{12,8},{9,1... | collective-permute-start | bytes 786440 | tf_op jit(solution)/shard_map/ppermute | solution.py:89
  261.1 2.7 collective-permute-start.11
  264.0 7.0 %collective-permute-done.11 = f32[64,8,128]{2,1,0:T(8,128)S(1)} collective-permute-done((f32[64,8,128]{2,1,0:T(8,128)S(1)}, f32[64,8,128]{2,1,0:T(8,128)S(1)}, u32[]{:S(2)}, u32[]{:S(2)}) %collective-permute-start.11) | collective-permute-done | bytes 262176 | tf_op jit(solution)/shard_map/ppermute | solution.py:137
  270.9 2.7 collective-permute-start.12
  (123 shorter events, 49.8 us)
Async XLA Ops:
  6.5 7.8 %copy-start.6 = (s32[256]{0:T(256)S(1)}, s32[256]{0:T(256)}, u32[]{:S(2)}) copy-start(s32[256]{0:T(256)} %param.7) | copy-start | bytes 3076
  6.5 7.9 %copy-start.7 = (s32[256]{0:T(256)S(1)}, s32[256]{0:T(256)}, u32[]{:S(2)}) copy-start(s32[256]{0:T(256)} %param.9) | copy-start | bytes 3076
  6.5 122.4 %all-gather.3.cloned.1.call-start = ((), (), s32[]{:S(2)}) async-start(), calls=%async_computation.7 | async-start | bytes 5570560 | tf_op jit(solution)/shard_map/all_gather | solution.py:106
  9.2 10.5 %all-to-all-start = ((f32[64,4,256]{2,0,1:T(8,128)}), f32[64,4,256]{2,0,1:T(8,128)S(1)}, u32[]{:S(2)}, u32[]{:S(2)}) async-start(f32[64,4,256]{2,0,1:T(8,128)} %bitcast.215), calls=%async_computation | async-start | bytes 524288 | tf_op jit(solution)/shard_map/all_to_all | solution.py:46
  91.6 39.2 %all-to-all-start.2 = ((f32[16,32,128]{2,1,0:T(8,128)}), f32[16,32,128]{2,1,0:T(8,128)S(1)}, u32[]{:S(2)}, u32[]{:S(2)}) async-start(f32[16,32,128]{2,1,0:T(8,128)} %bitcast.22), calls=%async_computation.2 | async-start | bytes 524288 | tf_op jit(solution)/shard_map/all_to_all | solution.py:114
  130.8 59.3 %copy-start.1 = (f32[16,32,128]{2,1,0:T(8,128)}, f32[16,32,128]{2,1,0:T(8,128)S(1)}, u32[]{:S(2)}) copy-start(f32[16,32,128]{2,1,0:T(8,128)S(1)} %all-to-all-done.2) | copy-start | bytes 786436
  131.4 9.0 %collective-permute-start = (f32[64,8,128]{2,1,0:T(8,128)S(1)}, f32[64,8,128]{2,1,0:T(8,128)S(1)}, u32[]{:S(2)}, u32[]{:S(2)}) collective-permute-start(f32[64,8,128]{2,1,0:T(8,128)S(1)} %select_bitcast_fusion.13), channel_id=1, source_target_pairs={{0,4},{4,0},{1,5},{5,1},{2,6},{6,2},{3,7},{7,3},{8,12},{12,8},{9,1... | collective-permute-start | bytes 786440 | tf_op jit(solution)/shard_map/ppermute | solution.py:127
  158.6 4.9 %collective-permute-start.1 = (f32[64,8,128]{2,1,0:T(8,128)S(1)}, f32[64,8,128]{2,1,0:T(8,128)S(1)}, u32[]{:S(2)}, u32[]{:S(2)}) collective-permute-start(f32[64,8,128]{2,1,0:T(8,128)S(1)} %reduce_sum.56), channel_id=1, source_target_pairs={{0,4},{4,0},{1,5},{5,1},{2,6},{6,2},{3,7},{7,3},{8,12},{12,8},{9,1... | collective-permute-start | bytes 786440 | tf_op jit(solution)/shard_map/ppermute | solution.py:89
  165.9 3.4 %collective-permute-start.2 = (f32[64,8,128]{2,1,0:T(8,128)S(1)}, f32[64,8,128]{2,1,0:T(8,128)S(1)}, u32[]{:S(2)}, u32[]{:S(2)}) collective-permute-start(f32[64,8,128]{2,1,0:T(8,128)S(1)} %select_bitcast_fusion.10), channel_id=1, source_target_pairs={{0,4},{4,0},{1,5},{5,1},{2,6},{6,2},{3,7},{7,3},{8,12},{12,8},{9,1... | collective-permute-start | bytes 786440 | tf_op jit(solution)/shard_map/ppermute | solution.py:127
  186.8 5.0 %collective-permute-start.3 = (f32[64,8,128]{2,1,0:T(8,128)S(1)}, f32[64,8,128]{2,1,0:T(8,128)S(1)}, u32[]{:S(2)}, u32[]{:S(2)}) collective-permute-start(f32[64,8,128]{2,1,0:T(8,128)S(1)} %reduce_sum.57), channel_id=1, source_target_pairs={{0,4},{4,0},{1,5},{5,1},{2,6},{6,2},{3,7},{7,3},{8,12},{12,8},{9,1... | collective-permute-start | bytes 786440 | tf_op jit(solution)/shard_map/ppermute | solution.py:89
  194.2 3.4 %collective-permute-start.4 = (f32[64,8,128]{2,1,0:T(8,128)S(1)}, f32[64,8,128]{2,1,0:T(8,128)S(1)}, u32[]{:S(2)}, u32[]{:S(2)}) collective-permute-start(f32[64,8,128]{2,1,0:T(8,128)S(1)} %select_bitcast_fusion.7), channel_id=1, source_target_pairs={{0,4},{4,0},{1,5},{5,1},{2,6},{6,2},{3,7},{7,3},{8,12},{12,8},{9,1... | collective-permute-start | bytes 786440 | tf_op jit(solution)/shard_map/ppermute | solution.py:127
  198.8 22.5 %all-to-all-start.5 = ((f32[4,64,8,128]{3,2,1,0:T(8,128)}), f32[4,64,8,128]{3,2,1,0:T(8,128)S(1)}, u32[]{:S(2)}, u32[]{:S(2)}) async-start(f32[4,64,8,128]{3,2,1,0:T(8,128)} %broadcast_in_dim.49), calls=%async_computation.5 | async-start | bytes 2097152 | tf_op jit(solution)/shard_map/all_to_all | solution.py:129
  202.5 15.3 %collective-permute-start.8 = (f32[1024,128]{1,0:T(8,128)S(1)}, f32[1024,128]{1,0:T(8,128)S(1)}, u32[]{:S(2)}, u32[]{:S(2)}) collective-permute-start(f32[1024,128]{1,0:T(8,128)S(1)} %bitcast.218), channel_id=1, source_target_pairs={{0,8},{8,0},{16,24},{24,16},{32,40},{40,32},{48,56},{56,48},{64,72... | collective-permute-start | bytes 1572872 | tf_op jit(solution)/shard_map/ppermute | solution.py:135
  218.6 22.1 %collective-permute-start.9 = (f32[1024,128]{1,0:T(8,128)S(1)}, f32[1024,128]{1,0:T(8,128)}, u32[]{:S(2)}, u32[]{:S(2)}) collective-permute-start(f32[1024,128]{1,0:T(8,128)S(1)} %bitcast.223), channel_id=1, source_target_pairs={{0,8},{8,0},{16,24},{24,16},{32,40},{40,32},{48,56},{56,48},{64,72... | collective-permute-start | bytes 1572872 | tf_op jit(solution)/shard_map/ppermute | solution.py:135
  221.4 4.9 %collective-permute-start.5 = (f32[64,8,128]{2,1,0:T(8,128)S(1)}, f32[64,8,128]{2,1,0:T(8,128)S(1)}, u32[]{:S(2)}, u32[]{:S(2)}) collective-permute-start(f32[64,8,128]{2,1,0:T(8,128)S(1)} %reduce_sum.58), channel_id=1, source_target_pairs={{0,4},{4,0},{1,5},{5,1},{2,6},{6,2},{3,7},{7,3},{8,12},{12,8},{9,1... | collective-permute-start | bytes 786440 | tf_op jit(solution)/shard_map/ppermute | solution.py:89
  228.6 14.3 %copy-start.5 = (f32[256,128]{1,0:T(8,128)S(1)}, f32[256,128]{1,0:T(8,128)}, u32[]{:S(2)}) copy-start(f32[256,128]{1,0:T(8,128)} %constant_dynamic-update-slice_fusion.7) | copy-start | bytes 393220
  228.7 6.8 %collective-permute-start.6 = (f32[64,8,128]{2,1,0:T(8,128)S(1)}, f32[64,8,128]{2,1,0:T(8,128)S(1)}, u32[]{:S(2)}, u32[]{:S(2)}) collective-permute-start(f32[64,8,128]{2,1,0:T(8,128)S(1)} %select_bitcast_fusion.4), channel_id=1, source_target_pairs={{0,4},{4,0},{1,5},{5,1},{2,6},{6,2},{3,7},{7,3},{8,12},{12,8},{9,1... | collective-permute-start | bytes 786440 | tf_op jit(solution)/shard_map/ppermute | solution.py:127
  232.8 14.9 %collective-permute-start.10 = (f32[1024,128]{1,0:T(8,128)S(1)}, f32[1024,128]{1,0:T(8,128)S(1)}, u32[]{:S(2)}, u32[]{:S(2)}) collective-permute-start(f32[1024,128]{1,0:T(8,128)S(1)} %bitcast.235), channel_id=1, source_target_pairs={{0,8},{8,0},{16,24},{24,16},{32,40},{40,32},{48,56},{56,48},{64,72... | collective-permute-start | bytes 1572872 | tf_op jit(solution)/shard_map/ppermute | solution.py:135
  236.5 18.3 %all-to-all-start.6 = ((f32[4,64,8,128]{3,2,1,0:T(8,128)}), f32[4,64,8,128]{3,2,1,0:T(8,128)S(1)}, u32[]{:S(2)}, u32[]{:S(2)}) async-start(f32[4,64,8,128]{3,2,1,0:T(8,128)} %broadcast_in_dim.50), calls=%async_computation.6 | async-start | bytes 2097152 | tf_op jit(solution)/shard_map/all_to_all | solution.py:129
  254.9 18.8 %copy-start = (f32[256,4096]{1,0:T(8,128)S(1)}, f32[256,4096]{1,0:T(8,128)}, u32[]{:S(2)}) copy-start(f32[256,4096]{1,0:T(8,128)} %panel_ref.1) | copy-start | bytes 12582916
  254.9 8.9 %collective-permute-start.7 = (f32[64,8,128]{2,1,0:T(8,128)S(1)}, f32[64,8,128]{2,1,0:T(8,128)S(1)}, u32[]{:S(2)}, u32[]{:S(2)}) collective-permute-start(f32[64,8,128]{2,1,0:T(8,128)S(1)} %reduce_sum.59), channel_id=1, source_target_pairs={{0,4},{4,0},{1,5},{5,1},{2,6},{6,2},{3,7},{7,3},{8,12},{12,8},{9,1... | collective-permute-start | bytes 786440 | tf_op jit(solution)/shard_map/ppermute | solution.py:89
  261.1 9.8 %collective-permute-start.11 = (f32[64,8,128]{2,1,0:T(8,128)S(1)}, f32[64,8,128]{2,1,0:T(8,128)S(1)}, u32[]{:S(2)}, u32[]{:S(2)}) collective-permute-start(f32[64,8,128]{2,1,0:T(8,128)S(1)} %reduce_sum.59), channel_id=1, source_target_pairs={{0,8},{8,0},{16,24},{24,16},{32,40},{40,32},{48,56},{56,48},{64,72... | collective-permute-start | bytes 786440 | tf_op jit(solution)/shard_map/ppermute | solution.py:137
  263.8 12.0 %copy-start.3 = (f32[1024,128]{1,0:T(8,128)S(1)}, f32[1024,128]{1,0:T(8,128)}, u32[]{:S(2)}) copy-start(f32[1024,128]{1,0:T(8,128)} %copy-done.2) | copy-start | bytes 1572868
  270.9 3.8 %collective-permute-start.12 = (f32[64,8,128]{2,1,0:T(8,128)S(1)}, f32[64,8,128]{2,1,0:T(8,128)S(1)}, u32[]{:S(2)}, u32[]{:S(2)}) collective-permute-start(f32[64,8,128]{2,1,0:T(8,128)S(1)} %collective-permute-done.11), channel_id=1, source_target_pairs={{0,4},{4,0},{1,5},{5,1},{2,6},{6,2},{3,7},{7,3},{8,12},{12,8},{9,1... | collective-permute-start | bytes 786440 | tf_op jit(solution)/shard_map/ppermute | solution.py:89
  (3 other events, 10.4 us)
Sparse Core Ops, SparseCore 0:
  9.5 119.4 all-gather.2

commit v10 on v9

--- a/solution.py
+++ b/solution.py
@@ -118,7 +118,13 @@
     left, right = residual[square:, :columns], residual[square:, columns:]
     below = [jnp.where(even, left, right), jnp.where(even, right, left)]
     start = ((lax.axis_index("x") * nz + zi) * nc + lax.axis_index("core")) * share
-    finished = []
+    finished, later = [[], []], []
+
+    def update(side, k, block):
+        factor = panel[square:, k * block_rows : (k + 1) * block_rows]
+        below[side] = below[side] - product(factor, block)
+        finished[side].append(lax.dynamic_slice_in_dim(block, start, share, 0))
+
     for k in range(sections):
         partial = product(weight[(k, k)], pending[k], ((0,), (0,)))
         partial = partial.reshape(nx * nz, nc, share, columns)
@@ -135,13 +141,14 @@
             traded = lax.ppermute(solved, "z", trade)
         else:
             traded = whole_block(lax.ppermute(mine, "z", trade), first)
-        factor = panel[square:, k * block_rows : (k + 1) * block_rows]
-        pieces = []
-        for h, block in enumerate((solved, traded)):
-            below[h] = below[h] - product(factor, block)
-            pieces.append(lax.dynamic_slice_in_dim(block, start, share, 0))
-        finished.append(pieces)
-    ends = [jnp.concatenate([f[h] for f in finished] + [below[h]], axis=0) for h in range(2)]
+        update(0, k, solved)
+        later.append((k, traded))
+        while later and (later[0][0] + 2 <= k or k + 1 == sections):
+            old, block = later.pop(0)
+            if old < k:
+                block = lax.optimization_barrier((mine, block))[1]
+            update(1, old, block)
+    ends = [jnp.concatenate(finished[h] + [below[h]], axis=0) for h in range(2)]
     return jnp.concatenate(
         [jnp.where(even, ends[0], ends[1]), jnp.where(even, ends[1], ends[0])], axis=1
     )

time: 286 us -> 279 us (0.976)
  waiting for transfers between devices: 68.9 us -> 58.7 us
  matrix products: 27.6 us -> 31.4 us
    ppermute x3, waiting for transfers between devices: 10.8 us -> 0.01 us  [shards(): traded = lax.ppermute(solved, 'z', trade)]
    all_to_all x2, waiting for transfers between devices: 7.11 us -> 14.6 us  [shards(): lax.all_to_all(copies, 'x', split_axis=0, concat_axis=0, tiled=True)]
    ppermute x1, waiting for transfers between devices: 6.98 us -> 0.01 us  [shards(): traded = whole_block(lax.ppermute(mine, 'z', trade), first)]
    dot_general x23, matrix products: 27.6 us -> 31.4 us  [product(): lax.dot_general(left, right, (contract, ((), ())), precision=lax.Precisio...]
  transfers between devices with their start and end apart: 18 -> 18, of which waited for: 11 -> 8; matrix products, arithmetic and copies ran while one was open for 10% -> 13% of each run, Pallas kernels for 0% -> 0%
where the time goes in v10:
time: 279 us; the launch traced here: 278 us
  blocking collectives  102 us (37%)
  waiting for transfers between devices  58.7 us (21%)
  starting transfers between devices  55.3 us (20%)
  matrix products  31.4 us (11%)
  between operations  14.2 us (5%)
  local copies, waits for them, and re-layouts  10.7 us (4%)
  other arithmetic  3.42 us (1%)
    all_to_all x1, blocking collectives, redistribute(): lax.all_to_all(jnp.stack(halves, axis=1), ROWS, split_axis=0, concat_axis...  67.1 us
    all_to_all x2, blocking collectives, shards(): lax.all_to_all(copies, 'x', split_axis=0, concat_axis=0, tiled=True)  35.1 us
    all_gather x1, waiting for transfers between devices, shards(): gathered = lax.all_gather(tiles, 'z')  34 us
    dot_general x23, matrix products, product(): lax.dot_general(left, right, (contract, ((), ())), precision=lax.Precisio...  31.4 us
    ppermute x5, starting transfers between devices, whole_block(): other = lax.ppermute(mine, 'core', SWAP)  14.8 us
    all_to_all x2, waiting for transfers between devices, shards(): lax.all_to_all(copies, 'x', split_axis=0, concat_axis=0, tiled=True)  14.6 us
    ppermute x4, starting transfers between devices, shards(): half = keep + lax.ppermute(give, 'core', SWAP)  14.1 us
    ppermute x3, starting transfers between devices, shards(): traded = lax.ppermute(solved, 'z', trade)  8.07 us
  transfers between devices with their start and end apart: 18, of which 8 were waited for; matrix products, arithmetic and copies ran while one was open for 13% of the time, Pallas kernels for 0%

profile of v10, /device:TPU:1, one launch (start us, length us, event | category | flops | bytes accessed | tf_op | source)
XLA Modules:
  0.0 277.7 jit_solution(709190388806344008)
XLA Ops:
  9.2 5.0 %all-to-all-start = ((f32[64,4,256]{2,0,1:T(8,128)}), f32[64,4,256]{2,0,1:T(8,128)S(1)}, u32[]{:S(2)}, u32[]{:S(2)}) async-start(f32[64,4,256]{2,0,1:T(8,128)} %bitcast.215), calls=%async_computation | async-start | bytes 524288 | tf_op jit(solution)/shard_map/all_to_all | solution.py:46
  14.5 5.3 %all-to-all-done = f32[64,4,256]{2,0,1:T(8,128)S(1)} async-done(((f32[64,4,256]{2,0,1:T(8,128)}), f32[64,4,256]{2,0,1:T(8,128)S(1)}, u32[]{:S(2)}, u32[]{:S(2)}) %all-to-all-start) | async-done | bytes 262176 | tf_op jit(solution)/shard_map/all_to_all | solution.py:46
  21.2 67.1 %all_to_all.49 = f32[128,2,640]{2,1,0:T(2,128)S(1)} all-to-all(f32[128,2,640]{2,1,0:T(2,128)S(1)} %copy.115), channel_id=1, replica_groups=mesh['x'=4,'z'=16,'core'=2,'rhs'=4] {'x','z','core'}, dimensions={0} | all-to-all | bytes 1310720 | tf_op jit(solution)/shard_map/all_to_all | solution.py:74
  91.6 3.5 %all-to-all-start.2 = ((f32[16,32,128]{2,1,0:T(8,128)}), f32[16,32,128]{2,1,0:T(8,128)S(1)}, u32[]{:S(2)}, u32[]{:S(2)}) async-start(f32[16,32,128]{2,1,0:T(8,128)} %bitcast.22), calls=%async_computation.2 | async-start | bytes 524288 | tf_op jit(solution)/shard_map/all_to_all | solution.py:114
  95.1 34.0 %all-gather.3.cloned.1.call-done = f32[160,8,1024]{2,1,0:T(8,128)} async-done(((f32[10,8,1024]{2,1,0:T(8,128)}), f32[160,8,1024]{2,1,0:T(8,128)}) %all-gather.3.cloned.1.call-update) | async-done | bytes 5242896 | tf_op jit(solution)/shard_map/all_gather | solution.py:106
  131.5 7.7 %collective-permute-start = (f32[64,8,128]{2,1,0:T(8,128)S(1)}, f32[64,8,128]{2,1,0:T(8,128)S(1)}, u32[]{:S(2)}, u32[]{:S(2)}) collective-permute-start(f32[64,8,128]{2,1,0:T(8,128)S(1)} %select_bitcast_fusion.13), channel_id=1, source_target_pairs={{0,4},{4,0},{1,5},{5,1},{2,6},{6,2},{3,7},{7,3},{8,12},{12,8},{9,1... | collective-permute-start | bytes 786440 | tf_op jit(solution)/shard_map/ppermute | solution.py:133
  140.5 17.8 %all_to_all.50 = f32[4,64,8,128]{3,2,1,0:T(8,128)S(1)} all-to-all(f32[4,64,8,128]{3,2,1,0:T(8,128)S(1)} %broadcast_in_dim.47), channel_id=1, replica_groups=mesh['x'=4,'z'=16,'core'=2,'rhs'=4] {'x'}, dimensions={0} | all-to-all | bytes 2097152 | tf_op jit(solution)/shard_map/all_to_all | solution.py:135
  158.4 3.7 %collective-permute-start.1 = (f32[64,8,128]{2,1,0:T(8,128)S(1)}, f32[64,8,128]{2,1,0:T(8,128)}, u32[]{:S(2)}, u32[]{:S(2)}) collective-permute-start(f32[64,8,128]{2,1,0:T(8,128)S(1)} %reduce_sum.56), channel_id=1, source_target_pairs={{0,4},{4,0},{1,5},{5,1},{2,6},{6,2},{3,7},{7,3},{8,12},{12,8},{9,1... | collective-permute-start | bytes 786440 | tf_op jit(solution)/shard_map/ppermute | solution.py:89
  166.8 2.3 collective-permute-start.2
  170.4 17.3 %all_to_all.51 = f32[4,64,8,128]{3,2,1,0:T(8,128)S(1)} all-to-all(f32[4,64,8,128]{3,2,1,0:T(8,128)S(1)} %broadcast_in_dim.48), channel_id=1, replica_groups=mesh['x'=4,'z'=16,'core'=2,'rhs'=4] {'x'}, dimensions={0} | all-to-all | bytes 2097152 | tf_op jit(solution)/shard_map/all_to_all | solution.py:135
  187.7 3.1 %collective-permute-start.3 = (f32[64,8,128]{2,1,0:T(8,128)S(1)}, f32[64,8,128]{2,1,0:T(8,128)S(1)}, u32[]{:S(2)}, u32[]{:S(2)}) collective-permute-start(f32[64,8,128]{2,1,0:T(8,128)S(1)} %reduce_sum.57), channel_id=1, source_target_pairs={{0,4},{4,0},{1,5},{5,1},{2,6},{6,2},{3,7},{7,3},{8,12},{12,8},{9,1... | collective-permute-start | bytes 786440 | tf_op jit(solution)/shard_map/ppermute | solution.py:89
  199.7 3.7 %all-to-all-start.5 = ((f32[4,64,8,128]{3,2,1,0:T(8,128)}), f32[4,64,8,128]{3,2,1,0:T(8,128)S(1)}, u32[]{:S(2)}, u32[]{:S(2)}) async-start(f32[4,64,8,128]{3,2,1,0:T(8,128)} %broadcast_in_dim.49), calls=%async_computation.5 | async-start | bytes 2097152 | tf_op jit(solution)/shard_map/all_to_all | solution.py:135
  203.6 2.8 %collective-permute-start.8 = (f32[1024,128]{1,0:T(8,128)S(1)}, f32[1024,128]{1,0:T(8,128)}, u32[]{:S(2)}, u32[]{:S(2)}) collective-permute-start(f32[1024,128]{1,0:T(8,128)S(1)} %bitcast.218), channel_id=1, source_target_pairs={{0,8},{8,0},{16,24},{24,16},{32,40},{40,32},{48,56},{56,48},{64,72... | collective-permute-start | bytes 1572872 | tf_op jit(solution)/shard_map/ppermute | solution.py:141
  210.2 8.3 %all-to-all-done.5 = f32[4,64,8,128]{3,2,1,0:T(8,128)S(1)} async-done(((f32[4,64,8,128]{3,2,1,0:T(8,128)}), f32[4,64,8,128]{3,2,1,0:T(8,128)S(1)}, u32[]{:S(2)}, u32[]{:S(2)}) %all-to-all-start.5) | async-done | bytes 1048608 | tf_op jit(solution)/shard_map/all_to_all | solution.py:135
  218.5 2.9 %collective-permute-start.5 = (f32[64,8,128]{2,1,0:T(8,128)S(1)}, f32[64,8,128]{2,1,0:T(8,128)S(1)}, u32[]{:S(2)}, u32[]{:S(2)}) collective-permute-start(f32[64,8,128]{2,1,0:T(8,128)S(1)} %reduce_sum.58), channel_id=1, source_target_pairs={{0,4},{4,0},{1,5},{5,1},{2,6},{6,2},{3,7},{7,3},{8,12},{12,8},{9,1... | collective-permute-start | bytes 786440 | tf_op jit(solution)/shard_map/ppermute | solution.py:89
  222.0 2.8 %collective-permute-start.9 = (f32[1024,128]{1,0:T(8,128)S(1)}, f32[1024,128]{1,0:T(8,128)}, u32[]{:S(2)}, u32[]{:S(2)}) collective-permute-start(f32[1024,128]{1,0:T(8,128)S(1)} %bitcast.223), channel_id=1, source_target_pairs={{0,8},{8,0},{16,24},{24,16},{32,40},{40,32},{48,56},{56,48},{64,72... | collective-permute-start | bytes 1572872 | tf_op jit(solution)/shard_map/ppermute | solution.py:141
  228.9 2.2 collective-permute-start.6
  234.3 3.5 %all-to-all-start.6 = ((f32[4,64,8,128]{3,2,1,0:T(8,128)}), f32[4,64,8,128]{3,2,1,0:T(8,128)S(1)}, u32[]{:S(2)}, u32[]{:S(2)}) async-start(f32[4,64,8,128]{3,2,1,0:T(8,128)} %broadcast_in_dim.50), calls=%async_computation.6 | async-start | bytes 2097152 | tf_op jit(solution)/shard_map/all_to_all | solution.py:135
  238.5 2.5 collective-permute-start.10
  240.9 2.2 fusion.4
  246.5 6.3 %all-to-all-done.6 = f32[4,64,8,128]{3,2,1,0:T(8,128)S(1)} async-done(((f32[4,64,8,128]{3,2,1,0:T(8,128)}), f32[4,64,8,128]{3,2,1,0:T(8,128)S(1)}, u32[]{:S(2)}, u32[]{:S(2)}) %all-to-all-start.6) | async-done | bytes 1048608 | tf_op jit(solution)/shard_map/all_to_all | solution.py:135
  252.9 2.5 collective-permute-start.11
  255.4 3.2 %collective-permute-start.7 = (f32[64,8,128]{2,1,0:T(8,128)S(1)}, f32[64,8,128]{2,1,0:T(8,128)S(1)}, u32[]{:S(2)}, u32[]{:S(2)}) collective-permute-start(f32[64,8,128]{2,1,0:T(8,128)S(1)} %reduce_sum.59), channel_id=1, source_target_pairs={{0,4},{4,0},{1,5},{5,1},{2,6},{6,2},{3,7},{7,3},{8,12},{12,8},{9,1... | collective-permute-start | bytes 786440 | tf_op jit(solution)/shard_map/ppermute | solution.py:89
  258.6 2.2 fusion.3
  (117 shorter events, 51.7 us)
Async XLA Ops:
  6.5 1.9 copy-start.1
  6.5 7.7 %copy-start.5 = (s32[1,128]{1,0:T(1,128)S(1)}, s32[1,128]{1,0:T(1,128)}, u32[]{:S(2)}) copy-start(s32[1,128]{1,0:T(1,128)} %param.8) | copy-start | bytes 1540
  6.5 7.8 %copy-start.3 = (s32[256]{0:T(256)S(1)}, s32[256]{0:T(256)}, u32[]{:S(2)}) copy-start(s32[256]{0:T(256)} %param.7) | copy-start | bytes 3076
  6.5 7.9 %copy-start.4 = (s32[256]{0:T(256)S(1)}, s32[256]{0:T(256)}, u32[]{:S(2)}) copy-start(s32[256]{0:T(256)} %param.9) | copy-start | bytes 3076
  6.5 122.5 %all-gather.3.cloned.1.call-start = ((), (), s32[]{:S(2)}) async-start(), calls=%async_computation.7 | async-start | bytes 5570560 | tf_op jit(solution)/shard_map/all_gather | solution.py:106
  9.2 10.5 %all-to-all-start = ((f32[64,4,256]{2,0,1:T(8,128)}), f32[64,4,256]{2,0,1:T(8,128)S(1)}, u32[]{:S(2)}, u32[]{:S(2)}) async-start(f32[64,4,256]{2,0,1:T(8,128)} %bitcast.215), calls=%async_computation | async-start | bytes 524288 | tf_op jit(solution)/shard_map/all_to_all | solution.py:46
  91.6 39.4 %all-to-all-start.2 = ((f32[16,32,128]{2,1,0:T(8,128)}), f32[16,32,128]{2,1,0:T(8,128)S(1)}, u32[]{:S(2)}, u32[]{:S(2)}) async-start(f32[16,32,128]{2,1,0:T(8,128)} %bitcast.22), calls=%async_computation.2 | async-start | bytes 524288 | tf_op jit(solution)/shard_map/all_to_all | solution.py:114
  130.9 60.1 %copy-start = (f32[16,32,128]{2,1,0:T(8,128)}, f32[16,32,128]{2,1,0:T(8,128)S(1)}, u32[]{:S(2)}) copy-start(f32[16,32,128]{2,1,0:T(8,128)S(1)} %all-to-all-done.2) | copy-start | bytes 786436
  131.5 8.8 %collective-permute-start = (f32[64,8,128]{2,1,0:T(8,128)S(1)}, f32[64,8,128]{2,1,0:T(8,128)S(1)}, u32[]{:S(2)}, u32[]{:S(2)}) collective-permute-start(f32[64,8,128]{2,1,0:T(8,128)S(1)} %select_bitcast_fusion.13), channel_id=1, source_target_pairs={{0,4},{4,0},{1,5},{5,1},{2,6},{6,2},{3,7},{7,3},{8,12},{12,8},{9,1... | collective-permute-start | bytes 786440 | tf_op jit(solution)/shard_map/ppermute | solution.py:133
  158.4 5.0 %collective-permute-start.1 = (f32[64,8,128]{2,1,0:T(8,128)S(1)}, f32[64,8,128]{2,1,0:T(8,128)}, u32[]{:S(2)}, u32[]{:S(2)}) collective-permute-start(f32[64,8,128]{2,1,0:T(8,128)S(1)} %reduce_sum.56), channel_id=1, source_target_pairs={{0,4},{4,0},{1,5},{5,1},{2,6},{6,2},{3,7},{7,3},{8,12},{12,8},{9,1... | collective-permute-start | bytes 786440 | tf_op jit(solution)/shard_map/ppermute | solution.py:89
  166.8 3.4 %collective-permute-start.2 = (f32[64,8,128]{2,1,0:T(8,128)S(1)}, f32[64,8,128]{2,1,0:T(8,128)S(1)}, u32[]{:S(2)}, u32[]{:S(2)}) collective-permute-start(f32[64,8,128]{2,1,0:T(8,128)S(1)} %select_bitcast_fusion.10), channel_id=1, source_target_pairs={{0,4},{4,0},{1,5},{5,1},{2,6},{6,2},{3,7},{7,3},{8,12},{12,8},{9,1... | collective-permute-start | bytes 786440 | tf_op jit(solution)/shard_map/ppermute | solution.py:133
  187.7 5.0 %collective-permute-start.3 = (f32[64,8,128]{2,1,0:T(8,128)S(1)}, f32[64,8,128]{2,1,0:T(8,128)S(1)}, u32[]{:S(2)}, u32[]{:S(2)}) collective-permute-start(f32[64,8,128]{2,1,0:T(8,128)S(1)} %reduce_sum.57), channel_id=1, source_target_pairs={{0,4},{4,0},{1,5},{5,1},{2,6},{6,2},{3,7},{7,3},{8,12},{12,8},{9,1... | collective-permute-start | bytes 786440 | tf_op jit(solution)/shard_map/ppermute | solution.py:89
  195.1 3.4 %collective-permute-start.4 = (f32[64,8,128]{2,1,0:T(8,128)S(1)}, f32[64,8,128]{2,1,0:T(8,128)S(1)}, u32[]{:S(2)}, u32[]{:S(2)}) collective-permute-start(f32[64,8,128]{2,1,0:T(8,128)S(1)} %select_bitcast_fusion.7), channel_id=1, source_target_pairs={{0,4},{4,0},{1,5},{5,1},{2,6},{6,2},{3,7},{7,3},{8,12},{12,8},{9,1... | collective-permute-start | bytes 786440 | tf_op jit(solution)/shard_map/ppermute | solution.py:133
  199.7 18.8 %all-to-all-start.5 = ((f32[4,64,8,128]{3,2,1,0:T(8,128)}), f32[4,64,8,128]{3,2,1,0:T(8,128)S(1)}, u32[]{:S(2)}, u32[]{:S(2)}) async-start(f32[4,64,8,128]{3,2,1,0:T(8,128)} %broadcast_in_dim.49), calls=%async_computation.5 | async-start | bytes 2097152 | tf_op jit(solution)/shard_map/all_to_all | solution.py:135
  203.6 34.8 %collective-permute-start.8 = (f32[1024,128]{1,0:T(8,128)S(1)}, f32[1024,128]{1,0:T(8,128)}, u32[]{:S(2)}, u32[]{:S(2)}) collective-permute-start(f32[1024,128]{1,0:T(8,128)S(1)} %bitcast.218), channel_id=1, source_target_pairs={{0,8},{8,0},{16,24},{24,16},{32,40},{40,32},{48,56},{56,48},{64,72... | collective-permute-start | bytes 1572872 | tf_op jit(solution)/shard_map/ppermute | solution.py:141
  218.5 8.0 %collective-permute-start.5 = (f32[64,8,128]{2,1,0:T(8,128)S(1)}, f32[64,8,128]{2,1,0:T(8,128)S(1)}, u32[]{:S(2)}, u32[]{:S(2)}) collective-permute-start(f32[64,8,128]{2,1,0:T(8,128)S(1)} %reduce_sum.58), channel_id=1, source_target_pairs={{0,4},{4,0},{1,5},{5,1},{2,6},{6,2},{3,7},{7,3},{8,12},{12,8},{9,1... | collective-permute-start | bytes 786440 | tf_op jit(solution)/shard_map/ppermute | solution.py:89
  222.0 36.6 %collective-permute-start.9 = (f32[1024,128]{1,0:T(8,128)S(1)}, f32[1024,128]{1,0:T(8,128)}, u32[]{:S(2)}, u32[]{:S(2)}) collective-permute-start(f32[1024,128]{1,0:T(8,128)S(1)} %bitcast.223), channel_id=1, source_target_pairs={{0,8},{8,0},{16,24},{24,16},{32,40},{40,32},{48,56},{56,48},{64,72... | collective-permute-start | bytes 1572872 | tf_op jit(solution)/shard_map/ppermute | solution.py:141
  228.9 4.3 %collective-permute-start.6 = (f32[64,8,128]{2,1,0:T(8,128)S(1)}, f32[64,8,128]{2,1,0:T(8,128)S(1)}, u32[]{:S(2)}, u32[]{:S(2)}) collective-permute-start(f32[64,8,128]{2,1,0:T(8,128)S(1)} %select_bitcast_fusion.4), channel_id=1, source_target_pairs={{0,4},{4,0},{1,5},{5,1},{2,6},{6,2},{3,7},{7,3},{8,12},{12,8},{9,1... | collective-permute-start | bytes 786440 | tf_op jit(solution)/shard_map/ppermute | solution.py:133
  234.3 18.5 %all-to-all-start.6 = ((f32[4,64,8,128]{3,2,1,0:T(8,128)}), f32[4,64,8,128]{3,2,1,0:T(8,128)S(1)}, u32[]{:S(2)}, u32[]{:S(2)}) async-start(f32[4,64,8,128]{3,2,1,0:T(8,128)} %broadcast_in_dim.50), calls=%async_computation.6 | async-start | bytes 2097152 | tf_op jit(solution)/shard_map/all_to_all | solution.py:135
  238.5 20.2 %collective-permute-start.10 = (f32[1024,128]{1,0:T(8,128)S(1)}, f32[1024,128]{1,0:T(8,128)S(1)}, u32[]{:S(2)}, u32[]{:S(2)}) collective-permute-start(f32[1024,128]{1,0:T(8,128)S(1)} %bitcast.235), channel_id=1, source_target_pairs={{0,8},{8,0},{16,24},{24,16},{32,40},{40,32},{48,56},{56,48},{64,72... | collective-permute-start | bytes 1572872 | tf_op jit(solution)/shard_map/ppermute | solution.py:141
  246.5 17.3 %copy-start.2 = (f32[256,128]{1,0:T(8,128)S(1)}, f32[256,128]{1,0:T(8,128)}, u32[]{:S(2)}) copy-start(f32[256,128]{1,0:T(8,128)} %constant_dynamic-update-slice_fusion.1) | copy-start | bytes 393220
  252.9 10.9 %collective-permute-start.11 = (f32[64,8,128]{2,1,0:T(8,128)S(1)}, f32[64,8,128]{2,1,0:T(8,128)S(1)}, u32[]{:S(2)}, u32[]{:S(2)}) collective-permute-start(f32[64,8,128]{2,1,0:T(8,128)S(1)} %reduce_sum.59), channel_id=1, source_target_pairs={{0,8},{8,0},{16,24},{24,16},{32,40},{40,32},{48,56},{56,48},{64,72... | collective-permute-start | bytes 786440 | tf_op jit(solution)/shard_map/ppermute | solution.py:143
  255.4 8.2 %collective-permute-start.7 = (f32[64,8,128]{2,1,0:T(8,128)S(1)}, f32[64,8,128]{2,1,0:T(8,128)S(1)}, u32[]{:S(2)}, u32[]{:S(2)}) collective-permute-start(f32[64,8,128]{2,1,0:T(8,128)S(1)} %reduce_sum.59), channel_id=1, source_target_pairs={{0,4},{4,0},{1,5},{5,1},{2,6},{6,2},{3,7},{7,3},{8,12},{12,8},{9,1... | collective-permute-start | bytes 786440 | tf_op jit(solution)/shard_map/ppermute | solution.py:89
  263.8 4.0 %collective-permute-start.12 = (f32[64,8,128]{2,1,0:T(8,128)S(1)}, f32[64,8,128]{2,1,0:T(8,128)S(1)}, u32[]{:S(2)}, u32[]{:S(2)}) collective-permute-start(f32[64,8,128]{2,1,0:T(8,128)S(1)} %collective-permute-done.11), channel_id=1, source_target_pairs={{0,4},{4,0},{1,5},{5,1},{2,6},{6,2},{3,7},{7,3},{8,12},{12,8},{9,1... | collective-permute-start | bytes 786440 | tf_op jit(solution)/shard_map/ppermute | solution.py:89
Sparse Core Ops, SparseCore 0:
  9.5 119.5 all-gather.2

commit v11 on v10

--- a/solution.py
+++ b/solution.py
@@ -45,7 +45,7 @@
     groups = lax.axis_size(ROWS)
     arrived = lax.all_to_all(targets, "rhs", split_axis=1, concat_axis=0, tiled=True)
     rows_local, columns = arrived.shape
-    capacity, tag = 4, 64
+    capacity, tag = 4, 32
     counts = send_count[0]
     dest = jnp.arange(groups, dtype=jnp.int32)
     starts = jnp.sum(jnp.where(dest[None, :] < dest[:, None], counts[None, :], 0), axis=1)
@@ -56,32 +56,24 @@
     listed = jnp.where(slot_number[:, None] < counts[None, :], listed, -1)
     picked = (listed[:, :, None] == position[None, None, :]).astype(jnp.float32)
     picked = picked.reshape(capacity * groups, rows_local)
-    landing = jnp.broadcast_to((recv_slot + 1).astype(jnp.float32)[:, None], (rows_local, 2 * tag))
+    landing = jnp.broadcast_to((recv_slot + 1).astype(jnp.float32)[:, None], (rows_local, tag * capacity))
     planes = product(picked, jnp.concatenate([arrived, landing], axis=1))
-    planes = planes.reshape(capacity, groups, columns + 2 * tag)
-    halves = [
-        jnp.concatenate(
-            [
-                planes[s, :, :columns],
-                planes[s + 1, :, :columns],
-                planes[s, :, columns : columns + tag],
-                planes[s + 1, :, columns : columns + tag],
-            ],
-            axis=1,
-        )
-        for s in range(0, capacity, 2)
-    ]
+    planes = planes.reshape(capacity, groups, columns + tag * capacity)
+    sent = jnp.concatenate(
+        [planes[s, :, :columns] for s in range(capacity)]
+        + [planes[s, :, columns + s * tag : columns + (s + 1) * tag] for s in range(capacity)],
+        axis=1,
+    )
     incoming = lax.all_to_all(
-        jnp.stack(halves, axis=1), ROWS, split_axis=0, concat_axis=0, tiled=True
-    )
+        sent[:, None], ROWS, split_axis=0, concat_axis=0, tiled=True
+    )[:, 0]
     total = 0.0
-    for h in range(capacity // 2):
-        half = incoming[:, h]
-        for s in range(2):
-            label = half[:, 2 * columns + s * tag : 2 * columns + s * tag + 1] - 1.0
-            placed = (label.astype(jnp.int32) == index[None, :]).astype(jnp.float32)
-            rows = half[:, s * columns : (s + 1) * columns]
-            total = total + product(placed, rows, ((0,), (0,)))
+    for s in range(capacity):
+        spot = capacity * columns + s * tag
+        label = incoming[:, spot : spot + 1] - 1.0
+        placed = (label.astype(jnp.int32) == index[None, :]).astype(jnp.float32)
+        rows = incoming[:, s * columns : (s + 1) * columns]
+        total = total + product(placed, rows, ((0,), (0,)))
     return total
 
 

time: 279 us -> 276 us (0.989)
    all_to_all x1, blocking collectives: 67.1 us -> 63.9 us  [redistribute(): lax.all_to_all(sent[:, None], ROWS, split_axis=0, concat_axis=0, tiled=True)]
  transfers between devices with their start and end apart: 18 -> 18, of which waited for: 8 -> 8; matrix products, arithmetic and copies ran while one was open for 13% -> 12% of each run, Pallas kernels for 0% -> 0%
where the time goes in v11:
time: 276 us; the launch traced here: 275 us
  blocking collectives  99.6 us (36%)
  waiting for transfers between devices  59.1 us (21%)
  starting transfers between devices  55.2 us (20%)
  matrix products  31.8 us (12%)
  between operations  14.1 us (5%)
  local copies, waits for them, and re-layouts  9.84 us (4%)
  other arithmetic  3.13 us (1%)
    all_to_all x1, blocking collectives, redistribute(): lax.all_to_all(sent[:, None], ROWS, split_axis=0, concat_axis=0, tiled=True)  63.9 us
    all_to_all x2, blocking collectives, shards(): lax.all_to_all(copies, 'x', split_axis=0, concat_axis=0, tiled=True)  35.7 us
    all_gather x1, waiting for transfers between devices, shards(): gathered = lax.all_gather(tiles, 'z')  35.1 us
    dot_general x23, matrix products, product(): lax.dot_general(left, right, (contract, ((), ())), precision=lax.Precisio...  31.8 us
    ppermute x5, starting transfers between devices, whole_block(): other = lax.ppermute(mine, 'core', SWAP)  15.5 us
    all_to_all x2, waiting for transfers between devices, shards(): lax.all_to_all(copies, 'x', split_axis=0, concat_axis=0, tiled=True)  13.8 us
    ppermute x4, starting transfers between devices, shards(): half = keep + lax.ppermute(give, 'core', SWAP)  13.3 us
    ppermute x3, starting transfers between devices, shards(): traded = lax.ppermute(solved, 'z', trade)  7.88 us
  transfers between devices with their start and end apart: 18, of which 8 were waited for; matrix products, arithmetic and copies ran while one was open for 12% of the time, Pallas kernels for 0%

profile of v11, /device:TPU:1, one launch (start us, length us, event | category | flops | bytes accessed | tf_op | source)
XLA Modules:
  0.0 274.7 jit_solution(8368046196780479067)
XLA Ops:
  9.2 5.0 %all-to-all-start = ((f32[64,4,256]{2,0,1:T(8,128)}), f32[64,4,256]{2,0,1:T(8,128)S(1)}, u32[]{:S(2)}, u32[]{:S(2)}) async-start(f32[64,4,256]{2,0,1:T(8,128)} %bitcast.209), calls=%async_computation | async-start | bytes 524288 | tf_op jit(solution)/shard_map/all_to_all | solution.py:46
  14.4 5.3 %all-to-all-done = f32[64,4,256]{2,0,1:T(8,128)S(1)} async-done(((f32[64,4,256]{2,0,1:T(8,128)}), f32[64,4,256]{2,0,1:T(8,128)S(1)}, u32[]{:S(2)}, u32[]{:S(2)}) %all-to-all-start) | async-done | bytes 262176 | tf_op jit(solution)/shard_map/all_to_all | solution.py:46
  21.3 63.9 %all_to_all.49 = f32[128,1,1152]{2,1,0:T(1,128)S(1)} all-to-all(f32[128,1,1152]{2,1,0:T(1,128)S(1)} %copy.112), channel_id=1, replica_groups=mesh['x'=4,'z'=16,'core'=2,'rhs'=4] {'x','z','core'}, dimensions={0} | all-to-all | bytes 1179648 | tf_op jit(solution)/shard_map/all_to_all | solution.py:67
  87.8 3.5 %all-to-all-start.2 = ((f32[16,32,128]{2,1,0:T(8,128)}), f32[16,32,128]{2,1,0:T(8,128)S(1)}, u32[]{:S(2)}, u32[]{:S(2)}) async-start(f32[16,32,128]{2,1,0:T(8,128)} %bitcast.20), calls=%async_computation.2 | async-start | bytes 524288 | tf_op jit(solution)/shard_map/all_to_all | solution.py:106
  91.4 35.1 %all-gather.3.cloned.1.call-done = f32[160,8,1024]{2,1,0:T(8,128)} async-done(((f32[10,8,1024]{2,1,0:T(8,128)}), f32[160,8,1024]{2,1,0:T(8,128)}) %all-gather.3.cloned.1.call-update) | async-done | bytes 5242896 | tf_op jit(solution)/shard_map/all_gather | solution.py:98
  129.0 7.1 %collective-permute-start = (f32[64,8,128]{2,1,0:T(8,128)S(1)}, f32[64,8,128]{2,1,0:T(8,128)S(1)}, u32[]{:S(2)}, u32[]{:S(2)}) collective-permute-start(f32[64,8,128]{2,1,0:T(8,128)S(1)} %select_bitcast_fusion.13), channel_id=1, source_target_pairs={{0,4},{4,0},{1,5},{5,1},{2,6},{6,2},{3,7},{7,3},{8,12},{12,8},{9,1... | collective-permute-start | bytes 786440 | tf_op jit(solution)/shard_map/ppermute | solution.py:125
  137.4 18.5 %all_to_all.50 = f32[4,64,8,128]{3,2,1,0:T(8,128)S(1)} all-to-all(f32[4,64,8,128]{3,2,1,0:T(8,128)S(1)} %broadcast_in_dim.50), channel_id=1, replica_groups=mesh['x'=4,'z'=16,'core'=2,'rhs'=4] {'x'}, dimensions={0} | all-to-all | bytes 2097152 | tf_op jit(solution)/shard_map/all_to_all | solution.py:127
  155.9 3.7 %collective-permute-start.1 = (f32[64,8,128]{2,1,0:T(8,128)S(1)}, f32[64,8,128]{2,1,0:T(8,128)}, u32[]{:S(2)}, u32[]{:S(2)}) collective-permute-start(f32[64,8,128]{2,1,0:T(8,128)S(1)} %reduce_sum.56), channel_id=1, source_target_pairs={{0,4},{4,0},{1,5},{5,1},{2,6},{6,2},{3,7},{7,3},{8,12},{12,8},{9,1... | collective-permute-start | bytes 786440 | tf_op jit(solution)/shard_map/ppermute | solution.py:81
  164.3 2.3 collective-permute-start.2
  167.8 17.3 %all_to_all.51 = f32[4,64,8,128]{3,2,1,0:T(8,128)S(1)} all-to-all(f32[4,64,8,128]{3,2,1,0:T(8,128)S(1)} %broadcast_in_dim.51), channel_id=1, replica_groups=mesh['x'=4,'z'=16,'core'=2,'rhs'=4] {'x'}, dimensions={0} | all-to-all | bytes 2097152 | tf_op jit(solution)/shard_map/all_to_all | solution.py:127
  185.2 3.1 %collective-permute-start.3 = (f32[64,8,128]{2,1,0:T(8,128)S(1)}, f32[64,8,128]{2,1,0:T(8,128)S(1)}, u32[]{:S(2)}, u32[]{:S(2)}) collective-permute-start(f32[64,8,128]{2,1,0:T(8,128)S(1)} %reduce_sum.57), channel_id=1, source_target_pairs={{0,4},{4,0},{1,5},{5,1},{2,6},{6,2},{3,7},{7,3},{8,12},{12,8},{9,1... | collective-permute-start | bytes 786440 | tf_op jit(solution)/shard_map/ppermute | solution.py:81
  197.2 3.5 %all-to-all-start.5 = ((f32[4,64,8,128]{3,2,1,0:T(8,128)}), f32[4,64,8,128]{3,2,1,0:T(8,128)S(1)}, u32[]{:S(2)}, u32[]{:S(2)}) async-start(f32[4,64,8,128]{3,2,1,0:T(8,128)} %broadcast_in_dim.52), calls=%async_computation.5 | async-start | bytes 2097152 | tf_op jit(solution)/shard_map/all_to_all | solution.py:127
  200.9 2.6 collective-permute-start.8
  205.2 10.5 %all-to-all-done.5 = f32[4,64,8,128]{3,2,1,0:T(8,128)S(1)} async-done(((f32[4,64,8,128]{3,2,1,0:T(8,128)}), f32[4,64,8,128]{3,2,1,0:T(8,128)S(1)}, u32[]{:S(2)}, u32[]{:S(2)}) %all-to-all-start.5) | async-done | bytes 1048608 | tf_op jit(solution)/shard_map/all_to_all | solution.py:127
  215.8 2.9 %collective-permute-start.5 = (f32[64,8,128]{2,1,0:T(8,128)S(1)}, f32[64,8,128]{2,1,0:T(8,128)S(1)}, u32[]{:S(2)}, u32[]{:S(2)}) collective-permute-start(f32[64,8,128]{2,1,0:T(8,128)S(1)} %reduce_sum.58), channel_id=1, source_target_pairs={{0,4},{4,0},{1,5},{5,1},{2,6},{6,2},{3,7},{7,3},{8,12},{12,8},{9,1... | collective-permute-start | bytes 786440 | tf_op jit(solution)/shard_map/ppermute | solution.py:81
  227.4 2.4 collective-permute-start.9
  230.9 3.5 %all-to-all-start.6 = ((f32[4,64,8,128]{3,2,1,0:T(8,128)}), f32[4,64,8,128]{3,2,1,0:T(8,128)S(1)}, u32[]{:S(2)}, u32[]{:S(2)}) async-start(f32[4,64,8,128]{3,2,1,0:T(8,128)} %broadcast_in_dim.53), calls=%async_computation.6 | async-start | bytes 2097152 | tf_op jit(solution)/shard_map/all_to_all | solution.py:127
  237.1 2.8 %collective-permute-start.10 = (f32[1024,128]{1,0:T(8,128)S(1)}, f32[1024,128]{1,0:T(8,128)S(1)}, u32[]{:S(2)}, u32[]{:S(2)}) collective-permute-start(f32[1024,128]{1,0:T(8,128)S(1)} %bitcast.229), channel_id=1, source_target_pairs={{0,8},{8,0},{16,24},{24,16},{32,40},{40,32},{48,56},{56,48},{64,72... | collective-permute-start | bytes 1572872 | tf_op jit(solution)/shard_map/ppermute | solution.py:133
  240.0 2.9 %fusion.4 = f32[224,128]{1,0:T(8,128)} fusion(f32[1024,128]{1,0:T(8,128)} %collective-permute-done.8, f32[256,4096]{1,0:T(8,128)} %panel_ref.1, f32[256,256]{1,0:T(8,128)S(1)} %convolution_add_fusion, pred[]{:T(512)S(6)} %eq.96), kind=kOutput, calls=%fused_computation.11 | convolution fusion | flops 352378880 | bytes 1785857 | tf_op jit(solution)/shard_map/dot_general | solution.py:12
  245.5 3.3 %all-to-all-done.6 = f32[4,64,8,128]{3,2,1,0:T(8,128)S(1)} async-done(((f32[4,64,8,128]{3,2,1,0:T(8,128)}), f32[4,64,8,128]{3,2,1,0:T(8,128)S(1)}, u32[]{:S(2)}, u32[]{:S(2)}) %all-to-all-start.6) | async-done | bytes 1048608 | tf_op jit(solution)/shard_map/all_to_all | solution.py:127
  248.9 3.0 %collective-permute-start.11 = (f32[64,8,128]{2,1,0:T(8,128)S(1)}, f32[64,8,128]{2,1,0:T(8,128)S(1)}, u32[]{:S(2)}, u32[]{:S(2)}) collective-permute-start(f32[64,8,128]{2,1,0:T(8,128)S(1)} %reduce_sum.59), channel_id=1, source_target_pairs={{0,8},{8,0},{16,24},{24,16},{32,40},{40,32},{48,56},{56,48},{64,72... | collective-permute-start | bytes 786440 | tf_op jit(solution)/shard_map/ppermute | solution.py:135
  251.9 3.9 %collective-permute-start.7 = (f32[64,8,128]{2,1,0:T(8,128)S(1)}, f32[64,8,128]{2,1,0:T(8,128)S(1)}, u32[]{:S(2)}, u32[]{:S(2)}) collective-permute-start(f32[64,8,128]{2,1,0:T(8,128)S(1)} %reduce_sum.59), channel_id=1, source_target_pairs={{0,4},{4,0},{1,5},{5,1},{2,6},{6,2},{3,7},{7,3},{8,12},{12,8},{9,1... | collective-permute-start | bytes 786440 | tf_op jit(solution)/shard_map/ppermute | solution.py:81
  255.8 2.1 fusion.3
  265.0 2.1 fusion.1
  (112 shorter events, 50.3 us)
Async XLA Ops:
  6.5 1.9 copy-start.1
  6.5 7.6 %copy-start.5 = (s32[1,128]{1,0:T(1,128)S(1)}, s32[1,128]{1,0:T(1,128)}, u32[]{:S(2)}) copy-start(s32[1,128]{1,0:T(1,128)} %param.8) | copy-start | bytes 1540
  6.5 7.7 %copy-start.3 = (s32[256]{0:T(256)S(1)}, s32[256]{0:T(256)}, u32[]{:S(2)}) copy-start(s32[256]{0:T(256)} %param.7) | copy-start | bytes 3076
  6.5 7.9 %copy-start.4 = (s32[256]{0:T(256)S(1)}, s32[256]{0:T(256)}, u32[]{:S(2)}) copy-start(s32[256]{0:T(256)} %param.9) | copy-start | bytes 3076
  6.5 119.9 %all-gather.3.cloned.1.call-start = ((), (), s32[]{:S(2)}) async-start(), calls=%async_computation.7 | async-start | bytes 5570560 | tf_op jit(solution)/shard_map/all_gather | solution.py:98
  9.2 10.5 %all-to-all-start = ((f32[64,4,256]{2,0,1:T(8,128)}), f32[64,4,256]{2,0,1:T(8,128)S(1)}, u32[]{:S(2)}, u32[]{:S(2)}) async-start(f32[64,4,256]{2,0,1:T(8,128)} %bitcast.209), calls=%async_computation | async-start | bytes 524288 | tf_op jit(solution)/shard_map/all_to_all | solution.py:46
  87.8 40.5 %all-to-all-start.2 = ((f32[16,32,128]{2,1,0:T(8,128)}), f32[16,32,128]{2,1,0:T(8,128)S(1)}, u32[]{:S(2)}, u32[]{:S(2)}) async-start(f32[16,32,128]{2,1,0:T(8,128)} %bitcast.20), calls=%async_computation.2 | async-start | bytes 524288 | tf_op jit(solution)/shard_map/all_to_all | solution.py:106
  128.3 60.2 %copy-start = (f32[16,32,128]{2,1,0:T(8,128)}, f32[16,32,128]{2,1,0:T(8,128)S(1)}, u32[]{:S(2)}) copy-start(f32[16,32,128]{2,1,0:T(8,128)S(1)} %all-to-all-done.2) | copy-start | bytes 786436
  129.0 8.3 %collective-permute-start = (f32[64,8,128]{2,1,0:T(8,128)S(1)}, f32[64,8,128]{2,1,0:T(8,128)S(1)}, u32[]{:S(2)}, u32[]{:S(2)}) collective-permute-start(f32[64,8,128]{2,1,0:T(8,128)S(1)} %select_bitcast_fusion.13), channel_id=1, source_target_pairs={{0,4},{4,0},{1,5},{5,1},{2,6},{6,2},{3,7},{7,3},{8,12},{12,8},{9,1... | collective-permute-start | bytes 786440 | tf_op jit(solution)/shard_map/ppermute | solution.py:125
  155.9 5.0 %collective-permute-start.1 = (f32[64,8,128]{2,1,0:T(8,128)S(1)}, f32[64,8,128]{2,1,0:T(8,128)}, u32[]{:S(2)}, u32[]{:S(2)}) collective-permute-start(f32[64,8,128]{2,1,0:T(8,128)S(1)} %reduce_sum.56), channel_id=1, source_target_pairs={{0,4},{4,0},{1,5},{5,1},{2,6},{6,2},{3,7},{7,3},{8,12},{12,8},{9,1... | collective-permute-start | bytes 786440 | tf_op jit(solution)/shard_map/ppermute | solution.py:81
  164.3 3.4 %collective-permute-start.2 = (f32[64,8,128]{2,1,0:T(8,128)S(1)}, f32[64,8,128]{2,1,0:T(8,128)S(1)}, u32[]{:S(2)}, u32[]{:S(2)}) collective-permute-start(f32[64,8,128]{2,1,0:T(8,128)S(1)} %select_bitcast_fusion.10), channel_id=1, source_target_pairs={{0,4},{4,0},{1,5},{5,1},{2,6},{6,2},{3,7},{7,3},{8,12},{12,8},{9,1... | collective-permute-start | bytes 786440 | tf_op jit(solution)/shard_map/ppermute | solution.py:125
  185.2 5.0 %collective-permute-start.3 = (f32[64,8,128]{2,1,0:T(8,128)S(1)}, f32[64,8,128]{2,1,0:T(8,128)S(1)}, u32[]{:S(2)}, u32[]{:S(2)}) collective-permute-start(f32[64,8,128]{2,1,0:T(8,128)S(1)} %reduce_sum.57), channel_id=1, source_target_pairs={{0,4},{4,0},{1,5},{5,1},{2,6},{6,2},{3,7},{7,3},{8,12},{12,8},{9,1... | collective-permute-start | bytes 786440 | tf_op jit(solution)/shard_map/ppermute | solution.py:81
  192.6 3.4 %collective-permute-start.4 = (f32[64,8,128]{2,1,0:T(8,128)S(1)}, f32[64,8,128]{2,1,0:T(8,128)S(1)}, u32[]{:S(2)}, u32[]{:S(2)}) collective-permute-start(f32[64,8,128]{2,1,0:T(8,128)S(1)} %select_bitcast_fusion.7), channel_id=1, source_target_pairs={{0,4},{4,0},{1,5},{5,1},{2,6},{6,2},{3,7},{7,3},{8,12},{12,8},{9,1... | collective-permute-start | bytes 786440 | tf_op jit(solution)/shard_map/ppermute | solution.py:125
  197.2 18.6 %all-to-all-start.5 = ((f32[4,64,8,128]{3,2,1,0:T(8,128)}), f32[4,64,8,128]{3,2,1,0:T(8,128)S(1)}, u32[]{:S(2)}, u32[]{:S(2)}) async-start(f32[4,64,8,128]{3,2,1,0:T(8,128)} %broadcast_in_dim.52), calls=%async_computation.5 | async-start | bytes 2097152 | tf_op jit(solution)/shard_map/all_to_all | solution.py:127
  200.9 36.2 %collective-permute-start.8 = (f32[1024,128]{1,0:T(8,128)S(1)}, f32[1024,128]{1,0:T(8,128)}, u32[]{:S(2)}, u32[]{:S(2)}) collective-permute-start(f32[1024,128]{1,0:T(8,128)S(1)} %bitcast.212), channel_id=1, source_target_pairs={{0,8},{8,0},{16,24},{24,16},{32,40},{40,32},{48,56},{56,48},{64,72... | collective-permute-start | bytes 1572872 | tf_op jit(solution)/shard_map/ppermute | solution.py:133
  215.8 5.2 %collective-permute-start.5 = (f32[64,8,128]{2,1,0:T(8,128)S(1)}, f32[64,8,128]{2,1,0:T(8,128)S(1)}, u32[]{:S(2)}, u32[]{:S(2)}) collective-permute-start(f32[64,8,128]{2,1,0:T(8,128)S(1)} %reduce_sum.58), channel_id=1, source_target_pairs={{0,4},{4,0},{1,5},{5,1},{2,6},{6,2},{3,7},{7,3},{8,12},{12,8},{9,1... | collective-permute-start | bytes 786440 | tf_op jit(solution)/shard_map/ppermute | solution.py:81
  223.4 6.4 %collective-permute-start.6 = (f32[64,8,128]{2,1,0:T(8,128)S(1)}, f32[64,8,128]{2,1,0:T(8,128)S(1)}, u32[]{:S(2)}, u32[]{:S(2)}) collective-permute-start(f32[64,8,128]{2,1,0:T(8,128)S(1)} %select_bitcast_fusion.4), channel_id=1, source_target_pairs={{0,4},{4,0},{1,5},{5,1},{2,6},{6,2},{3,7},{7,3},{8,12},{12,8},{9,1... | collective-permute-start | bytes 786440 | tf_op jit(solution)/shard_map/ppermute | solution.py:125
  227.4 28.4 %collective-permute-start.9 = (f32[1024,128]{1,0:T(8,128)S(1)}, f32[1024,128]{1,0:T(8,128)S(1)}, u32[]{:S(2)}, u32[]{:S(2)}) collective-permute-start(f32[1024,128]{1,0:T(8,128)S(1)} %bitcast.218), channel_id=1, source_target_pairs={{0,8},{8,0},{16,24},{24,16},{32,40},{40,32},{48,56},{56,48},{64,72... | collective-permute-start | bytes 1572872 | tf_op jit(solution)/shard_map/ppermute | solution.py:133
  230.9 17.9 %all-to-all-start.6 = ((f32[4,64,8,128]{3,2,1,0:T(8,128)}), f32[4,64,8,128]{3,2,1,0:T(8,128)S(1)}, u32[]{:S(2)}, u32[]{:S(2)}) async-start(f32[4,64,8,128]{3,2,1,0:T(8,128)} %broadcast_in_dim.53), calls=%async_computation.6 | async-start | bytes 2097152 | tf_op jit(solution)/shard_map/all_to_all | solution.py:127
  237.1 18.6 %collective-permute-start.10 = (f32[1024,128]{1,0:T(8,128)S(1)}, f32[1024,128]{1,0:T(8,128)S(1)}, u32[]{:S(2)}, u32[]{:S(2)}) collective-permute-start(f32[1024,128]{1,0:T(8,128)S(1)} %bitcast.229), channel_id=1, source_target_pairs={{0,8},{8,0},{16,24},{24,16},{32,40},{40,32},{48,56},{56,48},{64,72... | collective-permute-start | bytes 1572872 | tf_op jit(solution)/shard_map/ppermute | solution.py:133
  248.9 11.2 %copy-start.2 = (f32[256,128]{1,0:T(8,128)S(1)}, f32[256,128]{1,0:T(8,128)}, u32[]{:S(2)}) copy-start(f32[256,128]{1,0:T(8,128)} %constant_dynamic-update-slice_fusion.1) | copy-start | bytes 393220
  248.9 11.9 %collective-permute-start.11 = (f32[64,8,128]{2,1,0:T(8,128)S(1)}, f32[64,8,128]{2,1,0:T(8,128)S(1)}, u32[]{:S(2)}, u32[]{:S(2)}) collective-permute-start(f32[64,8,128]{2,1,0:T(8,128)S(1)} %reduce_sum.59), channel_id=1, source_target_pairs={{0,8},{8,0},{16,24},{24,16},{32,40},{40,32},{48,56},{56,48},{64,72... | collective-permute-start | bytes 786440 | tf_op jit(solution)/shard_map/ppermute | solution.py:135
  251.9 8.0 %collective-permute-start.7 = (f32[64,8,128]{2,1,0:T(8,128)S(1)}, f32[64,8,128]{2,1,0:T(8,128)S(1)}, u32[]{:S(2)}, u32[]{:S(2)}) collective-permute-start(f32[64,8,128]{2,1,0:T(8,128)S(1)} %reduce_sum.59), channel_id=1, source_target_pairs={{0,4},{4,0},{1,5},{5,1},{2,6},{6,2},{3,7},{7,3},{8,12},{12,8},{9,1... | collective-permute-start | bytes 786440 | tf_op jit(solution)/shard_map/ppermute | solution.py:81
  260.8 4.0 %collective-permute-start.12 = (f32[64,8,128]{2,1,0:T(8,128)S(1)}, f32[64,8,128]{2,1,0:T(8,128)S(1)}, u32[]{:S(2)}, u32[]{:S(2)}) collective-permute-start(f32[64,8,128]{2,1,0:T(8,128)S(1)} %collective-permute-done.11), channel_id=1, source_target_pairs={{0,4},{4,0},{1,5},{5,1},{2,6},{6,2},{3,7},{7,3},{8,12},{12,8},{9,1... | collective-permute-start | bytes 786440 | tf_op jit(solution)/shard_map/ppermute | solution.py:81
Sparse Core Ops, SparseCore 0:
  9.5 116.9 all-gather.2

commit v12 on v11

--- a/solution.py
+++ b/solution.py
@@ -77,8 +77,7 @@
     return total
 
 
-def whole_block(mine, first):
-    other = lax.ppermute(mine, "core", SWAP)
+def whole_block(mine, other, first):
     both = jnp.stack([jnp.where(first, mine, other), jnp.where(first, other, mine)], axis=1)
     return both.reshape(2 * mine.shape[0] * mine.shape[1], mine.shape[2])
 
@@ -95,6 +94,11 @@
     weight = {}
     names = [(j, k) for j in range(sections) for k in range(j + 1)]
     (tiles,) = pack_tiles(panel, inverse_columns, [names])
+    lane = jnp.arange(block_rows, dtype=jnp.int32)
+    apart = (lane // share % nc != lax.axis_index("core")).astype(jnp.int32)
+    moved = apart * (block_rows // nc) + lane // (nc * share) * share + lane % share
+    order = (moved[:, None] == lane[None, :]).astype(jnp.float32)
+    tiles = product(tiles.reshape(len(names) * share, block_rows), order).reshape(tiles.shape)
     gathered = lax.all_gather(tiles, "z")
     for i, name in enumerate(names):
         weight[name] = gathered[:, i].reshape(nz * share, block_rows)
@@ -119,20 +123,21 @@
 
     for k in range(sections):
         partial = product(weight[(k, k)], pending[k], ((0,), (0,)))
-        partial = partial.reshape(nx * nz, nc, share, columns)
-        keep = jnp.where(first, partial[:, 0], partial[:, 1])
-        give = jnp.where(first, partial[:, 1], partial[:, 0])
-        half = keep + lax.ppermute(give, "core", SWAP)
+        partial = partial.reshape(nc, nx * nz, share, columns)
+        half = partial[0] + lax.ppermute(partial[1], "core", SWAP)
         copies = jnp.broadcast_to(half[None], (nx,) + half.shape)
         mine = jnp.sum(lax.all_to_all(copies, "x", split_axis=0, concat_axis=0, tiled=True), axis=0)
-        solved = whole_block(mine, first)
+        other = lax.ppermute(mine, "core", SWAP)
+        apart = jnp.concatenate([mine, other], axis=0).reshape(block_rows, columns)
+        solved = whole_block(mine, other, first)
         for j in range(k + 1, sections):
-            pending[j] = pending[j] - product(weight[(j, k)], solved)
+            pending[j] = pending[j] - product(weight[(j, k)], apart)
         trade = [(i, i ^ 1) for i in range(nz)]
         if k + 1 < sections:
             traded = lax.ppermute(solved, "z", trade)
         else:
-            traded = whole_block(lax.ppermute(mine, "z", trade), first)
+            traded = lax.ppermute(mine, "z", trade)
+            traded = whole_block(traded, lax.ppermute(traded, "core", SWAP), first)
         update(0, k, solved)
         later.append((k, traded))
         while later and (later[0][0] + 2 <= k or k + 1 == sections):

time: 276 us -> 282 us (1.022)
  blocking collectives: 99.6 us -> 121 us
  waiting for transfers between devices: 59.1 us -> 41.2 us
  matrix products: 31.8 us -> 40.7 us
  local copies, waits for them, and re-layouts: 9.84 us -> 6.89 us
    all_to_all x0 -> x1, blocking collectives: none -> 22.1 us  [shards(): tops = lax.all_to_all(tops, 'z', split_axis=0, concat_axis=0, tiled=True)]
    all_gather x1, waiting for transfers between devices: 35.1 us -> 16.2 us  [shards(): gathered = lax.all_gather(tiles, 'z')]
    dot_general x23 -> x24, matrix products: 31.8 us -> 40.7 us  [product(): lax.dot_general(left, right, (contract, ((), ())), precision=lax.Precisio...]
    all_to_all x1 -> x0, starting transfers between devices: 3.53 us -> none  [shards(): tops = lax.all_to_all(tops, 'z', split_axis=0, concat_axis=0, tiled=True)]
  transfers between devices with their start and end apart: 18 -> 17, of which waited for: 8 -> 9; matrix products, arithmetic and copies ran while one was open for 12% -> 11% of each run, Pallas kernels for 0% -> 0%
where the time goes in v12:
time: 282 us; the launch traced here: 280 us
  blocking collectives  121 us (43%)
  starting transfers between devices  52.5 us (19%)
  waiting for transfers between devices  41.2 us (15%)
  matrix products  40.7 us (14%)
  between operations  14.1 us (5%)
  local copies, waits for them, and re-layouts  6.89 us (2%)
    all_to_all x1, blocking collectives, redistribute(): lax.all_to_all(sent[:, None], ROWS, split_axis=0, concat_axis=0, tiled=True)  63.9 us
    dot_general x24, matrix products, product(): lax.dot_general(left, right, (contract, ((), ())), precision=lax.Precisio...  40.7 us
    all_to_all x2, blocking collectives, shards(): lax.all_to_all(copies, 'x', split_axis=0, concat_axis=0, tiled=True)  35.2 us
    all_to_all x1, blocking collectives, shards(): tops = lax.all_to_all(tops, 'z', split_axis=0, concat_axis=0, tiled=True)  22.1 us
    all_gather x1, waiting for transfers between devices, shards(): gathered = lax.all_gather(tiles, 'z')  16.2 us
    ppermute x4, starting transfers between devices, shards(): half = partial[0] + lax.ppermute(partial[1], 'core', SWAP)  14.3 us
    all_to_all x2, waiting for transfers between devices, shards(): lax.all_to_all(copies, 'x', split_axis=0, concat_axis=0, tiled=True)  14.3 us
    ppermute x4, starting transfers between devices, shards(): other = lax.ppermute(mine, 'core', SWAP)  13.9 us
  transfers between devices with their start and end apart: 17, of which 9 were waited for; matrix products, arithmetic and copies ran while one was open for 11% of the time, Pallas kernels for 0%

profile of v12, /device:TPU:1, one launch (start us, length us, event | category | flops | bytes accessed | tf_op | source)
XLA Modules:
  0.0 280.3 jit_solution(5561822494721705640)
XLA Ops:
  8.4 3.4 %fusion.1 = f32[10,8,1024]{2,1,0:T(8,128)} fusion(f32[10,8,1024]{2,1,0:T(8,128)} %shard_map.64, s32[1024]{0:T(1024)S(1)} %fusion.72), kind=kOutput, calls=%fused_computation.2 | convolution fusion | flops 1007681536 | bytes 659456 | tf_op jit(solution)/shard_map/dot_general | solution.py:12
  12.6 5.0 %all-to-all-start = ((f32[64,4,256]{2,0,1:T(8,128)}), f32[64,4,256]{2,0,1:T(8,128)S(1)}, u32[]{:S(2)}, u32[]{:S(2)}) async-start(f32[64,4,256]{2,0,1:T(8,128)} %bitcast.194), calls=%async_computation | async-start | bytes 524288 | tf_op jit(solution)/shard_map/all_to_all | solution.py:46
  17.9 5.3 %all-to-all-done = f32[64,4,256]{2,0,1:T(8,128)S(1)} async-done(((f32[64,4,256]{2,0,1:T(8,128)}), f32[64,4,256]{2,0,1:T(8,128)S(1)}, u32[]{:S(2)}, u32[]{:S(2)}) %all-to-all-start) | async-done | bytes 262176 | tf_op jit(solution)/shard_map/all_to_all | solution.py:46
  24.8 63.9 %all_to_all.49 = f32[128,1,1152]{2,1,0:T(1,128)S(1)} all-to-all(f32[128,1,1152]{2,1,0:T(1,128)S(1)} %copy.27), channel_id=1, replica_groups=mesh['x'=4,'z'=16,'core'=2,'rhs'=4] {'x','z','core'}, dimensions={0} | all-to-all | bytes 1179648 | tf_op jit(solution)/shard_map/all_to_all | solution.py:67
  90.6 22.1 %all_to_all.50 = f32[16,32,128]{2,1,0:T(8,128)S(1)} all-to-all(f32[16,32,128]{2,1,0:T(8,128)S(1)} %bitcast.224), channel_id=1, replica_groups=mesh['x'=4,'z'=16,'core'=2,'rhs'=4] {'z'}, dimensions={0} | all-to-all | bytes 524288 | tf_op jit(solution)/shard_map/all_to_all | solution.py:110
  112.6 16.2 %all-gather.3.cloned.1.call-done = f32[160,8,1024]{2,1,0:T(8,128)} async-done(((f32[10,8,1024]{2,1,0:T(8,128)}), f32[160,8,1024]{2,1,0:T(8,128)}) %all-gather.3.cloned.1.call-update) | async-done | bytes 5242896 | tf_op jit(solution)/shard_map/all_gather | solution.py:102
  130.9 7.7 %collective-permute-start = (f32[64,8,128]{2,1,0:T(8,128)S(1)}, f32[64,8,128]{2,1,0:T(8,128)S(1)}, u32[]{:S(2)}, u32[]{:S(2)}) collective-permute-start(f32[64,8,128]{2,1,0:T(8,128)S(1)} %slice_bitcast_fusion.26), channel_id=1, source_target_pairs={{0,4},{4,0},{1,5},{5,1},{2,6},{6,2},{3,7},{7,3},{8,12},{12,8},{9,1... | collective-permute-start | bytes 786440 | tf_op jit(solution)/shard_map/ppermute | solution.py:127
  139.8 17.9 %all_to_all.51 = f32[4,64,8,128]{3,2,1,0:T(8,128)S(1)} all-to-all(f32[4,64,8,128]{3,2,1,0:T(8,128)S(1)} %broadcast_in_dim.50), channel_id=1, replica_groups=mesh['x'=4,'z'=16,'core'=2,'rhs'=4] {'x'}, dimensions={0} | all-to-all | bytes 2097152 | tf_op jit(solution)/shard_map/all_to_all | solution.py:129
  157.8 3.7 %collective-permute-start.1 = (f32[64,8,128]{2,1,0:T(8,128)S(1)}, f32[64,8,128]{2,1,0:T(8,128)S(1)}, u32[]{:S(2)}, u32[]{:S(2)}) collective-permute-start(f32[64,8,128]{2,1,0:T(8,128)S(1)} %reduce_sum.56), channel_id=1, source_target_pairs={{0,4},{4,0},{1,5},{5,1},{2,6},{6,2},{3,7},{7,3},{8,12},{12,8},{9,1... | collective-permute-start | bytes 786440 | tf_op jit(solution)/shard_map/ppermute | solution.py:130
  166.4 2.3 collective-permute-start.2
  170.0 17.3 %all_to_all.52 = f32[4,64,8,128]{3,2,1,0:T(8,128)S(1)} all-to-all(f32[4,64,8,128]{3,2,1,0:T(8,128)S(1)} %broadcast_in_dim.51), channel_id=1, replica_groups=mesh['x'=4,'z'=16,'core'=2,'rhs'=4] {'x'}, dimensions={0} | all-to-all | bytes 2097152 | tf_op jit(solution)/shard_map/all_to_all | solution.py:129
  187.3 3.3 %collective-permute-start.3 = (f32[64,8,128]{2,1,0:T(8,128)S(1)}, f32[64,8,128]{2,1,0:T(8,128)S(1)}, u32[]{:S(2)}, u32[]{:S(2)}) collective-permute-start(f32[64,8,128]{2,1,0:T(8,128)S(1)} %reduce_sum.57), channel_id=1, source_target_pairs={{0,4},{4,0},{1,5},{5,1},{2,6},{6,2},{3,7},{7,3},{8,12},{12,8},{9,1... | collective-permute-start | bytes 786440 | tf_op jit(solution)/shard_map/ppermute | solution.py:130
  197.0 2.3 collective-permute-start.4
  201.5 3.5 %all-to-all-start.5 = ((f32[4,64,8,128]{3,2,1,0:T(8,128)}), f32[4,64,8,128]{3,2,1,0:T(8,128)S(1)}, u32[]{:S(2)}, u32[]{:S(2)}) async-start(f32[4,64,8,128]{3,2,1,0:T(8,128)} %broadcast_in_dim.52), calls=%async_computation.5 | async-start | bytes 2097152 | tf_op jit(solution)/shard_map/all_to_all | solution.py:129
  205.2 2.5 collective-permute-start.8
  210.5 2.8 collective-permute-start.9
  213.3 6.6 %all-to-all-done.5 = f32[4,64,8,128]{3,2,1,0:T(8,128)S(1)} async-done(((f32[4,64,8,128]{3,2,1,0:T(8,128)}), f32[4,64,8,128]{3,2,1,0:T(8,128)S(1)}, u32[]{:S(2)}, u32[]{:S(2)}) %all-to-all-start.5) | async-done | bytes 1048608 | tf_op jit(solution)/shard_map/all_to_all | solution.py:129
  219.9 3.1 %collective-permute-start.5 = (f32[64,8,128]{2,1,0:T(8,128)S(1)}, f32[64,8,128]{2,1,0:T(8,128)S(1)}, u32[]{:S(2)}, u32[]{:S(2)}) collective-permute-start(f32[64,8,128]{2,1,0:T(8,128)S(1)} %reduce_sum.58), channel_id=1, source_target_pairs={{0,4},{4,0},{1,5},{5,1},{2,6},{6,2},{3,7},{7,3},{8,12},{12,8},{9,1... | collective-permute-start | bytes 786440 | tf_op jit(solution)/shard_map/ppermute | solution.py:130
  236.0 3.5 %all-to-all-start.6 = ((f32[4,64,8,128]{3,2,1,0:T(8,128)}), f32[4,64,8,128]{3,2,1,0:T(8,128)S(1)}, u32[]{:S(2)}, u32[]{:S(2)}) async-start(f32[4,64,8,128]{3,2,1,0:T(8,128)} %broadcast_in_dim.53), calls=%async_computation.6 | async-start | bytes 2097152 | tf_op jit(solution)/shard_map/all_to_all | solution.py:129
  239.7 2.5 collective-permute-start.10
  242.2 2.3 fusion.8
  246.6 7.6 %all-to-all-done.6 = f32[4,64,8,128]{3,2,1,0:T(8,128)S(1)} async-done(((f32[4,64,8,128]{3,2,1,0:T(8,128)}), f32[4,64,8,128]{3,2,1,0:T(8,128)S(1)}, u32[]{:S(2)}, u32[]{:S(2)}) %all-to-all-start.6) | async-done | bytes 1048608 | tf_op jit(solution)/shard_map/all_to_all | solution.py:129
  254.3 2.5 collective-permute-start.11
  256.8 3.7 %collective-permute-start.7 = (f32[64,8,128]{2,1,0:T(8,128)S(1)}, f32[64,8,128]{2,1,0:T(8,128)S(1)}, u32[]{:S(2)}, u32[]{:S(2)}) collective-permute-start(f32[64,8,128]{2,1,0:T(8,128)S(1)} %reduce_sum.59), channel_id=1, source_target_pairs={{0,4},{4,0},{1,5},{5,1},{2,6},{6,2},{3,7},{7,3},{8,12},{12,8},{9,1... | collective-permute-start | bytes 786440 | tf_op jit(solution)/shard_map/ppermute | solution.py:130
  (110 shorter events, 55.2 us)
Async XLA Ops:
  6.5 5.4 %copy-start.2 = (f32[64,1024]{1,0:T(8,128)S(1)}, f32[64,1024]{1,0:T(8,128)}, u32[]{:S(2)}) copy-start(f32[64,1024]{1,0:T(8,128)} %param.6) | copy-start | bytes 786436
  6.5 11.1 %copy-start.6 = (s32[1,128]{1,0:T(1,128)S(1)}, s32[1,128]{1,0:T(1,128)}, u32[]{:S(2)}) copy-start(s32[1,128]{1,0:T(1,128)} %param.8) | copy-start | bytes 1540
  6.5 11.2 %copy-start.4 = (s32[256]{0:T(256)S(1)}, s32[256]{0:T(256)}, u32[]{:S(2)}) copy-start(s32[256]{0:T(256)} %param.7) | copy-start | bytes 3076
  6.5 11.4 %copy-start.5 = (s32[256]{0:T(256)S(1)}, s32[256]{0:T(256)}, u32[]{:S(2)}) copy-start(s32[256]{0:T(256)} %param.9) | copy-start | bytes 3076
  6.5 122.2 %all-gather.3.cloned.1.call-start = ((), (), s32[]{:S(2)}) async-start(), calls=%async_computation.7 | async-start | bytes 5570560 | tf_op jit(solution)/shard_map/all_gather | solution.py:102
  12.6 10.5 %all-to-all-start = ((f32[64,4,256]{2,0,1:T(8,128)}), f32[64,4,256]{2,0,1:T(8,128)S(1)}, u32[]{:S(2)}, u32[]{:S(2)}) async-start(f32[64,4,256]{2,0,1:T(8,128)} %bitcast.194), calls=%async_computation | async-start | bytes 524288 | tf_op jit(solution)/shard_map/all_to_all | solution.py:46
  90.5 117.8 %copy-start = (f32[256,256]{1,0:T(8,128)}, f32[256,256]{1,0:T(8,128)S(1)}, u32[]{:S(2)}) copy-start(f32[256,256]{1,0:T(8,128)S(1)} %convolution_add_fusion) | copy-start | bytes 786436
  112.6 80.6 %copy-start.1 = (f32[16,32,128]{2,1,0:T(8,128)}, f32[16,32,128]{2,1,0:T(8,128)S(1)}, u32[]{:S(2)}) copy-start(f32[16,32,128]{2,1,0:T(8,128)S(1)} %all_to_all.50) | copy-start | bytes 786436
  130.9 8.9 %collective-permute-start = (f32[64,8,128]{2,1,0:T(8,128)S(1)}, f32[64,8,128]{2,1,0:T(8,128)S(1)}, u32[]{:S(2)}, u32[]{:S(2)}) collective-permute-start(f32[64,8,128]{2,1,0:T(8,128)S(1)} %slice_bitcast_fusion.26), channel_id=1, source_target_pairs={{0,4},{4,0},{1,5},{5,1},{2,6},{6,2},{3,7},{7,3},{8,12},{12,8},{9,1... | collective-permute-start | bytes 786440 | tf_op jit(solution)/shard_map/ppermute | solution.py:127
  157.8 4.9 %collective-permute-start.1 = (f32[64,8,128]{2,1,0:T(8,128)S(1)}, f32[64,8,128]{2,1,0:T(8,128)S(1)}, u32[]{:S(2)}, u32[]{:S(2)}) collective-permute-start(f32[64,8,128]{2,1,0:T(8,128)S(1)} %reduce_sum.56), channel_id=1, source_target_pairs={{0,4},{4,0},{1,5},{5,1},{2,6},{6,2},{3,7},{7,3},{8,12},{12,8},{9,1... | collective-permute-start | bytes 786440 | tf_op jit(solution)/shard_map/ppermute | solution.py:130
  166.4 3.4 %collective-permute-start.2 = (f32[64,8,128]{2,1,0:T(8,128)S(1)}, f32[64,8,128]{2,1,0:T(8,128)S(1)}, u32[]{:S(2)}, u32[]{:S(2)}) collective-permute-start(f32[64,8,128]{2,1,0:T(8,128)S(1)} %slice_bitcast_fusion.24), channel_id=1, source_target_pairs={{0,4},{4,0},{1,5},{5,1},{2,6},{6,2},{3,7},{7,3},{8,12},{12,8},{9,1... | collective-permute-start | bytes 786440 | tf_op jit(solution)/shard_map/ppermute | solution.py:127
  187.3 4.3 %collective-permute-start.3 = (f32[64,8,128]{2,1,0:T(8,128)S(1)}, f32[64,8,128]{2,1,0:T(8,128)S(1)}, u32[]{:S(2)}, u32[]{:S(2)}) collective-permute-start(f32[64,8,128]{2,1,0:T(8,128)S(1)} %reduce_sum.57), channel_id=1, source_target_pairs={{0,4},{4,0},{1,5},{5,1},{2,6},{6,2},{3,7},{7,3},{8,12},{12,8},{9,1... | collective-permute-start | bytes 786440 | tf_op jit(solution)/shard_map/ppermute | solution.py:130
  197.0 3.4 %collective-permute-start.4 = (f32[64,8,128]{2,1,0:T(8,128)S(1)}, f32[64,8,128]{2,1,0:T(8,128)S(1)}, u32[]{:S(2)}, u32[]{:S(2)}) collective-permute-start(f32[64,8,128]{2,1,0:T(8,128)S(1)} %slice_bitcast_fusion.22), channel_id=1, source_target_pairs={{0,4},{4,0},{1,5},{5,1},{2,6},{6,2},{3,7},{7,3},{8,12},{12,8},{9,1... | collective-permute-start | bytes 786440 | tf_op jit(solution)/shard_map/ppermute | solution.py:127
  201.5 18.3 %all-to-all-start.5 = ((f32[4,64,8,128]{3,2,1,0:T(8,128)}), f32[4,64,8,128]{3,2,1,0:T(8,128)S(1)}, u32[]{:S(2)}, u32[]{:S(2)}) async-start(f32[4,64,8,128]{3,2,1,0:T(8,128)} %broadcast_in_dim.52), calls=%async_computation.5 | async-start | bytes 2097152 | tf_op jit(solution)/shard_map/all_to_all | solution.py:129
  205.2 29.8 %collective-permute-start.8 = (f32[1024,128]{1,0:T(8,128)S(1)}, f32[1024,128]{1,0:T(8,128)}, u32[]{:S(2)}, u32[]{:S(2)}) collective-permute-start(f32[1024,128]{1,0:T(8,128)S(1)} %bitcast.221), channel_id=1, source_target_pairs={{0,8},{8,0},{16,24},{24,16},{32,40},{40,32},{48,56},{56,48},{64,72... | collective-permute-start | bytes 1572872 | tf_op jit(solution)/shard_map/ppermute | solution.py:137
  210.5 50.1 %collective-permute-start.9 = (f32[1024,128]{1,0:T(8,128)S(1)}, f32[1024,128]{1,0:T(8,128)}, u32[]{:S(2)}, u32[]{:S(2)}) collective-permute-start(f32[1024,128]{1,0:T(8,128)S(1)} %bitcast.211), channel_id=1, source_target_pairs={{0,8},{8,0},{16,24},{24,16},{32,40},{40,32},{48,56},{56,48},{64,72... | collective-permute-start | bytes 1572872 | tf_op jit(solution)/shard_map/ppermute | solution.py:137
  219.9 5.4 %collective-permute-start.5 = (f32[64,8,128]{2,1,0:T(8,128)S(1)}, f32[64,8,128]{2,1,0:T(8,128)S(1)}, u32[]{:S(2)}, u32[]{:S(2)}) collective-permute-start(f32[64,8,128]{2,1,0:T(8,128)S(1)} %reduce_sum.58), channel_id=1, source_target_pairs={{0,4},{4,0},{1,5},{5,1},{2,6},{6,2},{3,7},{7,3},{8,12},{12,8},{9,1... | collective-permute-start | bytes 786440 | tf_op jit(solution)/shard_map/ppermute | solution.py:130
  230.8 13.7 %copy-start.3 = (f32[256,128]{1,0:T(8,128)S(1)}, f32[256,128]{1,0:T(8,128)}, u32[]{:S(2)}) copy-start(f32[256,128]{1,0:T(8,128)} %constant_dynamic-update-slice_fusion.2) | copy-start | bytes 393220
  230.8 4.1 %collective-permute-start.6 = (f32[64,8,128]{2,1,0:T(8,128)S(1)}, f32[64,8,128]{2,1,0:T(8,128)S(1)}, u32[]{:S(2)}, u32[]{:S(2)}) collective-permute-start(f32[64,8,128]{2,1,0:T(8,128)S(1)} %slice_bitcast_fusion.20), channel_id=1, source_target_pairs={{0,4},{4,0},{1,5},{5,1},{2,6},{6,2},{3,7},{7,3},{8,12},{12,8},{9,1... | collective-permute-start | bytes 786440 | tf_op jit(solution)/shard_map/ppermute | solution.py:127
  236.0 18.2 %all-to-all-start.6 = ((f32[4,64,8,128]{3,2,1,0:T(8,128)}), f32[4,64,8,128]{3,2,1,0:T(8,128)S(1)}, u32[]{:S(2)}, u32[]{:S(2)}) async-start(f32[4,64,8,128]{3,2,1,0:T(8,128)} %broadcast_in_dim.53), calls=%async_computation.6 | async-start | bytes 2097152 | tf_op jit(solution)/shard_map/all_to_all | solution.py:129
  239.7 20.9 %collective-permute-start.10 = (f32[1024,128]{1,0:T(8,128)S(1)}, f32[1024,128]{1,0:T(8,128)S(1)}, u32[]{:S(2)}, u32[]{:S(2)}) collective-permute-start(f32[1024,128]{1,0:T(8,128)S(1)} %bitcast.214), channel_id=1, source_target_pairs={{0,8},{8,0},{16,24},{24,16},{32,40},{40,32},{48,56},{56,48},{64,72... | collective-permute-start | bytes 1572872 | tf_op jit(solution)/shard_map/ppermute | solution.py:137
  254.3 12.1 %collective-permute-start.11 = (f32[64,8,128]{2,1,0:T(8,128)S(1)}, f32[64,8,128]{2,1,0:T(8,128)S(1)}, u32[]{:S(2)}, u32[]{:S(2)}) collective-permute-start(f32[64,8,128]{2,1,0:T(8,128)S(1)} %reduce_sum.59), channel_id=1, source_target_pairs={{0,8},{8,0},{16,24},{24,16},{32,40},{40,32},{48,56},{56,48},{64,72... | collective-permute-start | bytes 786440 | tf_op jit(solution)/shard_map/ppermute | solution.py:139
  256.8 8.1 %collective-permute-start.7 = (f32[64,8,128]{2,1,0:T(8,128)S(1)}, f32[64,8,128]{2,1,0:T(8,128)S(1)}, u32[]{:S(2)}, u32[]{:S(2)}) collective-permute-start(f32[64,8,128]{2,1,0:T(8,128)S(1)} %reduce_sum.59), channel_id=1, source_target_pairs={{0,4},{4,0},{1,5},{5,1},{2,6},{6,2},{3,7},{7,3},{8,12},{12,8},{9,1... | collective-permute-start | bytes 786440 | tf_op jit(solution)/shard_map/ppermute | solution.py:130
  266.4 4.0 %collective-permute-start.12 = (f32[64,8,128]{2,1,0:T(8,128)S(1)}, f32[64,8,128]{2,1,0:T(8,128)S(1)}, u32[]{:S(2)}, u32[]{:S(2)}) collective-permute-start(f32[64,8,128]{2,1,0:T(8,128)S(1)} %collective-permute-done.11), channel_id=1, source_target_pairs={{0,4},{4,0},{1,5},{5,1},{2,6},{6,2},{3,7},{7,3},{8,12},{12,8},{9,1... | collective-permute-start | bytes 786440 | tf_op jit(solution)/shard_map/ppermute | solution.py:140
Sparse Core Ops, SparseCore 0:
  12.0 116.7 all-gather.2

commit v13 on v11

--- a/solution.py
+++ b/solution.py
@@ -111,6 +111,7 @@
     below = [jnp.where(even, left, right), jnp.where(even, right, left)]
     start = ((lax.axis_index("x") * nz + zi) * nc + lax.axis_index("core")) * share
     finished, later = [[], []], []
+    trade = [(i, i ^ 1) for i in range(nz)]
 
     def update(side, k, block):
         factor = panel[square:, k * block_rows : (k + 1) * block_rows]
@@ -123,18 +124,18 @@
         keep = jnp.where(first, partial[:, 0], partial[:, 1])
         give = jnp.where(first, partial[:, 1], partial[:, 0])
         half = keep + lax.ppermute(give, "core", SWAP)
+        if k > 0:
+            half, previous = lax.optimization_barrier((half, previous))
+            later.append((k - 1, lax.ppermute(previous, "z", trade)))
         copies = jnp.broadcast_to(half[None], (nx,) + half.shape)
         mine = jnp.sum(lax.all_to_all(copies, "x", split_axis=0, concat_axis=0, tiled=True), axis=0)
         solved = whole_block(mine, first)
         for j in range(k + 1, sections):
             pending[j] = pending[j] - product(weight[(j, k)], solved)
-        trade = [(i, i ^ 1) for i in range(nz)]
-        if k + 1 < sections:
-            traded = lax.ppermute(solved, "z", trade)
-        else:
-            traded = whole_block(lax.ppermute(mine, "z", trade), first)
         update(0, k, solved)
-        later.append((k, traded))
+        previous = solved
+        if k + 1 == sections:
+            later.append((k, whole_block(lax.ppermute(mine, "z", trade), first)))
         while later and (later[0][0] + 2 <= k or k + 1 == sections):
             old, block = later.pop(0)
             if old < k:

time: 276 us -> 289 us (1.047)
  waiting for transfers between devices: 59.1 us -> 67.5 us
  starting transfers between devices: 55.2 us -> 58.1 us
    ppermute x4, waiting for transfers between devices: 0.01 us -> 9.4 us  [the longest x3 9.36 us: shards(): later.append((k - 1, lax.ppermute(previous, 'z', trade)))]
  transfers between devices with their start and end apart: 18 -> 18, of which waited for: 8 -> 9; matrix products, arithmetic and copies ran while one was open for 12% -> 11% of each run, Pallas kernels for 0% -> 0%
where the time goes in v13:
time: 289 us; the launch traced here: 288 us
  blocking collectives  99.3 us (34%)
  waiting for transfers between devices  67.5 us (23%)
  starting transfers between devices  58.1 us (20%)
  matrix products  32.5 us (11%)
  between operations  14.1 us (5%)
  local copies, waits for them, and re-layouts  10.4 us (4%)
  other arithmetic  4.04 us (1%)
    all_to_all x1, blocking collectives, redistribute(): lax.all_to_all(sent[:, None], ROWS, split_axis=0, concat_axis=0, tiled=True)  63.9 us
    all_to_all x2, blocking collectives, shards(): lax.all_to_all(copies, 'x', split_axis=0, concat_axis=0, tiled=True)  35.4 us
    all_gather x1, waiting for transfers between devices, shards(): gathered = lax.all_gather(tiles, 'z')  35 us
    dot_general x23, matrix products, product(): lax.dot_general(left, right, (contract, ((), ())), precision=lax.Precisio...  32.5 us
    ppermute x5, starting transfers between devices, whole_block(): other = lax.ppermute(mine, 'core', SWAP)  18.2 us
    ppermute x4, starting transfers between devices, shards(): half = keep + lax.ppermute(give, 'core', SWAP)  13.6 us
    all_to_all x2, waiting for transfers between devices, shards(): lax.all_to_all(copies, 'x', split_axis=0, concat_axis=0, tiled=True)  13 us
    ppermute x3, waiting for transfers between devices, shards(): later.append((k - 1, lax.ppermute(previous, 'z', trade)))  9.36 us
  transfers between devices with their start and end apart: 18, of which 9 were waited for; matrix products, arithmetic and copies ran while one was open for 11% of the time, Pallas kernels for 0%

profile of v13, /device:TPU:1, one launch (start us, length us, event | category | flops | bytes accessed | tf_op | source)
XLA Modules:
  0.0 287.8 jit_solution(8267622870464391408)
XLA Ops:
  9.2 5.0 %all-to-all-start = ((f32[64,4,256]{2,0,1:T(8,128)}), f32[64,4,256]{2,0,1:T(8,128)S(1)}, u32[]{:S(2)}, u32[]{:S(2)}) async-start(f32[64,4,256]{2,0,1:T(8,128)} %bitcast.209), calls=%async_computation | async-start | bytes 524288 | tf_op jit(solution)/shard_map/all_to_all | solution.py:46
  14.4 5.3 %all-to-all-done = f32[64,4,256]{2,0,1:T(8,128)S(1)} async-done(((f32[64,4,256]{2,0,1:T(8,128)}), f32[64,4,256]{2,0,1:T(8,128)S(1)}, u32[]{:S(2)}, u32[]{:S(2)}) %all-to-all-start) | async-done | bytes 262176 | tf_op jit(solution)/shard_map/all_to_all | solution.py:46
  21.3 63.9 %all_to_all.49 = f32[128,1,1152]{2,1,0:T(1,128)S(1)} all-to-all(f32[128,1,1152]{2,1,0:T(1,128)S(1)} %copy.112), channel_id=1, replica_groups=mesh['x'=4,'z'=16,'core'=2,'rhs'=4] {'x','z','core'}, dimensions={0} | all-to-all | bytes 1179648 | tf_op jit(solution)/shard_map/all_to_all | solution.py:67
  87.8 3.5 %all-to-all-start.2 = ((f32[16,32,128]{2,1,0:T(8,128)}), f32[16,32,128]{2,1,0:T(8,128)S(1)}, u32[]{:S(2)}, u32[]{:S(2)}) async-start(f32[16,32,128]{2,1,0:T(8,128)} %bitcast.20), calls=%async_computation.2 | async-start | bytes 524288 | tf_op jit(solution)/shard_map/all_to_all | solution.py:106
  91.4 35.0 %all-gather.3.cloned.1.call-done = f32[160,8,1024]{2,1,0:T(8,128)} async-done(((f32[10,8,1024]{2,1,0:T(8,128)}), f32[160,8,1024]{2,1,0:T(8,128)}) %all-gather.3.cloned.1.call-update) | async-done | bytes 5242896 | tf_op jit(solution)/shard_map/all_gather | solution.py:98
  128.9 7.5 %collective-permute-start = (f32[64,8,128]{2,1,0:T(8,128)S(1)}, f32[64,8,128]{2,1,0:T(8,128)S(1)}, u32[]{:S(2)}, u32[]{:S(2)}) collective-permute-start(f32[64,8,128]{2,1,0:T(8,128)S(1)} %select_bitcast_fusion.13), channel_id=1, source_target_pairs={{0,4},{4,0},{1,5},{5,1},{2,6},{6,2},{3,7},{7,3},{8,12},{12,8},{9,1... | collective-permute-start | bytes 786440 | tf_op jit(solution)/shard_map/ppermute | solution.py:126
  137.6 18.1 %all_to_all.50 = f32[4,64,8,128]{3,2,1,0:T(8,128)S(1)} all-to-all(f32[4,64,8,128]{3,2,1,0:T(8,128)S(1)} %broadcast_in_dim.50), channel_id=1, replica_groups=mesh['x'=4,'z'=16,'core'=2,'rhs'=4] {'x'}, dimensions={0} | all-to-all | bytes 2097152 | tf_op jit(solution)/shard_map/all_to_all | solution.py:131
  155.8 3.7 %collective-permute-start.1 = (f32[64,8,128]{2,1,0:T(8,128)S(1)}, f32[64,8,128]{2,1,0:T(8,128)}, u32[]{:S(2)}, u32[]{:S(2)}) collective-permute-start(f32[64,8,128]{2,1,0:T(8,128)S(1)} %reduce_sum.56), channel_id=1, source_target_pairs={{0,4},{4,0},{1,5},{5,1},{2,6},{6,2},{3,7},{7,3},{8,12},{12,8},{9,1... | collective-permute-start | bytes 786440 | tf_op jit(solution)/shard_map/ppermute | solution.py:81
  164.2 2.3 collective-permute-start.2
  167.7 17.3 %all_to_all.51 = f32[4,64,8,128]{3,2,1,0:T(8,128)S(1)} all-to-all(f32[4,64,8,128]{3,2,1,0:T(8,128)S(1)} %broadcast_in_dim.51), channel_id=1, replica_groups=mesh['x'=4,'z'=16,'core'=2,'rhs'=4] {'x'}, dimensions={0} | all-to-all | bytes 2097152 | tf_op jit(solution)/shard_map/all_to_all | solution.py:131
  185.1 3.1 %collective-permute-start.3 = (f32[64,8,128]{2,1,0:T(8,128)S(1)}, f32[64,8,128]{2,1,0:T(8,128)S(1)}, u32[]{:S(2)}, u32[]{:S(2)}) collective-permute-start(f32[64,8,128]{2,1,0:T(8,128)S(1)} %reduce_sum.57), channel_id=1, source_target_pairs={{0,4},{4,0},{1,5},{5,1},{2,6},{6,2},{3,7},{7,3},{8,12},{12,8},{9,1... | collective-permute-start | bytes 786440 | tf_op jit(solution)/shard_map/ppermute | solution.py:81
  197.1 3.7 %all-to-all-start.5 = ((f32[4,64,8,128]{3,2,1,0:T(8,128)}), f32[4,64,8,128]{3,2,1,0:T(8,128)S(1)}, u32[]{:S(2)}, u32[]{:S(2)}) async-start(f32[4,64,8,128]{3,2,1,0:T(8,128)} %broadcast_in_dim.52), calls=%async_computation.5 | async-start | bytes 2097152 | tf_op jit(solution)/shard_map/all_to_all | solution.py:131
  202.7 13.0 %all-to-all-done.5 = f32[4,64,8,128]{3,2,1,0:T(8,128)S(1)} async-done(((f32[4,64,8,128]{3,2,1,0:T(8,128)}), f32[4,64,8,128]{3,2,1,0:T(8,128)S(1)}, u32[]{:S(2)}, u32[]{:S(2)}) %all-to-all-start.5) | async-done | bytes 1048608 | tf_op jit(solution)/shard_map/all_to_all | solution.py:131
  215.7 2.9 collective-permute-start.5
  227.3 3.1 %collective-permute-start.8 = (f32[1024,128]{1,0:T(8,128)S(1)}, f32[1024,128]{1,0:T(8,128)}, u32[]{:S(2)}, u32[]{:S(2)}) collective-permute-start(f32[1024,128]{1,0:T(8,128)S(1)} %bitcast.215), channel_id=1, source_target_pairs={{0,8},{8,0},{16,24},{24,16},{32,40},{40,32},{48,56},{56,48},{64,72... | collective-permute-start | bytes 1572872 | tf_op jit(solution)/shard_map/ppermute | solution.py:129
  231.5 3.5 %all-to-all-start.6 = ((f32[4,64,8,128]{3,2,1,0:T(8,128)}), f32[4,64,8,128]{3,2,1,0:T(8,128)S(1)}, u32[]{:S(2)}, u32[]{:S(2)}) async-start(f32[4,64,8,128]{3,2,1,0:T(8,128)} %broadcast_in_dim.53), calls=%async_computation.6 | async-start | bytes 2097152 | tf_op jit(solution)/shard_map/all_to_all | solution.py:131
  239.9 2.4 collective-permute-done.8
  242.3 3.1 %collective-permute-start.10 = (f32[1024,128]{1,0:T(8,128)S(1)}, f32[1024,128]{1,0:T(8,128)S(1)}, u32[]{:S(2)}, u32[]{:S(2)}) collective-permute-start(f32[1024,128]{1,0:T(8,128)S(1)} %bitcast.229), channel_id=1, source_target_pairs={{0,8},{8,0},{16,24},{24,16},{32,40},{40,32},{48,56},{56,48},{64,72... | collective-permute-start | bytes 1572872 | tf_op jit(solution)/shard_map/ppermute | solution.py:129
  245.4 2.9 fusion.4
  251.0 2.2 collective-permute-start.11
  253.2 4.6 %collective-permute-start.7 = (f32[64,8,128]{2,1,0:T(8,128)S(1)}, f32[64,8,128]{2,1,0:T(8,128)S(1)}, u32[]{:S(2)}, u32[]{:S(2)}) collective-permute-start(f32[64,8,128]{2,1,0:T(8,128)S(1)} %reduce_sum.59), channel_id=1, source_target_pairs={{0,4},{4,0},{1,5},{5,1},{2,6},{6,2},{3,7},{7,3},{8,12},{12,8},{9,1... | collective-permute-start | bytes 786440 | tf_op jit(solution)/shard_map/ppermute | solution.py:81
  257.9 6.9 %collective-permute-done.10 = f32[1024,128]{1,0:T(8,128)S(1)} collective-permute-done((f32[1024,128]{1,0:T(8,128)S(1)}, f32[1024,128]{1,0:T(8,128)S(1)}, u32[]{:S(2)}, u32[]{:S(2)}) %collective-permute-start.10) | collective-permute-done | bytes 524320 | tf_op jit(solution)/shard_map/ppermute | solution.py:129
  270.4 3.9 %collective-permute-start.12 = (f32[64,8,128]{2,1,0:T(8,128)S(1)}, f32[64,8,128]{2,1,0:T(8,128)S(1)}, u32[]{:S(2)}, u32[]{:S(2)}) collective-permute-start(f32[64,8,128]{2,1,0:T(8,128)S(1)} %collective-permute-done.11), channel_id=1, source_target_pairs={{0,4},{4,0},{1,5},{5,1},{2,6},{6,2},{3,7},{7,3},{8,12},{12,8},{9,1... | collective-permute-start | bytes 786440 | tf_op jit(solution)/shard_map/ppermute | solution.py:81
  274.3 2.7 fusion.6
  (110 shorter events, 54.2 us)
Async XLA Ops:
  6.5 1.9 copy-start.1
  6.5 7.6 %copy-start.4 = (s32[1,128]{1,0:T(1,128)S(1)}, s32[1,128]{1,0:T(1,128)}, u32[]{:S(2)}) copy-start(s32[1,128]{1,0:T(1,128)} %param.8) | copy-start | bytes 1540
  6.5 7.7 %copy-start.2 = (s32[256]{0:T(256)S(1)}, s32[256]{0:T(256)}, u32[]{:S(2)}) copy-start(s32[256]{0:T(256)} %param.7) | copy-start | bytes 3076
  6.5 7.9 %copy-start.3 = (s32[256]{0:T(256)S(1)}, s32[256]{0:T(256)}, u32[]{:S(2)}) copy-start(s32[256]{0:T(256)} %param.9) | copy-start | bytes 3076
  6.5 119.8 %all-gather.3.cloned.1.call-start = ((), (), s32[]{:S(2)}) async-start(), calls=%async_computation.7 | async-start | bytes 5570560 | tf_op jit(solution)/shard_map/all_gather | solution.py:98
  9.2 10.5 %all-to-all-start = ((f32[64,4,256]{2,0,1:T(8,128)}), f32[64,4,256]{2,0,1:T(8,128)S(1)}, u32[]{:S(2)}, u32[]{:S(2)}) async-start(f32[64,4,256]{2,0,1:T(8,128)} %bitcast.209), calls=%async_computation | async-start | bytes 524288 | tf_op jit(solution)/shard_map/all_to_all | solution.py:46
  87.8 40.4 %all-to-all-start.2 = ((f32[16,32,128]{2,1,0:T(8,128)}), f32[16,32,128]{2,1,0:T(8,128)S(1)}, u32[]{:S(2)}, u32[]{:S(2)}) async-start(f32[16,32,128]{2,1,0:T(8,128)} %bitcast.20), calls=%async_computation.2 | async-start | bytes 524288 | tf_op jit(solution)/shard_map/all_to_all | solution.py:106
  128.2 60.2 %copy-start = (f32[16,32,128]{2,1,0:T(8,128)}, f32[16,32,128]{2,1,0:T(8,128)S(1)}, u32[]{:S(2)}) copy-start(f32[16,32,128]{2,1,0:T(8,128)S(1)} %all-to-all-done.2) | copy-start | bytes 786436
  128.9 8.6 %collective-permute-start = (f32[64,8,128]{2,1,0:T(8,128)S(1)}, f32[64,8,128]{2,1,0:T(8,128)S(1)}, u32[]{:S(2)}, u32[]{:S(2)}) collective-permute-start(f32[64,8,128]{2,1,0:T(8,128)S(1)} %select_bitcast_fusion.13), channel_id=1, source_target_pairs={{0,4},{4,0},{1,5},{5,1},{2,6},{6,2},{3,7},{7,3},{8,12},{12,8},{9,1... | collective-permute-start | bytes 786440 | tf_op jit(solution)/shard_map/ppermute | solution.py:126
  155.8 5.0 %collective-permute-start.1 = (f32[64,8,128]{2,1,0:T(8,128)S(1)}, f32[64,8,128]{2,1,0:T(8,128)}, u32[]{:S(2)}, u32[]{:S(2)}) collective-permute-start(f32[64,8,128]{2,1,0:T(8,128)S(1)} %reduce_sum.56), channel_id=1, source_target_pairs={{0,4},{4,0},{1,5},{5,1},{2,6},{6,2},{3,7},{7,3},{8,12},{12,8},{9,1... | collective-permute-start | bytes 786440 | tf_op jit(solution)/shard_map/ppermute | solution.py:81
  164.2 3.4 %collective-permute-start.2 = (f32[64,8,128]{2,1,0:T(8,128)S(1)}, f32[64,8,128]{2,1,0:T(8,128)S(1)}, u32[]{:S(2)}, u32[]{:S(2)}) collective-permute-start(f32[64,8,128]{2,1,0:T(8,128)S(1)} %select_bitcast_fusion.10), channel_id=1, source_target_pairs={{0,4},{4,0},{1,5},{5,1},{2,6},{6,2},{3,7},{7,3},{8,12},{12,8},{9,1... | collective-permute-start | bytes 786440 | tf_op jit(solution)/shard_map/ppermute | solution.py:126
  185.1 5.0 %collective-permute-start.3 = (f32[64,8,128]{2,1,0:T(8,128)S(1)}, f32[64,8,128]{2,1,0:T(8,128)S(1)}, u32[]{:S(2)}, u32[]{:S(2)}) collective-permute-start(f32[64,8,128]{2,1,0:T(8,128)S(1)} %reduce_sum.57), channel_id=1, source_target_pairs={{0,4},{4,0},{1,5},{5,1},{2,6},{6,2},{3,7},{7,3},{8,12},{12,8},{9,1... | collective-permute-start | bytes 786440 | tf_op jit(solution)/shard_map/ppermute | solution.py:81
  192.5 3.4 %collective-permute-start.4 = (f32[64,8,128]{2,1,0:T(8,128)S(1)}, f32[64,8,128]{2,1,0:T(8,128)S(1)}, u32[]{:S(2)}, u32[]{:S(2)}) collective-permute-start(f32[64,8,128]{2,1,0:T(8,128)S(1)} %select_bitcast_fusion.7), channel_id=1, source_target_pairs={{0,4},{4,0},{1,5},{5,1},{2,6},{6,2},{3,7},{7,3},{8,12},{12,8},{9,1... | collective-permute-start | bytes 786440 | tf_op jit(solution)/shard_map/ppermute | solution.py:126
  197.1 18.6 %all-to-all-start.5 = ((f32[4,64,8,128]{3,2,1,0:T(8,128)}), f32[4,64,8,128]{3,2,1,0:T(8,128)S(1)}, u32[]{:S(2)}, u32[]{:S(2)}) async-start(f32[4,64,8,128]{3,2,1,0:T(8,128)} %broadcast_in_dim.52), calls=%async_computation.5 | async-start | bytes 2097152 | tf_op jit(solution)/shard_map/all_to_all | solution.py:131
  215.7 5.2 %collective-permute-start.5 = (f32[64,8,128]{2,1,0:T(8,128)S(1)}, f32[64,8,128]{2,1,0:T(8,128)S(1)}, u32[]{:S(2)}, u32[]{:S(2)}) collective-permute-start(f32[64,8,128]{2,1,0:T(8,128)S(1)} %reduce_sum.58), channel_id=1, source_target_pairs={{0,4},{4,0},{1,5},{5,1},{2,6},{6,2},{3,7},{7,3},{8,12},{12,8},{9,1... | collective-permute-start | bytes 786440 | tf_op jit(solution)/shard_map/ppermute | solution.py:81
  223.3 7.1 %collective-permute-start.6 = (f32[64,8,128]{2,1,0:T(8,128)S(1)}, f32[64,8,128]{2,1,0:T(8,128)S(1)}, u32[]{:S(2)}, u32[]{:S(2)}) collective-permute-start(f32[64,8,128]{2,1,0:T(8,128)S(1)} %select_bitcast_fusion.4), channel_id=1, source_target_pairs={{0,4},{4,0},{1,5},{5,1},{2,6},{6,2},{3,7},{7,3},{8,12},{12,8},{9,1... | collective-permute-start | bytes 786440 | tf_op jit(solution)/shard_map/ppermute | solution.py:126
  227.3 15.0 %collective-permute-start.8 = (f32[1024,128]{1,0:T(8,128)S(1)}, f32[1024,128]{1,0:T(8,128)}, u32[]{:S(2)}, u32[]{:S(2)}) collective-permute-start(f32[1024,128]{1,0:T(8,128)S(1)} %bitcast.215), channel_id=1, source_target_pairs={{0,8},{8,0},{16,24},{24,16},{32,40},{40,32},{48,56},{56,48},{64,72... | collective-permute-start | bytes 1572872 | tf_op jit(solution)/shard_map/ppermute | solution.py:129
  231.5 19.4 %all-to-all-start.6 = ((f32[4,64,8,128]{3,2,1,0:T(8,128)}), f32[4,64,8,128]{3,2,1,0:T(8,128)S(1)}, u32[]{:S(2)}, u32[]{:S(2)}) async-start(f32[4,64,8,128]{3,2,1,0:T(8,128)} %broadcast_in_dim.53), calls=%async_computation.6 | async-start | bytes 2097152 | tf_op jit(solution)/shard_map/all_to_all | solution.py:131
  237.7 20.2 %collective-permute-start.9 = (f32[1024,128]{1,0:T(8,128)S(1)}, f32[1024,128]{1,0:T(8,128)S(1)}, u32[]{:S(2)}, u32[]{:S(2)}) collective-permute-start(f32[1024,128]{1,0:T(8,128)S(1)} %bitcast.220), channel_id=1, source_target_pairs={{0,8},{8,0},{16,24},{24,16},{32,40},{40,32},{48,56},{56,48},{64,72... | collective-permute-start | bytes 1572872 | tf_op jit(solution)/shard_map/ppermute | solution.py:129
  242.3 22.5 %collective-permute-start.10 = (f32[1024,128]{1,0:T(8,128)S(1)}, f32[1024,128]{1,0:T(8,128)S(1)}, u32[]{:S(2)}, u32[]{:S(2)}) collective-permute-start(f32[1024,128]{1,0:T(8,128)S(1)} %bitcast.229), channel_id=1, source_target_pairs={{0,8},{8,0},{16,24},{24,16},{32,40},{40,32},{48,56},{56,48},{64,72... | collective-permute-start | bytes 1572872 | tf_op jit(solution)/shard_map/ppermute | solution.py:129
  251.0 19.4 %collective-permute-start.11 = (f32[64,8,128]{2,1,0:T(8,128)S(1)}, f32[64,8,128]{2,1,0:T(8,128)S(1)}, u32[]{:S(2)}, u32[]{:S(2)}) collective-permute-start(f32[64,8,128]{2,1,0:T(8,128)S(1)} %reduce_sum.59), channel_id=1, source_target_pairs={{0,8},{8,0},{16,24},{24,16},{32,40},{40,32},{48,56},{56,48},{64,72... | collective-permute-start | bytes 786440 | tf_op jit(solution)/shard_map/ppermute | solution.py:138
  253.2 15.7 %collective-permute-start.7 = (f32[64,8,128]{2,1,0:T(8,128)S(1)}, f32[64,8,128]{2,1,0:T(8,128)S(1)}, u32[]{:S(2)}, u32[]{:S(2)}) collective-permute-start(f32[64,8,128]{2,1,0:T(8,128)S(1)} %reduce_sum.59), channel_id=1, source_target_pairs={{0,4},{4,0},{1,5},{5,1},{2,6},{6,2},{3,7},{7,3},{8,12},{12,8},{9,1... | collective-permute-start | bytes 786440 | tf_op jit(solution)/shard_map/ppermute | solution.py:81
  270.4 6.6 %collective-permute-start.12 = (f32[64,8,128]{2,1,0:T(8,128)S(1)}, f32[64,8,128]{2,1,0:T(8,128)S(1)}, u32[]{:S(2)}, u32[]{:S(2)}) collective-permute-start(f32[64,8,128]{2,1,0:T(8,128)S(1)} %collective-permute-done.11), channel_id=1, source_target_pairs={{0,4},{4,0},{1,5},{5,1},{2,6},{6,2},{3,7},{7,3},{8,12},{12,8},{9,1... | collective-permute-start | bytes 786440 | tf_op jit(solution)/shard_map/ppermute | solution.py:81
Sparse Core Ops, SparseCore 0:
  9.5 116.8 all-gather.2

commit v14 on v11

--- a/solution.py
+++ b/solution.py
@@ -135,7 +135,7 @@
             traded = whole_block(lax.ppermute(mine, "z", trade), first)
         update(0, k, solved)
         later.append((k, traded))
-        while later and (later[0][0] + 2 <= k or k + 1 == sections):
+        while later and (later[0][0] + 1 <= k or k + 1 == sections):
             old, block = later.pop(0)
             if old < k:
                 block = lax.optimization_barrier((mine, block))[1]

time: 276 us -> 279 us (1.011)
  waiting for transfers between devices: 59.1 us -> 62.6 us
    ppermute x3, waiting for transfers between devices: 0.01 us -> 6.33 us  [shards(): traded = lax.ppermute(solved, 'z', trade)]
    all_to_all x2, waiting for transfers between devices: 13.8 us -> 8.47 us  [shards(): lax.all_to_all(copies, 'x', split_axis=0, concat_axis=0, tiled=True)]
  transfers between devices with their start and end apart: 18 -> 18, of which waited for: 8 -> 10; matrix products, arithmetic and copies ran while one was open for 12% -> 11% of each run, Pallas kernels for 0% -> 0%
where the time goes in v14:
time: 279 us; the launch traced here: 277 us
  blocking collectives  99.6 us (36%)
  waiting for transfers between devices  62.6 us (22%)
  starting transfers between devices  57 us (20%)
  matrix products  31.2 us (11%)
  between operations  14.1 us (5%)
  local copies, waits for them, and re-layouts  8.66 us (3%)
    all_to_all x1, blocking collectives, redistribute(): lax.all_to_all(sent[:, None], ROWS, split_axis=0, concat_axis=0, tiled=True)  63.9 us
    all_to_all x2, blocking collectives, shards(): lax.all_to_all(copies, 'x', split_axis=0, concat_axis=0, tiled=True)  35.7 us
    all_gather x1, waiting for transfers between devices, shards(): gathered = lax.all_gather(tiles, 'z')  35.1 us
    dot_general x23, matrix products, product(): lax.dot_general(left, right, (contract, ((), ())), precision=lax.Precisio...  31.2 us
    ppermute x5, starting transfers between devices, whole_block(): other = lax.ppermute(mine, 'core', SWAP)  17.7 us
    ppermute x4, starting transfers between devices, shards(): half = keep + lax.ppermute(give, 'core', SWAP)  13.4 us
    all_to_all x2, waiting for transfers between devices, shards(): lax.all_to_all(copies, 'x', split_axis=0, concat_axis=0, tiled=True)  8.47 us
    ppermute x3, starting transfers between devices, shards(): traded = lax.ppermute(solved, 'z', trade)  7.44 us
  transfers between devices with their start and end apart: 18, of which 10 were waited for; matrix products, arithmetic and copies ran while one was open for 11% of the time, Pallas kernels for 0%

profile of v14, /device:TPU:1, one launch (start us, length us, event | category | flops | bytes accessed | tf_op | source)
XLA Modules:
  0.0 277.2 jit_solution(13282789083758714403)
XLA Ops:
  9.2 5.0 %all-to-all-start = ((f32[64,4,256]{2,0,1:T(8,128)}), f32[64,4,256]{2,0,1:T(8,128)S(1)}, u32[]{:S(2)}, u32[]{:S(2)}) async-start(f32[64,4,256]{2,0,1:T(8,128)} %bitcast.209), calls=%async_computation | async-start | bytes 524288 | tf_op jit(solution)/shard_map/all_to_all | solution.py:46
  14.4 5.3 %all-to-all-done = f32[64,4,256]{2,0,1:T(8,128)S(1)} async-done(((f32[64,4,256]{2,0,1:T(8,128)}), f32[64,4,256]{2,0,1:T(8,128)S(1)}, u32[]{:S(2)}, u32[]{:S(2)}) %all-to-all-start) | async-done | bytes 262176 | tf_op jit(solution)/shard_map/all_to_all | solution.py:46
  21.3 63.9 %all_to_all.49 = f32[128,1,1152]{2,1,0:T(1,128)S(1)} all-to-all(f32[128,1,1152]{2,1,0:T(1,128)S(1)} %copy.112), channel_id=1, replica_groups=mesh['x'=4,'z'=16,'core'=2,'rhs'=4] {'x','z','core'}, dimensions={0} | all-to-all | bytes 1179648 | tf_op jit(solution)/shard_map/all_to_all | solution.py:67
  87.8 3.5 %all-to-all-start.2 = ((f32[16,32,128]{2,1,0:T(8,128)}), f32[16,32,128]{2,1,0:T(8,128)S(1)}, u32[]{:S(2)}, u32[]{:S(2)}) async-start(f32[16,32,128]{2,1,0:T(8,128)} %bitcast.20), calls=%async_computation.2 | async-start | bytes 524288 | tf_op jit(solution)/shard_map/all_to_all | solution.py:106
  91.4 35.1 %all-gather.3.cloned.1.call-done = f32[160,8,1024]{2,1,0:T(8,128)} async-done(((f32[10,8,1024]{2,1,0:T(8,128)}), f32[160,8,1024]{2,1,0:T(8,128)}) %all-gather.3.cloned.1.call-update) | async-done | bytes 5242896 | tf_op jit(solution)/shard_map/all_gather | solution.py:98
  129.0 7.1 %collective-permute-start = (f32[64,8,128]{2,1,0:T(8,128)S(1)}, f32[64,8,128]{2,1,0:T(8,128)S(1)}, u32[]{:S(2)}, u32[]{:S(2)}) collective-permute-start(f32[64,8,128]{2,1,0:T(8,128)S(1)} %select_bitcast_fusion.13), channel_id=1, source_target_pairs={{0,4},{4,0},{1,5},{5,1},{2,6},{6,2},{3,7},{7,3},{8,12},{12,8},{9,1... | collective-permute-start | bytes 786440 | tf_op jit(solution)/shard_map/ppermute | solution.py:125
  137.4 18.5 %all_to_all.50 = f32[4,64,8,128]{3,2,1,0:T(8,128)S(1)} all-to-all(f32[4,64,8,128]{3,2,1,0:T(8,128)S(1)} %broadcast_in_dim.50), channel_id=1, replica_groups=mesh['x'=4,'z'=16,'core'=2,'rhs'=4] {'x'}, dimensions={0} | all-to-all | bytes 2097152 | tf_op jit(solution)/shard_map/all_to_all | solution.py:127
  155.9 3.7 %collective-permute-start.1 = (f32[64,8,128]{2,1,0:T(8,128)S(1)}, f32[64,8,128]{2,1,0:T(8,128)S(1)}, u32[]{:S(2)}, u32[]{:S(2)}) collective-permute-start(f32[64,8,128]{2,1,0:T(8,128)S(1)} %reduce_sum.56), channel_id=1, source_target_pairs={{0,4},{4,0},{1,5},{5,1},{2,6},{6,2},{3,7},{7,3},{8,12},{12,8},{9,1... | collective-permute-start | bytes 786440 | tf_op jit(solution)/shard_map/ppermute | solution.py:81
  163.2 2.3 collective-permute-start.2
  166.8 17.3 %all_to_all.51 = f32[4,64,8,128]{3,2,1,0:T(8,128)S(1)} all-to-all(f32[4,64,8,128]{3,2,1,0:T(8,128)S(1)} %broadcast_in_dim.51), channel_id=1, replica_groups=mesh['x'=4,'z'=16,'core'=2,'rhs'=4] {'x'}, dimensions={0} | all-to-all | bytes 2097152 | tf_op jit(solution)/shard_map/all_to_all | solution.py:127
  184.1 3.1 %collective-permute-start.3 = (f32[64,8,128]{2,1,0:T(8,128)S(1)}, f32[64,8,128]{2,1,0:T(8,128)S(1)}, u32[]{:S(2)}, u32[]{:S(2)}) collective-permute-start(f32[64,8,128]{2,1,0:T(8,128)S(1)} %reduce_sum.57), channel_id=1, source_target_pairs={{0,4},{4,0},{1,5},{5,1},{2,6},{6,2},{3,7},{7,3},{8,12},{12,8},{9,1... | collective-permute-start | bytes 786440 | tf_op jit(solution)/shard_map/ppermute | solution.py:81
  196.1 3.5 %all-to-all-start.5 = ((f32[4,64,8,128]{3,2,1,0:T(8,128)}), f32[4,64,8,128]{3,2,1,0:T(8,128)S(1)}, u32[]{:S(2)}, u32[]{:S(2)}) async-start(f32[4,64,8,128]{3,2,1,0:T(8,128)} %broadcast_in_dim.52), calls=%async_computation.5 | async-start | bytes 2097152 | tf_op jit(solution)/shard_map/all_to_all | solution.py:127
  199.8 2.6 collective-permute-start.8
  206.2 8.5 %all-to-all-done.5 = f32[4,64,8,128]{3,2,1,0:T(8,128)S(1)} async-done(((f32[4,64,8,128]{3,2,1,0:T(8,128)}), f32[4,64,8,128]{3,2,1,0:T(8,128)S(1)}, u32[]{:S(2)}, u32[]{:S(2)}) %all-to-all-start.5) | async-done | bytes 1048608 | tf_op jit(solution)/shard_map/all_to_all | solution.py:127
  214.7 2.9 %collective-permute-start.5 = (f32[64,8,128]{2,1,0:T(8,128)S(1)}, f32[64,8,128]{2,1,0:T(8,128)S(1)}, u32[]{:S(2)}, u32[]{:S(2)}) collective-permute-start(f32[64,8,128]{2,1,0:T(8,128)S(1)} %reduce_sum.58), channel_id=1, source_target_pairs={{0,4},{4,0},{1,5},{5,1},{2,6},{6,2},{3,7},{7,3},{8,12},{12,8},{9,1... | collective-permute-start | bytes 786440 | tf_op jit(solution)/shard_map/ppermute | solution.py:81
  224.4 2.2 fusion.4
  226.6 2.4 collective-permute-start.9
  230.2 3.5 %all-to-all-start.6 = ((f32[4,64,8,128]{3,2,1,0:T(8,128)}), f32[4,64,8,128]{3,2,1,0:T(8,128)S(1)}, u32[]{:S(2)}, u32[]{:S(2)}) async-start(f32[4,64,8,128]{3,2,1,0:T(8,128)} %broadcast_in_dim.53), calls=%async_computation.6 | async-start | bytes 2097152 | tf_op jit(solution)/shard_map/all_to_all | solution.py:127
  235.8 5.7 %collective-permute-done.9 = f32[1024,128]{1,0:T(8,128)S(1)} collective-permute-done((f32[1024,128]{1,0:T(8,128)S(1)}, f32[1024,128]{1,0:T(8,128)S(1)}, u32[]{:S(2)}, u32[]{:S(2)}) %collective-permute-start.9) | collective-permute-done | bytes 524320 | tf_op jit(solution)/shard_map/ppermute | solution.py:133
  241.5 2.4 collective-permute-start.10
  248.2 2.9 %collective-permute-start.11 = (f32[64,8,128]{2,1,0:T(8,128)S(1)}, f32[64,8,128]{2,1,0:T(8,128)S(1)}, u32[]{:S(2)}, u32[]{:S(2)}) collective-permute-start(f32[64,8,128]{2,1,0:T(8,128)S(1)} %reduce_sum.59), channel_id=1, source_target_pairs={{0,8},{8,0},{16,24},{24,16},{32,40},{40,32},{48,56},{56,48},{64,72... | collective-permute-start | bytes 786440 | tf_op jit(solution)/shard_map/ppermute | solution.py:135
  251.1 3.8 %collective-permute-start.7 = (f32[64,8,128]{2,1,0:T(8,128)S(1)}, f32[64,8,128]{2,1,0:T(8,128)S(1)}, u32[]{:S(2)}, u32[]{:S(2)}) collective-permute-start(f32[64,8,128]{2,1,0:T(8,128)S(1)} %reduce_sum.59), channel_id=1, source_target_pairs={{0,4},{4,0},{1,5},{5,1},{2,6},{6,2},{3,7},{7,3},{8,12},{12,8},{9,1... | collective-permute-start | bytes 786440 | tf_op jit(solution)/shard_map/ppermute | solution.py:81
  258.4 2.7 collective-permute-done.11
  261.1 4.2 %collective-permute-start.12 = (f32[64,8,128]{2,1,0:T(8,128)S(1)}, f32[64,8,128]{2,1,0:T(8,128)S(1)}, u32[]{:S(2)}, u32[]{:S(2)}) collective-permute-start(f32[64,8,128]{2,1,0:T(8,128)S(1)} %collective-permute-done.11), channel_id=1, source_target_pairs={{0,4},{4,0},{1,5},{5,1},{2,6},{6,2},{3,7},{7,3},{8,12},{12,8},{9,1... | collective-permute-start | bytes 786440 | tf_op jit(solution)/shard_map/ppermute | solution.py:81
  (112 shorter events, 51.0 us)
Async XLA Ops:
  6.5 1.9 copy-start.1
  6.5 7.6 %copy-start.5 = (s32[1,128]{1,0:T(1,128)S(1)}, s32[1,128]{1,0:T(1,128)}, u32[]{:S(2)}) copy-start(s32[1,128]{1,0:T(1,128)} %param.8) | copy-start | bytes 1540
  6.5 7.7 %copy-start.3 = (s32[256]{0:T(256)S(1)}, s32[256]{0:T(256)}, u32[]{:S(2)}) copy-start(s32[256]{0:T(256)} %param.7) | copy-start | bytes 3076
  6.5 7.9 %copy-start.4 = (s32[256]{0:T(256)S(1)}, s32[256]{0:T(256)}, u32[]{:S(2)}) copy-start(s32[256]{0:T(256)} %param.9) | copy-start | bytes 3076
  6.5 119.9 %all-gather.3.cloned.1.call-start = ((), (), s32[]{:S(2)}) async-start(), calls=%async_computation.7 | async-start | bytes 5570560 | tf_op jit(solution)/shard_map/all_gather | solution.py:98
  9.2 10.5 %all-to-all-start = ((f32[64,4,256]{2,0,1:T(8,128)}), f32[64,4,256]{2,0,1:T(8,128)S(1)}, u32[]{:S(2)}, u32[]{:S(2)}) async-start(f32[64,4,256]{2,0,1:T(8,128)} %bitcast.209), calls=%async_computation | async-start | bytes 524288 | tf_op jit(solution)/shard_map/all_to_all | solution.py:46
  87.8 40.5 %all-to-all-start.2 = ((f32[16,32,128]{2,1,0:T(8,128)}), f32[16,32,128]{2,1,0:T(8,128)S(1)}, u32[]{:S(2)}, u32[]{:S(2)}) async-start(f32[16,32,128]{2,1,0:T(8,128)} %bitcast.20), calls=%async_computation.2 | async-start | bytes 524288 | tf_op jit(solution)/shard_map/all_to_all | solution.py:106
  128.3 59.1 %copy-start = (f32[16,32,128]{2,1,0:T(8,128)}, f32[16,32,128]{2,1,0:T(8,128)S(1)}, u32[]{:S(2)}) copy-start(f32[16,32,128]{2,1,0:T(8,128)S(1)} %all-to-all-done.2) | copy-start | bytes 786436
  129.0 8.3 %collective-permute-start = (f32[64,8,128]{2,1,0:T(8,128)S(1)}, f32[64,8,128]{2,1,0:T(8,128)S(1)}, u32[]{:S(2)}, u32[]{:S(2)}) collective-permute-start(f32[64,8,128]{2,1,0:T(8,128)S(1)} %select_bitcast_fusion.13), channel_id=1, source_target_pairs={{0,4},{4,0},{1,5},{5,1},{2,6},{6,2},{3,7},{7,3},{8,12},{12,8},{9,1... | collective-permute-start | bytes 786440 | tf_op jit(solution)/shard_map/ppermute | solution.py:125
  155.9 4.9 %collective-permute-start.1 = (f32[64,8,128]{2,1,0:T(8,128)S(1)}, f32[64,8,128]{2,1,0:T(8,128)S(1)}, u32[]{:S(2)}, u32[]{:S(2)}) collective-permute-start(f32[64,8,128]{2,1,0:T(8,128)S(1)} %reduce_sum.56), channel_id=1, source_target_pairs={{0,4},{4,0},{1,5},{5,1},{2,6},{6,2},{3,7},{7,3},{8,12},{12,8},{9,1... | collective-permute-start | bytes 786440 | tf_op jit(solution)/shard_map/ppermute | solution.py:81
  163.2 3.4 %collective-permute-start.2 = (f32[64,8,128]{2,1,0:T(8,128)S(1)}, f32[64,8,128]{2,1,0:T(8,128)S(1)}, u32[]{:S(2)}, u32[]{:S(2)}) collective-permute-start(f32[64,8,128]{2,1,0:T(8,128)S(1)} %select_bitcast_fusion.10), channel_id=1, source_target_pairs={{0,4},{4,0},{1,5},{5,1},{2,6},{6,2},{3,7},{7,3},{8,12},{12,8},{9,1... | collective-permute-start | bytes 786440 | tf_op jit(solution)/shard_map/ppermute | solution.py:125
  184.1 5.0 %collective-permute-start.3 = (f32[64,8,128]{2,1,0:T(8,128)S(1)}, f32[64,8,128]{2,1,0:T(8,128)S(1)}, u32[]{:S(2)}, u32[]{:S(2)}) collective-permute-start(f32[64,8,128]{2,1,0:T(8,128)S(1)} %reduce_sum.57), channel_id=1, source_target_pairs={{0,4},{4,0},{1,5},{5,1},{2,6},{6,2},{3,7},{7,3},{8,12},{12,8},{9,1... | collective-permute-start | bytes 786440 | tf_op jit(solution)/shard_map/ppermute | solution.py:81
  191.5 3.4 %collective-permute-start.4 = (f32[64,8,128]{2,1,0:T(8,128)S(1)}, f32[64,8,128]{2,1,0:T(8,128)S(1)}, u32[]{:S(2)}, u32[]{:S(2)}) collective-permute-start(f32[64,8,128]{2,1,0:T(8,128)S(1)} %select_bitcast_fusion.7), channel_id=1, source_target_pairs={{0,4},{4,0},{1,5},{5,1},{2,6},{6,2},{3,7},{7,3},{8,12},{12,8},{9,1... | collective-permute-start | bytes 786440 | tf_op jit(solution)/shard_map/ppermute | solution.py:125
  196.1 18.6 %all-to-all-start.5 = ((f32[4,64,8,128]{3,2,1,0:T(8,128)}), f32[4,64,8,128]{3,2,1,0:T(8,128)S(1)}, u32[]{:S(2)}, u32[]{:S(2)}) async-start(f32[4,64,8,128]{3,2,1,0:T(8,128)} %broadcast_in_dim.52), calls=%async_computation.5 | async-start | bytes 2097152 | tf_op jit(solution)/shard_map/all_to_all | solution.py:127
  199.8 18.4 %collective-permute-start.8 = (f32[1024,128]{1,0:T(8,128)S(1)}, f32[1024,128]{1,0:T(8,128)}, u32[]{:S(2)}, u32[]{:S(2)}) collective-permute-start(f32[1024,128]{1,0:T(8,128)S(1)} %bitcast.212), channel_id=1, source_target_pairs={{0,8},{8,0},{16,24},{24,16},{32,40},{40,32},{48,56},{56,48},{64,72... | collective-permute-start | bytes 1572872 | tf_op jit(solution)/shard_map/ppermute | solution.py:133
  214.7 5.2 %collective-permute-start.5 = (f32[64,8,128]{2,1,0:T(8,128)S(1)}, f32[64,8,128]{2,1,0:T(8,128)S(1)}, u32[]{:S(2)}, u32[]{:S(2)}) collective-permute-start(f32[64,8,128]{2,1,0:T(8,128)S(1)} %reduce_sum.58), channel_id=1, source_target_pairs={{0,4},{4,0},{1,5},{5,1},{2,6},{6,2},{3,7},{7,3},{8,12},{12,8},{9,1... | collective-permute-start | bytes 786440 | tf_op jit(solution)/shard_map/ppermute | solution.py:81
  222.3 13.5 %copy-start.2 = (f32[256,128]{1,0:T(8,128)S(1)}, f32[256,128]{1,0:T(8,128)}, u32[]{:S(2)}) copy-start(f32[256,128]{1,0:T(8,128)} %constant_dynamic-update-slice_fusion.3) | copy-start | bytes 393220
  222.3 6.7 %collective-permute-start.6 = (f32[64,8,128]{2,1,0:T(8,128)S(1)}, f32[64,8,128]{2,1,0:T(8,128)S(1)}, u32[]{:S(2)}, u32[]{:S(2)}) collective-permute-start(f32[64,8,128]{2,1,0:T(8,128)S(1)} %select_bitcast_fusion.4), channel_id=1, source_target_pairs={{0,4},{4,0},{1,5},{5,1},{2,6},{6,2},{3,7},{7,3},{8,12},{12,8},{9,1... | collective-permute-start | bytes 786440 | tf_op jit(solution)/shard_map/ppermute | solution.py:125
  226.6 14.9 %collective-permute-start.9 = (f32[1024,128]{1,0:T(8,128)S(1)}, f32[1024,128]{1,0:T(8,128)S(1)}, u32[]{:S(2)}, u32[]{:S(2)}) collective-permute-start(f32[1024,128]{1,0:T(8,128)S(1)} %bitcast.218), channel_id=1, source_target_pairs={{0,8},{8,0},{16,24},{24,16},{32,40},{40,32},{48,56},{56,48},{64,72... | collective-permute-start | bytes 1572872 | tf_op jit(solution)/shard_map/ppermute | solution.py:133
  230.2 17.9 %all-to-all-start.6 = ((f32[4,64,8,128]{3,2,1,0:T(8,128)}), f32[4,64,8,128]{3,2,1,0:T(8,128)S(1)}, u32[]{:S(2)}, u32[]{:S(2)}) async-start(f32[4,64,8,128]{3,2,1,0:T(8,128)} %broadcast_in_dim.53), calls=%async_computation.6 | async-start | bytes 2097152 | tf_op jit(solution)/shard_map/all_to_all | solution.py:127
  241.5 14.0 %collective-permute-start.10 = (f32[1024,128]{1,0:T(8,128)S(1)}, f32[1024,128]{1,0:T(8,128)S(1)}, u32[]{:S(2)}, u32[]{:S(2)}) collective-permute-start(f32[1024,128]{1,0:T(8,128)S(1)} %bitcast.229), channel_id=1, source_target_pairs={{0,8},{8,0},{16,24},{24,16},{32,40},{40,32},{48,56},{56,48},{64,72... | collective-permute-start | bytes 1572872 | tf_op jit(solution)/shard_map/ppermute | solution.py:133
  248.2 12.9 %collective-permute-start.11 = (f32[64,8,128]{2,1,0:T(8,128)S(1)}, f32[64,8,128]{2,1,0:T(8,128)S(1)}, u32[]{:S(2)}, u32[]{:S(2)}) collective-permute-start(f32[64,8,128]{2,1,0:T(8,128)S(1)} %reduce_sum.59), channel_id=1, source_target_pairs={{0,8},{8,0},{16,24},{24,16},{32,40},{40,32},{48,56},{56,48},{64,72... | collective-permute-start | bytes 786440 | tf_op jit(solution)/shard_map/ppermute | solution.py:135
  251.1 6.5 %collective-permute-start.7 = (f32[64,8,128]{2,1,0:T(8,128)S(1)}, f32[64,8,128]{2,1,0:T(8,128)S(1)}, u32[]{:S(2)}, u32[]{:S(2)}) collective-permute-start(f32[64,8,128]{2,1,0:T(8,128)S(1)} %reduce_sum.59), channel_id=1, source_target_pairs={{0,4},{4,0},{1,5},{5,1},{2,6},{6,2},{3,7},{7,3},{8,12},{12,8},{9,1... | collective-permute-start | bytes 786440 | tf_op jit(solution)/shard_map/ppermute | solution.py:81
  261.1 6.2 %collective-permute-start.12 = (f32[64,8,128]{2,1,0:T(8,128)S(1)}, f32[64,8,128]{2,1,0:T(8,128)S(1)}, u32[]{:S(2)}, u32[]{:S(2)}) collective-permute-start(f32[64,8,128]{2,1,0:T(8,128)S(1)} %collective-permute-done.11), channel_id=1, source_target_pairs={{0,4},{4,0},{1,5},{5,1},{2,6},{6,2},{3,7},{7,3},{8,12},{12,8},{9,1... | collective-permute-start | bytes 786440 | tf_op jit(solution)/shard_map/ppermute | solution.py:81
Sparse Core Ops, SparseCore 0:
  9.5 116.9 all-gather.2
